TPU v7x, 32 devices: a whole 2x2x4 slice. The times are simulated.
32 devices in a mesh: dp: 8 (over z, core), tp: 4 (over y, x).
Axes of the slice: x: 2, y: 2, z: 4, core: 2. Of those that a mesh axis runs over, the one named last changes fastest.
Arguments:
- block_in: bfloat16 [3, 4096, 2048], P(None, ('dp', 'tp')), may hold values from -6 to 6
- cotangent: bfloat16 [3, 4096, 2048], P(None, ('dp', 'tp')), may hold values from -6 to 6
- segments: int32 [3, 4096], replicated, may hold values from 0 to 4095, as said below
- master: float32 [20736, 2048], P('tp', 'dp')
- moment_one: float32 [20736, 2048], P('tp', 'dp'), may hold values from -6 to 6
- moment_two: float32 [20736, 2048], P('tp', 'dp'), may hold values from 1 to 1000
- vectors: float32 [22656], replicated
- vec_one: float32 [22656], replicated, may hold values from -6 to 6
- vec_two: float32 [22656], replicated, may hold values from 1 to 1000
- step_count: int32 [1], replicated, may hold values from 1 to 9
- learning_rate: float32 [1], replicated, may hold values from 0.1 to 0.4
Outputs:
- block_out: bfloat16 [3, 4096, 2048], P(None, ('dp', 'tp'))
- grad_in: bfloat16 [3, 4096, 2048], P(None, ('dp', 'tp'))
- new_master: float32 [20736, 2048], P('tp', 'dp')
- new_moment_one: float32 [20736, 2048], P('tp', 'dp')
- new_moment_two: float32 [20736, 2048], P('tp', 'dp')
- new_vectors: float32 [22656], replicated
- new_vec_one: float32 [22656], replicated
- new_vec_two: float32 [22656], replicated
Inputs may be any that keep to these rules, and one draw needn't show every extreme that they name: `segments`: A token's id is the index, within its micro-batch, of its document's first token, so ids never fall along the tokens. Packed sequences begin at token 0 and at every token 1024 + k * 2048; a new document begins at each of them, so no document spans two sequences. The last token of each micro-batch is a document of its own.
All inputs are finite; a program needn't handle non-finite values.
Results may differ from a plain program's by a relative error of at most 0.015.
The roundings to bfloat16 on the way count: a program that leaves them out, or rounds other values in their place, can miss the bound.
Values may be sent and summed in bfloat16 or wider, within the bound.
No kernel may reach another device: no remote copies, remote signals or barrier semaphores. Data moves between devices by JAX's collectives and lax.ppermute only.
A program may use at most 384 MiB of HBM per device.

v0:
```python
import math

import jax
import jax.numpy as jnp
from jax import lax
from jax.sharding import PartitionSpec as P

D = 2048
H = 16
HD = 128
FF = 8192


norm_eps = 1e-05
gelu_coef = math.sqrt(2.0 / math.pi)
beta_one = 0.9
beta_two = 0.95
adam_eps = 1e-08
decay_rate = 0.1
masked_score = -1e30


def passed_along(value, axis, steps):
    count = lax.axis_size(axis)
    leading, last = (max(0, -steps), min(count, count - steps))
    return lax.ppermute(value, axis, [(source, source + steps) for source in range(leading, last)])


def layer_norm_fwd(values, gain, shift):
    mean_row = jnp.mean(values, -1, keepdims=True)
    centered = values - mean_row
    var_row = jnp.mean(centered * centered, -1, keepdims=True)
    inverse = lax.rsqrt(var_row + norm_eps)
    normed = centered * inverse
    return (normed * gain + shift, normed, inverse)


def layer_norm_back(grad_norm, normed, inverse, gain):
    scaled = grad_norm * gain
    return inverse * (
        scaled
        - jnp.mean(scaled, -1, keepdims=True)
        - normed * jnp.mean(scaled * normed, -1, keepdims=True)
    )


def gelu_tanh(values):
    inner = gelu_coef * (values + 0.044715 * values * values * values)
    return 0.5 * values * (1.0 + jnp.tanh(inner))


def gelu_slope(values):
    tangent = jnp.tanh(gelu_coef * (values + 0.044715 * values * values * values))
    return 0.5 * (1.0 + tangent) + 0.5 * values * (1.0 - tangent * tangent) * gelu_coef * (
        1.0 + 3.0 * 0.044715 * values * values
    )


def rows_by_rows(left, right):
    return lax.dot_general(
        left, right, (((1,), (1,)), ((), ())), preferred_element_type=jnp.float32
    )


def cols_by_cols(left, right):
    return lax.dot_general(
        left, right, (((0,), (0,)), ((), ())), preferred_element_type=jnp.float32
    )


def plain_dot(left, right):
    return jnp.dot(left, right, preferred_element_type=jnp.float32)


def vector_sizes():
    return [D, D, H * HD, HD, D, D, D, FF, D]


def widen(rows_low):
    return lax.all_gather(rows_low, "tp", axis=0, tiled=True)


def narrow(left, right):
    return lax.psum_scatter(plain_dot(left, right), "tp", scatter_dimension=0, tiled=True)


def place_piece(piece, start_at, total):
    return lax.dynamic_update_slice(jnp.zeros((total,), jnp.float32), piece, (start_at,))


def attend_forward(queries, keyvals, allowed):
    stretch_rows = queries.shape[0]
    heads_here = queries.shape[1] // HD
    key_part = keyvals[:, :HD]
    value_part = keyvals[:, HD:]
    score_scale = 1.0 / math.sqrt(HD)
    stacked = queries.reshape(stretch_rows, heads_here, HD).transpose(1, 0, 2)

    def one_head(query_head):
        scores = jnp.where(allowed, rows_by_rows(query_head, key_part) * score_scale, masked_score)
        row_peak = jnp.max(scores, -1, keepdims=True)
        exp_scores = jnp.exp(scores - row_peak)
        row_total = jnp.sum(exp_scores, -1, keepdims=True)
        probs_low = (exp_scores / row_total).astype(jnp.bfloat16)
        return (plain_dot(probs_low, value_part), (row_peak + jnp.log(row_total))[:, 0])

    head_outs, log_sums = lax.map(one_head, stacked)
    attended = (
        head_outs.transpose(1, 0, 2).reshape(stretch_rows, heads_here * HD).astype(jnp.bfloat16)
    )
    return (attended, log_sums)


def attend_backward(queries, keyvals, allowed, log_sums, grad_heads):
    stretch_rows = queries.shape[0]
    heads_here = queries.shape[1] // HD
    key_rows = keyvals.shape[0]
    key_part = keyvals[:, :HD]
    value_part = keyvals[:, HD:]
    score_scale = 1.0 / math.sqrt(HD)
    stacked = queries.reshape(stretch_rows, heads_here, HD).transpose(1, 0, 2)
    grad_stack = grad_heads.reshape(stretch_rows, heads_here, HD).transpose(1, 0, 2)

    def one_head(running, inputs):
        query_head, grad_head, log_head = inputs
        scores = jnp.where(allowed, rows_by_rows(query_head, key_part) * score_scale, masked_score)
        probs = jnp.exp(scores - log_head[:, None])
        probs_low = probs.astype(jnp.bfloat16)
        grad_probs = rows_by_rows(grad_head, value_part)
        delta_row = jnp.sum(probs * grad_probs, -1, keepdims=True)
        grad_scores = (probs * (grad_probs - delta_row)).astype(jnp.bfloat16)
        grad_query = plain_dot(grad_scores, key_part) * score_scale
        key_grad = cols_by_cols(grad_scores, query_head) * score_scale
        value_grad = cols_by_cols(probs_low, grad_head)
        return ((running[0] + key_grad, running[1] + value_grad), grad_query)

    zero_acc = jnp.zeros((key_rows, HD), jnp.float32)
    (key_total, value_total), grad_queries = lax.scan(
        one_head, (zero_acc, zero_acc), (stacked, grad_stack, log_sums)
    )
    grad_query_all = grad_queries.transpose(1, 0, 2).reshape(stretch_rows, heads_here * HD)
    return (grad_query_all, jnp.concatenate([key_total, value_total], 1))


def adam_step(weights, grads, first, second, step_count, learning_rate):
    steps_float = step_count[0].astype(jnp.float32)
    first_new = beta_one * first + (1.0 - beta_one) * grads
    second_new = beta_two * second + (1.0 - beta_two) * grads * grads
    corr_one = 1.0 - jnp.power(beta_one, steps_float)
    corr_two = 1.0 - jnp.power(beta_two, steps_float)
    update = first_new / corr_one / (jnp.sqrt(second_new / corr_two) + adam_eps)
    return (weights - learning_rate[0] * (update + decay_rate * weights), first_new, second_new)


def body(
    block_in,
    cotangent,
    segments,
    master,
    moment_one,
    moment_two,
    vectors,
    vec_one,
    vec_two,
    step_count,
    learning_rate,
):
    tp_size = lax.axis_size("tp")
    tp_index = lax.axis_index("tp")
    dp_index = lax.axis_index("dp")
    micro_count, local_rows, model_width = block_in.shape
    stretch_rows = local_rows * tp_size
    query_rows = H * HD // tp_size
    kv_share = 2 * HD // tp_size
    ff_rows = FF // tp_size
    bounds = [query_rows, kv_share, query_rows, ff_rows, ff_rows]
    vec_pieces = []
    cursor = 0
    for length in vector_sizes():
        vec_pieces.append(vectors[cursor : cursor + length])
        cursor += length
    (
        gain_one,
        shift_one,
        bias_query_all,
        bias_value,
        bias_out,
        gain_two,
        shift_two,
        bias_up_all,
        bias_down,
    ) = vec_pieces
    bias_query = lax.dynamic_slice_in_dim(bias_query_all, tp_index * query_rows, query_rows)
    bias_up = lax.dynamic_slice_in_dim(bias_up_all, tp_index * ff_rows, ff_rows)
    keyval_bias = jnp.concatenate([jnp.zeros((HD,), jnp.float32), bias_value])
    positions = jnp.arange(stretch_rows)
    causal = positions[None, :] <= positions[:, None]
    stretch_slot = jnp.minimum((dp_index + 2) % 4, dp_index)
    block_grads = jnp.zeros((master.shape[0], model_width), jnp.float32)
    vec_grads = jnp.zeros(vectors.shape, jnp.float32)
    outputs = []
    input_grads = []
    for mb_index in range(micro_count):
        gathered = lax.all_gather(master.astype(jnp.bfloat16), "dp", axis=1, tiled=True)
        pieces = []
        row_start = 0
        for unpack_length in bounds:
            pieces.append(gathered[row_start : row_start + unpack_length])
            row_start += unpack_length
        w_query, kv_piece, w_out, w_up, w_down = pieces
        w_keyval = lax.all_gather(kv_piece, "tp", axis=0, tiled=True)
        block_rows = block_in[mb_index].astype(jnp.float32)
        ln_out_one, normed_one, inverse_one = layer_norm_fwd(block_rows, gain_one, shift_one)
        hidden_one = ln_out_one.astype(jnp.bfloat16)
        hidden_all = widen(hidden_one)
        queries = (rows_by_rows(hidden_all, w_query) + bias_query).astype(jnp.bfloat16)
        kv_local = (rows_by_rows(hidden_one, w_keyval) + keyval_bias).astype(jnp.bfloat16)
        kv_own = lax.all_gather(kv_local, "tp", axis=0, tiled=True)
        seg_row = segments[mb_index]
        seg_own = lax.dynamic_slice_in_dim(seg_row, dp_index * stretch_rows, stretch_rows)
        kv_parts = []
        allow_parts = []
        for back in range(3, 0, -1):
            kv_parts.append(passed_along(kv_own, "dp", back))
            seg_back = lax.dynamic_slice_in_dim(
                seg_row, jnp.maximum(dp_index - back, 0) * stretch_rows, stretch_rows
            )
            allow_parts.append((seg_own[:, None] == seg_back[None, :]) & (stretch_slot >= back))
        keyvals = jnp.concatenate(kv_parts + [kv_own], 0)
        allowed = jnp.concatenate(
            allow_parts + [(seg_own[:, None] == seg_own[None, :]) & causal], 1
        )
        attended, log_sums = attend_forward(queries, keyvals, allowed)
        residual = block_rows + narrow(attended, w_out) + bias_out
        ln_out_two, normed_two, inverse_two = layer_norm_fwd(residual, gain_two, shift_two)
        hidden_two = ln_out_two.astype(jnp.bfloat16)
        hidden_two_all = widen(hidden_two)
        pre_act = rows_by_rows(hidden_two_all, w_up) + bias_up
        activated = gelu_tanh(pre_act).astype(jnp.bfloat16)
        result = residual + narrow(activated, w_down) + bias_down
        outputs.append(result.astype(jnp.bfloat16))
        grad_low = cotangent[mb_index]
        grad_low_all = widen(grad_low)
        grad_down = cols_by_cols(activated, grad_low_all)
        grad_bias_down = jnp.sum(grad_low.astype(jnp.float32), 0)
        grad_pre = (rows_by_rows(grad_low_all, w_down) * gelu_slope(pre_act)).astype(jnp.bfloat16)
        grad_up = cols_by_cols(grad_pre, hidden_two_all)
        grad_bias_up = jnp.sum(grad_pre.astype(jnp.float32), 0)
        grad_hidden_two = narrow(grad_pre, w_up)
        grad_resid = grad_low.astype(jnp.float32) + layer_norm_back(
            grad_hidden_two, normed_two, inverse_two, gain_two
        )
        grad_gain_two = jnp.sum(grad_hidden_two * normed_two, 0)
        grad_shift_two = jnp.sum(grad_hidden_two, 0)
        grad_att = grad_resid.astype(jnp.bfloat16)
        grad_att_all = widen(grad_att)
        grad_out_w = cols_by_cols(attended, grad_att_all)
        grad_bias_out = jnp.sum(grad_resid, 0)
        grad_heads = rows_by_rows(grad_att_all, w_out).astype(jnp.bfloat16)
        grad_query_f, grad_keyvals = attend_backward(
            queries, keyvals, allowed, log_sums, grad_heads
        )
        grad_query = grad_query_f.astype(jnp.bfloat16)
        grad_bias_query = jnp.sum(grad_query.astype(jnp.float32), 0)
        grad_w_query = cols_by_cols(grad_query, hidden_all)
        kv_total = grad_keyvals[3 * stretch_rows :]
        for back in range(1, 4):
            piece_start = (3 - back) * stretch_rows
            kv_total = kv_total + passed_along(
                grad_keyvals[piece_start : piece_start + stretch_rows], "dp", -back
            )
        grad_kv_rows = lax.psum_scatter(kv_total, "tp", scatter_dimension=0, tiled=True).astype(
            jnp.bfloat16
        )
        grad_bias_value = jnp.sum(grad_kv_rows[:, HD:].astype(jnp.float32), 0)
        grad_w_keyval = lax.psum_scatter(
            cols_by_cols(grad_kv_rows, hidden_one).astype(jnp.bfloat16),
            "tp",
            scatter_dimension=0,
            tiled=True,
        ).astype(jnp.float32)
        grad_hidden_one = narrow(grad_query, w_query) + plain_dot(grad_kv_rows, w_keyval)
        grad_rows = grad_resid + layer_norm_back(grad_hidden_one, normed_one, inverse_one, gain_one)
        grad_gain_one = jnp.sum(grad_hidden_one * normed_one, 0)
        grad_shift_one = jnp.sum(grad_hidden_one, 0)
        input_grads.append(grad_rows.astype(jnp.bfloat16))
        batch_grads = jnp.concatenate(
            [grad_w_query, grad_w_keyval, grad_out_w, grad_up, grad_down], 0
        )
        block_grads = block_grads + batch_grads
        vec_batch = jnp.concatenate(
            [
                grad_gain_one,
                grad_shift_one,
                place_piece(grad_bias_query, tp_index * query_rows, H * HD),
                grad_bias_value,
                grad_bias_out,
                grad_gain_two,
                grad_shift_two,
                place_piece(grad_bias_up, tp_index * ff_rows, FF),
                grad_bias_down,
            ]
        )
        vec_grads = vec_grads + vec_batch
    shard_grads = lax.psum_scatter(block_grads, "dp", scatter_dimension=1, tiled=True)
    vec_total = lax.psum(vec_grads, ("dp", "tp"))
    new_master, new_moment_one, new_moment_two = adam_step(
        master, shard_grads, moment_one, moment_two, step_count, learning_rate
    )
    new_vectors, new_vec_one, new_vec_two = adam_step(
        vectors, vec_total, vec_one, vec_two, step_count, learning_rate
    )
    return (
        jnp.stack(outputs),
        jnp.stack(input_grads),
        new_master,
        new_moment_one,
        new_moment_two,
        new_vectors,
        new_vec_one,
        new_vec_two,
    )


def solution(mesh):
    in_specs = (
        P(None, ("dp", "tp"), None),
        P(None, ("dp", "tp"), None),
        P(),
        P("tp", "dp"),
        P("tp", "dp"),
        P("tp", "dp"),
        P(),
        P(),
        P(),
        P(),
        P(),
    )
    out_specs = (
        P(None, ("dp", "tp"), None),
        P(None, ("dp", "tp"), None),
        P("tp", "dp"),
        P("tp", "dp"),
        P("tp", "dp"),
        P(),
        P(),
        P(),
    )
    return jax.shard_map(body, mesh=mesh, in_specs=in_specs, out_specs=out_specs, check_vma=False)
```

profile of v0, /device:TPU:0, one launch (start us, length us, event | category | flops | bytes accessed | tf_op | source)
XLA Modules:
  0.0 2228.4 jit_solution(4555082235540098901)
XLA Ops:
  12.0 191.1 %all-gather.20.cloned.1.call-done = bf16[5184,2048]{1,0:T(8,128)(2,1)} async-done(((bf16[5184,256]{1,0:T(8,128)(2,1)}), bf16[5184,2048]{1,0:T(8,128)(2,1)}) %all-gather.20.cloned.1.call-update) | async-done | bytes 21233680 | tf_op jit(solution)/shard_map/all_gather | solution.py:204
  211.7 18.7 all-gather.22.cloned.1.call-done
  232.1 9.0 all_gather.64
  251.4 16.2 all-gather.30.cloned.1.call-done
  274.1 18.7 while.83
  292.8 5.8 fusion.196
  302.2 8.9 all_gather.61
  329.0 11.7 while.82
  349.0 10.4 all_gather.58
  360.9 6.8 collective-permute-start.1
  367.7 5.1 collective-permute-start
  380.3 11.7 while.81
  393.2 5.2 fusion.200
  399.5 56.5 %reduce-scatter.24.cloned.1.call-done = f32[128,2048]{1,0:T(8,128)} async-done(((f32[512,2048]{1,0:T(8,128)}), f32[128,2048]{1,0:T(8,128)}) %reduce-scatter.24.cloned.1.call-update) | async-done | bytes 1048592 | tf_op jit(solution)/shard_map/reduce_scatter | solution.py:84
  456.1 56.3 %reduce-scatter.20.cloned.1.call-done = f32[128,2048]{1,0:T(8,128)} async-done(((f32[512,2048]{1,0:T(8,128)}), f32[128,2048]{1,0:T(8,128)}) %reduce-scatter.20.cloned.1.call-update) | async-done | bytes 1048592 | tf_op jit(solution)/shard_map/reduce_scatter | solution.py:84
  521.3 31.5 %all-gather.24.cloned.1.call-done = bf16[512,2048]{1,0:T(8,128)(2,1)} async-done(((bf16[128,2048]{1,0:T(8,128)(2,1)}), bf16[512,2048]{1,0:T(8,128)(2,1)}) %all-gather.24.cloned.1.call-update) | async-done | bytes 2097168 | tf_op jit(solution)/shard_map/all_gather | solution.py:80
  552.8 10.6 fusion.113
  563.4 27.2 %all-gather.40.cloned.1.call-done = bf16[1,512,2048]{2,1,0:T(8,128)(2,1)} async-done(((bf16[1,128,2048]{2,1,0:T(8,128)(2,1)}), bf16[1,512,2048]{2,1,0:T(8,128)(2,1)}) %all-gather.40.cloned.1.call-update) | async-done | bytes 2097168 | tf_op jit(solution)/shard_map/all_gather | solution.py:80
  590.6 11.0 convert_reduce_fusion.2
  602.9 9.4 fusion.107
  612.6 15.9 all-gather.28.cloned.1.call-done
  628.5 10.6 fusion.111
  639.1 26.6 %all-gather.42.cloned.1.call-done = bf16[1,512,2048]{2,1,0:T(8,128)(2,1)} async-done(((bf16[1,128,2048]{2,1,0:T(8,128)(2,1)}), bf16[1,512,2048]{2,1,0:T(8,128)(2,1)}) %all-gather.42.cloned.1.call-update) | async-done | bytes 2097168 | tf_op jit(solution)/shard_map/all_gather | solution.py:80
  665.7 11.0 convert_reduce_fusion.1
  678.0 9.4 fusion.105
  687.7 15.3 all-gather.32.cloned.1.call-done
  703.0 10.6 fusion.109
  713.6 26.6 %all-gather.44.cloned.1.call-done = bf16[1,512,2048]{2,1,0:T(8,128)(2,1)} async-done(((bf16[1,128,2048]{2,1,0:T(8,128)(2,1)}), bf16[1,512,2048]{2,1,0:T(8,128)(2,1)}) %all-gather.44.cloned.1.call-update) | async-done | bytes 2097168 | tf_op jit(solution)/shard_map/all_gather | solution.py:80
  740.2 11.0 convert_reduce_fusion
  752.5 9.5 fusion.103
  762.5 11.9 fusion.101
  774.5 11.8 fusion.97
  786.4 11.7 fusion.99
  798.2 53.9 %reduce-scatter.38.cloned.1.call-done = f32[128,2048]{1,0:T(8,128)} async-done(((f32[512,2048]{1,0:T(8,128)}), f32[128,2048]{1,0:T(8,128)}) %reduce-scatter.38.cloned.1.call-update) | async-done | bytes 1048592 | tf_op jit(solution)/shard_map/reduce_scatter | solution.py:84
  852.1 55.8 %reduce-scatter.44.cloned.1.call-done = f32[128,2048]{1,0:T(8,128)} async-done(((f32[512,2048]{1,0:T(8,128)}), f32[128,2048]{1,0:T(8,128)}) %reduce-scatter.44.cloned.1.call-update) | async-done | bytes 1048592 | tf_op jit(solution)/shard_map/reduce_scatter | solution.py:84
  911.7 51.8 %reduce-scatter.22.cloned.1.call-done = f32[128,2048]{1,0:T(8,128)} async-done(((f32[512,2048]{1,0:T(8,128)}), f32[128,2048]{1,0:T(8,128)}) %reduce-scatter.22.cloned.1.call-update) | async-done | bytes 1048592 | tf_op jit(solution)/shard_map/reduce_scatter | solution.py:84
  963.5 56.0 %reduce-scatter.30.cloned.1.call-done = f32[128,2048]{1,0:T(8,128)} async-done(((f32[512,2048]{1,0:T(8,128)}), f32[128,2048]{1,0:T(8,128)}) %reduce-scatter.30.cloned.1.call-update) | async-done | bytes 1048592 | tf_op jit(solution)/shard_map/reduce_scatter | solution.py:84
  1019.5 5.5 fusion.227
  1026.9 48.1 %reduce-scatter.26.cloned.1.call-done = f32[128,2048]{1,0:T(8,128)} async-done(((f32[512,2048]{1,0:T(8,128)}), f32[128,2048]{1,0:T(8,128)}) %reduce-scatter.26.cloned.1.call-update) | async-done | bytes 1048592 | tf_op jit(solution)/shard_map/reduce_scatter | solution.py:84
  1081.6 30.8 %all-gather.34.cloned.1.call-done = bf16[512,2048]{1,0:T(8,128)(2,1)} async-done(((bf16[128,2048]{1,0:T(8,128)(2,1)}), bf16[512,2048]{1,0:T(8,128)(2,1)}) %all-gather.34.cloned.1.call-update) | async-done | bytes 2097168 | tf_op jit(solution)/shard_map/all_gather | solution.py:80
  1119.5 51.4 %while.84 = (s32[]{:T(128)}, f32[2048,128]{1,0:T(8,128)}, f32[2048,128]{1,0:T(8,128)}, bf16[4,512,128]{1,2,0:T(8,128)(2,1)}, bf16[4,512,128]{2,1,0:T(8,128)(2,1)...) while((s32[]{:T(128)}, f32[2048,128]{1,0:T(8,128)}, ...), condition=%wide.region_35.36_spmd.clone, body=%wide.region_33.35_spmd.clone.sunk | while | flops 1353055744 | bytes 49948912 | solution.py:138
  1175.5 11.5 all-gather.38.cloned.1.call-done
  1194.3 51.2 %while.86 = (s32[]{:T(128)}, f32[2048,128]{1,0:T(8,128)}, f32[2048,128]{1,0:T(8,128)}, bf16[4,512,128]{1,2,0:T(8,128)(2,1)}, bf16[4,512,128]{2,1,0:T(8,128)(2,1)...) while((s32[]{:T(128)}, f32[2048,128]{1,0:T(8,128)}, ...), condition=%wide.region_55.56_spmd.clone, body=%wide.region_53.55_spmd.clone.sunk | while | flops 1353055744 | bytes 49948912 | solution.py:138
  1259.4 8.4 collective-permute-done.11
  1267.7 11.2 collective-permute-done.10
  1280.8 44.9 %while.85 = (s32[]{:T(128)}, f32[2048,128]{1,0:T(8,128)S(1)}, f32[2048,128]{1,0:T(8,128)}, bf16[4,512,128]{1,2,0:T(8,128)(2,1)}, bf16[4,512,128]{2,1,0:T(8,128)(...) while((s32[]{:T(128)}, f32[2048,128]{1,0:T(8,128)S(1)}, ...), condition=%wide.region_45.46_spmd.clone, body=%wide.region_43.45_spmd.clone.sunk | while | flops 1353055744 | bytes 49948912 | solution.py:138
  1340.6 23.9 %collective-permute-done.14 = f32[512,256]{1,0:T(8,128)S(1)} collective-permute-done((f32[512,256]{1,0:T(8,128)S(1)}, f32[512,256]{1,0:T(8,128)S(1)}, u32[]{:S(2)}, u32[]{:S(2)}) %collective-permute-start.14) | collective-permute-done | bytes 524320 | tf_op jit(solution)/shard_map/ppermute | solution.py:26
  1364.5 11.7 collective-permute-done.13
  1383.2 23.6 %reduce-scatter.42.cloned.1.call-done = f32[128,256]{1,0:T(8,128)} async-done(((f32[512,256]{1,0:T(8,128)}), f32[128,256]{1,0:T(8,128)}) %reduce-scatter.42.cloned.1.call-update) | async-done | bytes 131088 | tf_op jit(solution)/shard_map/reduce_scatter | solution.py:272
  1444.0 8.3 convolution_dynamic-update-slice_fusion.5
  1452.3 16.4 reduce-scatter.54.cloned.1.call-done
  1475.4 24.0 %reduce-scatter.52.cloned.1.call-done = bf16[64,2048]{1,0:T(8,128)(2,1)} async-done(((bf16[256,2048]{1,0:T(8,128)(2,1)}), bf16[64,2048]{1,0:T(8,128)(2,1)}) %reduce-scatter.52.cloned.1.call-update) | async-done | bytes 262160 | tf_op jit(solution)/shard_map/reduce_scatter | solution.py:276
  1504.7 8.4 convolution_dynamic-update-slice_fusion.1
  1513.1 8.5 convolution_dynamic-update-slice_fusion.3
  1521.7 8.8 convolution_dynamic-update-slice_fusion.4
  1530.5 9.0 convolution_dynamic-update-slice_fusion
  1539.5 8.8 convolution_dynamic-update-slice_fusion.2
  1548.3 7.0 reduce-scatter.40.cloned.1.call-done
  1557.8 53.8 %reduce-scatter.34.cloned.1.call-done = f32[128,2048]{1,0:T(8,128)} async-done(((f32[512,2048]{1,0:T(8,128)}), f32[128,2048]{1,0:T(8,128)}) %reduce-scatter.34.cloned.1.call-update) | async-done | bytes 1048592 | tf_op jit(solution)/shard_map/reduce_scatter | solution.py:84
  1614.1 53.4 %reduce-scatter.46.cloned.1.call-done = f32[128,2048]{1,0:T(8,128)} async-done(((f32[512,2048]{1,0:T(8,128)}), f32[128,2048]{1,0:T(8,128)}) %reduce-scatter.46.cloned.1.call-update) | async-done | bytes 1048592 | tf_op jit(solution)/shard_map/reduce_scatter | solution.py:84
  1672.9 55.6 %add_add_fusion = f32[5184,2048]{1,0:T(8,128)} fusion(f32[5184,2048]{1,0:T(8,128)} %convolution_dynamic-update-slice_fusion, f32[5184,2048]{1,0:T(8,128)} %convolution_dynamic-update-slice_fusion.4, f32[5184,2048]{1,0:T(8,128)} %convolution_dynamic-update-slice_fusion.2), kind=kLoop, calls=%fused_computation.105 | loop fusion | flops 21233664 | bytes 169869312 | tf_op jit(solution)/shard_map/add | solution.py:290
  1737.0 57.1 %all-reduce.3.cloned.1.call-done = f32[22656]{0:T(1024)} async-done(((f32[22656]{0:T(1024)}), f32[22656]{0:T(1024)}) %all-reduce.3.cloned.1.call-update) | async-done | bytes 90640 | tf_op jit(solution)/shard_map/psum | solution.py:306
  1795.7 410.9 %reduce-scatter.56.cloned.1.call-done = f32[5184,256]{1,0:T(8,128)} async-done(((f32[5184,2048]{1,0:T(8,128)}), f32[5184,256]{1,0:T(8,128)}) %reduce-scatter.56.cloned.1.call-update) | async-done | bytes 5308432 | tf_op jit(solution)/shard_map/reduce_scatter | solution.py:305
  2206.6 14.4 multiply_subtract_fusion
  (776 shorter events, 409.5 us)
Async XLA Ops:
  7.2 196.0 %all-gather.20.cloned.1.call-start = ((), (), s32[]{:S(2)}) async-start(), calls=%async_computation.20 | async-start | bytes 23887872 | tf_op jit(solution)/shard_map/all_gather | solution.py:204
  11.6 193.9 %copy-start.71 = (f32[22656]{0:T(1024)S(1)}, f32[22656]{0:T(1024)}, u32[]{:S(2)}) copy-start(f32[22656]{0:T(1024)} %param.29) | copy-start | bytes 271876
  11.6 197.5 %copy-start.81 = (s32[3,4096]{1,0:T(4,128)S(1)}, s32[3,4096]{1,0:T(4,128)}, u32[]{:S(2)}) copy-start(s32[3,4096]{1,0:T(4,128)} %param.25) | copy-start | bytes 147460
  11.6 197.6 %slice-start = ((f32[22656]{0:T(1024)}), f32[128]{0:T(128)S(1)}, s32[]{:S(2)}) async-start(f32[22656]{0:T(1024)} %param.29), calls=%async_computation.53 | async-start | bytes 1024 | tf_op jit(solution)/shard_map/slice | solution.py:180
  11.6 218.7 %all-gather.22.cloned.1.call-start = ((), (), s32[]{:S(2)}) async-start(), calls=%async_computation.21 | async-start | bytes 1310720 | tf_op jit(solution)/shard_map/all_gather | solution.py:211
  12.0 197.1 %copy-start.100 = (f32[128]{0:T(128)}, f32[128]{0:T(128)S(1)}, u32[]{:S(2)}) copy-start(f32[128]{0:T(128)S(1)} %broadcast_multiply_fusion.17) | copy-start | bytes 1540
  12.0 197.1 %copy-start.96 = (f32[128]{0:T(128)}, f32[128]{0:T(128)S(1)}, u32[]{:S(2)}) copy-start(f32[128]{0:T(128)S(1)} %get-tuple-element.652) | copy-start | bytes 1540
  12.0 197.1 %copy-start.98 = (f32[128]{0:T(128)}, f32[128]{0:T(128)S(1)}, u32[]{:S(2)}) copy-start(f32[128]{0:T(128)S(1)} %get-tuple-element.651) | copy-start | bytes 1540
  204.8 62.8 %all-gather.30.cloned.1.call-start = ((), (), s32[]{:S(2)}) async-start(), calls=%async_computation.29 | async-start | bytes 2621440 | tf_op jit(solution)/shard_map/all_gather | solution.py:80
  207.8 113.2 %all-gather.26.cloned.1.call-start = ((), (), s32[]{:S(2)}) async-start(), calls=%async_computation.25 | async-start | bytes 2621440 | tf_op jit(solution)/shard_map/all_gather | solution.py:80
  208.4 164.5 %all-gather.18.cloned.1.call-start = ((), (), s32[]{:S(2)}) async-start(), calls=%async_computation.19 | async-start | bytes 2621440 | tf_op jit(solution)/shard_map/all_gather | solution.py:80
  209.0 190.5 %reduce-scatter.28.cloned.1.call-start = ((), (), s32[]{:S(2)}) async-start(), calls=%async_computation.30 | async-start | bytes 5242880 | tf_op jit(solution)/shard_map/reduce_scatter | solution.py:84
  241.1 32.1 %collective-permute-start.8 = (bf16[512,256]{1,0:T(8,128)(2,1)S(1)}, bf16[512,256]{1,0:T(8,128)(2,1)S(1)}, u32[]{:S(2)}, u32[]{:S(2)}) collective-permute-start(bf16[512,256]{1,0:T(8,128)(2,1)S(1)} %all_gather.64), channel_id=1, source_target_pairs={{0,4},{4,8},{8,12},{12,16},{16,20},{20,24},{24,28},{1,5},{5,9},{9,... | collective-permute-start | bytes 786440 | tf_op jit(solution)/shard_map/ppermute | solution.py:26
  242.4 30.7 %collective-permute-start.7 = (bf16[512,256]{1,0:T(8,128)(2,1)S(1)}, bf16[512,256]{1,0:T(8,128)(2,1)S(1)}, u32[]{:S(2)}, u32[]{:S(2)}) collective-permute-start(bf16[512,256]{1,0:T(8,128)(2,1)S(1)} %all_gather.64), channel_id=1, source_target_pairs={{0,8},{4,12},{8,16},{12,20},{16,24},{20,28},{1,9},{5,13},{9,17},{1... | collective-permute-start | bytes 786440 | tf_op jit(solution)/shard_map/ppermute | solution.py:26
  246.4 25.7 %collective-permute-start.6 = (bf16[512,256]{1,0:T(8,128)(2,1)S(1)}, bf16[512,256]{1,0:T(8,128)(2,1)}, u32[]{:S(2)}, u32[]{:S(2)}) collective-permute-start(bf16[512,256]{1,0:T(8,128)(2,1)S(1)} %all_gather.64), channel_id=1, source_target_pairs={{0,12},{4,16},{8,20},{12,24},{16,28},{1,13},{5,17},{9,21},{13,25},... | collective-permute-start | bytes 786440 | tf_op jit(solution)/shard_map/ppermute | solution.py:26
  298.7 157.4 %reduce-scatter.24.cloned.1.call-start = ((), (), s32[]{:S(2)}) async-start(), calls=%async_computation.26 | async-start | bytes 5242880 | tf_op jit(solution)/shard_map/reduce_scatter | solution.py:84
  311.2 17.7 collective-permute-start.5
  312.5 16.3 collective-permute-start.4
  316.5 12.3 collective-permute-start.3
  346.9 165.5 %reduce-scatter.20.cloned.1.call-start = ((), (), s32[]{:S(2)}) async-start(), calls=%async_computation.22 | async-start | bytes 5242880 | tf_op jit(solution)/shard_map/reduce_scatter | solution.py:84
  359.4 20.8 collective-permute-start.2
  360.9 19.2 collective-permute-start.1
  367.7 12.3 collective-permute-start
  398.5 154.3 %all-gather.24.cloned.1.call-start = ((), (), s32[]{:S(2)}) async-start(), calls=%async_computation.23 | async-start | bytes 2621440 | tf_op jit(solution)/shard_map/all_gather | solution.py:80
  517.3 73.2 %all-gather.40.cloned.1.call-start = ((), (), s32[]{:S(2)}) async-start(), calls=%async_computation.50 | async-start | bytes 2621440 | tf_op jit(solution)/shard_map/all_gather | solution.py:80
  518.6 109.9 %all-gather.28.cloned.1.call-start = ((), (), s32[]{:S(2)}) async-start(), calls=%async_computation.27 | async-start | bytes 2621440 | tf_op jit(solution)/shard_map/all_gather | solution.py:80
  519.3 146.3 %all-gather.42.cloned.1.call-start = ((), (), s32[]{:S(2)}) async-start(), calls=%async_computation.51 | async-start | bytes 2621440 | tf_op jit(solution)/shard_map/all_gather | solution.py:80
  519.9 183.1 %all-gather.32.cloned.1.call-start = ((), (), s32[]{:S(2)}) async-start(), calls=%async_computation.31 | async-start | bytes 2621440 | tf_op jit(solution)/shard_map/all_gather | solution.py:80
  520.6 219.5 %all-gather.44.cloned.1.call-start = ((), (), s32[]{:S(2)}) async-start(), calls=%async_computation.52 | async-start | bytes 2621440 | tf_op jit(solution)/shard_map/all_gather | solution.py:80
  521.2 277.0 %reduce-scatter.32.cloned.1.call-start = ((), (), s32[]{:S(2)}) async-start(), calls=%async_computation.33 | async-start | bytes 5242880 | tf_op jit(solution)/shard_map/reduce_scatter | solution.py:84
  521.3 265.1 %copy-start.91 = (f32[2048]{0:T(1024)}, f32[2048]{0:T(1024)S(1)}, u32[]{:S(2)}) copy-start(f32[2048]{0:T(1024)S(1)} %dynamic_slice.85) | copy-start | bytes 24580
  612.4 239.8 %reduce-scatter.38.cloned.1.call-start = ((), (), s32[]{:S(2)}) async-start(), calls=%async_computation.37 | async-start | bytes 5242880 | tf_op jit(solution)/shard_map/reduce_scatter | solution.py:84
  687.4 220.5 %reduce-scatter.44.cloned.1.call-start = ((), (), s32[]{:S(2)}) async-start(), calls=%async_computation.41 | async-start | bytes 5242880 | tf_op jit(solution)/shard_map/reduce_scatter | solution.py:84
  762.0 201.5 %reduce-scatter.22.cloned.1.call-start = ((), (), s32[]{:S(2)}) async-start(), calls=%async_computation.24 | async-start | bytes 5242880 | tf_op jit(solution)/shard_map/reduce_scatter | solution.py:84
  774.5 245.0 %reduce-scatter.30.cloned.1.call-start = ((), (), s32[]{:S(2)}) async-start(), calls=%async_computation.32 | async-start | bytes 5242880 | tf_op jit(solution)/shard_map/reduce_scatter | solution.py:84
  786.3 288.7 %reduce-scatter.26.cloned.1.call-start = ((), (), s32[]{:S(2)}) async-start(), calls=%async_computation.28 | async-start | bytes 5242880 | tf_op jit(solution)/shard_map/reduce_scatter | solution.py:84
  798.1 221.3 %copy-start.77 = (f32[2048]{0:T(1024)S(1)}, f32[2048]{0:T(1024)}, u32[]{:S(2)}) copy-start(f32[2048]{0:T(1024)} %get-tuple-element.599) | copy-start | bytes 24580
  798.1 314.2 %all-gather.34.cloned.1.call-start = ((), (), s32[]{:S(2)}) async-start(), calls=%async_computation.34 | async-start | bytes 2621440 | tf_op jit(solution)/shard_map/all_gather | solution.py:80
  1026.8 144.1 %all-gather.36.cloned.1.call-start = ((), (), s32[]{:S(2)}) async-start(), calls=%async_computation.38 | async-start | bytes 2621440 | tf_op jit(solution)/shard_map/all_gather | solution.py:80
  1080.4 106.6 %all-gather.38.cloned.1.call-start = ((), (), s32[]{:S(2)}) async-start(), calls=%async_computation.42 | async-start | bytes 2621440 | tf_op jit(solution)/shard_map/all_gather | solution.py:80
  1081.5 296.7 %reduce-scatter.36.cloned.1.call-start = ((), (), s32[]{:S(2)}) async-start(), calls=%async_computation.36 | async-start | bytes 655360 | tf_op jit(solution)/shard_map/reduce_scatter | solution.py:272
  1248.5 9.5 collective-permute-start.9
  1249.8 17.9 collective-permute-start.11
  1251.5 27.4 %collective-permute-start.10 = (f32[512,256]{1,0:T(8,128)S(1)}, f32[512,256]{1,0:T(8,128)S(1)}, u32[]{:S(2)}, u32[]{:S(2)}) collective-permute-start(f32[512,256]{1,0:T(8,128)S(1)} %get-tuple-element.569), channel_id=1, source_target_pairs={{8,0},{12,4},{16,8},{20,12},{24,16},{28,20},{9,1},{13,5},{17,9},{2... | collective-permute-start | bytes 1572872 | tf_op jit(solution)/shard_map/ppermute | solution.py:26
  1255.5 73.5 %collective-permute-start.15 = (f32[512,256]{1,0:T(8,128)}, f32[512,256]{1,0:T(8,128)}, u32[]{:S(2)}, u32[]{:S(2)}) collective-permute-start(f32[512,256]{1,0:T(8,128)} %get-tuple-element.573), channel_id=1, source_target_pairs={{4,0},{8,4},{12,8},{16,12},{20,16},{24,20},{28,24},{5,1},{9,5},{13... | collective-permute-start | bytes 1572872 | tf_op jit(solution)/shard_map/ppermute | solution.py:26
  1256.7 72.2 %collective-permute-start.17 = (f32[512,256]{1,0:T(8,128)}, f32[512,256]{1,0:T(8,128)}, u32[]{:S(2)}, u32[]{:S(2)}) collective-permute-start(f32[512,256]{1,0:T(8,128)} %get-tuple-element.574), channel_id=1, source_target_pairs={{12,0},{16,4},{20,8},{24,12},{28,16},{13,1},{17,5},{21,9},{25,13},... | collective-permute-start | bytes 1572872 | tf_op jit(solution)/shard_map/ppermute | solution.py:26
  1258.1 70.9 %collective-permute-start.16 = (f32[512,256]{1,0:T(8,128)}, f32[512,256]{1,0:T(8,128)}, u32[]{:S(2)}, u32[]{:S(2)}) collective-permute-start(f32[512,256]{1,0:T(8,128)} %get-tuple-element.575), channel_id=1, source_target_pairs={{8,0},{12,4},{16,8},{20,12},{24,16},{28,20},{9,1},{13,5},{17,9},{2... | collective-permute-start | bytes 1572872 | tf_op jit(solution)/shard_map/ppermute | solution.py:26
  1279.9 100.8 %reduce-scatter.48.cloned.1.call-start = ((), (), s32[]{:S(2)}) async-start(), calls=%async_computation.44 | async-start | bytes 655360 | tf_op jit(solution)/shard_map/reduce_scatter | solution.py:272
  1331.5 75.3 %reduce-scatter.42.cloned.1.call-start = ((), (), s32[]{:S(2)}) async-start(), calls=%async_computation.40 | async-start | bytes 655360 | tf_op jit(solution)/shard_map/reduce_scatter | solution.py:272
  1333.1 7.5 collective-permute-start.12
  1334.4 30.1 %collective-permute-start.14 = (f32[512,256]{1,0:T(8,128)S(1)}, f32[512,256]{1,0:T(8,128)S(1)}, u32[]{:S(2)}, u32[]{:S(2)}) collective-permute-start(f32[512,256]{1,0:T(8,128)S(1)} %get-tuple-element.571), channel_id=1, source_target_pairs={{12,0},{16,4},{20,8},{24,12},{28,16},{13,1},{17,5},{21,9},{25,13},... | collective-permute-start | bytes 1572872 | tf_op jit(solution)/shard_map/ppermute | solution.py:26
  1335.7 40.4 %collective-permute-start.13 = (f32[512,256]{1,0:T(8,128)S(1)}, f32[512,256]{1,0:T(8,128)S(1)}, u32[]{:S(2)}, u32[]{:S(2)}) collective-permute-start(f32[512,256]{1,0:T(8,128)S(1)} %get-tuple-element.572), channel_id=1, source_target_pairs={{8,0},{12,4},{16,8},{20,12},{24,16},{28,20},{9,1},{13,5},{17,9},{2... | collective-permute-start | bytes 1572872 | tf_op jit(solution)/shard_map/ppermute | solution.py:26
  1378.2 60.6 %reduce-scatter.50.cloned.1.call-start = ((), (), s32[]{:S(2)}) async-start(), calls=%async_computation.45 | async-start | bytes 1310720 | tf_op jit(solution)/shard_map/reduce_scatter | solution.py:276
  1380.7 88.1 %reduce-scatter.54.cloned.1.call-start = ((), (), s32[]{:S(2)}) async-start(), calls=%async_computation.47 | async-start | bytes 1310720 | tf_op jit(solution)/shard_map/reduce_scatter | solution.py:276
  1383.1 116.3 %reduce-scatter.52.cloned.1.call-start = ((), (), s32[]{:S(2)}) async-start(), calls=%async_computation.46 | async-start | bytes 1310720 | tf_op jit(solution)/shard_map/reduce_scatter | solution.py:276
  1409.2 146.1 %reduce-scatter.40.cloned.1.call-start = ((), (), s32[]{:S(2)}) async-start(), calls=%async_computation.39 | async-start | bytes 5242880 | tf_op jit(solution)/shard_map/reduce_scatter | solution.py:84
  1414.2 197.3 %reduce-scatter.34.cloned.1.call-start = ((), (), s32[]{:S(2)}) async-start(), calls=%async_computation.35 | async-start | bytes 5242880 | tf_op jit(solution)/shard_map/reduce_scatter | solution.py:84
  1419.3 248.2 %reduce-scatter.46.cloned.1.call-start = ((), (), s32[]{:S(2)}) async-start(), calls=%async_computation.43 | async-start | bytes 5242880 | tf_op jit(solution)/shard_map/reduce_scatter | solution.py:84
  1426.9 367.2 %all-reduce.3.cloned.1.call-start = ((), (), s32[]{:S(2)}) async-start(), calls=%async_computation.49 | async-start | bytes 188416 | tf_op jit(solution)/shard_map/psum | solution.py:306
  1548.2 119.3 %copy-start.101 = (f32[128]{0:T(128)S(1)}, f32[128]{0:T(128)}, u32[]{:S(2)}) copy-start(f32[128]{0:T(128)} %copy-done.100) | copy-start | bytes 1540
  1548.2 119.3 %copy-start.105 = (f32[128]{0:T(128)S(1)}, f32[128]{0:T(128)}, u32[]{:S(2)}) copy-start(f32[128]{0:T(128)} %copy-done.104) | copy-start | bytes 1540
  1548.3 119.3 %copy-start.107 = (f32[128]{0:T(128)S(1)}, f32[128]{0:T(128)}, u32[]{:S(2)}) copy-start(f32[128]{0:T(128)} %copy-done.106) | copy-start | bytes 1540
  1548.3 119.3 %copy-start.109 = (f32[128]{0:T(128)S(1)}, f32[128]{0:T(128)}, u32[]{:S(2)}) copy-start(f32[128]{0:T(128)} %copy-done.108) | copy-start | bytes 1540
  1672.8 533.8 %reduce-scatter.56.cloned.1.call-start = ((), (), s32[]{:S(2)}) async-start(), calls=%async_computation.48 | async-start | bytes 47775744 | tf_op jit(solution)/shard_map/reduce_scatter | solution.py:305
  (147 other events, 2616.8 us)
Sparse Core Ops, SparseCore 0:
  11.7 191.3 all-gather.19
  205.5 24.8 all-gather.21
  232.2 35.2 all-gather.29
  269.3 35.2 all-gather.25
  306.3 35.3 all-gather.17
  345.1 54.4 reduce-scatter.27
  403.4 52.6 reduce-scatter.23
  459.6 52.6 reduce-scatter.19
  517.5 35.2 all-gather.23
  555.2 35.2 all-gather.39
  593.1 35.2 all-gather.27
  630.3 35.2 all-gather.41
  667.6 35.2 all-gather.31
  704.8 35.2 all-gather.43
  743.8 52.6 reduce-scatter.31
  799.4 52.6 reduce-scatter.37
  855.2 52.6 reduce-scatter.43
  910.8 52.6 reduce-scatter.21
  966.7 52.6 reduce-scatter.29
  1022.3 52.6 reduce-scatter.25
  1077.0 35.2 all-gather.33
  1114.3 35.3 all-gather.35
  1151.7 35.2 all-gather.37
  1280.0 34.7 reduce-scatter.35
  1331.7 34.8 reduce-scatter.47
  1378.3 28.4 reduce-scatter.41
  1409.5 27.7 reduce-scatter.49
  1441.0 27.7 reduce-scatter.53
  1471.7 27.6 reduce-scatter.51
  1502.5 52.7 reduce-scatter.39
  1558.8 52.6 reduce-scatter.33
  1614.8 52.6 reduce-scatter.45
  1673.5 120.5 all-reduce.2
  1796.5 410.0 reduce-scatter.55
where the time goes:
time: 2240 us; the launch traced here: 2230 us
  waiting for transfers between devices  1510 us (67%)
  matrix products  406 us (18%)
  other arithmetic  139 us (6%)
  local copies, waits for them, and re-layouts  80.2 us (4%)
  starting transfers between devices  48.4 us (2%)
  blocking collectives  28.3 us (1%)
    reduce_scatter x12, waiting for transfers between devices, narrow(): lax.psum_scatter(plain_dot(left, right), 'tp', scatter_dimension=0, tiled...  493 us
    reduce_scatter x1, waiting for transfers between devices, body(): lax.psum_scatter(block_grads, 'dp', scatter_dimension=1, tiled=True)  411 us
    all_gather x12, waiting for transfers between devices, widen(): return lax.all_gather(rows_low, 'tp', axis=0, tiled=True)  202 us
    all_gather x1, waiting for transfers between devices, body(): lax.all_gather(master.astype(jnp.bfloat16), 'dp', axis=1, tiled=True)  191 us
    dot_general x51, matrix products, rows_by_rows(): lax.dot_general(left, right, (((1,), (1,)), ((), ())), preferred_element_...  149 us
    dot_general x39, matrix products, cols_by_cols(): lax.dot_general(left, right, (((0,), (0,)), ((), ())), preferred_element_...  130 us
    dot_general x39, matrix products, plain_dot(): return jnp.dot(left, right, preferred_element_type=jnp.float32)  126 us
    ppermute x18, waiting for transfers between devices, passed_along(): lax.ppermute(value, axis, [(source, source + steps) for source in range(l...  65.9 us
  transfers between devices with their start and end apart: 52, of which 34 were waited for; matrix products, arithmetic and copies ran while one was open for 23% of the time, Pallas kernels for 0%

commit v1 on v0

v1 whole, which is shorter than its diff:
```python
import math

import jax
import jax.numpy as jnp
from jax import lax
from jax.experimental import pallas as pl
from jax.experimental.pallas import tpu as pltpu
from jax.sharding import PartitionSpec as P

D = 2048
H = 16
HD = 128
FF = 8192
CHIP_ROWS = 1024
KEY_ROWS = 2 * CHIP_ROWS
KEY_BLOCK = 256
HEAD_GROUP = 4


norm_eps = 1e-05
gelu_coef = math.sqrt(2.0 / math.pi)
beta_one = 0.9
beta_two = 0.95
adam_eps = 1e-08
decay_rate = 0.1
masked_score = -1e30
score_scale = 1.0 / math.sqrt(HD)

bf16 = jnp.bfloat16
f32 = jnp.float32


def layer_norm_fwd(values, gain, shift):
    mean_row = jnp.mean(values, -1, keepdims=True)
    centered = values - mean_row
    var_row = jnp.mean(centered * centered, -1, keepdims=True)
    inverse = lax.rsqrt(var_row + norm_eps)
    normed = centered * inverse
    return (normed * gain + shift, normed, inverse)


def layer_norm_back(grad_norm, normed, inverse, gain):
    scaled = grad_norm * gain
    return inverse * (
        scaled
        - jnp.mean(scaled, -1, keepdims=True)
        - normed * jnp.mean(scaled * normed, -1, keepdims=True)
    )


def gelu_tanh(values):
    inner = gelu_coef * (values + 0.044715 * values * values * values)
    return 0.5 * values * (1.0 + jnp.tanh(inner))


def gelu_slope(values):
    tangent = jnp.tanh(gelu_coef * (values + 0.044715 * values * values * values))
    return 0.5 * (1.0 + tangent) + 0.5 * values * (1.0 - tangent * tangent) * gelu_coef * (
        1.0 + 3.0 * 0.044715 * values * values
    )


def rows_by_rows(left, right):
    return lax.dot_general(left, right, (((1,), (1,)), ((), ())), preferred_element_type=f32)


def cols_by_cols(left, right):
    return lax.dot_general(left, right, (((0,), (0,)), ((), ())), preferred_element_type=f32)


def plain_dot(left, right):
    return jnp.dot(left, right, preferred_element_type=f32)


def vector_sizes():
    return [D, D, H * HD, HD, D, D, D, FF, D]


def swap(value, axis, step):
    count = lax.axis_size(axis)
    return lax.ppermute(value, axis, [(source, source ^ step) for source in range(count)])


def swap_core(value):
    return swap(value, "dp", 1)


def spread(value):
    return [value] + [swap(value, "tp", m) for m in range(1, lax.axis_size("tp"))]


def collect(pieces):
    total = pieces[0].astype(f32)
    for m in range(1, len(pieces)):
        total = total + swap(pieces[m].astype(bf16), "tp", m).astype(f32)
    return total


def sum_everywhere(value):
    for axis in ("dp", "tp"):
        step = 1
        while step < lax.axis_size(axis):
            value = value + swap(value, axis, step)
            step *= 2
    return value


def attend_forward_kernel(bounds, q_ref, k_ref, vt_ref, bias_ref, out_ref, log_ref, keep_ref):
    rows = q_ref.shape[1]
    tile_heads = bias_ref.shape[2] // rows
    tiles = HEAD_GROUP // tile_heads
    width = HEAD_GROUP * rows
    batch = pl.program_id(0)
    first = bounds[batch, 0]
    last = bounds[batch, 1]
    queries = jnp.concatenate(
        [q_ref[0, :, h * HD : (h + 1) * HD] for h in range(HEAD_GROUP)], 0
    )

    def score_block(block, peak):
        start = pl.multiple_of(block * KEY_BLOCK, KEY_BLOCK)
        scores = rows_by_rows(k_ref[0, pl.ds(start, KEY_BLOCK), :], queries) * score_scale
        bias = bias_ref[0, pl.ds(start, KEY_BLOCK), :]
        scores = scores + jnp.concatenate([bias] * tiles, 1)
        keep_ref[pl.ds(start, KEY_BLOCK), :] = scores
        return jnp.maximum(peak, jnp.max(scores, 0, keepdims=True))

    peak = lax.fori_loop(first, last, score_block, jnp.full((1, width), masked_score, f32))

    def exp_block(block, total):
        start = pl.multiple_of(block * KEY_BLOCK, KEY_BLOCK)
        powers = jnp.exp(keep_ref[pl.ds(start, KEY_BLOCK), :] - peak)
        keep_ref[pl.ds(start, KEY_BLOCK), :] = powers
        return total + jnp.sum(powers, 0, keepdims=True)

    total = lax.fori_loop(first, last, exp_block, jnp.zeros((1, width), f32))
    share = 1.0 / total

    def value_block(block, acc):
        start = pl.multiple_of(block * KEY_BLOCK, KEY_BLOCK)
        probs = (keep_ref[pl.ds(start, KEY_BLOCK), :] * share).astype(bf16)
        return acc + plain_dot(vt_ref[0, :, pl.ds(start, KEY_BLOCK)], probs)

    acc = lax.fori_loop(first, last, value_block, jnp.zeros((HD, width), f32))
    for h in range(HEAD_GROUP):
        out_ref[0, :, h * HD : (h + 1) * HD] = acc[:, h * rows : (h + 1) * rows].T.astype(bf16)
    log_ref[0, 0] = peak + jnp.log(total)


def attend_backward_kernel(
    bounds,
    q_ref,
    g_ref,
    k_ref,
    kt_ref,
    v_ref,
    bias_ref,
    log_ref,
    dq_ref,
    dk_ref,
    dv_ref,
    prob_ref,
    dprob_ref,
):
    rows = q_ref.shape[1]
    tile_heads = bias_ref.shape[2] // rows
    tiles = HEAD_GROUP // tile_heads
    width = HEAD_GROUP * rows
    batch = pl.program_id(0)
    first = bounds[batch, 0]
    last = bounds[batch, 1]

    @pl.when(pl.program_id(1) == 0)
    def _():
        dk_ref[...] = jnp.zeros_like(dk_ref)
        dv_ref[...] = jnp.zeros_like(dv_ref)

    queries = jnp.concatenate(
        [q_ref[0, :, h * HD : (h + 1) * HD] for h in range(HEAD_GROUP)], 0
    )
    grads = jnp.concatenate([g_ref[0, :, h * HD : (h + 1) * HD] for h in range(HEAD_GROUP)], 0)
    log_row = log_ref[0, 0]

    def prob_block(block, delta):
        start = pl.multiple_of(block * KEY_BLOCK, KEY_BLOCK)
        scores = rows_by_rows(k_ref[0, pl.ds(start, KEY_BLOCK), :], queries) * score_scale
        bias = bias_ref[0, pl.ds(start, KEY_BLOCK), :]
        probs = jnp.exp(scores + jnp.concatenate([bias] * tiles, 1) - log_row)
        dprobs = rows_by_rows(v_ref[0, pl.ds(start, KEY_BLOCK), :], grads)
        prob_ref[pl.ds(start, KEY_BLOCK), :] = probs
        dprob_ref[pl.ds(start, KEY_BLOCK), :] = dprobs
        return delta + jnp.sum(probs * dprobs, 0, keepdims=True)

    delta = lax.fori_loop(first, last, prob_block, jnp.zeros((1, width), f32))

    def grad_block(block, acc):
        start = pl.multiple_of(block * KEY_BLOCK, KEY_BLOCK)
        probs = prob_ref[pl.ds(start, KEY_BLOCK), :]
        grad_scores = (probs * (dprob_ref[pl.ds(start, KEY_BLOCK), :] - delta)).astype(bf16)
        dk_ref[0, pl.ds(start, KEY_BLOCK), :] += plain_dot(grad_scores, queries) * score_scale
        dv_ref[0, pl.ds(start, KEY_BLOCK), :] += plain_dot(probs.astype(bf16), grads)
        return acc + plain_dot(kt_ref[0, :, pl.ds(start, KEY_BLOCK)], grad_scores)

    acc = lax.fori_loop(first, last, grad_block, jnp.zeros((HD, width), f32)) * score_scale
    for h in range(HEAD_GROUP):
        dq_ref[0, :, h * HD : (h + 1) * HD] = acc[:, h * rows : (h + 1) * rows].T.astype(bf16)


def attend_forward(queries, keys, vals_t, bias, bounds):
    batches, rows, cols = queries.shape
    groups = cols // (HEAD_GROUP * HD)
    width = HEAD_GROUP * rows
    row_spec = pl.BlockSpec((1, rows, HEAD_GROUP * HD), lambda b, g, *_: (b, 0, g))
    return pl.pallas_call(
        attend_forward_kernel,
        name="attend_forward",
        grid_spec=pltpu.PrefetchScalarGridSpec(
            num_scalar_prefetch=1,
            grid=(batches, groups),
            in_specs=[
                row_spec,
                pl.BlockSpec((1, KEY_ROWS, HD), lambda b, g, *_: (b, 0, 0)),
                pl.BlockSpec((1, HD, KEY_ROWS), lambda b, g, *_: (b, 0, 0)),
                pl.BlockSpec((1, KEY_ROWS, bias.shape[2]), lambda b, g, *_: (b, 0, 0)),
            ],
            out_specs=[
                row_spec,
                pl.BlockSpec((1, 1, 1, width), lambda b, g, *_: (b, g, 0, 0)),
            ],
            scratch_shapes=[pltpu.VMEM((KEY_ROWS, width), f32)],
        ),
        out_shape=[
            jax.ShapeDtypeStruct(queries.shape, bf16),
            jax.ShapeDtypeStruct((batches, groups, 1, width), f32),
        ],
        compiler_params=pltpu.CompilerParams(
            dimension_semantics=("arbitrary", "arbitrary"), vmem_limit_bytes=32 << 20
        ),
        cost_estimate=pl.CostEstimate(
            flops=4 * batches * rows * cols * KEY_ROWS,
            transcendentals=batches * rows * (cols // HD) * KEY_ROWS,
            bytes_accessed=batches * (4 * rows * cols + KEY_ROWS * HD * 8),
        ),
    )(bounds, queries, keys, vals_t, bias)


def attend_backward(queries, grads, keys, keys_t, vals, bias, log_sums, bounds):
    batches, rows, cols = queries.shape
    groups = cols // (HEAD_GROUP * HD)
    width = HEAD_GROUP * rows
    row_spec = pl.BlockSpec((1, rows, HEAD_GROUP * HD), lambda b, g, *_: (b, 0, g))
    key_spec = pl.BlockSpec((1, KEY_ROWS, HD), lambda b, g, *_: (b, 0, 0))
    return pl.pallas_call(
        attend_backward_kernel,
        name="attend_backward",
        grid_spec=pltpu.PrefetchScalarGridSpec(
            num_scalar_prefetch=1,
            grid=(batches, groups),
            in_specs=[
                row_spec,
                row_spec,
                key_spec,
                pl.BlockSpec((1, HD, KEY_ROWS), lambda b, g, *_: (b, 0, 0)),
                key_spec,
                pl.BlockSpec((1, KEY_ROWS, bias.shape[2]), lambda b, g, *_: (b, 0, 0)),
                pl.BlockSpec((1, 1, 1, width), lambda b, g, *_: (b, g, 0, 0)),
            ],
            out_specs=[row_spec, key_spec, key_spec],
            scratch_shapes=[
                pltpu.VMEM((KEY_ROWS, width), f32),
                pltpu.VMEM((KEY_ROWS, width), f32),
            ],
        ),
        out_shape=[
            jax.ShapeDtypeStruct(queries.shape, bf16),
            jax.ShapeDtypeStruct(keys.shape, f32),
            jax.ShapeDtypeStruct(keys.shape, f32),
        ],
        compiler_params=pltpu.CompilerParams(
            dimension_semantics=("arbitrary", "arbitrary"), vmem_limit_bytes=40 << 20
        ),
        cost_estimate=pl.CostEstimate(
            flops=10 * batches * rows * cols * KEY_ROWS,
            transcendentals=batches * rows * (cols // HD) * KEY_ROWS,
            bytes_accessed=batches * (6 * rows * cols + KEY_ROWS * HD * 20),
        ),
    )(bounds, queries, grads, keys, keys_t, vals, bias, log_sums)


def adam_step(weights, grads, first, second, step_count, learning_rate):
    steps_float = step_count[0].astype(f32)
    first_new = beta_one * first + (1.0 - beta_one) * grads
    second_new = beta_two * second + (1.0 - beta_two) * grads * grads
    corr_one = 1.0 - jnp.power(beta_one, steps_float)
    corr_two = 1.0 - jnp.power(beta_two, steps_float)
    update = first_new / corr_one / (jnp.sqrt(second_new / corr_two) + adam_eps)
    return (weights - learning_rate[0] * (update + decay_rate * weights), first_new, second_new)


def body(
    block_in,
    cotangent,
    segments,
    master,
    moment_one,
    moment_two,
    vectors,
    vec_one,
    vec_two,
    step_count,
    learning_rate,
):
    tp_size = lax.axis_size("tp")
    dp_size = lax.axis_size("dp")
    tp_index = lax.axis_index("tp")
    dp_index = lax.axis_index("dp")
    core = dp_index % 2
    chip = dp_index // 2
    batches, rows, _ = block_in.shape
    stretch = rows * tp_size
    query_rows = H * HD // tp_size
    kv_share = 2 * HD // tp_size
    ff_rows = FF // tp_size
    half = query_rows // 2
    kv_half = kv_share // 2
    row_starts = [0]
    for length in [query_rows, kv_share, query_rows, ff_rows, ff_rows]:
        row_starts.append(row_starts[-1] + length)
    parity = [[2 * i + c for i in range(dp_size // 2)] for c in range(2)]

    vec_pieces = []
    cursor = 0
    for length in vector_sizes():
        vec_pieces.append(vectors[cursor : cursor + length])
        cursor += length
    (
        gain_one,
        shift_one,
        bias_query_all,
        bias_value,
        bias_out,
        gain_two,
        shift_two,
        bias_up_all,
        bias_down,
    ) = vec_pieces
    bias_up = lax.dynamic_slice_in_dim(bias_up_all, tp_index * ff_rows, ff_rows)
    keyval_bias = jnp.concatenate([jnp.zeros((HD,), f32), bias_value])

    sides = [core, 1 - core]
    block_of = [tp_index ^ m for m in range(tp_size)]
    query_starts = [
        block_of[m] * query_rows + side * half for side in sides for m in range(tp_size)
    ]
    kv_starts = [
        block_of[m] * kv_share + side * kv_half for side in sides for m in range(tp_size)
    ]
    bias_query = jnp.concatenate(
        [lax.dynamic_slice_in_dim(bias_query_all, start, half) for start in query_starts]
    )

    def shard(first, last):
        return master[row_starts[first] : row_starts[last]].astype(bf16)

    def gather_columns(piece):
        return lax.all_gather(piece, "dp", axis=1, tiled=True)

    qkv_rows = gather_columns(shard(0, 2))
    out_shard, qkv_rows = lax.optimization_barrier((shard(2, 3), qkv_rows))
    out_rows = gather_columns(out_shard)
    up_shard, out_rows = lax.optimization_barrier((shard(3, 4), out_rows))
    w_up = gather_columns(up_shard)
    down_shard, w_up = lax.optimization_barrier((shard(4, 5), w_up))
    w_down = gather_columns(down_shard)

    def split_sides(block):
        size = block.shape[0] // 2
        return [lax.dynamic_slice_in_dim(block, side * size, size) for side in sides]

    def widen_rows(own, other):
        received = spread(own)
        crossed = swap_core(jnp.concatenate(received[1:], 0))
        return jnp.concatenate(received + [other, crossed], 0)

    kv_blocks = spread(qkv_rows[query_rows:])
    w_keyval = jnp.zeros((2 * HD, D), bf16)
    for m in range(tp_size):
        w_keyval = lax.dynamic_update_slice_in_dim(
            w_keyval, kv_blocks[m], block_of[m] * kv_share, 0
        )
    w_query = widen_rows(*split_sides(qkv_rows[:query_rows]))
    w_out = widen_rows(*split_sides(out_rows))

    block_rows = block_in.astype(f32).reshape(batches * rows, D)
    ln_one, normed_one, inverse_one = layer_norm_fwd(block_rows, gain_one, shift_one)
    hidden_one = ln_one.astype(bf16)
    kv_local = (rows_by_rows(hidden_one, w_keyval) + keyval_bias).astype(bf16)
    kv_local = kv_local.reshape(batches, 1, rows, 2 * HD)
    kv_stretch = jnp.zeros((batches, tp_size, rows, 2 * HD), bf16)
    for m, piece in enumerate(spread(kv_local)):
        kv_stretch = lax.dynamic_update_slice_in_dim(kv_stretch, piece, block_of[m], 1)
    kv_stretch = kv_stretch.reshape(batches, 1, stretch, 2 * HD)

    def both_sides(own, other):
        pair = jnp.zeros((batches, 2, stretch, 2 * HD), bf16)
        pair = lax.dynamic_update_slice_in_dim(pair, own, core, 1)
        return lax.dynamic_update_slice_in_dim(pair, other, 1 - core, 1)

    to_next = [(d, d + 2) for d in range(dp_size - 2) if (d // 2) % 2 == 1]
    to_last = [(target, source) for source, target in to_next]
    kv_before = lax.ppermute(kv_stretch, "dp", to_next)
    kv_here = both_sides(kv_stretch, swap_core(kv_stretch))
    kv_before = both_sides(kv_before, swap_core(kv_before))
    keyvals = jnp.concatenate([kv_before, kv_here], 1).reshape(batches, KEY_ROWS, 2 * HD)
    keys = keyvals[:, :, :HD]
    vals = keyvals[:, :, HD:]
    keys_t = keys.transpose(0, 2, 1)
    vals_t = vals.transpose(0, 2, 1)

    own_first = dp_index * stretch + tp_index * rows
    seg_own = lax.dynamic_slice_in_dim(segments, own_first, rows, 1)
    seg_padded = jnp.pad(segments, ((0, 0), (CHIP_ROWS, 0)), constant_values=-1)
    seg_keys = lax.dynamic_slice_in_dim(seg_padded, chip * CHIP_ROWS, KEY_ROWS, 1)
    key_base = (chip - 1) * CHIP_ROWS
    key_place = key_base + jnp.arange(KEY_ROWS)
    tile_heads = max(1, 128 // rows)
    own_place = own_first + jnp.arange(rows)
    allowed = (seg_keys[:, :, None] == seg_own[:, None, :]) & (
        key_place[None, :, None] <= own_place[None, None, :]
    )
    bias = jnp.where(jnp.tile(allowed, (1, 1, tile_heads)), 0.0, masked_score).astype(f32)
    last_block = jnp.broadcast_to(
        (own_first - key_base + rows + KEY_BLOCK - 1) // KEY_BLOCK, (batches,)
    )
    first_block = jnp.maximum(seg_own[:, 0] - key_base, 0) // KEY_BLOCK
    bounds = jnp.stack([first_block, last_block], 1).astype(jnp.int32)

    queries = (rows_by_rows(hidden_one, w_query) + bias_query).astype(bf16)
    queries = queries.reshape(batches, rows, H * HD)
    attended, log_sums = attend_forward(queries, keys, vals_t, bias, bounds)
    attended = attended.reshape(batches * rows, H * HD)
    residual = block_rows + plain_dot(attended, w_out) + bias_out
    ln_two, normed_two, inverse_two = layer_norm_fwd(residual, gain_two, shift_two)
    hidden_two = ln_two.astype(bf16)

    outputs = []
    wide_hidden = []
    wide_cot = []
    wide_act = []
    wide_pre_grad = []
    grad_two_parts = []
    for b in range(batches):
        own = slice(b * rows, (b + 1) * rows)
        hidden_all = jnp.concatenate(spread(hidden_two[own]), 0)
        cot_all = jnp.concatenate(spread(cotangent[b]), 0)
        pre_act = rows_by_rows(hidden_all, w_up) + bias_up
        activated = gelu_tanh(pre_act).astype(bf16)
        grad_pre = (rows_by_rows(cot_all, w_down) * gelu_slope(pre_act)).astype(bf16)
        grad_hidden = plain_dot(grad_pre, w_up)
        grad_two_parts.append(
            collect([grad_hidden[m * rows : (m + 1) * rows] for m in range(tp_size)])
        )
        product = plain_dot(activated, w_down)
        summed = collect([product[m * rows : (m + 1) * rows] for m in range(tp_size)])
        outputs.append((residual[own] + summed + bias_down).astype(bf16))
        wide_hidden.append(hidden_all)
        wide_cot.append(cot_all)
        wide_act.append(activated)
        wide_pre_grad.append(grad_pre)

    grad_down = cols_by_cols(jnp.concatenate(wide_act, 0), jnp.concatenate(wide_cot, 0))
    grad_up = cols_by_cols(jnp.concatenate(wide_pre_grad, 0), jnp.concatenate(wide_hidden, 0))
    grad_bias_up = sum(jnp.sum(part.astype(f32), 0) for part in wide_pre_grad)

    def scatter_columns(full):
        return lax.psum_scatter(full, "dp", scatter_dimension=1, tiled=True)

    shard_down = scatter_columns(grad_down.astype(bf16)).astype(f32)
    shard_up = scatter_columns(grad_up.astype(bf16)).astype(f32)

    cot_rows = cotangent.astype(f32).reshape(batches * rows, D)
    grad_bias_down = jnp.sum(cot_rows, 0)
    grad_hidden_two = jnp.concatenate(grad_two_parts, 0)
    grad_resid = cot_rows + layer_norm_back(grad_hidden_two, normed_two, inverse_two, gain_two)
    grad_gain_two = jnp.sum(grad_hidden_two * normed_two, 0)
    grad_shift_two = jnp.sum(grad_hidden_two, 0)
    grad_att = grad_resid.astype(bf16)
    grad_bias_out = jnp.sum(grad_resid, 0)
    grad_heads = rows_by_rows(grad_att, w_out).astype(bf16).reshape(batches, rows, H * HD)
    grad_query, grad_key, grad_val = attend_backward(
        queries, grad_heads, keys, keys_t, vals, bias, log_sums, bounds
    )
    grad_query = grad_query.reshape(batches * rows, H * HD)
    grad_bias_query = jnp.sum(grad_query.astype(f32), 0)

    kv_grads = jnp.concatenate([grad_key, grad_val], 2)
    kv_grads = kv_grads.reshape(batches, 2, 2, stretch, 2 * HD)
    kv_kept = lax.dynamic_slice_in_dim(kv_grads, core, 1, 2)
    kv_sent = lax.dynamic_slice_in_dim(kv_grads, 1 - core, 1, 2).astype(bf16)
    kv_kept = kv_kept + swap_core(kv_sent).astype(f32)
    kv_kept = kv_kept.reshape(batches, 2, tp_size, rows, 2 * HD)
    kv_total = kv_kept[:, 1] + lax.ppermute(kv_kept[:, 0].astype(bf16), "dp", to_last).astype(f32)
    grad_kv = collect([lax.dynamic_slice_in_dim(kv_total, at, 1, 1) for at in block_of])
    grad_kv = grad_kv.astype(bf16).reshape(batches * rows, 2 * HD)
    grad_bias_value = jnp.sum(grad_kv[:, HD:].astype(f32), 0)

    grad_hidden_one = plain_dot(grad_query, w_query) + plain_dot(grad_kv, w_keyval)
    grad_rows = grad_resid + layer_norm_back(grad_hidden_one, normed_one, inverse_one, gain_one)
    grad_gain_one = jnp.sum(grad_hidden_one * normed_one, 0)
    grad_shift_one = jnp.sum(grad_hidden_one, 0)
    input_grads = grad_rows.astype(bf16).reshape(batches, rows, D)

    def reduce_blocks(own, other):
        own = own + swap_core(other.astype(bf16)).astype(f32)
        size = own.shape[0] // tp_size
        return collect([own[m * size : (m + 1) * size] for m in range(tp_size)])

    cols_half = H * HD // 2
    part_out = reduce_blocks(
        cols_by_cols(attended[:, :cols_half], grad_att),
        cols_by_cols(attended[:, cols_half:], grad_att),
    )
    part_query = reduce_blocks(
        cols_by_cols(grad_query[:, :cols_half], hidden_one),
        cols_by_cols(grad_query[:, cols_half:], hidden_one),
    )
    grad_w_keyval = cols_by_cols(grad_kv, hidden_one)
    kv_rows = [lax.dynamic_slice_in_dim(grad_w_keyval, start, kv_half) for start in kv_starts]
    part_keyval = reduce_blocks(
        jnp.concatenate(kv_rows[:tp_size], 0), jnp.concatenate(kv_rows[tp_size:], 0)
    )
    part_all = jnp.concatenate([part_query, part_keyval, part_out], 0).astype(bf16)
    part_all = lax.psum_scatter(
        part_all, "dp", scatter_dimension=1, axis_index_groups=parity, tiled=True
    )
    width = part_all.shape[1] // 2
    mine = lax.dynamic_slice_in_dim(part_all, core * width, width, 1)
    theirs = swap_core(lax.dynamic_slice_in_dim(part_all, (1 - core) * width, width, 1))
    low_half = jnp.where(core == 0, mine, theirs)
    high_half = jnp.where(core == 0, theirs, mine)
    pieces = []
    at = 0
    for size in (half, kv_half, half):
        pieces += [low_half[at : at + size], high_half[at : at + size]]
        at += size
    shard_attention = jnp.concatenate(pieces, 0).astype(f32)

    whole_bias_query = jnp.zeros((H * HD,), f32)
    for index, start in enumerate(query_starts):
        whole_bias_query = lax.dynamic_update_slice_in_dim(
            whole_bias_query, grad_bias_query[index * half : (index + 1) * half], start, 0
        )
    whole_bias_up = lax.dynamic_update_slice_in_dim(
        jnp.zeros((FF,), f32), grad_bias_up, tp_index * ff_rows, 0
    )
    vec_grads = jnp.concatenate(
        [
            grad_gain_one,
            grad_shift_one,
            whole_bias_query,
            grad_bias_value,
            grad_bias_out,
            grad_gain_two,
            grad_shift_two,
            whole_bias_up,
            grad_bias_down,
        ]
    )
    vec_total = sum_everywhere(vec_grads.reshape(-1, 128)).reshape(-1)
    new_vectors, new_vec_one, new_vec_two = adam_step(
        vectors, vec_total, vec_one, vec_two, step_count, learning_rate
    )
    updated = []
    for first, last, grads in (
        (0, 3, shard_attention),
        (3, 4, shard_up),
        (4, 5, shard_down),
    ):
        at = slice(row_starts[first], row_starts[last])
        updated.append(
            adam_step(
                master[at], grads, moment_one[at], moment_two[at], step_count, learning_rate
            )
        )
    new_master, new_moment_one, new_moment_two = (
        jnp.concatenate(parts, 0) for parts in zip(*updated)
    )
    return (
        jnp.stack(outputs),
        input_grads,
        new_master,
        new_moment_one,
        new_moment_two,
        new_vectors,
        new_vec_one,
        new_vec_two,
    )


def solution(mesh):
    in_specs = (
        P(None, ("dp", "tp"), None),
        P(None, ("dp", "tp"), None),
        P(),
        P("tp", "dp"),
        P("tp", "dp"),
        P("tp", "dp"),
        P(),
        P(),
        P(),
        P(),
        P(),
    )
    out_specs = (
        P(None, ("dp", "tp"), None),
        P(None, ("dp", "tp"), None),
        P("tp", "dp"),
        P("tp", "dp"),
        P("tp", "dp"),
        P(),
        P(),
        P(),
    )
    return jax.shard_map(body, mesh=mesh, in_specs=in_specs, out_specs=out_specs, check_vma=False)
```

time: 2240 us -> 968 us (0.43)
  waiting for transfers between devices: 1510 us -> 450 us
  matrix products: 406 us -> 190 us
  starting transfers between devices: 48.4 us -> 133 us
  other arithmetic: 139 us -> 58.4 us
  blocking collectives: 28.3 us -> 0 us
  Pallas kernels: 0 us -> 23.6 us
    reduce_scatter x19 -> x3, waiting for transfers between devices: 968 us -> 55.2 us  [the longest x2 55.2 us: scatter_columns(): return lax.psum_scatter(full, 'dp', scatter_dimension=1, tiled=True)]
    all_gather x14 -> x4, waiting for transfers between devices: 411 us -> 61.7 us  [gather_columns(): return lax.all_gather(piece, 'dp', axis=1, tiled=True)]
    ppermute x18 -> x76, waiting for transfers between devices: 65.9 us -> 333 us  [the longest x74 333 us: swap(): lax.ppermute(value, axis, [(source, source ^ step) for source in range(co...]
    ppermute x18 -> x76, starting transfers between devices: 45.7 us -> 132 us  [the longest x74 130 us: swap(): lax.ppermute(value, axis, [(source, source ^ step) for source in range(co...]
    dot_general x39 -> x7, matrix products: 130 us -> 49.9 us  [cols_by_cols(): lax.dot_general(left, right, (((0,), (0,)), ((), ())), preferred_element_...]
    dot_general x51 -> x9, matrix products: 149 us -> 81.4 us  [rows_by_rows(): lax.dot_general(left, right, (((1,), (1,)), ((), ())), preferred_element_...]
    dot_general x39 -> x9, matrix products: 126 us -> 58.5 us  [plain_dot(): return jnp.dot(left, right, preferred_element_type=f32)]
    add x17 -> x8, other arithmetic: 61.7 us -> 2.2 us  [the longest x1 1.92 us: body(): kv_kept = kv_kept + swap_core(kv_sent).astype(f32)]
  transfers between devices with their start and end apart: 52 -> 83, of which waited for: 34 -> 36; matrix products, arithmetic and copies ran while one was open for 23% -> 30% of each run, Pallas kernels for 0% -> 1%
where the time goes in v1:
time: 968 us; the launch traced here: 960 us
  waiting for transfers between devices  450 us (46%)
  matrix products  190 us (20%)
  starting transfers between devices  133 us (14%)
  local copies, waits for them, and re-layouts  87.1 us (9%)
  other arithmetic  58.4 us (6%)
  Pallas kernels  23.6 us (2%)
  between operations  17.9 us (2%)
    ppermute x74, waiting for transfers between devices, swap(): lax.ppermute(value, axis, [(source, source ^ step) for source in range(co...  333 us
    ppermute x74, starting transfers between devices, swap(): lax.ppermute(value, axis, [(source, source ^ step) for source in range(co...  130 us
    dot_general x9, matrix products, rows_by_rows(): lax.dot_general(left, right, (((1,), (1,)), ((), ())), preferred_element_...  81.4 us
    all_gather x4, waiting for transfers between devices, gather_columns(): return lax.all_gather(piece, 'dp', axis=1, tiled=True)  61.7 us
    dot_general x9, matrix products, plain_dot(): return jnp.dot(left, right, preferred_element_type=f32)  58.5 us
    reduce_scatter x2, waiting for transfers between devices, scatter_columns(): return lax.psum_scatter(full, 'dp', scatter_dimension=1, tiled=True)  55.2 us
    dot_general x7, matrix products, cols_by_cols(): lax.dot_general(left, right, (((0,), (0,)), ((), ())), preferred_element_...  49.9 us
    unnamed x247, local copies, waits for them, and re-layouts  48.1 us
  transfers between devices with their start and end apart: 83, of which 36 were waited for; matrix products, arithmetic and copies ran while one was open for 30% of the time, Pallas kernels for 1%

profile of v1, /device:TPU:0, one launch (start us, length us, event | category | flops | bytes accessed | tf_op | source)
XLA Modules:
  0.0 959.9 jit_solution(15426031260169082480)
XLA Ops:
  7.2 2.8 convert.73
  14.1 33.8 %all-gather.5.cloned.1.call-done = bf16[576,2048]{1,0:T(8,128)(2,1)} async-done(((bf16[576,256]{1,0:T(8,128)(2,1)}), bf16[576,2048]{1,0:T(8,128)(2,1)}) %all-gather.5.cloned.1.call-update) | async-done | bytes 2359312 | tf_op jit(solution)/shard_map/all_gather | solution.py:366
  48.0 3.7 fusion.180
  51.7 27.9 %all-gather.7.cloned.1.call-done = bf16[512,2048]{1,0:T(8,128)(2,1)} async-done(((bf16[512,256]{1,0:T(8,128)(2,1)}), bf16[512,2048]{1,0:T(8,128)(2,1)}) %all-gather.7.cloned.1.call-update) | async-done | bytes 2097168 | tf_op jit(solution)/shard_map/all_gather | solution.py:366
  96.8 4.7 collective-permute-done.5
  106.1 42.7 %collective-permute-done.7 = bf16[3,1,128,256]{3,2,0,1:T(8,128)(2,1)S(1)} collective-permute-done((bf16[3,1,128,256]{3,2,0,1:T(8,128)(2,1)S(1)}, bf16[3,1,128,256]{3,2,0,1:T(8,128)(2,1)S(1)}, u32[]{:S(2)}, u32[]{:S(2)}) %collective-permute-start.7) | collective-permute-done | bytes 196640 | tf_op jit(solution)/shard_map/ppermute | solution.py:81
  152.3 3.8 collective-permute-done.9
  174.3 18.1 %collective-permute-done.13 = bf16[256,2048]{1,0:T(8,128)(2,1)S(1)} collective-permute-done((bf16[256,2048]{1,0:T(8,128)(2,1)S(1)}, bf16[256,2048]{1,0:T(8,128)(2,1)S(1)}, u32[]{:S(2)}, u32[]{:S(2)}) %collective-permute-start.13) | collective-permute-done | bytes 1048608 | tf_op jit(solution)/shard_map/ppermute | solution.py:81
  192.5 23.0 %collective-permute-done.14 = bf16[256,2048]{1,0:T(8,128)(2,1)S(1)} collective-permute-done((bf16[256,2048]{1,0:T(8,128)(2,1)S(1)}, bf16[256,2048]{1,0:T(8,128)(2,1)S(1)}, u32[]{:S(2)}, u32[]{:S(2)}) %collective-permute-start.14) | collective-permute-done | bytes 1048608 | tf_op jit(solution)/shard_map/ppermute | solution.py:81
  217.8 3.1 fusion.183
  220.9 2.6 copy.23.vt_ref
  223.8 4.1 constant_dynamic-update-slice_fusion
  227.8 7.0 add_convert_fusion.1
  234.9 9.1 attend_forward.1
  249.1 3.7 fusion.193
  255.8 6.8 collective-permute-start.18
  264.0 22.6 %collective-permute-done.18 = bf16[128,2048]{1,0:T(8,128)(2,1)S(1)} collective-permute-done((bf16[128,2048]{1,0:T(8,128)(2,1)S(1)}, bf16[128,2048]{1,0:T(8,128)(2,1)S(1)}, u32[]{:S(2)}, u32[]{:S(2)}) %collective-permute-start.18) | collective-permute-done | bytes 524320 | tf_op jit(solution)/shard_map/ppermute | solution.py:81
  292.1 2.8 collective-permute-start.25
  298.6 5.7 collective-permute-done.23
  306.2 12.0 %collective-permute-done.24 = bf16[128,2048]{1,0:T(8,128)(2,1)} collective-permute-done((bf16[128,2048]{1,0:T(8,128)(2,1)}, bf16[128,2048]{1,0:T(8,128)(2,1)}, u32[]{:S(2)}, u32[]{:S(2)}) %collective-permute-start.24) | collective-permute-done | bytes 524320 | tf_op jit(solution)/shard_map/ppermute | solution.py:81
  327.3 10.6 %fusion.69 = f32[512,2048]{1,0:T(8,128)} fusion(bf16[2048,2048]{1,0:T(8,128)(2,1)} %all-gather.9.cloned.1.call-done, bf16[128,2048]{1,0:T(8,128)(2,1)} %collective-permute-done.25, bf16[128,2048]{1,0:T(8,128)(2,1)} %collective-permute-done.24, bf16[128,2048]{1,0:T(8,128)(2,1)} %collective-permute-done.23, bf16[128,2048]{1,0:T(8,128)(2,1)} %get-tuple-element.112), kind=kOutput, calls=%fused_computation.121 | convolution fusion | flops 4303355904 | bytes 14680064 | tf_op jit(solution)/shard_map/dot_general | solution.py:64
  340.1 22.1 %collective-permute-done.30 = bf16[128,2048]{1,0:T(8,128)(2,1)S(1)} collective-permute-done((bf16[128,2048]{1,0:T(8,128)(2,1)S(1)}, bf16[128,2048]{1,0:T(8,128)(2,1)S(1)}, u32[]{:S(2)}, u32[]{:S(2)}) %collective-permute-start.30) | collective-permute-done | bytes 524320 | tf_op jit(solution)/shard_map/ppermute | solution.py:81
  364.5 6.5 fusion.77
  371.0 15.1 %multiply_convert_fusion.2 = (bf16[512,2048]{1,0:T(8,128)(2,1)}, bf16[512,2048]{1,0:T(8,128)(2,1)}, bf16[512,2048]{1,0:T(8,128)(2,1)}, f32[512,2048]{1,0:T(8,128)}) fusion(f32[2048]{0:T(1024)S(1)} %dynamic_slice.107, f32[512,2048]{1,0:T(8,128)} %fusion.69, f32[512,2048]{1,0:T(8,128)} %fusion.77, bf16[2048,2048]{1,0:T(8,128)(2,1)} %all-gather.9.cloned.1.call-done, ...), kind=kOutput, calls=%fused_computation.50 | convolution fusion | flops 4334813184 | bytes 29368320 | tf_op jit(solution)/shard_map/dot_general | solution.py:64
  389.7 12.7 %convert_reduce_fusion.2 = (f32[2048]{0:T(1024)}, bf16[512,2048]{1,0:T(8,128)(2,1)S(1)}) fusion(f32[512,2048]{1,0:T(8,128)} %get-tuple-element.142, f32[2048]{0:T(1024)S(1)} %dynamic_slice.107, bf16[2048,2048]{1,0:T(8,128)(2,1)} %all-gather.11.cloned.1.call-done, bf16[128,2048]{1,0:T(8,128)(2,1)} %collective-permute-done.37, ...), kind=kOutput, calls=%fused_computation.47 | convolution fusion | flops 4326422528 | bytes 16793600 | tf_op jit(solution)/shard_map/dot_general | solution.py:64
  402.4 7.7 fusion.199
  413.8 12.6 %convert_reduce_fusion.1 = (f32[2048]{0:T(1024)}, bf16[512,2048]{1,0:T(8,128)(2,1)S(1)}) fusion(f32[512,2048]{1,0:T(8,128)} %fusion.69, f32[2048]{0:T(1024)S(1)} %dynamic_slice.107, bf16[2048,2048]{1,0:T(8,128)(2,1)} %all-gather.11.cloned.1.call-done, bf16[128,2048]{1,0:T(8,128)(2,1)} %collective-permute-done.43, ...), kind=kOutput, calls=%fused_computation.46 | convolution fusion | flops 4326422528 | bytes 16793600 | tf_op jit(solution)/shard_map/dot_general | solution.py:64
  426.4 10.2 %fusion.198 = (bf16[512,2048]{1,0:T(8,128)(2,1)S(1)}, f32[512,2048]{1,0:T(8,128)}) fusion(bf16[512,2048]{1,0:T(8,128)(2,1)S(1)} %get-tuple-element.165, bf16[2048,2048]{1,0:T(8,128)(2,1)} %all-gather.9.cloned.1.call-done), kind=kOutput, calls=%fused_computation.380 | convolution fusion | flops 4296015872 | bytes 16777216 | tf_op jit(solution)/shard_map/dot_general | solution.py:72
  440.3 12.8 %convert_reduce_fusion = (f32[2048]{0:T(1024)}, bf16[512,2048]{1,0:T(8,128)(2,1)S(1)}) fusion(f32[512,2048]{1,0:T(8,128)} %fusion.77, f32[2048]{0:T(1024)S(1)} %dynamic_slice.107, bf16[2048,2048]{1,0:T(8,128)(2,1)} %all-gather.11.cloned.1.call-done, bf16[128,2048]{1,0:T(8,128)(2,1)S(1)} %collective-permute-done.49, ...), kind=kOutput, calls=%fused_computation.45 | convolution fusion | flops 4326422528 | bytes 16793600 | tf_op jit(solution)/shard_map/dot_general | solution.py:64
  453.1 7.7 fusion.197
  466.8 9.8 %collective-permute-done.46 = bf16[128,2048]{1,0:T(8,128)(2,1)S(1)} collective-permute-done((bf16[128,2048]{1,0:T(8,128)(2,1)S(1)}, bf16[128,2048]{1,0:T(8,128)(2,1)S(1)}, u32[]{:S(2)}, u32[]{:S(2)}) %collective-permute-start.46) | collective-permute-done | bytes 524320 | tf_op jit(solution)/shard_map/ppermute | solution.py:81
  479.0 8.8 collective-permute-done.50
  487.8 6.6 collective-permute-done.52
  499.4 3.5 convolution_convert_fusion.4
  502.9 14.5 %attend_backward.1 = (bf16[3,128,2048]{2,1,0:T(8,128)(2,1)S(1)}, f32[3,2048,128]{2,1,0:T(8,128)S(1)}, f32[3,2048,128]{2,1,0:T(8,128)}) custom-call(s32[3,2]{1,0:T(4,128)S(1)} %stack.16.bounds, bf16[3,128,2048]{2,1,0:T(8,128)(2,1)S(1)} %bitcast.149, bf16[3,128,2048]{2,1,0:T(8,128)(2,1)S(1)} %bitcast.150, bf16[3,2048,128]{2,1,0:T(8,128)(2,1)S(1)} %copy-done.3, ...), custom_call_target="tpu_custom_call" | custom-call | flops 16106127360 | bytes 20447232 | tf_op jit(solution)/shard_map/attend_backward/pallas_call | solution.py:253
  517.4 2.6 pad_maximum_fusion
  520.0 2.6 copy-done.19
  523.9 2.6 collective-permute-start.53
  537.5 4.4 convolution_convert_fusion.2
  542.8 5.7 collective-permute-start.56
  551.0 6.6 collective-permute-done.56
  579.2 43.1 %collective-permute-done.65 = bf16[32,2048]{1,0:T(8,128)(2,1)S(1)} collective-permute-done((bf16[32,2048]{1,0:T(8,128)(2,1)S(1)}, bf16[32,2048]{1,0:T(8,128)(2,1)S(1)}, u32[]{:S(2)}, u32[]{:S(2)}) %collective-permute-start.65) | collective-permute-done | bytes 131104 | tf_op jit(solution)/shard_map/ppermute | solution.py:81
  626.3 2.7 fusion.60
  629.0 16.0 %collective-permute-done.67 = bf16[256,2048]{1,0:T(8,128)(2,1)S(1)} collective-permute-done((bf16[256,2048]{1,0:T(8,128)(2,1)S(1)}, bf16[256,2048]{1,0:T(8,128)(2,1)S(1)}, u32[]{:S(2)}, u32[]{:S(2)}) %collective-permute-start.67) | collective-permute-done | bytes 1048608 | tf_op jit(solution)/shard_map/ppermute | solution.py:81
  645.0 22.9 %collective-permute-done.68 = bf16[256,2048]{1,0:T(8,128)(2,1)S(1)} collective-permute-done((bf16[256,2048]{1,0:T(8,128)(2,1)S(1)}, bf16[256,2048]{1,0:T(8,128)(2,1)S(1)}, u32[]{:S(2)}, u32[]{:S(2)}) %collective-permute-start.68) | collective-permute-done | bytes 1048608 | tf_op jit(solution)/shard_map/ppermute | solution.py:81
  678.8 18.4 %convolution_convert_fusion = bf16[2048,2048]{1,0:T(8,128)(2,1)} fusion(bf16[1536,2048]{1,0:T(8,128)(2,1)} %constant_dynamic-update-slice_fusion.25, bf16[512,2048]{1,0:T(8,128)(2,1)S(1)} %copy-done.86, bf16[512,2048]{1,0:T(8,128)(2,1)} %get-tuple-element.134, bf16[512,2048]{1,0:T(8,128)(2,1)S(1)} %copy-done.84), kind=kOutput, calls=%fused_computation.2 | convolution fusion | flops 12907970560 | bytes 20971520 | tf_op jit(solution)/shard_map/dot_general | solution.py:68
  703.3 19.2 %convolution_convert_fusion.1 = bf16[2048,2048]{1,0:T(8,128)(2,1)} fusion(bf16[1536,2048]{1,0:T(8,128)(2,1)} %constant_dynamic-update-slice_fusion.13, bf16[512,2048]{1,0:T(8,128)(2,1)} %copy-done.91, bf16[512,2048]{1,0:T(8,128)(2,1)} %copy-done.90, bf16[512,2048]{1,0:T(8,128)(2,1)S(1)} %copy-done.89), kind=kOutput, calls=%fused_computation.3 | convolution fusion | flops 12907970560 | bytes 20971520 | tf_op jit(solution)/shard_map/dot_general | solution.py:68
  725.6 7.6 fusion.196
  736.9 7.0 fusion.195
  746.3 7.2 fusion.194
  761.5 9.3 collective-permute-done.32
  772.5 8.2 collective-permute-done.33
  783.2 10.1 %collective-permute-done.20 = bf16[128,2048]{1,0:T(8,128)(2,1)S(1)} collective-permute-done((bf16[128,2048]{1,0:T(8,128)(2,1)S(1)}, bf16[128,2048]{1,0:T(8,128)(2,1)S(1)}, u32[]{:S(2)}, u32[]{:S(2)}) %collective-permute-start.20) | collective-permute-done | bytes 524320 | tf_op jit(solution)/shard_map/ppermute | solution.py:81
  794.4 7.7 collective-permute-done.22
  804.2 6.8 fusion.49
  812.7 38.6 %collective-permute-start.72 = (f32[177,128]{1,0:T(8,128)S(1)}, f32[177,128]{1,0:T(8,128)S(1)}, u32[]{:S(2)}, u32[]{:S(2)}) collective-permute-start(f32[177,128]{1,0:T(8,128)S(1)} %bitcast_add_fusion.2), channel_id=1, source_target_pairs={{0,8},{4,12},{8,0},{12,4},{16,24},{20,28},{24,16},{28,20},{1,9},{5... | collective-permute-start | bytes 271880 | tf_op jit(solution)/shard_map/ppermute | solution.py:81
  851.3 4.9 collective-permute-done.72
  858.3 10.1 %collective-permute-done.73 = f32[177,128]{1,0:T(8,128)S(1)} collective-permute-done((f32[177,128]{1,0:T(8,128)S(1)}, f32[177,128]{1,0:T(8,128)S(1)}, u32[]{:S(2)}, u32[]{:S(2)}) %collective-permute-start.73) | collective-permute-done | bytes 90656 | tf_op jit(solution)/shard_map/ppermute | solution.py:81
  879.6 2.8 multiply_subtract_fusion.2
  882.4 55.2 %reduce-scatter.6.cloned.1.call-done = bf16[2048,256]{1,0:T(8,128)(2,1)} async-done(((bf16[2048,2048]{1,0:T(8,128)(2,1)}), bf16[2048,256]{1,0:T(8,128)(2,1)}) %reduce-scatter.6.cloned.1.call-update) | async-done | bytes 1048592 | tf_op jit(solution)/shard_map/reduce_scatter | solution.py:476
  937.6 6.8 multiply_subtract_fusion.1
  944.4 2.7 pad_maximum_fusion.3
  947.2 2.7 pad_maximum_fusion.2
  949.9 2.7 pad_maximum_fusion.1
  (508 shorter events, 203.4 us)
Async XLA Ops:
  7.2 40.7 %all-gather.5.cloned.1.call-start = ((), (), s32[]{:S(2)}) async-start(), calls=%async_computation.3 | async-start | bytes 2654208 | tf_op jit(solution)/shard_map/all_gather | solution.py:366
  12.3 67.4 %all-gather.7.cloned.1.call-start = ((), (), s32[]{:S(2)}) async-start(), calls=%async_computation.4 | async-start | bytes 2359296 | tf_op jit(solution)/shard_map/all_gather | solution.py:366
  47.9 175.5 %all-gather.9.cloned.1.call-start = ((), (), s32[]{:S(2)}) async-start(), calls=%async_computation.5 | async-start | bytes 9437184 | tf_op jit(solution)/shard_map/all_gather | solution.py:366
  79.7 310.0 %all-gather.11.cloned.1.call-start = ((), (), s32[]{:S(2)}) async-start(), calls=%async_computation.6 | async-start | bytes 9437184 | tf_op jit(solution)/shard_map/all_gather | solution.py:366
  86.7 14.8 %collective-permute-start.5 = (bf16[64,2048]{1,0:T(8,128)(2,1)S(1)}, bf16[64,2048]{1,0:T(8,128)(2,1)S(1)}, u32[]{:S(2)}, u32[]{:S(2)}) collective-permute-start(bf16[64,2048]{1,0:T(8,128)(2,1)S(1)} %get-tuple-element.81), channel_id=1, source_target_pairs={{0,2},{1,3},{2,0},{3,1},{4,6},{5,7},{6,4},{7,5},{8,10},{9,11},{10,... | collective-permute-start | bytes 786440 | tf_op jit(solution)/shard_map/ppermute | solution.py:81
  90.5 67.7 %collective-permute-start = (bf16[256,2048]{1,0:T(8,128)(2,1)S(1)}, bf16[256,2048]{1,0:T(8,128)(2,1)S(1)}, u32[]{:S(2)}, u32[]{:S(2)}) collective-permute-start(bf16[256,2048]{1,0:T(8,128)(2,1)S(1)} %get-tuple-element.62), channel_id=1, source_target_pairs={{0,1},{1,0},{2,3},{3,2},{4,5},{5,4},{6,7},{7,6},{8,9},{9,8},{10,11... | collective-permute-start | bytes 3145736 | tf_op jit(solution)/shard_map/ppermute | solution.py:81
  91.7 66.5 %collective-permute-start.1 = (bf16[256,2048]{1,0:T(8,128)(2,1)S(1)}, bf16[256,2048]{1,0:T(8,128)(2,1)S(1)}, u32[]{:S(2)}, u32[]{:S(2)}) collective-permute-start(bf16[256,2048]{1,0:T(8,128)(2,1)S(1)} %get-tuple-element.62), channel_id=1, source_target_pairs={{0,2},{1,3},{2,0},{3,1},{4,6},{5,7},{6,4},{7,5},{8,10},{9,11},{10,... | collective-permute-start | bytes 3145736 | tf_op jit(solution)/shard_map/ppermute | solution.py:81
  94.6 63.7 %collective-permute-start.2 = (bf16[256,2048]{1,0:T(8,128)(2,1)S(1)}, bf16[256,2048]{1,0:T(8,128)(2,1)S(1)}, u32[]{:S(2)}, u32[]{:S(2)}) collective-permute-start(bf16[256,2048]{1,0:T(8,128)(2,1)S(1)} %get-tuple-element.62), channel_id=1, source_target_pairs={{0,3},{1,2},{2,1},{3,0},{4,7},{5,6},{6,5},{7,4},{8,11},{9,10},{10,... | collective-permute-start | bytes 3145736 | tf_op jit(solution)/shard_map/ppermute | solution.py:81
  102.2 46.6 %collective-permute-start.7 = (bf16[3,1,128,256]{3,2,0,1:T(8,128)(2,1)S(1)}, bf16[3,1,128,256]{3,2,0,1:T(8,128)(2,1)S(1)}, u32[]{:S(2)}, u32[]{:S(2)}) collective-permute-start(bf16[3,1,128,256]{3,2,0,1:T(8,128)(2,1)S(1)} %bitcast.162), channel_id=1, source_target_pairs={{0,1},{1,0},{2,3},{3,2},{4,5},{5,4},{6,7},{7,6},{8,9},{9,8},{10,11... | collective-permute-start | bytes 589832 | tf_op jit(solution)/shard_map/ppermute | solution.py:81
  103.2 48.4 %collective-permute-start.8 = (bf16[3,1,128,256]{3,2,0,1:T(8,128)(2,1)S(1)}, bf16[3,1,128,256]{3,2,0,1:T(8,128)(2,1)S(1)}, u32[]{:S(2)}, u32[]{:S(2)}) collective-permute-start(bf16[3,1,128,256]{3,2,0,1:T(8,128)(2,1)S(1)} %bitcast.163), channel_id=1, source_target_pairs={{0,2},{1,3},{2,0},{3,1},{4,6},{5,7},{6,4},{7,5},{8,10},{9,11},{10,... | collective-permute-start | bytes 589832 | tf_op jit(solution)/shard_map/ppermute | solution.py:81
  161.0 62.8 %collective-permute-start.3 = (bf16[768,2048]{1,0:T(8,128)(2,1)}, bf16[768,2048]{1,0:T(8,128)(2,1)}, u32[]{:S(2)}, u32[]{:S(2)}) collective-permute-start(bf16[768,2048]{1,0:T(8,128)(2,1)} %pad_maximum_fusion.4), channel_id=1, source_target_pairs={{0,4},{4,0},{8,12},{12,8},{16,20},{20,16},{24,28},{28,24},{1,5},{5... | collective-permute-start | bytes 9437192 | tf_op jit(solution)/shard_map/ppermute | solution.py:81
  166.5 26.0 %collective-permute-start.13 = (bf16[256,2048]{1,0:T(8,128)(2,1)S(1)}, bf16[256,2048]{1,0:T(8,128)(2,1)S(1)}, u32[]{:S(2)}, u32[]{:S(2)}) collective-permute-start(bf16[256,2048]{1,0:T(8,128)(2,1)S(1)} %get-tuple-element.60), channel_id=1, source_target_pairs={{0,1},{1,0},{2,3},{3,2},{4,5},{5,4},{6,7},{7,6},{8,9},{9,8},{10,11... | collective-permute-start | bytes 3145736 | tf_op jit(solution)/shard_map/ppermute | solution.py:81
  167.8 47.7 %collective-permute-start.14 = (bf16[256,2048]{1,0:T(8,128)(2,1)S(1)}, bf16[256,2048]{1,0:T(8,128)(2,1)S(1)}, u32[]{:S(2)}, u32[]{:S(2)}) collective-permute-start(bf16[256,2048]{1,0:T(8,128)(2,1)S(1)} %get-tuple-element.60), channel_id=1, source_target_pairs={{0,2},{1,3},{2,0},{3,1},{4,6},{5,7},{6,4},{7,5},{8,10},{9,11},{10,... | collective-permute-start | bytes 3145736 | tf_op jit(solution)/shard_map/ppermute | solution.py:81
  169.3 46.2 %collective-permute-start.15 = (bf16[256,2048]{1,0:T(8,128)(2,1)S(1)}, bf16[256,2048]{1,0:T(8,128)(2,1)S(1)}, u32[]{:S(2)}, u32[]{:S(2)}) collective-permute-start(bf16[256,2048]{1,0:T(8,128)(2,1)S(1)} %get-tuple-element.60), channel_id=1, source_target_pairs={{0,3},{1,2},{2,1},{3,0},{4,7},{5,6},{6,5},{7,4},{8,11},{9,10},{10,... | collective-permute-start | bytes 3145736 | tf_op jit(solution)/shard_map/ppermute | solution.py:81
  217.8 28.9 %collective-permute-start.16 = (bf16[768,2048]{1,0:T(8,128)(2,1)}, bf16[768,2048]{1,0:T(8,128)(2,1)}, u32[]{:S(2)}, u32[]{:S(2)}) collective-permute-start(bf16[768,2048]{1,0:T(8,128)(2,1)} %pad_maximum_fusion.6), channel_id=1, source_target_pairs={{0,4},{4,0},{8,12},{12,8},{16,20},{20,16},{24,28},{28,24},{1,5},{5... | collective-permute-start | bytes 9437192 | tf_op jit(solution)/shard_map/ppermute | solution.py:81
  223.5 651.1 %reduce-scatter.4.cloned.1.call-start = ((), (), s32[]{:S(2)}) async-start(), calls=%async_computation.7 | async-start | bytes 2785280 | tf_op jit(solution)/shard_map/reduce_scatter | solution.py:533
  255.8 30.9 %collective-permute-start.18 = (bf16[128,2048]{1,0:T(8,128)(2,1)S(1)}, bf16[128,2048]{1,0:T(8,128)(2,1)S(1)}, u32[]{:S(2)}, u32[]{:S(2)}) collective-permute-start(bf16[128,2048]{1,0:T(8,128)(2,1)S(1)} %get-tuple-element.114), channel_id=1, source_target_pairs={{0,2},{1,3},{2,0},{3,1},{4,6},{5,7},{6,4},{7,5},{8,10},{9,11},{10,... | collective-permute-start | bytes 1572872 | tf_op jit(solution)/shard_map/ppermute | solution.py:81
  262.6 24.1 %collective-permute-start.19 = (bf16[128,2048]{1,0:T(8,128)(2,1)S(1)}, bf16[128,2048]{1,0:T(8,128)(2,1)S(1)}, u32[]{:S(2)}, u32[]{:S(2)}) collective-permute-start(bf16[128,2048]{1,0:T(8,128)(2,1)S(1)} %get-tuple-element.114), channel_id=1, source_target_pairs={{0,3},{1,2},{2,1},{3,0},{4,7},{5,6},{6,5},{7,4},{8,11},{9,10},{10,... | collective-permute-start | bytes 1572872 | tf_op jit(solution)/shard_map/ppermute | solution.py:81
  289.2 15.1 %collective-permute-start.23 = (bf16[128,2048]{1,0:T(8,128)(2,1)}, bf16[128,2048]{1,0:T(8,128)(2,1)}, u32[]{:S(2)}, u32[]{:S(2)}) collective-permute-start(bf16[128,2048]{1,0:T(8,128)(2,1)} %get-tuple-element.112), channel_id=1, source_target_pairs={{0,1},{1,0},{2,3},{3,2},{4,5},{5,4},{6,7},{7,6},{8,9},{9,8},{10,11... | collective-permute-start | bytes 1572872 | tf_op jit(solution)/shard_map/ppermute | solution.py:81
  291.8 26.3 %collective-permute-start.24 = (bf16[128,2048]{1,0:T(8,128)(2,1)}, bf16[128,2048]{1,0:T(8,128)(2,1)}, u32[]{:S(2)}, u32[]{:S(2)}) collective-permute-start(bf16[128,2048]{1,0:T(8,128)(2,1)} %get-tuple-element.112), channel_id=1, source_target_pairs={{0,2},{1,3},{2,0},{3,1},{4,6},{5,7},{6,4},{7,5},{8,10},{9,11},{10,... | collective-permute-start | bytes 1572872 | tf_op jit(solution)/shard_map/ppermute | solution.py:81
  292.1 27.9 %collective-permute-start.25 = (bf16[128,2048]{1,0:T(8,128)(2,1)}, bf16[128,2048]{1,0:T(8,128)(2,1)}, u32[]{:S(2)}, u32[]{:S(2)}) collective-permute-start(bf16[128,2048]{1,0:T(8,128)(2,1)} %get-tuple-element.112), channel_id=1, source_target_pairs={{0,3},{1,2},{2,1},{3,0},{4,7},{5,6},{6,5},{7,4},{8,11},{9,10},{10,... | collective-permute-start | bytes 1572872 | tf_op jit(solution)/shard_map/ppermute | solution.py:81
  296.2 89.9 %collective-permute-start.35 = (bf16[128,2048]{1,0:T(8,128)(2,1)}, bf16[128,2048]{1,0:T(8,128)(2,1)}, u32[]{:S(2)}, u32[]{:S(2)}) collective-permute-start(bf16[128,2048]{1,0:T(8,128)(2,1)} %get-tuple-element.118), channel_id=1, source_target_pairs={{0,1},{1,0},{2,3},{3,2},{4,5},{5,4},{6,7},{7,6},{8,9},{9,8},{10,11... | collective-permute-start | bytes 1572872 | tf_op jit(solution)/shard_map/ppermute | solution.py:81
  296.5 90.3 %collective-permute-start.36 = (bf16[128,2048]{1,0:T(8,128)(2,1)}, bf16[128,2048]{1,0:T(8,128)(2,1)}, u32[]{:S(2)}, u32[]{:S(2)}) collective-permute-start(bf16[128,2048]{1,0:T(8,128)(2,1)} %get-tuple-element.118), channel_id=1, source_target_pairs={{0,2},{1,3},{2,0},{3,1},{4,6},{5,7},{6,4},{7,5},{8,10},{9,11},{10,... | collective-permute-start | bytes 1572872 | tf_op jit(solution)/shard_map/ppermute | solution.py:81
  323.8 14.9 %collective-permute-start.29 = (bf16[128,2048]{1,0:T(8,128)(2,1)S(1)}, bf16[128,2048]{1,0:T(8,128)(2,1)S(1)}, u32[]{:S(2)}, u32[]{:S(2)}) collective-permute-start(bf16[128,2048]{1,0:T(8,128)(2,1)S(1)} %get-tuple-element.110), channel_id=1, source_target_pairs={{0,1},{1,0},{2,3},{3,2},{4,5},{5,4},{6,7},{7,6},{8,9},{9,8},{10,11... | collective-permute-start | bytes 1572872 | tf_op jit(solution)/shard_map/ppermute | solution.py:81
  325.6 36.7 %collective-permute-start.30 = (bf16[128,2048]{1,0:T(8,128)(2,1)S(1)}, bf16[128,2048]{1,0:T(8,128)(2,1)S(1)}, u32[]{:S(2)}, u32[]{:S(2)}) collective-permute-start(bf16[128,2048]{1,0:T(8,128)(2,1)S(1)} %get-tuple-element.110), channel_id=1, source_target_pairs={{0,2},{1,3},{2,0},{3,1},{4,6},{5,7},{6,4},{7,5},{8,10},{9,11},{10,... | collective-permute-start | bytes 1572872 | tf_op jit(solution)/shard_map/ppermute | solution.py:81
  325.8 37.8 %collective-permute-start.31 = (bf16[128,2048]{1,0:T(8,128)(2,1)S(1)}, bf16[128,2048]{1,0:T(8,128)(2,1)S(1)}, u32[]{:S(2)}, u32[]{:S(2)}) collective-permute-start(bf16[128,2048]{1,0:T(8,128)(2,1)S(1)} %get-tuple-element.110), channel_id=1, source_target_pairs={{0,3},{1,2},{2,1},{3,0},{4,7},{5,6},{6,5},{7,4},{8,11},{9,10},{10,... | collective-permute-start | bytes 1572872 | tf_op jit(solution)/shard_map/ppermute | solution.py:81
  338.7 49.4 %collective-permute-start.37 = (bf16[128,2048]{1,0:T(8,128)(2,1)}, bf16[128,2048]{1,0:T(8,128)(2,1)}, u32[]{:S(2)}, u32[]{:S(2)}) collective-permute-start(bf16[128,2048]{1,0:T(8,128)(2,1)} %get-tuple-element.118), channel_id=1, source_target_pairs={{0,3},{1,2},{2,1},{3,0},{4,7},{5,6},{6,5},{7,4},{8,11},{9,10},{10,... | collective-permute-start | bytes 1572872 | tf_op jit(solution)/shard_map/ppermute | solution.py:81
  362.3 74.5 %collective-permute-start.47 = (bf16[128,2048]{1,0:T(8,128)(2,1)}, bf16[128,2048]{1,0:T(8,128)(2,1)}, u32[]{:S(2)}, u32[]{:S(2)}) collective-permute-start(bf16[128,2048]{1,0:T(8,128)(2,1)} %get-tuple-element.119), channel_id=1, source_target_pairs={{0,1},{1,0},{2,3},{3,2},{4,5},{5,4},{6,7},{7,6},{8,9},{9,8},{10,11... | collective-permute-start | bytes 1572872 | tf_op jit(solution)/shard_map/ppermute | solution.py:81
  363.7 74.5 %collective-permute-start.48 = (bf16[128,2048]{1,0:T(8,128)(2,1)}, bf16[128,2048]{1,0:T(8,128)(2,1)}, u32[]{:S(2)}, u32[]{:S(2)}) collective-permute-start(bf16[128,2048]{1,0:T(8,128)(2,1)} %get-tuple-element.119), channel_id=1, source_target_pairs={{0,2},{1,3},{2,0},{3,1},{4,6},{5,7},{6,4},{7,5},{8,10},{9,11},{10,... | collective-permute-start | bytes 1572872 | tf_op jit(solution)/shard_map/ppermute | solution.py:81
  386.1 24.1 %collective-permute-start.41 = (bf16[128,2048]{1,0:T(8,128)(2,1)}, bf16[128,2048]{1,0:T(8,128)(2,1)}, u32[]{:S(2)}, u32[]{:S(2)}) collective-permute-start(bf16[128,2048]{1,0:T(8,128)(2,1)} %get-tuple-element.120), channel_id=1, source_target_pairs={{0,1},{1,0},{2,3},{3,2},{4,5},{5,4},{6,7},{7,6},{8,9},{9,8},{10,11... | collective-permute-start | bytes 1572872 | tf_op jit(solution)/shard_map/ppermute | solution.py:81
  386.8 24.8 %collective-permute-start.42 = (bf16[128,2048]{1,0:T(8,128)(2,1)}, bf16[128,2048]{1,0:T(8,128)(2,1)}, u32[]{:S(2)}, u32[]{:S(2)}) collective-permute-start(bf16[128,2048]{1,0:T(8,128)(2,1)} %get-tuple-element.120), channel_id=1, source_target_pairs={{0,2},{1,3},{2,0},{3,1},{4,6},{5,7},{6,4},{7,5},{8,10},{9,11},{10,... | collective-permute-start | bytes 1572872 | tf_op jit(solution)/shard_map/ppermute | solution.py:81
  388.1 25.0 %collective-permute-start.43 = (bf16[128,2048]{1,0:T(8,128)(2,1)}, bf16[128,2048]{1,0:T(8,128)(2,1)}, u32[]{:S(2)}, u32[]{:S(2)}) collective-permute-start(bf16[128,2048]{1,0:T(8,128)(2,1)} %get-tuple-element.120), channel_id=1, source_target_pairs={{0,3},{1,2},{2,1},{3,0},{4,7},{5,6},{6,5},{7,4},{8,11},{9,10},{10,... | collective-permute-start | bytes 1572872 | tf_op jit(solution)/shard_map/ppermute | solution.py:81
  410.3 29.3 %collective-permute-start.49 = (bf16[128,2048]{1,0:T(8,128)(2,1)}, bf16[128,2048]{1,0:T(8,128)(2,1)S(1)}, u32[]{:S(2)}, u32[]{:S(2)}) collective-permute-start(bf16[128,2048]{1,0:T(8,128)(2,1)} %get-tuple-element.119), channel_id=1, source_target_pairs={{0,3},{1,2},{2,1},{3,0},{4,7},{5,6},{6,5},{7,4},{8,11},{9,10},{10,... | collective-permute-start | bytes 1572872 | tf_op jit(solution)/shard_map/ppermute | solution.py:81
  411.7 49.2 %collective-permute-start.38 = (bf16[128,2048]{1,0:T(8,128)(2,1)S(1)}, bf16[128,2048]{1,0:T(8,128)(2,1)S(1)}, u32[]{:S(2)}, u32[]{:S(2)}) collective-permute-start(bf16[128,2048]{1,0:T(8,128)(2,1)S(1)} %get-tuple-element.91), channel_id=1, source_target_pairs={{0,1},{1,0},{2,3},{3,2},{4,5},{5,4},{6,7},{7,6},{8,9},{9,8},{10,11... | collective-permute-start | bytes 1572872 | tf_op jit(solution)/shard_map/ppermute | solution.py:81
  413.1 49.3 %collective-permute-start.39 = (bf16[128,2048]{1,0:T(8,128)(2,1)S(1)}, bf16[128,2048]{1,0:T(8,128)(2,1)S(1)}, u32[]{:S(2)}, u32[]{:S(2)}) collective-permute-start(bf16[128,2048]{1,0:T(8,128)(2,1)S(1)} %get-tuple-element.93), channel_id=1, source_target_pairs={{0,2},{1,3},{2,0},{3,1},{4,6},{5,7},{6,4},{7,5},{8,10},{9,11},{10,... | collective-permute-start | bytes 1572872 | tf_op jit(solution)/shard_map/ppermute | solution.py:81
  436.8 27.1 %collective-permute-start.40 = (bf16[128,2048]{1,0:T(8,128)(2,1)S(1)}, bf16[128,2048]{1,0:T(8,128)(2,1)S(1)}, u32[]{:S(2)}, u32[]{:S(2)}) collective-permute-start(bf16[128,2048]{1,0:T(8,128)(2,1)S(1)} %get-tuple-element.92), channel_id=1, source_target_pairs={{0,3},{1,2},{2,1},{3,0},{4,7},{5,6},{6,5},{7,4},{8,11},{9,10},{10,... | collective-permute-start | bytes 1572872 | tf_op jit(solution)/shard_map/ppermute | solution.py:81
  438.2 26.4 %collective-permute-start.44 = (bf16[128,2048]{1,0:T(8,128)(2,1)S(1)}, bf16[128,2048]{1,0:T(8,128)(2,1)S(1)}, u32[]{:S(2)}, u32[]{:S(2)}) collective-permute-start(bf16[128,2048]{1,0:T(8,128)(2,1)S(1)} %get-tuple-element.94), channel_id=1, source_target_pairs={{0,1},{1,0},{2,3},{3,2},{4,5},{5,4},{6,7},{7,6},{8,9},{9,8},{10,11... | collective-permute-start | bytes 1572872 | tf_op jit(solution)/shard_map/ppermute | solution.py:81
  439.6 27.3 %collective-permute-start.45 = (bf16[128,2048]{1,0:T(8,128)(2,1)S(1)}, bf16[128,2048]{1,0:T(8,128)(2,1)S(1)}, u32[]{:S(2)}, u32[]{:S(2)}) collective-permute-start(bf16[128,2048]{1,0:T(8,128)(2,1)S(1)} %get-tuple-element.96), channel_id=1, source_target_pairs={{0,2},{1,3},{2,0},{3,1},{4,6},{5,7},{6,4},{7,5},{8,10},{9,11},{10,... | collective-permute-start | bytes 1572872 | tf_op jit(solution)/shard_map/ppermute | solution.py:81
  460.9 15.8 %collective-permute-start.46 = (bf16[128,2048]{1,0:T(8,128)(2,1)S(1)}, bf16[128,2048]{1,0:T(8,128)(2,1)S(1)}, u32[]{:S(2)}, u32[]{:S(2)}) collective-permute-start(bf16[128,2048]{1,0:T(8,128)(2,1)S(1)} %get-tuple-element.95), channel_id=1, source_target_pairs={{0,3},{1,2},{2,1},{3,0},{4,7},{5,6},{6,5},{7,4},{8,11},{9,10},{10,... | collective-permute-start | bytes 1572872 | tf_op jit(solution)/shard_map/ppermute | solution.py:81
  462.4 25.4 %collective-permute-start.50 = (bf16[128,2048]{1,0:T(8,128)(2,1)S(1)}, bf16[128,2048]{1,0:T(8,128)(2,1)S(1)}, u32[]{:S(2)}, u32[]{:S(2)}) collective-permute-start(bf16[128,2048]{1,0:T(8,128)(2,1)S(1)} %get-tuple-element.97), channel_id=1, source_target_pairs={{0,1},{1,0},{2,3},{3,2},{4,5},{5,4},{6,7},{7,6},{8,9},{9,8},{10,11... | collective-permute-start | bytes 1572872 | tf_op jit(solution)/shard_map/ppermute | solution.py:81
  463.9 24.0 %collective-permute-start.51 = (bf16[128,2048]{1,0:T(8,128)(2,1)S(1)}, bf16[128,2048]{1,0:T(8,128)(2,1)S(1)}, u32[]{:S(2)}, u32[]{:S(2)}) collective-permute-start(bf16[128,2048]{1,0:T(8,128)(2,1)S(1)} %get-tuple-element.99), channel_id=1, source_target_pairs={{0,2},{1,3},{2,0},{3,1},{4,6},{5,7},{6,4},{7,5},{8,10},{9,11},{10,... | collective-permute-start | bytes 1572872 | tf_op jit(solution)/shard_map/ppermute | solution.py:81
  464.6 29.8 %collective-permute-start.52 = (bf16[128,2048]{1,0:T(8,128)(2,1)S(1)}, bf16[128,2048]{1,0:T(8,128)(2,1)S(1)}, u32[]{:S(2)}, u32[]{:S(2)}) collective-permute-start(bf16[128,2048]{1,0:T(8,128)(2,1)S(1)} %get-tuple-element.98), channel_id=1, source_target_pairs={{0,3},{1,2},{2,1},{3,0},{4,7},{5,6},{6,5},{7,4},{8,11},{9,10},{10,... | collective-permute-start | bytes 1572872 | tf_op jit(solution)/shard_map/ppermute | solution.py:81
  536.3 30.5 %collective-permute-start.58 = (bf16[1024,2048]{1,0:T(8,128)(2,1)S(1)}, bf16[1024,2048]{1,0:T(8,128)(2,1)S(1)}, u32[]{:S(2)}, u32[]{:S(2)}) collective-permute-start(bf16[1024,2048]{1,0:T(8,128)(2,1)S(1)} %convolution_convert_fusion.3), channel_id=1, source_target_pairs={{0,4},{4,0},{8,12},{12,8},{16,20},{20,16},{24,28},{28,24},{1,5},{5... | collective-permute-start | bytes 12582920 | tf_op jit(solution)/shard_map/ppermute | solution.py:81
  541.9 30.8 %collective-permute-start.66 = (bf16[1024,2048]{1,0:T(8,128)(2,1)}, bf16[1024,2048]{1,0:T(8,128)(2,1)S(1)}, u32[]{:S(2)}, u32[]{:S(2)}) collective-permute-start(bf16[1024,2048]{1,0:T(8,128)(2,1)} %convolution_convert_fusion.2), channel_id=1, source_target_pairs={{0,4},{4,0},{8,12},{12,8},{16,20},{20,16},{24,28},{28,24},{1,5},{5... | collective-permute-start | bytes 12582920 | tf_op jit(solution)/shard_map/ppermute | solution.py:81
  542.8 14.7 %collective-permute-start.56 = (bf16[3,1,128,256]{3,2,1,0:T(8,128)(2,1)S(1)}, bf16[3,1,128,256]{3,2,1,0:T(8,128)(2,1)S(1)}, u32[]{:S(2)}, u32[]{:S(2)}) collective-permute-start(bf16[3,1,128,256]{3,2,1,0:T(8,128)(2,1)S(1)} %get-tuple-element.117), channel_id=1, source_target_pairs={{0,2},{1,3},{2,0},{3,1},{4,6},{5,7},{6,4},{7,5},{8,10},{9,11},{10,... | collective-permute-start | bytes 589832 | tf_op jit(solution)/shard_map/ppermute | solution.py:81
  571.0 53.0 %collective-permute-start.59 = (bf16[256,2048]{1,0:T(8,128)(2,1)}, bf16[256,2048]{1,0:T(8,128)(2,1)}, u32[]{:S(2)}, u32[]{:S(2)}) collective-permute-start(bf16[256,2048]{1,0:T(8,128)(2,1)} %get-tuple-element.68), channel_id=1, source_target_pairs={{0,1},{1,0},{2,3},{3,2},{4,5},{5,4},{6,7},{7,6},{8,9},{9,8},{10,11... | collective-permute-start | bytes 3145736 | tf_op jit(solution)/shard_map/ppermute | solution.py:81
  571.4 54.9 %collective-permute-start.60 = (bf16[256,2048]{1,0:T(8,128)(2,1)}, bf16[256,2048]{1,0:T(8,128)(2,1)}, u32[]{:S(2)}, u32[]{:S(2)}) collective-permute-start(bf16[256,2048]{1,0:T(8,128)(2,1)} %get-tuple-element.70), channel_id=1, source_target_pairs={{0,2},{1,3},{2,0},{3,1},{4,6},{5,7},{6,4},{7,5},{8,10},{9,11},{10,... | collective-permute-start | bytes 3145736 | tf_op jit(solution)/shard_map/ppermute | solution.py:81
  572.7 53.5 %collective-permute-start.61 = (bf16[256,2048]{1,0:T(8,128)(2,1)}, bf16[256,2048]{1,0:T(8,128)(2,1)}, u32[]{:S(2)}, u32[]{:S(2)}) collective-permute-start(bf16[256,2048]{1,0:T(8,128)(2,1)} %get-tuple-element.69), channel_id=1, source_target_pairs={{0,3},{1,2},{2,1},{3,0},{4,7},{5,6},{6,5},{7,4},{8,11},{9,10},{10,... | collective-permute-start | bytes 3145736 | tf_op jit(solution)/shard_map/ppermute | solution.py:81
  576.9 45.4 %collective-permute-start.65 = (bf16[32,2048]{1,0:T(8,128)(2,1)S(1)}, bf16[32,2048]{1,0:T(8,128)(2,1)S(1)}, u32[]{:S(2)}, u32[]{:S(2)}) collective-permute-start(bf16[32,2048]{1,0:T(8,128)(2,1)S(1)} %get-tuple-element.124), channel_id=1, source_target_pairs={{0,3},{1,2},{2,1},{3,0},{4,7},{5,6},{6,5},{7,4},{8,11},{9,10},{10,... | collective-permute-start | bytes 393224 | tf_op jit(solution)/shard_map/ppermute | solution.py:81
  578.6 66.4 %collective-permute-start.67 = (bf16[256,2048]{1,0:T(8,128)(2,1)S(1)}, bf16[256,2048]{1,0:T(8,128)(2,1)S(1)}, u32[]{:S(2)}, u32[]{:S(2)}) collective-permute-start(bf16[256,2048]{1,0:T(8,128)(2,1)S(1)} %get-tuple-element.71), channel_id=1, source_target_pairs={{0,1},{1,0},{2,3},{3,2},{4,5},{5,4},{6,7},{7,6},{8,9},{9,8},{10,11... | collective-permute-start | bytes 3145736 | tf_op jit(solution)/shard_map/ppermute | solution.py:81
  622.3 45.6 %collective-permute-start.68 = (bf16[256,2048]{1,0:T(8,128)(2,1)S(1)}, bf16[256,2048]{1,0:T(8,128)(2,1)S(1)}, u32[]{:S(2)}, u32[]{:S(2)}) collective-permute-start(bf16[256,2048]{1,0:T(8,128)(2,1)S(1)} %get-tuple-element.73), channel_id=1, source_target_pairs={{0,2},{1,3},{2,0},{3,1},{4,6},{5,7},{6,4},{7,5},{8,10},{9,11},{10,... | collective-permute-start | bytes 3145736 | tf_op jit(solution)/shard_map/ppermute | solution.py:81
  624.0 43.9 %collective-permute-start.69 = (bf16[256,2048]{1,0:T(8,128)(2,1)S(1)}, bf16[256,2048]{1,0:T(8,128)(2,1)S(1)}, u32[]{:S(2)}, u32[]{:S(2)}) collective-permute-start(bf16[256,2048]{1,0:T(8,128)(2,1)S(1)} %get-tuple-element.72), channel_id=1, source_target_pairs={{0,3},{1,2},{2,1},{3,0},{4,7},{5,6},{6,5},{7,4},{8,11},{9,10},{10,... | collective-permute-start | bytes 3145736 | tf_op jit(solution)/shard_map/ppermute | solution.py:81
  670.1 212.3 %reduce-scatter.8.cloned.1.call-start = ((), (), s32[]{:S(2)}) async-start(), calls=%async_computation.9 | async-start | bytes 9437184 | tf_op jit(solution)/shard_map/reduce_scatter | solution.py:476
  697.2 240.4 %reduce-scatter.6.cloned.1.call-start = ((), (), s32[]{:S(2)}) async-start(), calls=%async_computation.8 | async-start | bytes 9437184 | tf_op jit(solution)/shard_map/reduce_scatter | solution.py:476
  733.4 21.1 %collective-permute-start.26 = (bf16[128,2048]{1,0:T(8,128)(2,1)S(1)}, bf16[128,2048]{1,0:T(8,128)(2,1)S(1)}, u32[]{:S(2)}, u32[]{:S(2)}) collective-permute-start(bf16[128,2048]{1,0:T(8,128)(2,1)S(1)} %get-tuple-element.103), channel_id=1, source_target_pairs={{0,1},{1,0},{2,3},{3,2},{4,5},{5,4},{6,7},{7,6},{8,9},{9,8},{10,11... | collective-permute-start | bytes 1572872 | tf_op jit(solution)/shard_map/ppermute | solution.py:81
  734.8 23.5 %collective-permute-start.27 = (bf16[128,2048]{1,0:T(8,128)(2,1)S(1)}, bf16[128,2048]{1,0:T(8,128)(2,1)S(1)}, u32[]{:S(2)}, u32[]{:S(2)}) collective-permute-start(bf16[128,2048]{1,0:T(8,128)(2,1)S(1)} %get-tuple-element.105), channel_id=1, source_target_pairs={{0,2},{1,3},{2,0},{3,1},{4,6},{5,7},{6,4},{7,5},{8,10},{9,11},{10,... | collective-permute-start | bytes 1572872 | tf_op jit(solution)/shard_map/ppermute | solution.py:81
  735.4 25.2 %collective-permute-start.28 = (bf16[128,2048]{1,0:T(8,128)(2,1)S(1)}, bf16[128,2048]{1,0:T(8,128)(2,1)S(1)}, u32[]{:S(2)}, u32[]{:S(2)}) collective-permute-start(bf16[128,2048]{1,0:T(8,128)(2,1)S(1)} %get-tuple-element.104), channel_id=1, source_target_pairs={{0,3},{1,2},{2,1},{3,0},{4,7},{5,6},{6,5},{7,4},{8,11},{9,10},{10,... | collective-permute-start | bytes 1572872 | tf_op jit(solution)/shard_map/ppermute | solution.py:81
  744.1 26.7 %collective-permute-start.32 = (bf16[128,2048]{1,0:T(8,128)(2,1)S(1)}, bf16[128,2048]{1,0:T(8,128)(2,1)S(1)}, u32[]{:S(2)}, u32[]{:S(2)}) collective-permute-start(bf16[128,2048]{1,0:T(8,128)(2,1)S(1)} %get-tuple-element.106), channel_id=1, source_target_pairs={{0,1},{1,0},{2,3},{3,2},{4,5},{5,4},{6,7},{7,6},{8,9},{9,8},{10,11... | collective-permute-start | bytes 1572872 | tf_op jit(solution)/shard_map/ppermute | solution.py:81
  745.6 35.2 %collective-permute-start.33 = (bf16[128,2048]{1,0:T(8,128)(2,1)S(1)}, bf16[128,2048]{1,0:T(8,128)(2,1)S(1)}, u32[]{:S(2)}, u32[]{:S(2)}) collective-permute-start(bf16[128,2048]{1,0:T(8,128)(2,1)S(1)} %get-tuple-element.108), channel_id=1, source_target_pairs={{0,2},{1,3},{2,0},{3,1},{4,6},{5,7},{6,4},{7,5},{8,10},{9,11},{10,... | collective-permute-start | bytes 1572872 | tf_op jit(solution)/shard_map/ppermute | solution.py:81
  754.5 28.7 %collective-permute-start.34 = (bf16[128,2048]{1,0:T(8,128)(2,1)S(1)}, bf16[128,2048]{1,0:T(8,128)(2,1)S(1)}, u32[]{:S(2)}, u32[]{:S(2)}) collective-permute-start(bf16[128,2048]{1,0:T(8,128)(2,1)S(1)} %get-tuple-element.107), channel_id=1, source_target_pairs={{0,3},{1,2},{2,1},{3,0},{4,7},{5,6},{6,5},{7,4},{8,11},{9,10},{10,... | collective-permute-start | bytes 1572872 | tf_op jit(solution)/shard_map/ppermute | solution.py:81
  758.3 35.0 %collective-permute-start.20 = (bf16[128,2048]{1,0:T(8,128)(2,1)S(1)}, bf16[128,2048]{1,0:T(8,128)(2,1)S(1)}, u32[]{:S(2)}, u32[]{:S(2)}) collective-permute-start(bf16[128,2048]{1,0:T(8,128)(2,1)S(1)} %get-tuple-element.100), channel_id=1, source_target_pairs={{0,1},{1,0},{2,3},{3,2},{4,5},{5,4},{6,7},{7,6},{8,9},{9,8},{10,11... | collective-permute-start | bytes 1572872 | tf_op jit(solution)/shard_map/ppermute | solution.py:81
  760.7 33.7 %collective-permute-start.21 = (bf16[128,2048]{1,0:T(8,128)(2,1)S(1)}, bf16[128,2048]{1,0:T(8,128)(2,1)S(1)}, u32[]{:S(2)}, u32[]{:S(2)}) collective-permute-start(bf16[128,2048]{1,0:T(8,128)(2,1)S(1)} %get-tuple-element.102), channel_id=1, source_target_pairs={{0,2},{1,3},{2,0},{3,1},{4,6},{5,7},{6,4},{7,5},{8,10},{9,11},{10,... | collective-permute-start | bytes 1572872 | tf_op jit(solution)/shard_map/ppermute | solution.py:81
  770.8 31.3 %collective-permute-start.22 = (bf16[128,2048]{1,0:T(8,128)(2,1)S(1)}, bf16[128,2048]{1,0:T(8,128)(2,1)S(1)}, u32[]{:S(2)}, u32[]{:S(2)}) collective-permute-start(bf16[128,2048]{1,0:T(8,128)(2,1)S(1)} %get-tuple-element.101), channel_id=1, source_target_pairs={{0,3},{1,2},{2,1},{3,0},{4,7},{5,6},{6,5},{7,4},{8,11},{9,10},{10,... | collective-permute-start | bytes 1572872 | tf_op jit(solution)/shard_map/ppermute | solution.py:81
  812.7 43.5 %collective-permute-start.72 = (f32[177,128]{1,0:T(8,128)S(1)}, f32[177,128]{1,0:T(8,128)S(1)}, u32[]{:S(2)}, u32[]{:S(2)}) collective-permute-start(f32[177,128]{1,0:T(8,128)S(1)} %bitcast_add_fusion.2), channel_id=1, source_target_pairs={{0,8},{4,12},{8,0},{12,4},{16,24},{20,28},{24,16},{28,20},{1,9},{5... | collective-permute-start | bytes 271880 | tf_op jit(solution)/shard_map/ppermute | solution.py:81
  (118 other events, 1491.0 us)
Sparse Core Ops, SparseCore 0:
  12.4 35.5 all-gather.4
  50.1 29.5 all-gather.6
  81.3 83.9 all-gather.8
  223.6 92.9 all-gather.10
  670.2 81.6 reduce-scatter.3
  754.1 89.0 reduce-scatter.7
  845.4 92.1 reduce-scatter.5

commit v2 on v1

--- a/solution.py
+++ b/solution.py
@@ -1,3 +1,4 @@
+import functools
 import math
 
 import jax
@@ -29,6 +30,8 @@
 bf16 = jnp.bfloat16
 f32 = jnp.float32
 
+cheap = pl.CostEstimate(flops=1 << 20, transcendentals=0, bytes_accessed=1 << 20)
+
 
 def layer_norm_fwd(values, gain, shift):
     mean_row = jnp.mean(values, -1, keepdims=True)
@@ -85,15 +88,38 @@
     return swap(value, "dp", 1)
 
 
+def spread_directly(value):
+    return [value] + [swap(value, "tp", m) for m in range(1, lax.axis_size("tp"))]
+
+
+def cut(value):
+    at = value.shape[-2] // 2
+    return (value[..., :at, :], value[..., at:, :])
+
+
 def spread(value):
-    return [value] + [swap(value, "tp", m) for m in range(1, lax.axis_size("tp"))]
-
-
-def collect(pieces):
+    if lax.axis_size("tp") != 4:
+        return spread_directly(value)
+    first = swap(value, "tp", 1)
+    second = swap(value, "tp", 2)
+    far_top = swap(cut(first)[0], "tp", 2)
+    far_low = swap(cut(second)[1], "tp", 1)
+    return [value, first, second, jnp.concatenate([far_top, far_low], -2)]
+
+
+def deliver(pieces):
+    return [pieces[0]] + [swap(pieces[m].astype(bf16), "tp", m) for m in range(1, len(pieces))]
+
+
+def total_of(pieces):
     total = pieces[0].astype(f32)
-    for m in range(1, len(pieces)):
-        total = total + swap(pieces[m].astype(bf16), "tp", m).astype(f32)
+    for piece in pieces[1:]:
+        total = total + piece.astype(f32)
     return total
+
+
+def after(value, *others):
+    return lax.optimization_barrier((value,) + others)[0]
 
 
 def sum_everywhere(value):
@@ -236,11 +262,7 @@
         compiler_params=pltpu.CompilerParams(
             dimension_semantics=("arbitrary", "arbitrary"), vmem_limit_bytes=32 << 20
         ),
-        cost_estimate=pl.CostEstimate(
-            flops=4 * batches * rows * cols * KEY_ROWS,
-            transcendentals=batches * rows * (cols // HD) * KEY_ROWS,
-            bytes_accessed=batches * (4 * rows * cols + KEY_ROWS * HD * 8),
-        ),
+        cost_estimate=cheap,
     )(bounds, queries, keys, vals_t, bias)
 
 
@@ -279,12 +301,156 @@
         compiler_params=pltpu.CompilerParams(
             dimension_semantics=("arbitrary", "arbitrary"), vmem_limit_bytes=40 << 20
         ),
-        cost_estimate=pl.CostEstimate(
-            flops=10 * batches * rows * cols * KEY_ROWS,
-            transcendentals=batches * rows * (cols // HD) * KEY_ROWS,
-            bytes_accessed=batches * (6 * rows * cols + KEY_ROWS * HD * 20),
-        ),
+        cost_estimate=cheap,
     )(bounds, queries, grads, keys, keys_t, vals, bias, log_sums)
+
+
+def gelu_parts(values):
+    square = values * values
+    return jnp.tanh(values * (gelu_coef + (gelu_coef * 0.044715) * square)), square
+
+
+def ffn_up_kernel(*refs):
+    count = len(refs) - 4
+    hidden_refs = refs[:count]
+    weight_ref, bias_ref, pre_ref, act_ref = refs[count:]
+    rows = hidden_refs[0].shape[0]
+    for m in range(count):
+        at = pl.ds(m * rows, rows)
+        values = rows_by_rows(hidden_refs[m][...], weight_ref[...]) + bias_ref[...]
+        pre_ref[at, :] = values
+        tangent, _ = gelu_parts(values)
+        act_ref[at, :] = (0.5 * values * (1.0 + tangent)).astype(bf16)
+
+
+def ffn_back_kernel(*refs, count):
+    weight_ref = refs[count]
+    pre_refs, (grad_ref, sum_ref) = refs[count + 1 : -2], refs[-2:]
+    cot_refs = refs[:count]
+    rows = cot_refs[0].shape[0]
+    total = jnp.zeros(sum_ref.shape, f32)
+    for m in range(count):
+        at = pl.ds(m * rows, rows)
+        values = piece_of(pre_refs, m, rows)
+        tangent, square = gelu_parts(values)
+        slope = 0.5 * (1.0 + tangent) + (0.5 * gelu_coef) * values * (1.0 - tangent * tangent) * (
+            1.0 + (3.0 * 0.044715) * square
+        )
+        grad = (rows_by_rows(cot_refs[m][...], weight_ref[...]) * slope).astype(bf16)
+        grad_ref[at, :] = grad
+        total = total + jnp.sum(grad.astype(f32), 0, keepdims=True)
+    sum_ref[...] = total
+
+
+def piece_of(refs, index, rows):
+    at = index * rows
+    for ref in refs:
+        if at < ref.shape[0]:
+            return ref[pl.ds(at, rows), :]
+        at -= ref.shape[0]
+
+
+def ffn_product_kernel(*refs, lefts):
+    right_ref, out_refs = refs[lefts], refs[lefts + 1 :]
+    for m, out_ref in enumerate(out_refs):
+        left = piece_of(refs[:lefts], m, out_ref.shape[0])
+        out_ref[...] = plain_dot(left, right_ref[...]).astype(bf16)
+
+
+def ffn_weight_kernel(*refs, lefts):
+    right_refs, out_ref = refs[lefts:-1], refs[-1]
+    rows = right_refs[0].shape[0]
+    total = None
+    for m, right_ref in enumerate(right_refs):
+        part = cols_by_cols(piece_of(refs[:lefts], m, rows), right_ref[...])
+        total = part if total is None else total + part
+    out_ref[...] = total.astype(bf16)
+
+
+def ffn_params():
+    return pltpu.CompilerParams(
+        dimension_semantics=("arbitrary",), vmem_limit_bytes=56 << 20
+    )
+
+
+def whole_specs(pieces):
+    return [pl.BlockSpec(piece.shape, lambda i: (0, 0)) for piece in pieces]
+
+
+def ffn_up(pieces, weights, bias, tile=256):
+    units, width = weights.shape
+    rows = len(pieces) * pieces[0].shape[0]
+    out_spec = pl.BlockSpec((rows, tile), lambda i: (0, i))
+    return pl.pallas_call(
+        ffn_up_kernel,
+        name="ffn_up",
+        grid=(units // tile,),
+        in_specs=whole_specs(pieces)
+        + [
+            pl.BlockSpec((tile, width), lambda i: (i, 0)),
+            pl.BlockSpec((1, tile), lambda i: (0, i)),
+        ],
+        out_specs=[out_spec, out_spec],
+        out_shape=[
+            jax.ShapeDtypeStruct((rows, units), f32),
+            jax.ShapeDtypeStruct((rows, units), bf16),
+        ],
+        compiler_params=ffn_params(),
+        cost_estimate=cheap,
+    )(*pieces, weights, bias.reshape(1, units))
+
+
+def ffn_back(pieces, weights, pre_acts, tile=256):
+    units, width = weights.shape
+    rows = len(pieces) * pieces[0].shape[0]
+    out_spec = pl.BlockSpec((rows, tile), lambda i: (0, i))
+    sum_spec = pl.BlockSpec((1, tile), lambda i: (0, i))
+    return pl.pallas_call(
+        functools.partial(ffn_back_kernel, count=len(pieces)),
+        name="ffn_back",
+        grid=(units // tile,),
+        in_specs=whole_specs(pieces)
+        + [pl.BlockSpec((tile, width), lambda i: (i, 0))]
+        + [pl.BlockSpec((part.shape[0], tile), lambda i: (0, i)) for part in pre_acts],
+        out_specs=[out_spec, sum_spec],
+        out_shape=[
+            jax.ShapeDtypeStruct((rows, units), bf16),
+            jax.ShapeDtypeStruct((1, units), f32),
+        ],
+        compiler_params=ffn_params(),
+        cost_estimate=cheap,
+    )(*pieces, weights, *pre_acts)
+
+
+def ffn_product(lefts, right, count, tile=256):
+    units, width = right.shape
+    piece = sum(left.shape[0] for left in lefts) // count
+    return pl.pallas_call(
+        functools.partial(ffn_product_kernel, lefts=len(lefts)),
+        name="ffn_product",
+        grid=(width // tile,),
+        in_specs=whole_specs(lefts) + [pl.BlockSpec((units, tile), lambda i: (0, i))],
+        out_specs=[pl.BlockSpec((piece, tile), lambda i: (0, i))] * count,
+        out_shape=[jax.ShapeDtypeStruct((piece, width), bf16)] * count,
+        compiler_params=ffn_params(),
+        cost_estimate=cheap,
+    )(*lefts, right)
+
+
+def ffn_weight(lefts, pieces, tile=256):
+    units = lefts[0].shape[1]
+    width = pieces[0].shape[1]
+    return pl.pallas_call(
+        functools.partial(ffn_weight_kernel, lefts=len(lefts)),
+        name="ffn_weight",
+        grid=(units // tile,),
+        in_specs=[pl.BlockSpec((left.shape[0], tile), lambda i: (0, i)) for left in lefts]
+        + whole_specs(pieces),
+        out_specs=pl.BlockSpec((tile, width), lambda i: (i, 0)),
+        out_shape=jax.ShapeDtypeStruct((units, width), bf16),
+        compiler_params=ffn_params(),
+        cost_estimate=cheap,
+    )(*lefts, *pieces)
 
 
 def adam_step(weights, grads, first, second, step_count, learning_rate):
@@ -295,6 +461,45 @@
     corr_two = 1.0 - jnp.power(beta_two, steps_float)
     update = first_new / corr_one / (jnp.sqrt(second_new / corr_two) + adam_eps)
     return (weights - learning_rate[0] * (update + decay_rate * weights), first_new, second_new)
+
+
+def adam_kernel(scalars, weights, grads, first, second, *refs):
+    new_weights, new_first, new_second = refs[-3:]
+    rate = scalars[0]
+    grad = grads[...].astype(f32)
+    first_new = beta_one * first[...] + (1.0 - beta_one) * grad
+    second_new = beta_two * second[...] + (1.0 - beta_two) * grad * grad
+    update = first_new / scalars[1] / (jnp.sqrt(second_new / scalars[2]) + adam_eps)
+    new_weights[...] = weights[...] - rate * (update + decay_rate * weights[...])
+    new_first[...] = first_new
+    new_second[...] = second_new
+
+
+def adam_rows(scalars, weights, grads, first, second, start, block, filled):
+    count, width = grads.shape
+
+    def placed(i, *_):
+        return (pl.multiple_of(start + i * block, 8), 0)
+
+    whole = pl.BlockSpec((pl.Element(block), pl.Element(width)), placed)
+    piece = pl.BlockSpec((block, width), lambda i, *_: (i, 0))
+    return pl.pallas_call(
+        adam_kernel,
+        name="adam_rows",
+        grid_spec=pltpu.PrefetchScalarGridSpec(
+            num_scalar_prefetch=1,
+            grid=(count // block,),
+            in_specs=[whole, piece, whole, whole]
+            + [pl.BlockSpec(memory_space=pl.ANY)] * len(filled),
+            out_specs=[whole] * 3,
+        ),
+        out_shape=[jax.ShapeDtypeStruct(weights.shape, f32)] * 3,
+        input_output_aliases={5 + i: i for i in range(len(filled))},
+        compiler_params=pltpu.CompilerParams(
+            dimension_semantics=("arbitrary",), vmem_limit_bytes=56 << 20
+        ),
+        cost_estimate=cheap,
+    )(scalars, weights, grads, first, second, *filled)
 
 
 def body(
@@ -365,53 +570,50 @@
     def gather_columns(piece):
         return lax.all_gather(piece, "dp", axis=1, tiled=True)
 
-    qkv_rows = gather_columns(shard(0, 2))
-    out_shard, qkv_rows = lax.optimization_barrier((shard(2, 3), qkv_rows))
-    out_rows = gather_columns(out_shard)
-    up_shard, out_rows = lax.optimization_barrier((shard(3, 4), out_rows))
-    w_up = gather_columns(up_shard)
-    down_shard, w_up = lax.optimization_barrier((shard(4, 5), w_up))
-    w_down = gather_columns(down_shard)
-
+    kv_rows = gather_columns(shard(1, 2))
+    query_rows_all = gather_columns(shard(0, 1))
+    out_rows = gather_columns(shard(2, 3))
+    w_up = gather_columns(shard(3, 4))
+    w_down = gather_columns(shard(4, 5))
     def split_sides(block):
         size = block.shape[0] // 2
         return [lax.dynamic_slice_in_dim(block, side * size, size) for side in sides]
 
-    def widen_rows(own, other):
-        received = spread(own)
+    def widen_rows(received, other):
         crossed = swap_core(jnp.concatenate(received[1:], 0))
         return jnp.concatenate(received + [other, crossed], 0)
 
-    kv_blocks = spread(qkv_rows[query_rows:])
     w_keyval = jnp.zeros((2 * HD, D), bf16)
-    for m in range(tp_size):
-        w_keyval = lax.dynamic_update_slice_in_dim(
-            w_keyval, kv_blocks[m], block_of[m] * kv_share, 0
-        )
-    w_query = widen_rows(*split_sides(qkv_rows[:query_rows]))
-    w_out = widen_rows(*split_sides(out_rows))
+    for m, piece in enumerate(spread_directly(kv_rows)):
+        w_keyval = lax.dynamic_update_slice_in_dim(w_keyval, piece, block_of[m] * kv_share, 0)
+    query_own, query_other = split_sides(query_rows_all)
+    query_got = spread_directly(query_own)
+    w_query = widen_rows(query_got, query_other)
 
     block_rows = block_in.astype(f32).reshape(batches * rows, D)
     ln_one, normed_one, inverse_one = layer_norm_fwd(block_rows, gain_one, shift_one)
     hidden_one = ln_one.astype(bf16)
     kv_local = (rows_by_rows(hidden_one, w_keyval) + keyval_bias).astype(bf16)
-    kv_local = kv_local.reshape(batches, 1, rows, 2 * HD)
-    kv_stretch = jnp.zeros((batches, tp_size, rows, 2 * HD), bf16)
-    for m, piece in enumerate(spread(kv_local)):
-        kv_stretch = lax.dynamic_update_slice_in_dim(kv_stretch, piece, block_of[m], 1)
-    kv_stretch = kv_stretch.reshape(batches, 1, stretch, 2 * HD)
-
-    def both_sides(own, other):
-        pair = jnp.zeros((batches, 2, stretch, 2 * HD), bf16)
-        pair = lax.dynamic_update_slice_in_dim(pair, own, core, 1)
-        return lax.dynamic_update_slice_in_dim(pair, other, 1 - core, 1)
-
+    kv_local = kv_local.reshape(1, batches, 1, rows, 2 * HD)
     to_next = [(d, d + 2) for d in range(dp_size - 2) if (d // 2) % 2 == 1]
     to_last = [(target, source) for source, target in to_next]
-    kv_before = lax.ppermute(kv_stretch, "dp", to_next)
-    kv_here = both_sides(kv_stretch, swap_core(kv_stretch))
-    kv_before = both_sides(kv_before, swap_core(kv_before))
-    keyvals = jnp.concatenate([kv_before, kv_here], 1).reshape(batches, KEY_ROWS, 2 * HD)
+    kv_pair = jnp.concatenate([lax.ppermute(kv_local, "dp", to_next), kv_local], 0)
+    kv_stretch = jnp.zeros((2, batches, tp_size, rows, 2 * HD), bf16)
+    kv_pieces = spread_directly(after(kv_pair, *query_got))
+    out_own, out_other = split_sides(after(out_rows, *kv_pieces))
+    out_got = spread_directly(out_own)
+    w_out = widen_rows(out_got, out_other)
+    early = max(1, batches - 1)
+    cot_early = cotangent[:early].reshape(early * rows, D)
+    cot_early = spread_directly(after(cot_early, *out_got))
+    for m, piece in enumerate(kv_pieces):
+        kv_stretch = lax.dynamic_update_slice_in_dim(kv_stretch, piece, block_of[m], 2)
+    kv_stretch = kv_stretch.reshape(2, batches, stretch, 2 * HD).transpose(1, 0, 2, 3)
+    kv_stretch = kv_stretch.reshape(batches, 2, 1, stretch, 2 * HD)
+    keyvals = jnp.zeros((batches, 2, 2, stretch, 2 * HD), bf16)
+    keyvals = lax.dynamic_update_slice_in_dim(keyvals, kv_stretch, core, 2)
+    keyvals = lax.dynamic_update_slice_in_dim(keyvals, swap_core(kv_stretch), 1 - core, 2)
+    keyvals = keyvals.reshape(batches, KEY_ROWS, 2 * HD)
     keys = keyvals[:, :, :HD]
     vals = keyvals[:, :, HD:]
     keys_t = keys.transpose(0, 2, 1)
@@ -443,64 +645,89 @@
     ln_two, normed_two, inverse_two = layer_norm_fwd(residual, gain_two, shift_two)
     hidden_two = ln_two.astype(bf16)
 
-    outputs = []
-    wide_hidden = []
-    wide_cot = []
-    wide_act = []
-    wide_pre_grad = []
-    grad_two_parts = []
-    for b in range(batches):
-        own = slice(b * rows, (b + 1) * rows)
-        hidden_all = jnp.concatenate(spread(hidden_two[own]), 0)
-        cot_all = jnp.concatenate(spread(cotangent[b]), 0)
-        pre_act = rows_by_rows(hidden_all, w_up) + bias_up
-        activated = gelu_tanh(pre_act).astype(bf16)
-        grad_pre = (rows_by_rows(cot_all, w_down) * gelu_slope(pre_act)).astype(bf16)
-        grad_hidden = plain_dot(grad_pre, w_up)
-        grad_two_parts.append(
-            collect([grad_hidden[m * rows : (m + 1) * rows] for m in range(tp_size)])
-        )
-        product = plain_dot(activated, w_down)
-        summed = collect([product[m * rows : (m + 1) * rows] for m in range(tp_size)])
-        outputs.append((residual[own] + summed + bias_down).astype(bf16))
-        wide_hidden.append(hidden_all)
-        wide_cot.append(cot_all)
-        wide_act.append(activated)
-        wide_pre_grad.append(grad_pre)
-
-    grad_down = cols_by_cols(jnp.concatenate(wide_act, 0), jnp.concatenate(wide_cot, 0))
-    grad_up = cols_by_cols(jnp.concatenate(wide_pre_grad, 0), jnp.concatenate(wide_hidden, 0))
-    grad_bias_up = sum(jnp.sum(part.astype(f32), 0) for part in wide_pre_grad)
+    hidden_got = spread(hidden_two)
+    cot_late = cotangent[early:].reshape((batches - early) * rows, D)
+    cot_late = spread_directly(after(cot_late, *hidden_got))
 
     def scatter_columns(full):
         return lax.psum_scatter(full, "dp", scatter_dimension=1, tiled=True)
 
-    shard_down = scatter_columns(grad_down.astype(bf16)).astype(f32)
-    shard_up = scatter_columns(grad_up.astype(bf16)).astype(f32)
+    near = tp_size - 1
+    ups = [ffn_up(part, w_up, bias_up) for part in (hidden_got[:near], hidden_got[near:])]
+    pre_act = [up[0] for up in ups]
+    activated = [up[1] for up in ups]
+    product = ffn_product(activated, w_down, tp_size)
+    received = deliver(product)
+    cot_late = after(cot_late, product)
+    cot_got = [jnp.concatenate(pair, 0) for pair in zip(cot_early, cot_late)]
+    grad_down = ffn_weight(activated, cot_got)
+    grad_pre, grad_bias_up = ffn_back(after(cot_got, grad_down), w_down, pre_act)
+    grad_bias_up = grad_bias_up[0]
+    grad_hidden = ffn_product([grad_pre], w_up, tp_size)
+    shard_down = scatter_columns(after(grad_down, *grad_hidden, *received))
+    grad_hidden_parts = deliver(grad_hidden)
+    grad_up = ffn_weight([after(grad_pre, *grad_hidden)], hidden_got)
+    shard_up = scatter_columns(after(grad_up, *grad_hidden_parts))
+    grad_hidden_two = total_of(after(grad_hidden_parts, grad_up))
 
     cot_rows = cotangent.astype(f32).reshape(batches * rows, D)
     grad_bias_down = jnp.sum(cot_rows, 0)
-    grad_hidden_two = jnp.concatenate(grad_two_parts, 0)
     grad_resid = cot_rows + layer_norm_back(grad_hidden_two, normed_two, inverse_two, gain_two)
     grad_gain_two = jnp.sum(grad_hidden_two * normed_two, 0)
     grad_shift_two = jnp.sum(grad_hidden_two, 0)
     grad_att = grad_resid.astype(bf16)
     grad_bias_out = jnp.sum(grad_resid, 0)
+    cols_half = H * HD // 2
+    out_grad_own = cols_by_cols(attended[:, :cols_half], grad_att)
+    out_grad_other = cols_by_cols(attended[:, cols_half:], grad_att).astype(bf16)
     grad_heads = rows_by_rows(grad_att, w_out).astype(bf16).reshape(batches, rows, H * HD)
+
+    def reduce_core(own, other):
+        own = (own + swap_core(other.astype(bf16)).astype(f32)).astype(bf16)
+        size = own.shape[0] // tp_size
+        return [own[m * size : (m + 1) * size] for m in range(tp_size)]
+
+    out_pieces = reduce_core(out_grad_own, out_grad_other)
+    grad_heads = after(grad_heads, *out_pieces)
+    out_pieces = deliver(out_pieces)
     grad_query, grad_key, grad_val = attend_backward(
         queries, grad_heads, keys, keys_t, vals, bias, log_sums, bounds
     )
+    grad_query, received = lax.optimization_barrier((grad_query, received))
+    result = residual + total_of(received) + bias_down
+    outputs = result.astype(bf16).reshape(batches, rows, D)
     grad_query = grad_query.reshape(batches * rows, H * HD)
     grad_bias_query = jnp.sum(grad_query.astype(f32), 0)
+
+    query_grad_other = ffn_weight([grad_query[:, cols_half:]], [hidden_one])
+    query_pieces = reduce_core(
+        cols_by_cols(grad_query[:, :cols_half], hidden_one), query_grad_other
+    )
+    out_pieces, shard_up, shard_down = lax.optimization_barrier((out_pieces, shard_up, shard_down))
+    part_out = part_out_sum = total_of(out_pieces).astype(bf16)
+
+    def scatter_chips(part):
+        return lax.psum_scatter(
+            part, "dp", scatter_dimension=1, axis_index_groups=parity, tiled=True
+        )
+
+    part_out = scatter_chips(part_out)
+    query_got = deliver(query_pieces)
+    grad_query = after(grad_query, *query_pieces)
 
     kv_grads = jnp.concatenate([grad_key, grad_val], 2)
     kv_grads = kv_grads.reshape(batches, 2, 2, stretch, 2 * HD)
     kv_kept = lax.dynamic_slice_in_dim(kv_grads, core, 1, 2)
     kv_sent = lax.dynamic_slice_in_dim(kv_grads, 1 - core, 1, 2).astype(bf16)
     kv_kept = kv_kept + swap_core(kv_sent).astype(f32)
+    kv_kept = after(kv_kept, *out_pieces, query_grad_other)
     kv_kept = kv_kept.reshape(batches, 2, tp_size, rows, 2 * HD)
-    kv_total = kv_kept[:, 1] + lax.ppermute(kv_kept[:, 0].astype(bf16), "dp", to_last).astype(f32)
-    grad_kv = collect([lax.dynamic_slice_in_dim(kv_total, at, 1, 1) for at in block_of])
+    kv_total = total_of(
+        deliver([lax.dynamic_slice_in_dim(kv_kept, at, 1, 2) for at in block_of])
+    )
+    grad_kv = kv_total[:, 1] + lax.ppermute(
+        kv_total[:, 0].astype(bf16), "dp", to_last
+    ).astype(f32)
     grad_kv = grad_kv.astype(bf16).reshape(batches * rows, 2 * HD)
     grad_bias_value = jnp.sum(grad_kv[:, HD:].astype(f32), 0)
 
@@ -510,29 +737,17 @@
     grad_shift_one = jnp.sum(grad_hidden_one, 0)
     input_grads = grad_rows.astype(bf16).reshape(batches, rows, D)
 
-    def reduce_blocks(own, other):
-        own = own + swap_core(other.astype(bf16)).astype(f32)
-        size = own.shape[0] // tp_size
-        return collect([own[m * size : (m + 1) * size] for m in range(tp_size)])
-
-    cols_half = H * HD // 2
-    part_out = reduce_blocks(
-        cols_by_cols(attended[:, :cols_half], grad_att),
-        cols_by_cols(attended[:, cols_half:], grad_att),
-    )
-    part_query = reduce_blocks(
-        cols_by_cols(grad_query[:, :cols_half], hidden_one),
-        cols_by_cols(grad_query[:, cols_half:], hidden_one),
-    )
-    grad_w_keyval = cols_by_cols(grad_kv, hidden_one)
+    grad_w_keyval = cols_by_cols(after(grad_kv, part_out_sum), hidden_one)
     kv_rows = [lax.dynamic_slice_in_dim(grad_w_keyval, start, kv_half) for start in kv_starts]
-    part_keyval = reduce_blocks(
+    kv_parts = reduce_core(
         jnp.concatenate(kv_rows[:tp_size], 0), jnp.concatenate(kv_rows[tp_size:], 0)
     )
-    part_all = jnp.concatenate([part_query, part_keyval, part_out], 0).astype(bf16)
-    part_all = lax.psum_scatter(
-        part_all, "dp", scatter_dimension=1, axis_index_groups=parity, tiled=True
-    )
+    query_got, kv_parts = lax.optimization_barrier((query_got, kv_parts))
+    part_keyval = total_of(deliver(kv_parts))
+    part_query = total_of(query_got)
+    part_all = jnp.concatenate([part_query, part_keyval], 0).astype(bf16)
+    part_all = scatter_chips(after(part_all, part_out))
+    part_all = jnp.concatenate([part_all, part_out], 0)
     width = part_all.shape[1] // 2
     mine = lax.dynamic_slice_in_dim(part_all, core * width, width, 1)
     theirs = swap_core(lax.dynamic_slice_in_dim(part_all, (1 - core) * width, width, 1))
@@ -543,7 +758,7 @@
     for size in (half, kv_half, half):
         pieces += [low_half[at : at + size], high_half[at : at + size]]
         at += size
-    shard_attention = jnp.concatenate(pieces, 0).astype(f32)
+    shard_attention = jnp.concatenate(pieces, 0)
 
     whole_bias_query = jnp.zeros((H * HD,), f32)
     for index, start in enumerate(query_starts):
@@ -570,23 +785,27 @@
     new_vectors, new_vec_one, new_vec_two = adam_step(
         vectors, vec_total, vec_one, vec_two, step_count, learning_rate
     )
-    updated = []
-    for first, last, grads in (
-        (0, 3, shard_attention),
-        (3, 4, shard_up),
-        (4, 5, shard_down),
+    steps_float = step_count[0].astype(f32)
+    scalars = jnp.stack(
+        [
+            learning_rate[0],
+            1.0 - jnp.power(beta_one, steps_float),
+            1.0 - jnp.power(beta_two, steps_float),
+        ]
+    )
+    state = ()
+    for start, grads in (
+        (row_starts[4], shard_down),
+        (row_starts[3], shard_up),
+        (0, shard_attention),
     ):
-        at = slice(row_starts[first], row_starts[last])
-        updated.append(
-            adam_step(
-                master[at], grads, moment_one[at], moment_two[at], step_count, learning_rate
-            )
-        )
-    new_master, new_moment_one, new_moment_two = (
-        jnp.concatenate(parts, 0) for parts in zip(*updated)
-    )
+        block = grads.shape[0] // 2
+        if start == 0:
+            grads = after(grads, *state)
+        state = adam_rows(scalars, master, grads, moment_one, moment_two, start, block, state)
+    new_master, new_moment_one, new_moment_two = state
     return (
-        jnp.stack(outputs),
+        outputs,
         input_grads,
         new_master,
         new_moment_one,

time: 968 us -> 764 us (0.79)
  waiting for transfers between devices: 450 us -> 238 us
  Pallas kernels: 23.6 us -> 184 us
  matrix products: 190 us -> 48.1 us
  blocking collectives: 0 us -> 16.6 us
  other arithmetic: 58.4 us -> 43.5 us
    pallas_call x0 -> x11, Pallas kernels: none -> 160 us  [the longest x3 52.3 us: ffn_weight(): pl.pallas_call(functools.partial(ffn_weight_kernel, lefts=len(lefts)), na...]
    ppermute x74 -> x53, waiting for transfers between devices: 333 us -> 232 us  [swap(): lax.ppermute(value, axis, [(source, source ^ step) for source in range(co...]
    dot_general x9 -> x3, matrix products: 81.4 us -> 16.9 us  [rows_by_rows(): lax.dot_general(left, right, (((1,), (1,)), ((), ())), preferred_element_...]
    all_gather x4, waiting for transfers between devices: 61.7 us -> 0.01 us  [gather_columns(): return lax.all_gather(piece, 'dp', axis=1, tiled=True)]
    reduce_scatter x2, waiting for transfers between devices: 55.2 us -> 5.14 us  [scatter_columns(): return lax.psum_scatter(full, 'dp', scatter_dimension=1, tiled=True)]
    dot_general x9 -> x3, matrix products: 58.5 us -> 14.8 us  [plain_dot(): return jnp.dot(left, right, preferred_element_type=f32)]
    dot_general x7 -> x4, matrix products: 49.9 us -> 16.4 us  [cols_by_cols(): lax.dot_general(left, right, (((0,), (0,)), ((), ())), preferred_element_...]
    all_gather x0 -> x1, blocking collectives: none -> 16.6 us  [gather_columns(): return lax.all_gather(piece, 'dp', axis=1, tiled=True)]
  transfers between devices with their start and end apart: 83 -> 63, of which waited for: 36 -> 27; matrix products, arithmetic and copies ran while one was open for 30% -> 22% of each run, Pallas kernels for 1% -> 24%
where the time goes in v2:
time: 764 us; the launch traced here: 765 us
  waiting for transfers between devices  238 us (31%)
  Pallas kernels  184 us (24%)
  starting transfers between devices  126 us (16%)
  local copies, waits for them, and re-layouts  91.5 us (12%)
  matrix products  48.1 us (6%)
  other arithmetic  43.5 us (6%)
  between operations  17.2 us (2%)
  blocking collectives  16.6 us (2%)
    ppermute x53, waiting for transfers between devices, swap(): lax.ppermute(value, axis, [(source, source ^ step) for source in range(co...  232 us
    ppermute x53, starting transfers between devices, swap(): lax.ppermute(value, axis, [(source, source ^ step) for source in range(co...  123 us
    pallas_call x3, Pallas kernels, ffn_weight(): pl.pallas_call(functools.partial(ffn_weight_kernel, lefts=len(lefts)), na...  52.3 us
    unnamed x152, local copies, waits for them, and re-layouts  37.9 us
    pallas_call x2, Pallas kernels, ffn_product(): pl.pallas_call(functools.partial(ffn_product_kernel, lefts=len(lefts)), n...  36.9 us
    pallas_call x2, Pallas kernels, ffn_up(): pl.pallas_call(ffn_up_kernel, name='ffn_up', grid=(units // tile,), in_sp...  28.3 us
    pallas_call x1, Pallas kernels, ffn_back(): pl.pallas_call(functools.partial(ffn_back_kernel, count=len(pieces)), nam...  25.8 us
    pallas_call x3, Pallas kernels, adam_rows(): pl.pallas_call(adam_kernel, name='adam_rows', grid_spec=pltpu.PrefetchSca...  17.1 us
  transfers between devices with their start and end apart: 63, of which 27 were waited for; matrix products, arithmetic and copies ran while one was open for 22% of the time, Pallas kernels for 24%

profile of v2, /device:TPU:0, one launch (start us, length us, event | category | flops | bytes accessed | tf_op | source)
XLA Modules:
  0.0 764.6 jit_solution(14100014823271485995)
XLA Ops:
  7.2 2.8 convert.28
  13.2 3.1 fusion.43
  16.4 16.6 %all_gather.16 = bf16[64,2048]{1,0:T(8,128)(2,1)S(1)} all-gather(bf16[64,256]{1,0:T(8,128)(2,1)S(1)} %slice-done), channel_id=1, replica_groups=mesh['dp'=8,'tp'=4] {'dp'}, dimensions={1}, use_global_device_ids=true | all-gather | bytes 294912 | tf_op jit(solution)/shard_map/all_gather | solution.py:571
  54.6 2.5 constant_dynamic-update-slice_fusion.4
  69.5 13.8 %collective-permute-done = bf16[256,2048]{1,0:T(8,128)(2,1)S(1)} collective-permute-done((bf16[256,2048]{1,0:T(8,128)(2,1)S(1)}, bf16[256,2048]{1,0:T(8,128)(2,1)S(1)}, u32[]{:S(2)}, u32[]{:S(2)}) %collective-permute-start) | collective-permute-done | bytes 1048608 | tf_op jit(solution)/shard_map/ppermute | solution.py:84
  83.3 22.1 %collective-permute-done.1 = bf16[256,2048]{1,0:T(8,128)(2,1)S(1)} collective-permute-done((bf16[256,2048]{1,0:T(8,128)(2,1)S(1)}, bf16[256,2048]{1,0:T(8,128)(2,1)S(1)}, u32[]{:S(2)}, u32[]{:S(2)}) %collective-permute-start.1) | collective-permute-done | bytes 1048608 | tf_op jit(solution)/shard_map/ppermute | solution.py:84
  113.8 4.6 collective-permute-done.10
  118.4 5.0 collective-permute-done.8
  133.7 18.0 %collective-permute-done.12 = bf16[256,2048]{1,0:T(8,128)(2,1)S(1)} collective-permute-done((bf16[256,2048]{1,0:T(8,128)(2,1)S(1)}, bf16[256,2048]{1,0:T(8,128)(2,1)S(1)}, u32[]{:S(2)}, u32[]{:S(2)}) %collective-permute-start.12) | collective-permute-done | bytes 1048608 | tf_op jit(solution)/shard_map/ppermute | solution.py:84
  151.8 22.7 %collective-permute-done.13 = bf16[256,2048]{1,0:T(8,128)(2,1)S(1)} collective-permute-done((bf16[256,2048]{1,0:T(8,128)(2,1)S(1)}, bf16[256,2048]{1,0:T(8,128)(2,1)S(1)}, u32[]{:S(2)}, u32[]{:S(2)}) %collective-permute-start.13) | collective-permute-done | bytes 1048608 | tf_op jit(solution)/shard_map/ppermute | solution.py:84
  178.5 3.4 fusion.42
  183.6 2.6 copy.29.vt_ref
  186.2 4.1 constant_dynamic-update-slice_fusion
  190.3 7.0 add_convert_fusion.4
  197.4 9.3 %attend_forward.1 = (bf16[3,128,2048]{2,1,0:T(8,128)(2,1)S(1)}, f32[3,4,1,512]{3,2,1,0:T(1,128)S(1)}) custom-call(s32[3,2]{1,0:T(4,128)S(1)} %stack.4.bounds, bf16[3,128,2048]{2,1,0:T(8,128)(2,1)S(1)} %bitcast.102, bf16[3,2048,128]{2,1,0:T(8,128)(2,1)S(1)} %copy-done.1, bf16[3,128,2048]{2,1,0:T(8,128)(2,1)S(1)} %copy-done.3, ...), custom_call_target="tpu_custom_call" | custom-call | flops 1048576 | bytes 1048576 | tf_op jit(solution)/shard_map/attend_forward/pallas_call | solution.py:240
  206.9 2.9 constant_dynamic-update-slice_fusion.6
  209.8 3.7 fusion.47
  215.5 6.6 collective-permute-start.17
  222.1 19.7 %collective-permute-done.16.refs_1_.refs_2_ = bf16[384,2048]{1,0:T(8,128)(2,1)S(1)} collective-permute-done((bf16[384,2048]{1,0:T(8,128)(2,1)S(1)}, bf16[384,2048]{1,0:T(8,128)(2,1)S(1)}, u32[]{:S(2)}, u32[]{:S(2)}) %collective-permute-start.16) | collective-permute-done | bytes 1572896 | tf_op jit(solution)/shard_map/ppermute | solution.py:84
  241.9 9.4 %collective-permute-start.18 = (bf16[192,2048]{1,0:T(8,128)(2,1)S(1)}, bf16[192,2048]{1,0:T(8,128)(2,1)S(1)}, u32[]{:S(2)}, u32[]{:S(2)}) collective-permute-start(bf16[192,2048]{1,0:T(8,128)(2,1)S(1)} %slice.227), channel_id=1, source_target_pairs={{0,2},{1,3},{2,0},{3,1},{4,6},{5,7},{6,4},{7,5},{8,10},{9,11},{10,... | collective-permute-start | bytes 2359304 | tf_op jit(solution)/shard_map/ppermute | solution.py:84
  253.6 2.5 collective-permute-start.25
  258.1 22.1 %collective-permute-done.18 = bf16[192,2048]{1,0:T(8,128)(2,1)S(1)} collective-permute-done((bf16[192,2048]{1,0:T(8,128)(2,1)S(1)}, bf16[192,2048]{1,0:T(8,128)(2,1)S(1)}, u32[]{:S(2)}, u32[]{:S(2)}) %collective-permute-start.18) | collective-permute-done | bytes 786464 | tf_op jit(solution)/shard_map/ppermute | solution.py:84
  283.3 2.3 constant_dynamic-update-slice_fusion.14
  287.7 17.8 %ffn_up.2 = (f32[1152,2048]{1,0:T(8,128)}, bf16[1152,2048]{1,0:T(8,128)(2,1)}) custom-call(bf16[384,2048]{1,0:T(8,128)(2,1)} %copy-done.22, bf16[384,2048]{1,0:T(8,128)(2,1)} %copy-done.30, bf16[384,2048]{1,0:T(8,128)(2,1)} %copy-done.31, bf16[2048,2048]{1,0:T(8,128)(2,1)} %all-gather.9.cloned.1.call-done.refs_3_.refs_1_, f32[1,2048]{1,0:T(1,128)} %bitcast.128), custom_call_target="tpu_custom_call" | custom-call | flops 1048576 | bytes 1048576 | tf_op jit(solution)/shard_map/ffn_up/pallas_call | solution.py:384
  305.5 10.4 %ffn_up.3 = (f32[384,2048]{1,0:T(8,128)}, bf16[384,2048]{1,0:T(8,128)(2,1)}) custom-call(bf16[384,2048]{1,0:T(8,128)(2,1)} %constant_dynamic-update-slice_fusion.11.refs_0_.refs_4_, bf16[2048,2048]{1,0:T(8,128)(2,1)} %all-gather.9.cloned.1.call-done.refs_3_.refs_1_, f32[1,2048]{1,0:T(1,128)} %bitcast.129), custom_call_target="tpu_custom_call" | custom-call | flops 1048576 | bytes 1048576 | tf_op jit(solution)/shard_map/ffn_up/pallas_call | solution.py:384
  316.0 18.4 %ffn_product.2 = (bf16[384,2048]{1,0:T(8,128)(2,1)}, bf16[384,2048]{1,0:T(8,128)(2,1)}, bf16[384,2048]{1,0:T(8,128)(2,1)}, bf16[384,2048]{1,0:T(8,128)(2,1)}) custom-call(bf16[1152,2048]{1,0:T(8,128)(2,1)} %get-tuple-element.85.refs_0_, bf16[384,2048]{1,0:T(8,128)(2,1)} %get-tuple-element.86.refs_1_, ...), custom_call_target="tpu_custom_call" | custom-call | flops 1048576 | bytes 1048576 | tf_op jit(solution)/shard_map/ffn_product/pallas_call | solution.py:428
  347.9 2.3 constant_dynamic-update-slice_fusion.13.refs_2_.refs_0_
  350.2 23.1 %ffn_weight.3 = bf16[2048,2048]{1,0:T(8,128)(2,1)} custom-call(bf16[1152,2048]{1,0:T(8,128)(2,1)} %get-tuple-element.85.refs_0_, bf16[384,2048]{1,0:T(8,128)(2,1)} %get-tuple-element.86.refs_1_, bf16[384,2048]{1,0:T(8,128)(2,1)} %constant_dynamic-update-slice_fusion.13.refs_2_.refs_0_, bf16[384,2048]{1,0:T(8,128)(2,1)} %copy-done.26, ...), custom_call_target="tpu_custom_call" | custom-call | flops 1048576 | bytes 1048576 | tf_op jit(solution)/shard_map/ffn_weight/pallas_call | solution.py:443
  373.3 25.8 %ffn_back.1 = (bf16[1536,2048]{1,0:T(8,128)(2,1)}, f32[1,2048]{1,0:T(1,128)}) custom-call(bf16[384,2048]{1,0:T(8,128)(2,1)} %constant_dynamic-update-slice_fusion.13.refs_2_.refs_0_, bf16[384,2048]{1,0:T(8,128)(2,1)} %copy-done.26, bf16[384,2048]{1,0:T(8,128)(2,1)} %copy-done.27, bf16[384,2048]{1,0:T(8,128)(2,1)} %copy-done.28, ...), custom_call_target="tpu_custom_call" | custom-call | flops 1048576 | bytes 1048576 | tf_op jit(solution)/shard_map/ffn_back/pallas_call | solution.py:408
  399.1 18.4 %ffn_product.3 = (bf16[384,2048]{1,0:T(8,128)(2,1)}, bf16[384,2048]{1,0:T(8,128)(2,1)}, bf16[384,2048]{1,0:T(8,128)(2,1)}, bf16[384,2048]{1,0:T(8,128)(2,1)}) custom-call(bf16[1536,2048]{1,0:T(8,128)(2,1)} %get-tuple-element.106.refs_0_, bf16[2048,2048]{1,0:T(8,128)(2,1)} %all-gather.9.cloned.1.call-done.refs_3_.refs_1_), custom_call_target="tpu_custom_call" | custom-call | flops 1048576 | bytes 1048576 | tf_op jit(solution)/shard_map/ffn_product/pallas_call | solution.py:428
  421.1 23.1 %ffn_weight.4 = bf16[2048,2048]{1,0:T(8,128)(2,1)} custom-call(bf16[1536,2048]{1,0:T(8,128)(2,1)} %get-tuple-element.106.refs_0_, bf16[384,2048]{1,0:T(8,128)(2,1)} %copy-done.22, bf16[384,2048]{1,0:T(8,128)(2,1)} %copy-done.30, bf16[384,2048]{1,0:T(8,128)(2,1)} %copy-done.31, bf16[384,2048]{1,0:T(8,128)(2,1)} %constant_dynamic-update-slice_fusion.11.refs_0_.refs_4_), custom_call_target="tpu_custom_call" | custom-call | flops 1048576 | bytes 1048576 | tf_op jit(solution)/shard_map/ffn_weight/pallas_call | solution.py:443
  444.2 3.9 collective-permute-done.27
  448.1 21.8 %collective-permute-done.28 = bf16[384,2048]{1,0:T(8,128)(2,1)} collective-permute-done((bf16[384,2048]{1,0:T(8,128)(2,1)}, bf16[384,2048]{1,0:T(8,128)(2,1)}, u32[]{:S(2)}, u32[]{:S(2)}) %collective-permute-start.28) | collective-permute-done | bytes 1572896 | tf_op jit(solution)/shard_map/ppermute | solution.py:84
  470.0 5.2 multiply_reduce_fusion
  475.2 3.4 fusion.39
  478.7 4.4 convolution_convert_fusion
  483.1 20.8 %collective-permute-start.29 = (bf16[1024,2048]{1,0:T(8,128)(2,1)}, bf16[1024,2048]{1,0:T(8,128)(2,1)}, u32[]{:S(2)}, u32[]{:S(2)}) collective-permute-start(bf16[1024,2048]{1,0:T(8,128)(2,1)} %convolution_convert_fusion), channel_id=1, source_target_pairs={{0,4},{4,0},{8,12},{12,8},{16,20},{20,16},{24,28},{28,24},{1,5},{5... | collective-permute-start | bytes 12582920 | tf_op jit(solution)/shard_map/ppermute | solution.py:84
  505.9 8.0 %convolution_convert_fusion.1 = bf16[384,2048]{1,0:T(8,128)(2,1)S(1)} fusion(bf16[2048,2048]{1,0:T(8,128)(2,1)} %copy-done.41, f32[384,2048]{1,0:T(8,128)} %copy-done.23), kind=kOutput, calls=%fused_computation.40 | convolution fusion | flops 3222798336 | bytes 13107200 | tf_op jit(solution)/shard_map/dot_general | solution.py:67
  513.9 4.6 add_convert_fusion.1
  522.4 14.5 %attend_backward.1 = (bf16[3,128,2048]{2,1,0:T(8,128)(2,1)S(1)}, f32[3,2048,128]{2,1,0:T(8,128)S(1)}, f32[3,2048,128]{2,1,0:T(8,128)}) custom-call(s32[3,2]{1,0:T(4,128)S(1)} %stack.4.bounds, bf16[3,128,2048]{2,1,0:T(8,128)(2,1)S(1)} %bitcast.103, bf16[3,128,2048]{2,1,0:T(8,128)(2,1)S(1)} %bitcast.107, bf16[3,2048,128]{2,1,0:T(8,128)(2,1)S(1)} %copy-done.2, ...), custom_call_target="tpu_custom_call" | custom-call | flops 1048576 | bytes 1048576 | tf_op jit(solution)/shard_map/attend_backward/pallas_call | solution.py:275
  539.5 6.1 ffn_weight.5
  545.7 12.4 %collective-permute-start.33 = (bf16[1024,2048]{1,0:T(8,128)(2,1)}, bf16[1024,2048]{1,0:T(8,128)(2,1)}, u32[]{:S(2)}, u32[]{:S(2)}) collective-permute-start(bf16[1024,2048]{1,0:T(8,128)(2,1)} %ffn_weight.5), channel_id=1, source_target_pairs={{0,4},{4,0},{8,12},{12,8},{16,20},{20,16},{24,28},{28,24},{1,5},{5... | collective-permute-start | bytes 12582920 | tf_op jit(solution)/shard_map/ppermute | solution.py:84
  560.4 5.1 collective-permute-start.36
  566.9 3.3 pad_maximum_fusion
  571.4 2.4 collective-permute-done.34
  575.8 6.6 add_convert_fusion
  582.5 3.9 collective-permute-done.35
  586.4 24.5 %collective-permute-done.36 = bf16[256,2048]{1,0:T(8,128)(2,1)} collective-permute-done((bf16[256,2048]{1,0:T(8,128)(2,1)}, bf16[256,2048]{1,0:T(8,128)(2,1)}, u32[]{:S(2)}, u32[]{:S(2)}) %collective-permute-start.36) | collective-permute-done | bytes 1048608 | tf_op jit(solution)/shard_map/ppermute | solution.py:84
  612.7 5.1 reduce-scatter.5.cloned.1.call-done.grads
  623.2 4.4 fusion.40
  631.7 2.4 collective-permute-start.44
  634.1 5.5 collective-permute-done.39
  645.4 3.2 add_convert_fusion.6
  652.1 9.3 %fusion.14 = (f32[2048]{0:T(1024)S(1)}, f32[384]{0:T(512)S(1)}, f32[384]{0:T(512)S(1)}, f32[2048]{0:T(1024)S(1)}, f32[384,2048]{1,0:T(8,128)}) fusion(bf16[3,128,2048]{2,1,0:T(8,128)(2,1)S(1)} %copy-done.14, f32[384]{0:T(512)S(1)} %copy-done.53, f32[384]{0:T(512)S(1)} %copy-done.51, f32[2048]{0:T(1024)S(1)} %copy-done.45, f32[384,2048]{1,0:T(8,128)S(1)} %fusion.48, ...), kind=kOutput, calls=%fused_computation.25 | convolution fusion | flops 3229871104 | bytes 17856512 | tf_op jit(solution)/shard_map/dot_general | solution.py:75
  664.4 18.3 %collective-permute-done.43 = bf16[256,2048]{1,0:T(8,128)(2,1)} collective-permute-done((bf16[256,2048]{1,0:T(8,128)(2,1)}, bf16[256,2048]{1,0:T(8,128)(2,1)}, u32[]{:S(2)}, u32[]{:S(2)}) %collective-permute-start.43) | collective-permute-done | bytes 1048608 | tf_op jit(solution)/shard_map/ppermute | solution.py:84
  686.8 2.6 add_convert_fusion.5
  693.1 6.1 adam_rows.3
  699.2 6.6 adam_rows.4
  705.8 3.2 collective-permute-start.51
  709.0 3.4 collective-permute-done.51
  712.4 18.9 %collective-permute-start.52 = (f32[177,128]{1,0:T(8,128)S(1)}, f32[177,128]{1,0:T(8,128)S(1)}, u32[]{:S(2)}, u32[]{:S(2)}) collective-permute-start(f32[177,128]{1,0:T(8,128)S(1)} %fusion.64), channel_id=1, source_target_pairs={{0,16},{4,20},{8,24},{12,28},{16,0},{20,4},{24,8},{28,12},{1,17},{... | collective-permute-start | bytes 271880 | tf_op jit(solution)/shard_map/ppermute | solution.py:84
  731.3 8.0 %collective-permute-done.52 = f32[177,128]{1,0:T(8,128)S(1)} collective-permute-done((f32[177,128]{1,0:T(8,128)S(1)}, f32[177,128]{1,0:T(8,128)S(1)}, u32[]{:S(2)}, u32[]{:S(2)}) %collective-permute-start.52) | collective-permute-done | bytes 90656 | tf_op jit(solution)/shard_map/ppermute | solution.py:84
  740.8 5.9 fusion.13
  753.2 4.3 adam_rows.5
  (358 shorter events, 143.0 us)
Async XLA Ops:
  7.2 47.5 %all-gather.5.cloned.1.call-start = ((), (), s32[]{:S(2)}) async-start(), calls=%async_computation.4 | async-start | bytes 2359296 | tf_op jit(solution)/shard_map/all_gather | solution.py:571
  12.3 101.5 %all-gather.7.cloned.1.call-start = ((), (), s32[]{:S(2)}) async-start(), calls=%async_computation.5 | async-start | bytes 2359296 | tf_op jit(solution)/shard_map/all_gather | solution.py:571
  13.1 274.6 %all-gather.9.cloned.1.call-start = ((), (), s32[]{:S(2)}) async-start(), calls=%async_computation.6 | async-start | bytes 9437184 | tf_op jit(solution)/shard_map/all_gather | solution.py:571
  16.3 299.7 %all-gather.11.cloned.1.call-start = ((), (), s32[]{:S(2)}) async-start(), calls=%async_computation.7 | async-start | bytes 9437184 | tf_op jit(solution)/shard_map/all_gather | solution.py:571
  33.0 20.0 %collective-permute-start.4 = (bf16[64,2048]{1,0:T(8,128)(2,1)S(1)}, bf16[64,2048]{1,0:T(8,128)(2,1)}, u32[]{:S(2)}, u32[]{:S(2)}) collective-permute-start(bf16[64,2048]{1,0:T(8,128)(2,1)S(1)} %all_gather.16), channel_id=1, source_target_pairs={{0,1},{1,0},{2,3},{3,2},{4,5},{5,4},{6,7},{7,6},{8,9},{9,8},{10,11... | collective-permute-start | bytes 786440 | tf_op jit(solution)/shard_map/ppermute | solution.py:84
  34.4 26.2 %collective-permute-start.5 = (bf16[64,2048]{1,0:T(8,128)(2,1)S(1)}, bf16[64,2048]{1,0:T(8,128)(2,1)}, u32[]{:S(2)}, u32[]{:S(2)}) collective-permute-start(bf16[64,2048]{1,0:T(8,128)(2,1)S(1)} %all_gather.16), channel_id=1, source_target_pairs={{0,2},{1,3},{2,0},{3,1},{4,6},{5,7},{6,4},{7,5},{8,10},{9,11},{10,... | collective-permute-start | bytes 786440 | tf_op jit(solution)/shard_map/ppermute | solution.py:84
  35.9 26.4 %collective-permute-start.6 = (bf16[64,2048]{1,0:T(8,128)(2,1)S(1)}, bf16[64,2048]{1,0:T(8,128)(2,1)}, u32[]{:S(2)}, u32[]{:S(2)}) collective-permute-start(bf16[64,2048]{1,0:T(8,128)(2,1)S(1)} %all_gather.16), channel_id=1, source_target_pairs={{0,3},{1,2},{2,1},{3,0},{4,7},{5,6},{6,5},{7,4},{8,11},{9,10},{10,... | collective-permute-start | bytes 786440 | tf_op jit(solution)/shard_map/ppermute | solution.py:84
  36.5 576.2 %reduce-scatter.7.cloned.1.call-start = ((), (), s32[]{:S(2)}) async-start(), calls=%async_computation.9 | async-start | bytes 9437184 | tf_op jit(solution)/shard_map/reduce_scatter | solution.py:653
  57.2 26.1 %collective-permute-start = (bf16[256,2048]{1,0:T(8,128)(2,1)S(1)}, bf16[256,2048]{1,0:T(8,128)(2,1)S(1)}, u32[]{:S(2)}, u32[]{:S(2)}) collective-permute-start(bf16[256,2048]{1,0:T(8,128)(2,1)S(1)} %get-tuple-element.169), channel_id=1, source_target_pairs={{0,1},{1,0},{2,3},{3,2},{4,5},{5,4},{6,7},{7,6},{8,9},{9,8},{10,11... | collective-permute-start | bytes 3145736 | tf_op jit(solution)/shard_map/ppermute | solution.py:84
  58.6 46.7 %collective-permute-start.1 = (bf16[256,2048]{1,0:T(8,128)(2,1)S(1)}, bf16[256,2048]{1,0:T(8,128)(2,1)S(1)}, u32[]{:S(2)}, u32[]{:S(2)}) collective-permute-start(bf16[256,2048]{1,0:T(8,128)(2,1)S(1)} %get-tuple-element.169), channel_id=1, source_target_pairs={{0,2},{1,3},{2,0},{3,1},{4,6},{5,7},{6,4},{7,5},{8,10},{9,11},{10,... | collective-permute-start | bytes 3145736 | tf_op jit(solution)/shard_map/ppermute | solution.py:84
  60.1 45.3 %collective-permute-start.2 = (bf16[256,2048]{1,0:T(8,128)(2,1)S(1)}, bf16[256,2048]{1,0:T(8,128)(2,1)S(1)}, u32[]{:S(2)}, u32[]{:S(2)}) collective-permute-start(bf16[256,2048]{1,0:T(8,128)(2,1)S(1)} %get-tuple-element.169), channel_id=1, source_target_pairs={{0,3},{1,2},{2,1},{3,0},{4,7},{5,6},{6,5},{7,4},{8,11},{9,10},{10,... | collective-permute-start | bytes 3145736 | tf_op jit(solution)/shard_map/ppermute | solution.py:84
  65.8 3.6 collective-permute-start.7
  105.4 13.1 %collective-permute-start.10 = (bf16[2,3,1,128,256]{4,3,1,2,0:T(8,128)(2,1)S(1)}, bf16[2,3,1,128,256]{4,3,1,2,0:T(8,128)(2,1)}, u32[]{:S(2)}, u32[]{:S(2)}) collective-permute-start(bf16[2,3,1,128,256]{4,3,1,2,0:T(8,128)(2,1)S(1)} %pad_maximum_fusion.5), channel_id=1, source_target_pairs={{0,3},{1,2},{2,1},{3,0},{4,7},{5,6},{6,5},{7,4},{8,11},{9,10},{10,... | collective-permute-start | bytes 1179656 | tf_op jit(solution)/shard_map/ppermute | solution.py:84
  106.8 16.6 %collective-permute-start.8 = (bf16[2,3,1,128,256]{4,3,1,2,0:T(8,128)(2,1)S(1)}, bf16[2,3,1,128,256]{4,3,1,2,0:T(8,128)(2,1)}, u32[]{:S(2)}, u32[]{:S(2)}) collective-permute-start(bf16[2,3,1,128,256]{4,3,1,2,0:T(8,128)(2,1)S(1)} %pad_maximum_fusion.5), channel_id=1, source_target_pairs={{0,1},{1,0},{2,3},{3,2},{4,5},{5,4},{6,7},{7,6},{8,9},{9,8},{10,11... | collective-permute-start | bytes 1179656 | tf_op jit(solution)/shard_map/ppermute | solution.py:84
  108.3 16.0 %collective-permute-start.9 = (bf16[2,3,1,128,256]{4,3,1,2,0:T(8,128)(2,1)S(1)}, bf16[2,3,1,128,256]{4,3,1,2,0:T(8,128)(2,1)}, u32[]{:S(2)}, u32[]{:S(2)}) collective-permute-start(bf16[2,3,1,128,256]{4,3,1,2,0:T(8,128)(2,1)S(1)} %pad_maximum_fusion.5), channel_id=1, source_target_pairs={{0,2},{1,3},{2,0},{3,1},{4,6},{5,7},{6,4},{7,5},{8,10},{9,11},{10,... | collective-permute-start | bytes 1179656 | tf_op jit(solution)/shard_map/ppermute | solution.py:84
  110.6 75.6 %collective-permute-start.3 = (bf16[768,2048]{1,0:T(8,128)(2,1)}, bf16[768,2048]{1,0:T(8,128)(2,1)}, u32[]{:S(2)}, u32[]{:S(2)}) collective-permute-start(bf16[768,2048]{1,0:T(8,128)(2,1)} %pad_maximum_fusion.1), channel_id=1, source_target_pairs={{0,4},{4,0},{8,12},{12,8},{16,20},{20,16},{24,28},{28,24},{1,5},{5... | collective-permute-start | bytes 9437192 | tf_op jit(solution)/shard_map/ppermute | solution.py:84
  125.7 26.1 %collective-permute-start.12 = (bf16[256,2048]{1,0:T(8,128)(2,1)S(1)}, bf16[256,2048]{1,0:T(8,128)(2,1)S(1)}, u32[]{:S(2)}, u32[]{:S(2)}) collective-permute-start(bf16[256,2048]{1,0:T(8,128)(2,1)S(1)} %get-tuple-element.167), channel_id=1, source_target_pairs={{0,1},{1,0},{2,3},{3,2},{4,5},{5,4},{6,7},{7,6},{8,9},{9,8},{10,11... | collective-permute-start | bytes 3145736 | tf_op jit(solution)/shard_map/ppermute | solution.py:84
  127.2 47.3 %collective-permute-start.13 = (bf16[256,2048]{1,0:T(8,128)(2,1)S(1)}, bf16[256,2048]{1,0:T(8,128)(2,1)S(1)}, u32[]{:S(2)}, u32[]{:S(2)}) collective-permute-start(bf16[256,2048]{1,0:T(8,128)(2,1)S(1)} %get-tuple-element.167), channel_id=1, source_target_pairs={{0,2},{1,3},{2,0},{3,1},{4,6},{5,7},{6,4},{7,5},{8,10},{9,11},{10,... | collective-permute-start | bytes 3145736 | tf_op jit(solution)/shard_map/ppermute | solution.py:84
  127.8 46.6 %collective-permute-start.14 = (bf16[256,2048]{1,0:T(8,128)(2,1)S(1)}, bf16[256,2048]{1,0:T(8,128)(2,1)S(1)}, u32[]{:S(2)}, u32[]{:S(2)}) collective-permute-start(bf16[256,2048]{1,0:T(8,128)(2,1)S(1)} %get-tuple-element.167), channel_id=1, source_target_pairs={{0,3},{1,2},{2,1},{3,0},{4,7},{5,6},{6,5},{7,4},{8,11},{9,10},{10,... | collective-permute-start | bytes 3145736 | tf_op jit(solution)/shard_map/ppermute | solution.py:84
  132.5 45.8 %collective-permute-start.11 = (bf16[3,2,1,512,256]{4,3,2,1,0:T(8,128)(2,1)S(1)}, bf16[3,2,1,512,256]{4,3,2,1,0:T(8,128)(2,1)S(1)}, u32[]{:S(2)}, u32[]{:S(2)}) collective-permute-start(bf16[3,2,1,512,256]{4,3,2,1,0:T(8,128)(2,1)S(1)} %bitcast.116), channel_id=1, source_target_pairs={{0,4},{4,0},{8,12},{12,8},{16,20},{20,16},{24,28},{28,24},{1,5},{5... | collective-permute-start | bytes 4718600 | tf_op jit(solution)/shard_map/ppermute | solution.py:84
  176.2 30.6 %collective-permute-start.15 = (bf16[768,2048]{1,0:T(8,128)(2,1)}, bf16[768,2048]{1,0:T(8,128)(2,1)}, u32[]{:S(2)}, u32[]{:S(2)}) collective-permute-start(bf16[768,2048]{1,0:T(8,128)(2,1)} %pad_maximum_fusion.2), channel_id=1, source_target_pairs={{0,4},{4,0},{8,12},{12,8},{16,20},{20,16},{24,28},{28,24},{1,5},{5... | collective-permute-start | bytes 9437192 | tf_op jit(solution)/shard_map/ppermute | solution.py:84
  213.5 256.6 %copy-start.10 = (f32[384,2048]{1,0:T(8,128)}, f32[384,2048]{1,0:T(8,128)S(1)}, u32[]{:S(2)}) copy-start(f32[384,2048]{1,0:T(8,128)S(1)} %get-tuple-element.213) | copy-start | bytes 9437188
  214.8 27.0 %collective-permute-start.16 = (bf16[384,2048]{1,0:T(8,128)(2,1)S(1)}, bf16[384,2048]{1,0:T(8,128)(2,1)S(1)}, u32[]{:S(2)}, u32[]{:S(2)}) collective-permute-start(bf16[384,2048]{1,0:T(8,128)(2,1)S(1)} %add_convert_fusion.3.refs_0_.refs_1_), channel_id=1, source_target_pairs={{0,1},{1,0},{2,3},{3,2},{4,5},{5,4},{6,7},{7,6},{8,9},{9,8},{10,11... | collective-permute-start | bytes 4718600 | tf_op jit(solution)/shard_map/ppermute | solution.py:84
  215.5 35.8 %collective-permute-start.17 = (bf16[384,2048]{1,0:T(8,128)(2,1)S(1)}, bf16[384,2048]{1,0:T(8,128)(2,1)S(1)}, u32[]{:S(2)}, u32[]{:S(2)}) collective-permute-start(bf16[384,2048]{1,0:T(8,128)(2,1)S(1)} %add_convert_fusion.3.refs_0_.refs_1_), channel_id=1, source_target_pairs={{0,2},{1,3},{2,0},{3,1},{4,6},{5,7},{6,4},{7,5},{8,10},{9,11},{10,... | collective-permute-start | bytes 4718600 | tf_op jit(solution)/shard_map/ppermute | solution.py:84
  241.9 38.3 %collective-permute-start.18 = (bf16[192,2048]{1,0:T(8,128)(2,1)S(1)}, bf16[192,2048]{1,0:T(8,128)(2,1)S(1)}, u32[]{:S(2)}, u32[]{:S(2)}) collective-permute-start(bf16[192,2048]{1,0:T(8,128)(2,1)S(1)} %slice.227), channel_id=1, source_target_pairs={{0,2},{1,3},{2,0},{3,1},{4,6},{5,7},{6,4},{7,5},{8,10},{9,11},{10,... | collective-permute-start | bytes 2359304 | tf_op jit(solution)/shard_map/ppermute | solution.py:84
  252.5 28.6 %collective-permute-start.19 = (bf16[192,2048]{1,0:T(8,128)(2,1)S(1)}, bf16[192,2048]{1,0:T(8,128)(2,1)S(1)}, u32[]{:S(2)}, u32[]{:S(2)}) collective-permute-start(bf16[192,2048]{1,0:T(8,128)(2,1)S(1)} %slice.228), channel_id=1, source_target_pairs={{0,1},{1,0},{2,3},{3,2},{4,5},{5,4},{6,7},{7,6},{8,9},{9,8},{10,11... | collective-permute-start | bytes 2359304 | tf_op jit(solution)/shard_map/ppermute | solution.py:84
  253.6 80.8 %collective-permute-start.25 = (bf16[256,2048]{1,0:T(8,128)(2,1)}, bf16[256,2048]{1,0:T(8,128)(2,1)}, u32[]{:S(2)}, u32[]{:S(2)}) collective-permute-start(bf16[256,2048]{1,0:T(8,128)(2,1)} %bitcast.14), channel_id=1, source_target_pairs={{0,3},{1,2},{2,1},{3,0},{4,7},{5,6},{6,5},{7,4},{8,11},{9,10},{10,... | collective-permute-start | bytes 3145736 | tf_op jit(solution)/shard_map/ppermute | solution.py:84
  256.1 79.6 %collective-permute-start.24 = (bf16[256,2048]{1,0:T(8,128)(2,1)}, bf16[256,2048]{1,0:T(8,128)(2,1)}, u32[]{:S(2)}, u32[]{:S(2)}) collective-permute-start(bf16[256,2048]{1,0:T(8,128)(2,1)} %bitcast.14), channel_id=1, source_target_pairs={{0,2},{1,3},{2,0},{3,1},{4,6},{5,7},{6,4},{7,5},{8,10},{9,11},{10,... | collective-permute-start | bytes 3145736 | tf_op jit(solution)/shard_map/ppermute | solution.py:84
  257.1 79.2 %collective-permute-start.23 = (bf16[256,2048]{1,0:T(8,128)(2,1)}, bf16[256,2048]{1,0:T(8,128)(2,1)}, u32[]{:S(2)}, u32[]{:S(2)}) collective-permute-start(bf16[256,2048]{1,0:T(8,128)(2,1)} %bitcast.14), channel_id=1, source_target_pairs={{0,1},{1,0},{2,3},{3,2},{4,5},{5,4},{6,7},{7,6},{8,9},{9,8},{10,11... | collective-permute-start | bytes 3145736 | tf_op jit(solution)/shard_map/ppermute | solution.py:84
  282.2 55.8 %collective-permute-start.20 = (bf16[128,2048]{1,0:T(8,128)(2,1)}, bf16[128,2048]{1,0:T(8,128)(2,1)}, u32[]{:S(2)}, u32[]{:S(2)}) collective-permute-start(bf16[128,2048]{1,0:T(8,128)(2,1)} %slice_bitcast_fusion), channel_id=1, source_target_pairs={{0,1},{1,0},{2,3},{3,2},{4,5},{5,4},{6,7},{7,6},{8,9},{9,8},{10,11... | collective-permute-start | bytes 1572872 | tf_op jit(solution)/shard_map/ppermute | solution.py:84
  285.7 57.6 %collective-permute-start.21 = (bf16[128,2048]{1,0:T(8,128)(2,1)}, bf16[128,2048]{1,0:T(8,128)(2,1)}, u32[]{:S(2)}, u32[]{:S(2)}) collective-permute-start(bf16[128,2048]{1,0:T(8,128)(2,1)} %slice_bitcast_fusion), channel_id=1, source_target_pairs={{0,2},{1,3},{2,0},{3,1},{4,6},{5,7},{6,4},{7,5},{8,10},{9,11},{10,... | collective-permute-start | bytes 1572872 | tf_op jit(solution)/shard_map/ppermute | solution.py:84
  334.4 10.5 %collective-permute-start.22 = (bf16[128,2048]{1,0:T(8,128)(2,1)}, bf16[128,2048]{1,0:T(8,128)(2,1)S(1)}, u32[]{:S(2)}, u32[]{:S(2)}) collective-permute-start(bf16[128,2048]{1,0:T(8,128)(2,1)} %slice_bitcast_fusion), channel_id=1, source_target_pairs={{0,3},{1,2},{2,1},{3,0},{4,7},{5,6},{6,5},{7,4},{8,11},{9,10},{10,... | collective-permute-start | bytes 1572872 | tf_op jit(solution)/shard_map/ppermute | solution.py:84
  335.7 81.8 %collective-permute-start.30 = (bf16[384,2048]{1,0:T(8,128)(2,1)}, bf16[384,2048]{1,0:T(8,128)(2,1)}, u32[]{:S(2)}, u32[]{:S(2)}) collective-permute-start(bf16[384,2048]{1,0:T(8,128)(2,1)} %get-tuple-element.88), channel_id=1, source_target_pairs={{0,1},{1,0},{2,3},{3,2},{4,5},{5,4},{6,7},{7,6},{8,9},{9,8},{10,11... | collective-permute-start | bytes 4718600 | tf_op jit(solution)/shard_map/ppermute | solution.py:84
  336.3 81.1 %collective-permute-start.31 = (bf16[384,2048]{1,0:T(8,128)(2,1)}, bf16[384,2048]{1,0:T(8,128)(2,1)}, u32[]{:S(2)}, u32[]{:S(2)}) collective-permute-start(bf16[384,2048]{1,0:T(8,128)(2,1)} %get-tuple-element.89), channel_id=1, source_target_pairs={{0,2},{1,3},{2,0},{3,1},{4,6},{5,7},{6,4},{7,5},{8,10},{9,11},{10,... | collective-permute-start | bytes 4718600 | tf_op jit(solution)/shard_map/ppermute | solution.py:84
  338.0 79.5 %collective-permute-start.32 = (bf16[384,2048]{1,0:T(8,128)(2,1)}, bf16[384,2048]{1,0:T(8,128)(2,1)}, u32[]{:S(2)}, u32[]{:S(2)}) collective-permute-start(bf16[384,2048]{1,0:T(8,128)(2,1)} %get-tuple-element.90), channel_id=1, source_target_pairs={{0,3},{1,2},{2,1},{3,0},{4,7},{5,6},{6,5},{7,4},{8,11},{9,10},{10,... | collective-permute-start | bytes 4718600 | tf_op jit(solution)/shard_map/ppermute | solution.py:84
  417.5 200.3 %reduce-scatter.5.cloned.1.call-start = ((), (), s32[]{:S(2)}) async-start(), calls=%async_computation.8 | async-start | bytes 9437184 | tf_op jit(solution)/shard_map/reduce_scatter | solution.py:653
  417.6 26.6 %collective-permute-start.26 = (bf16[384,2048]{1,0:T(8,128)(2,1)}, bf16[384,2048]{1,0:T(8,128)(2,1)}, u32[]{:S(2)}, u32[]{:S(2)}) collective-permute-start(bf16[384,2048]{1,0:T(8,128)(2,1)} %get-tuple-element.103), channel_id=1, source_target_pairs={{0,1},{1,0},{2,3},{3,2},{4,5},{5,4},{6,7},{7,6},{8,9},{9,8},{10,11... | collective-permute-start | bytes 4718600 | tf_op jit(solution)/shard_map/ppermute | solution.py:84
  419.4 28.7 %collective-permute-start.27 = (bf16[384,2048]{1,0:T(8,128)(2,1)}, bf16[384,2048]{1,0:T(8,128)(2,1)}, u32[]{:S(2)}, u32[]{:S(2)}) collective-permute-start(bf16[384,2048]{1,0:T(8,128)(2,1)} %get-tuple-element.104), channel_id=1, source_target_pairs={{0,2},{1,3},{2,0},{3,1},{4,6},{5,7},{6,4},{7,5},{8,10},{9,11},{10,... | collective-permute-start | bytes 4718600 | tf_op jit(solution)/shard_map/ppermute | solution.py:84
  419.4 50.5 %collective-permute-start.28 = (bf16[384,2048]{1,0:T(8,128)(2,1)}, bf16[384,2048]{1,0:T(8,128)(2,1)}, u32[]{:S(2)}, u32[]{:S(2)}) collective-permute-start(bf16[384,2048]{1,0:T(8,128)(2,1)} %get-tuple-element.105), channel_id=1, source_target_pairs={{0,3},{1,2},{2,1},{3,0},{4,7},{5,6},{6,5},{7,4},{8,11},{9,10},{10,... | collective-permute-start | bytes 4718600 | tf_op jit(solution)/shard_map/ppermute | solution.py:84
  470.0 222.3 %reduce-scatter.9.cloned.1.call-start = ((), (), s32[]{:S(2)}) async-start(), calls=%async_computation.10 | async-start | bytes 1310720 | tf_op jit(solution)/shard_map/reduce_scatter | solution.py:710
  483.1 30.8 %collective-permute-start.29 = (bf16[1024,2048]{1,0:T(8,128)(2,1)}, bf16[1024,2048]{1,0:T(8,128)(2,1)}, u32[]{:S(2)}, u32[]{:S(2)}) collective-permute-start(bf16[1024,2048]{1,0:T(8,128)(2,1)} %convolution_convert_fusion), channel_id=1, source_target_pairs={{0,4},{4,0},{8,12},{12,8},{16,20},{20,16},{24,28},{28,24},{1,5},{5... | collective-permute-start | bytes 12582920 | tf_op jit(solution)/shard_map/ppermute | solution.py:84
  545.7 30.2 %collective-permute-start.33 = (bf16[1024,2048]{1,0:T(8,128)(2,1)}, bf16[1024,2048]{1,0:T(8,128)(2,1)}, u32[]{:S(2)}, u32[]{:S(2)}) collective-permute-start(bf16[1024,2048]{1,0:T(8,128)(2,1)} %ffn_weight.5), channel_id=1, source_target_pairs={{0,4},{4,0},{8,12},{12,8},{16,20},{20,16},{24,28},{28,24},{1,5},{5... | collective-permute-start | bytes 12582920 | tf_op jit(solution)/shard_map/ppermute | solution.py:84
  560.1 26.3 %collective-permute-start.35 = (bf16[256,2048]{1,0:T(8,128)(2,1)}, bf16[256,2048]{1,0:T(8,128)(2,1)S(1)}, u32[]{:S(2)}, u32[]{:S(2)}) collective-permute-start(bf16[256,2048]{1,0:T(8,128)(2,1)} %get-tuple-element.176), channel_id=1, source_target_pairs={{0,1},{1,0},{2,3},{3,2},{4,5},{5,4},{6,7},{7,6},{8,9},{9,8},{10,11... | collective-permute-start | bytes 3145736 | tf_op jit(solution)/shard_map/ppermute | solution.py:84
  560.4 50.4 %collective-permute-start.36 = (bf16[256,2048]{1,0:T(8,128)(2,1)}, bf16[256,2048]{1,0:T(8,128)(2,1)}, u32[]{:S(2)}, u32[]{:S(2)}) collective-permute-start(bf16[256,2048]{1,0:T(8,128)(2,1)} %get-tuple-element.175), channel_id=1, source_target_pairs={{0,2},{1,3},{2,0},{3,1},{4,6},{5,7},{6,4},{7,5},{8,10},{9,11},{10,... | collective-permute-start | bytes 3145736 | tf_op jit(solution)/shard_map/ppermute | solution.py:84
  565.5 47.2 %collective-permute-start.37 = (bf16[256,2048]{1,0:T(8,128)(2,1)}, bf16[256,2048]{1,0:T(8,128)(2,1)}, u32[]{:S(2)}, u32[]{:S(2)}) collective-permute-start(bf16[256,2048]{1,0:T(8,128)(2,1)} %get-tuple-element.174), channel_id=1, source_target_pairs={{0,3},{1,2},{2,1},{3,0},{4,7},{5,6},{6,5},{7,4},{8,11},{9,10},{10,... | collective-permute-start | bytes 3145736 | tf_op jit(solution)/shard_map/ppermute | solution.py:84
  570.3 3.5 collective-permute-start.34
  619.6 12.1 %collective-permute-start.38 = (bf16[3,2,1,128,256]{4,3,2,1,0:T(8,128)(2,1)S(1)}, bf16[3,2,1,128,256]{4,3,2,1,0:T(8,128)(2,1)S(1)}, u32[]{:S(2)}, u32[]{:S(2)}) collective-permute-start(bf16[3,2,1,128,256]{4,3,2,1,0:T(8,128)(2,1)S(1)} %get-tuple-element.178), channel_id=1, source_target_pairs={{0,1},{1,0},{2,3},{3,2},{4,5},{5,4},{6,7},{7,6},{8,9},{9,8},{10,11... | collective-permute-start | bytes 1179656 | tf_op jit(solution)/shard_map/ppermute | solution.py:84
  621.2 18.5 %collective-permute-start.39 = (bf16[3,2,1,128,256]{4,3,2,1,0:T(8,128)(2,1)S(1)}, bf16[3,2,1,128,256]{4,3,2,1,0:T(8,128)(2,1)S(1)}, u32[]{:S(2)}, u32[]{:S(2)}) collective-permute-start(bf16[3,2,1,128,256]{4,3,2,1,0:T(8,128)(2,1)S(1)} %get-tuple-element.180), channel_id=1, source_target_pairs={{0,2},{1,3},{2,0},{3,1},{4,6},{5,7},{6,4},{7,5},{8,10},{9,11},{10,... | collective-permute-start | bytes 1179656 | tf_op jit(solution)/shard_map/ppermute | solution.py:84
  622.6 18.5 %collective-permute-start.40 = (bf16[3,2,1,128,256]{4,3,2,1,0:T(8,128)(2,1)S(1)}, bf16[3,2,1,128,256]{4,3,2,1,0:T(8,128)(2,1)S(1)}, u32[]{:S(2)}, u32[]{:S(2)}) collective-permute-start(bf16[3,2,1,128,256]{4,3,2,1,0:T(8,128)(2,1)S(1)} %get-tuple-element.179), channel_id=1, source_target_pairs={{0,3},{1,2},{2,1},{3,0},{4,7},{5,6},{6,5},{7,4},{8,11},{9,10},{10,... | collective-permute-start | bytes 1179656 | tf_op jit(solution)/shard_map/ppermute | solution.py:84
  627.6 36.9 %collective-permute-start.42 = (bf16[256,2048]{1,0:T(8,128)(2,1)}, bf16[256,2048]{1,0:T(8,128)(2,1)}, u32[]{:S(2)}, u32[]{:S(2)}) collective-permute-start(bf16[256,2048]{1,0:T(8,128)(2,1)} %get-tuple-element.172), channel_id=1, source_target_pairs={{0,1},{1,0},{2,3},{3,2},{4,5},{5,4},{6,7},{7,6},{8,9},{9,8},{10,11... | collective-permute-start | bytes 3145736 | tf_op jit(solution)/shard_map/ppermute | solution.py:84
  629.0 53.7 %collective-permute-start.43 = (bf16[256,2048]{1,0:T(8,128)(2,1)}, bf16[256,2048]{1,0:T(8,128)(2,1)}, u32[]{:S(2)}, u32[]{:S(2)}) collective-permute-start(bf16[256,2048]{1,0:T(8,128)(2,1)} %get-tuple-element.171), channel_id=1, source_target_pairs={{0,2},{1,3},{2,0},{3,1},{4,6},{5,7},{6,4},{7,5},{8,10},{9,11},{10,... | collective-permute-start | bytes 3145736 | tf_op jit(solution)/shard_map/ppermute | solution.py:84
  631.7 51.6 %collective-permute-start.44 = (bf16[256,2048]{1,0:T(8,128)(2,1)}, bf16[256,2048]{1,0:T(8,128)(2,1)}, u32[]{:S(2)}, u32[]{:S(2)}) collective-permute-start(bf16[256,2048]{1,0:T(8,128)(2,1)} %get-tuple-element.170), channel_id=1, source_target_pairs={{0,3},{1,2},{2,1},{3,0},{4,7},{5,6},{6,5},{7,4},{8,11},{9,10},{10,... | collective-permute-start | bytes 3145736 | tf_op jit(solution)/shard_map/ppermute | solution.py:84
  644.0 4.9 collective-permute-start.41
  648.6 99.7 %reduce-scatter.11.cloned.1.call-start = ((), (), s32[]{:S(2)}) async-start(), calls=%async_computation.11 | async-start | bytes 1474560 | tf_op jit(solution)/shard_map/reduce_scatter | solution.py:710
  662.3 2.0 collective-permute-start.45
  683.3 6.1 collective-permute-start.46
  684.8 6.4 collective-permute-start.47
  685.2 6.0 collective-permute-start.48
  692.4 13.4 %collective-permute-start.50 = (f32[177,128]{1,0:T(8,128)S(1)}, f32[177,128]{1,0:T(8,128)S(1)}, u32[]{:S(2)}, u32[]{:S(2)}) collective-permute-start(f32[177,128]{1,0:T(8,128)S(1)} %bitcast.123), channel_id=1, source_target_pairs={{0,4},{4,0},{8,12},{12,8},{16,20},{20,16},{24,28},{28,24},{1,5},{5... | collective-permute-start | bytes 271880 | tf_op jit(solution)/shard_map/ppermute | solution.py:84
  705.8 6.6 collective-permute-start.51
  712.4 26.8 %collective-permute-start.52 = (f32[177,128]{1,0:T(8,128)S(1)}, f32[177,128]{1,0:T(8,128)S(1)}, u32[]{:S(2)}, u32[]{:S(2)}) collective-permute-start(f32[177,128]{1,0:T(8,128)S(1)} %fusion.64), channel_id=1, source_target_pairs={{0,16},{4,20},{8,24},{12,28},{16,0},{20,4},{24,8},{28,12},{1,17},{... | collective-permute-start | bytes 271880 | tf_op jit(solution)/shard_map/ppermute | solution.py:84
  739.3 7.4 collective-permute-start.53
  746.7 4.6 collective-permute-start.54
  750.3 1.8 collective-permute-start.49
  (59 other events, 790.5 us)
Sparse Core Ops, SparseCore 0:
  12.5 34.4 all-gather.4
  49.1 29.8 all-gather.6
  80.6 84.7 all-gather.8
  166.9 80.6 all-gather.10
  417.6 110.0 reduce-scatter.6
  529.9 87.9 reduce-scatter.4
  648.7 40.4 reduce-scatter.8
  692.5 45.7 reduce-scatter.10

commit v3 on v2

--- a/solution.py
+++ b/solution.py
@@ -104,11 +104,34 @@
     second = swap(value, "tp", 2)
     far_top = swap(cut(first)[0], "tp", 2)
     far_low = swap(cut(second)[1], "tp", 1)
-    return [value, first, second, jnp.concatenate([far_top, far_low], -2)]
+    return [value, first, second, far_top, far_low]
 
 
 def deliver(pieces):
     return [pieces[0]] + [swap(pieces[m].astype(bf16), "tp", m) for m in range(1, len(pieces))]
+
+
+def far_cuts(count, rows):
+    return [rows] * count if count != 4 else [rows] + [rows // 2] * 6
+
+
+def row_halves(value):
+    at = value.shape[0] // 2
+    return (slice(0, at), slice(at, 2 * at))
+
+
+def deliver_halves(pieces):
+    if len(pieces) != 7:
+        own, *others = deliver(pieces)
+        return (own, *([piece[part] for piece in others] for part in row_halves(own)))
+    own, one_top, one_low, two_top, two_low, far_top, far_low = pieces
+    for_two = swap(far_top, "tp", 1)
+    for_one = swap(far_low, "tp", 2)
+    got_one_top = swap(one_top, "tp", 1)
+    got_two_low = swap(two_low, "tp", 2)
+    got_one_low = swap((one_low.astype(f32) + for_one.astype(f32)).astype(bf16), "tp", 1)
+    got_two_top = swap((two_top.astype(f32) + for_two.astype(f32)).astype(bf16), "tp", 2)
+    return (own, [got_one_top, got_two_top], [got_one_low, got_two_low])
 
 
 def total_of(pieces):
@@ -310,59 +333,57 @@
     return jnp.tanh(values * (gelu_coef + (gelu_coef * 0.044715) * square)), square
 
 
+def rows_at(refs, at, rows):
+    for ref in refs:
+        if at < ref.shape[0]:
+            return ref[pl.ds(at, rows), :]
+        at -= ref.shape[0]
+
+
+def spans(refs):
+    at = 0
+    for ref in refs:
+        yield ref, at, ref.shape[0]
+        at += ref.shape[0]
+
+
 def ffn_up_kernel(*refs):
-    count = len(refs) - 4
-    hidden_refs = refs[:count]
-    weight_ref, bias_ref, pre_ref, act_ref = refs[count:]
-    rows = hidden_refs[0].shape[0]
-    for m in range(count):
-        at = pl.ds(m * rows, rows)
-        values = rows_by_rows(hidden_refs[m][...], weight_ref[...]) + bias_ref[...]
-        pre_ref[at, :] = values
+    hidden_refs, (weight_ref, bias_ref, pre_ref, act_ref) = refs[:-4], refs[-4:]
+    for hidden_ref, at, rows in spans(hidden_refs):
+        values = rows_by_rows(hidden_ref[...], weight_ref[...]) + bias_ref[...]
+        pre_ref[pl.ds(at, rows), :] = values
         tangent, _ = gelu_parts(values)
-        act_ref[at, :] = (0.5 * values * (1.0 + tangent)).astype(bf16)
+        act_ref[pl.ds(at, rows), :] = (0.5 * values * (1.0 + tangent)).astype(bf16)
 
 
 def ffn_back_kernel(*refs, count):
-    weight_ref = refs[count]
+    cot_refs, weight_ref = refs[:count], refs[count]
     pre_refs, (grad_ref, sum_ref) = refs[count + 1 : -2], refs[-2:]
-    cot_refs = refs[:count]
-    rows = cot_refs[0].shape[0]
     total = jnp.zeros(sum_ref.shape, f32)
-    for m in range(count):
-        at = pl.ds(m * rows, rows)
-        values = piece_of(pre_refs, m, rows)
+    for cot_ref, at, rows in spans(cot_refs):
+        values = rows_at(pre_refs, at, rows)
         tangent, square = gelu_parts(values)
         slope = 0.5 * (1.0 + tangent) + (0.5 * gelu_coef) * values * (1.0 - tangent * tangent) * (
             1.0 + (3.0 * 0.044715) * square
         )
-        grad = (rows_by_rows(cot_refs[m][...], weight_ref[...]) * slope).astype(bf16)
-        grad_ref[at, :] = grad
+        grad = (rows_by_rows(cot_ref[...], weight_ref[...]) * slope).astype(bf16)
+        grad_ref[pl.ds(at, rows), :] = grad
         total = total + jnp.sum(grad.astype(f32), 0, keepdims=True)
     sum_ref[...] = total
 
 
-def piece_of(refs, index, rows):
-    at = index * rows
-    for ref in refs:
-        if at < ref.shape[0]:
-            return ref[pl.ds(at, rows), :]
-        at -= ref.shape[0]
-
-
 def ffn_product_kernel(*refs, lefts):
     right_ref, out_refs = refs[lefts], refs[lefts + 1 :]
-    for m, out_ref in enumerate(out_refs):
-        left = piece_of(refs[:lefts], m, out_ref.shape[0])
+    for out_ref, at, rows in spans(out_refs):
+        left = rows_at(refs[:lefts], at, rows)
         out_ref[...] = plain_dot(left, right_ref[...]).astype(bf16)
 
 
 def ffn_weight_kernel(*refs, lefts):
     right_refs, out_ref = refs[lefts:-1], refs[-1]
-    rows = right_refs[0].shape[0]
     total = None
-    for m, right_ref in enumerate(right_refs):
-        part = cols_by_cols(piece_of(refs[:lefts], m, rows), right_ref[...])
+    for right_ref, at, rows in spans(right_refs):
+        part = cols_by_cols(rows_at(refs[:lefts], at, rows), right_ref[...])
         total = part if total is None else total + part
     out_ref[...] = total.astype(bf16)
 
@@ -379,7 +400,7 @@
 
 def ffn_up(pieces, weights, bias, tile=256):
     units, width = weights.shape
-    rows = len(pieces) * pieces[0].shape[0]
+    rows = sum(piece.shape[0] for piece in pieces)
     out_spec = pl.BlockSpec((rows, tile), lambda i: (0, i))
     return pl.pallas_call(
         ffn_up_kernel,
@@ -402,7 +423,7 @@
 
 def ffn_back(pieces, weights, pre_acts, tile=256):
     units, width = weights.shape
-    rows = len(pieces) * pieces[0].shape[0]
+    rows = sum(piece.shape[0] for piece in pieces)
     out_spec = pl.BlockSpec((rows, tile), lambda i: (0, i))
     sum_spec = pl.BlockSpec((1, tile), lambda i: (0, i))
     return pl.pallas_call(
@@ -422,35 +443,205 @@
     )(*pieces, weights, *pre_acts)
 
 
-def ffn_product(lefts, right, count, tile=256):
+def ffn_product(lefts, right, sizes, tile=256):
     units, width = right.shape
-    piece = sum(left.shape[0] for left in lefts) // count
     return pl.pallas_call(
         functools.partial(ffn_product_kernel, lefts=len(lefts)),
         name="ffn_product",
         grid=(width // tile,),
         in_specs=whole_specs(lefts) + [pl.BlockSpec((units, tile), lambda i: (0, i))],
-        out_specs=[pl.BlockSpec((piece, tile), lambda i: (0, i))] * count,
-        out_shape=[jax.ShapeDtypeStruct((piece, width), bf16)] * count,
+        out_specs=[pl.BlockSpec((size, tile), lambda i: (0, i)) for size in sizes],
+        out_shape=[jax.ShapeDtypeStruct((size, width), bf16) for size in sizes],
         compiler_params=ffn_params(),
         cost_estimate=cheap,
     )(*lefts, right)
 
 
-def ffn_weight(lefts, pieces, tile=256):
-    units = lefts[0].shape[1]
+def ffn_weight(lefts, pieces, tile=256, first=0):
+    units = lefts[0].shape[1] - first
+    skip = first // tile
     width = pieces[0].shape[1]
     return pl.pallas_call(
         functools.partial(ffn_weight_kernel, lefts=len(lefts)),
         name="ffn_weight",
         grid=(units // tile,),
-        in_specs=[pl.BlockSpec((left.shape[0], tile), lambda i: (0, i)) for left in lefts]
+        in_specs=[pl.BlockSpec((left.shape[0], tile), lambda i: (0, i + skip)) for left in lefts]
         + whole_specs(pieces),
         out_specs=pl.BlockSpec((tile, width), lambda i: (i, 0)),
         out_shape=jax.ShapeDtypeStruct((units, width), bf16),
         compiler_params=ffn_params(),
         cost_estimate=cheap,
     )(*lefts, *pieces)
+
+
+def weight_pieces_kernel(left_ref, right_ref, add_ref, *out_refs):
+    total = cols_by_cols(left_ref[...], right_ref[...]) + add_ref[...].astype(f32)
+    for m, out_ref in enumerate(out_refs):
+
+        @pl.when(pl.program_id(0) == m)
+        def _():
+            out_ref[...] = total.astype(bf16)
+
+
+def weight_pieces(left, right, addend, count):
+    rows, width = right.shape
+    tile = addend.shape[0] // count
+    return pl.pallas_call(
+        weight_pieces_kernel,
+        name="weight_pieces",
+        grid=(count,),
+        in_specs=[pl.BlockSpec((rows, tile), lambda i: (0, i))]
+        + whole_specs([right])
+        + [pl.BlockSpec((tile, width), lambda i: (i, 0))],
+        out_specs=[pl.BlockSpec((tile, width), lambda i: (0, 0))] * count,
+        out_shape=[jax.ShapeDtypeStruct((tile, width), bf16)] * count,
+        compiler_params=ffn_params(),
+        cost_estimate=cheap,
+    )(left, right, addend)
+
+
+def onto_rows_kernel(*refs):
+    left_ref, bias_ref, piece_refs, out_ref = refs[0], refs[1], refs[2:-1], refs[-1]
+    for m, piece_ref in enumerate(piece_refs):
+
+        @pl.when(pl.program_id(0) == m)
+        def _():
+            out_ref[...] = (rows_by_rows(left_ref[...], piece_ref[...]) + bias_ref[...]).astype(bf16)
+
+
+def onto_rows(left, pieces, bias):
+    tile = pieces[0].shape[0]
+    width = tile * len(pieces)
+    return pl.pallas_call(
+        onto_rows_kernel,
+        name="onto_rows",
+        grid=(len(pieces),),
+        in_specs=whole_specs([left])
+        + [pl.BlockSpec((1, tile), lambda i: (0, i))]
+        + whole_specs(pieces),
+        out_specs=pl.BlockSpec((left.shape[0], tile), lambda i: (0, i)),
+        out_shape=jax.ShapeDtypeStruct((left.shape[0], width), bf16),
+        compiler_params=ffn_params(),
+        cost_estimate=cheap,
+    )(left, bias.reshape(1, width), *pieces)
+
+
+def onto_columns_kernel(*refs, lefts):
+    piece_refs, out_ref = refs[lefts:-1], refs[-1]
+    total = None
+    at, index = 0, 0
+    for piece_ref in piece_refs:
+        size = piece_ref.shape[0]
+        if at == refs[index].shape[1]:
+            at, index = 0, index + 1
+        part = plain_dot(refs[index][:, at : at + size], piece_ref[...])
+        total = part if total is None else total + part
+        at += size
+    out_ref[...] = total
+
+
+def onto_columns(lefts, pieces, tile=512):
+    rows, width = lefts[0].shape[0], pieces[0].shape[1]
+    return pl.pallas_call(
+        functools.partial(onto_columns_kernel, lefts=len(lefts)),
+        name="onto_columns",
+        grid=(width // tile,),
+        in_specs=whole_specs(lefts)
+        + [pl.BlockSpec((piece.shape[0], tile), lambda i: (0, i)) for piece in pieces],
+        out_specs=pl.BlockSpec((rows, tile), lambda i: (0, i)),
+        out_shape=jax.ShapeDtypeStruct((rows, width), f32),
+        compiler_params=ffn_params(),
+        cost_estimate=cheap,
+    )(*lefts, *pieces)
+
+
+def place_keys_kernel(starts, *refs):
+    piece_refs, (key_ref, key_t_ref, val_ref, val_t_ref) = refs[:-4], refs[-4:]
+    rows = piece_refs[0].shape[2]
+    for index, piece_ref in enumerate(piece_refs):
+        for which in range(2):
+            at = pl.ds(pl.multiple_of(which * CHIP_ROWS + starts[index], rows), rows)
+            key_ref[0, at, :] = piece_ref[which, 0, :, :HD]
+            val_ref[0, at, :] = piece_ref[which, 0, :, HD:]
+    for first in range(0, KEY_ROWS, 128):
+        at = slice(first, first + 128)
+        key_t_ref[0, :, at] = key_ref[0, at, :].T
+        val_t_ref[0, :, at] = val_ref[0, at, :].T
+
+
+def place_keys(starts, pieces):
+    batches, rows = pieces[0].shape[1:3]
+    tall = pl.BlockSpec((1, KEY_ROWS, HD), lambda b, *_: (b, 0, 0))
+    wide = pl.BlockSpec((1, HD, KEY_ROWS), lambda b, *_: (b, 0, 0))
+    return pl.pallas_call(
+        place_keys_kernel,
+        name="place_keys",
+        grid_spec=pltpu.PrefetchScalarGridSpec(
+            num_scalar_prefetch=1,
+            grid=(batches,),
+            in_specs=[pl.BlockSpec((2, 1, rows, 2 * HD), lambda b, *_: (0, b, 0, 0))] * len(pieces),
+            out_specs=[tall, wide, tall, wide],
+        ),
+        out_shape=[
+            jax.ShapeDtypeStruct((batches, KEY_ROWS, HD), bf16),
+            jax.ShapeDtypeStruct((batches, HD, KEY_ROWS), bf16),
+        ]
+        * 2,
+        compiler_params=ffn_params(),
+        cost_estimate=cheap,
+    )(starts, *pieces)
+
+
+def norm_back_kernel(*refs, count):
+    own_ref, cot_ref, normed_ref, inverse_ref, gain_ref = refs[:5]
+    top_refs, low_refs = refs[5 : 5 + count], refs[5 + count : 5 + 2 * count]
+    resid_ref, low_resid_ref, sum_ref = refs[5 + 2 * count :]
+    is_top = pl.program_id(0) < 2
+    grad = own_ref[...].astype(f32)
+    for top_ref, low_ref in zip(top_refs, low_refs):
+        grad = grad + jnp.where(is_top, top_ref[...], low_ref[...]).astype(f32)
+    normed = normed_ref[...]
+    resid = cot_ref[...].astype(f32) + layer_norm_back(
+        grad, normed, inverse_ref[...], gain_ref[...]
+    )
+    resid_ref[...] = resid
+    low_resid_ref[...] = resid.astype(bf16)
+    sums = [jnp.sum(part, 0, keepdims=True) for part in (grad * normed, grad, resid)]
+
+    @pl.when(pl.program_id(0) == 0)
+    def _():
+        sum_ref[...] = jnp.zeros_like(sum_ref)
+
+    for index, part in enumerate(sums):
+        sum_ref[index : index + 1, :] += part
+
+
+def norm_back(own, tops, lows, cot, normed, inverse, gain):
+    rows, width = own.shape
+    block = rows // 4
+    by_block = pl.BlockSpec((block, width), lambda i: (i, 0))
+    return pl.pallas_call(
+        functools.partial(norm_back_kernel, count=len(tops)),
+        name="norm_back",
+        grid=(4,),
+        in_specs=[
+            by_block,
+            by_block,
+            by_block,
+            pl.BlockSpec((block, 1), lambda i: (i, 0)),
+            pl.BlockSpec((1, width), lambda i: (0, 0)),
+        ]
+        + [pl.BlockSpec((block, width), lambda i: (jnp.minimum(i, 1), 0))] * len(tops)
+        + [pl.BlockSpec((block, width), lambda i: (jnp.maximum(i - 2, 0), 0))] * len(lows),
+        out_specs=[by_block, by_block, pl.BlockSpec((8, width), lambda i: (0, 0))],
+        out_shape=[
+            jax.ShapeDtypeStruct((rows, width), f32),
+            jax.ShapeDtypeStruct((rows, width), bf16),
+            jax.ShapeDtypeStruct((8, width), f32),
+        ],
+        compiler_params=ffn_params(),
+        cost_estimate=cheap,
+    )(own, cot, normed, inverse, gain.reshape(1, width), *tops, *lows)
 
 
 def adam_step(weights, grads, first, second, step_count, learning_rate):
@@ -580,8 +771,7 @@
         return [lax.dynamic_slice_in_dim(block, side * size, size) for side in sides]
 
     def widen_rows(received, other):
-        crossed = swap_core(jnp.concatenate(received[1:], 0))
-        return jnp.concatenate(received + [other, crossed], 0)
+        return received + [other] + [swap_core(piece) for piece in received[1:]]
 
     w_keyval = jnp.zeros((2 * HD, D), bf16)
     for m, piece in enumerate(spread_directly(kv_rows)):
@@ -594,30 +784,17 @@
     ln_one, normed_one, inverse_one = layer_norm_fwd(block_rows, gain_one, shift_one)
     hidden_one = ln_one.astype(bf16)
     kv_local = (rows_by_rows(hidden_one, w_keyval) + keyval_bias).astype(bf16)
-    kv_local = kv_local.reshape(1, batches, 1, rows, 2 * HD)
+    kv_local = kv_local.reshape(1, batches, rows, 2 * HD)
     to_next = [(d, d + 2) for d in range(dp_size - 2) if (d // 2) % 2 == 1]
     to_last = [(target, source) for source, target in to_next]
     kv_pair = jnp.concatenate([lax.ppermute(kv_local, "dp", to_next), kv_local], 0)
-    kv_stretch = jnp.zeros((2, batches, tp_size, rows, 2 * HD), bf16)
     kv_pieces = spread_directly(after(kv_pair, *query_got))
-    out_own, out_other = split_sides(after(out_rows, *kv_pieces))
-    out_got = spread_directly(out_own)
-    w_out = widen_rows(out_got, out_other)
-    early = max(1, batches - 1)
-    cot_early = cotangent[:early].reshape(early * rows, D)
-    cot_early = spread_directly(after(cot_early, *out_got))
-    for m, piece in enumerate(kv_pieces):
-        kv_stretch = lax.dynamic_update_slice_in_dim(kv_stretch, piece, block_of[m], 2)
-    kv_stretch = kv_stretch.reshape(2, batches, stretch, 2 * HD).transpose(1, 0, 2, 3)
-    kv_stretch = kv_stretch.reshape(batches, 2, 1, stretch, 2 * HD)
-    keyvals = jnp.zeros((batches, 2, 2, stretch, 2 * HD), bf16)
-    keyvals = lax.dynamic_update_slice_in_dim(keyvals, kv_stretch, core, 2)
-    keyvals = lax.dynamic_update_slice_in_dim(keyvals, swap_core(kv_stretch), 1 - core, 2)
-    keyvals = keyvals.reshape(batches, KEY_ROWS, 2 * HD)
-    keys = keyvals[:, :, :HD]
-    vals = keyvals[:, :, HD:]
-    keys_t = keys.transpose(0, 2, 1)
-    vals_t = vals.transpose(0, 2, 1)
+    out_own, out_other = split_sides(out_rows)
+    out_got = spread_directly(after(out_own, *kv_pieces))
+    key_starts = jnp.stack([side * stretch + at * rows for side in sides for at in block_of])
+    keys, keys_t, vals, vals_t = place_keys(
+        key_starts.astype(jnp.int32), kv_pieces + [swap_core(piece) for piece in kv_pieces]
+    )
 
     own_first = dp_index * stretch + tp_index * rows
     seg_own = lax.dynamic_slice_in_dim(segments, own_first, rows, 1)
@@ -637,58 +814,61 @@
     first_block = jnp.maximum(seg_own[:, 0] - key_base, 0) // KEY_BLOCK
     bounds = jnp.stack([first_block, last_block], 1).astype(jnp.int32)
 
-    queries = (rows_by_rows(hidden_one, w_query) + bias_query).astype(bf16)
+    queries = onto_rows(hidden_one, w_query, bias_query)
     queries = queries.reshape(batches, rows, H * HD)
     attended, log_sums = attend_forward(queries, keys, vals_t, bias, bounds)
     attended = attended.reshape(batches * rows, H * HD)
-    residual = block_rows + plain_dot(attended, w_out) + bias_out
+    w_out = widen_rows(after(out_got, attended), out_other)
+    residual = block_rows + onto_columns([attended], w_out) + bias_out
     ln_two, normed_two, inverse_two = layer_norm_fwd(residual, gain_two, shift_two)
     hidden_two = ln_two.astype(bf16)
 
     hidden_got = spread(hidden_two)
-    cot_late = cotangent[early:].reshape((batches - early) * rows, D)
-    cot_late = spread_directly(after(cot_late, *hidden_got))
+    cot_got = spread_directly(after(cotangent.reshape(batches * rows, D), *hidden_got))
 
     def scatter_columns(full):
         return lax.psum_scatter(full, "dp", scatter_dimension=1, tiled=True)
 
-    near = tp_size - 1
-    ups = [ffn_up(part, w_up, bias_up) for part in (hidden_got[:near], hidden_got[near:])]
-    pre_act = [up[0] for up in ups]
-    activated = [up[1] for up in ups]
-    product = ffn_product(activated, w_down, tp_size)
+    pre_act, activated = ffn_up(hidden_got, w_up, bias_up)
+    product = ffn_product([activated], w_down, [batches * rows] * tp_size)
     received = deliver(product)
-    cot_late = after(cot_late, product)
-    cot_got = [jnp.concatenate(pair, 0) for pair in zip(cot_early, cot_late)]
-    grad_down = ffn_weight(activated, cot_got)
-    grad_pre, grad_bias_up = ffn_back(after(cot_got, grad_down), w_down, pre_act)
+    cot_got = after(cot_got, product)
+    grad_down = ffn_weight([activated], cot_got)
+    grad_pre, grad_bias_up = ffn_back(after(cot_got, grad_down), w_down, [pre_act])
     grad_bias_up = grad_bias_up[0]
-    grad_hidden = ffn_product([grad_pre], w_up, tp_size)
+    grad_hidden = ffn_product([grad_pre], w_up, far_cuts(tp_size, batches * rows))
     shard_down = scatter_columns(after(grad_down, *grad_hidden, *received))
-    grad_hidden_parts = deliver(grad_hidden)
+    grad_two_own, grad_two_tops, grad_two_lows = deliver_halves(grad_hidden)
     grad_up = ffn_weight([after(grad_pre, *grad_hidden)], hidden_got)
-    shard_up = scatter_columns(after(grad_up, *grad_hidden_parts))
-    grad_hidden_two = total_of(after(grad_hidden_parts, grad_up))
-
-    cot_rows = cotangent.astype(f32).reshape(batches * rows, D)
-    grad_bias_down = jnp.sum(cot_rows, 0)
-    grad_resid = cot_rows + layer_norm_back(grad_hidden_two, normed_two, inverse_two, gain_two)
-    grad_gain_two = jnp.sum(grad_hidden_two * normed_two, 0)
-    grad_shift_two = jnp.sum(grad_hidden_two, 0)
-    grad_att = grad_resid.astype(bf16)
-    grad_bias_out = jnp.sum(grad_resid, 0)
+    shard_up = scatter_columns(after(grad_up, *grad_two_tops, *grad_two_lows))
+
+    cot_rows = cotangent.reshape(batches * rows, D)
+    grad_bias_down = jnp.sum(cot_rows.astype(f32), 0)
+    grad_resid, grad_att, norm_sums = norm_back(
+        after(grad_two_own, grad_up),
+        grad_two_tops,
+        grad_two_lows,
+        cot_rows,
+        normed_two,
+        inverse_two,
+        gain_two,
+    )
+    grad_gain_two, grad_shift_two, grad_bias_out = norm_sums[0], norm_sums[1], norm_sums[2]
     cols_half = H * HD // 2
-    out_grad_own = cols_by_cols(attended[:, :cols_half], grad_att)
-    out_grad_other = cols_by_cols(attended[:, cols_half:], grad_att).astype(bf16)
-    grad_heads = rows_by_rows(grad_att, w_out).astype(bf16).reshape(batches, rows, H * HD)
+
+    def halves_of(left, right):
+        return (cols_by_cols(left[:, :cols_half], right), cols_by_cols(left[:, cols_half:], right))
 
     def reduce_core(own, other):
-        own = (own + swap_core(other.astype(bf16)).astype(f32)).astype(bf16)
+        own = (own + other.astype(f32)).astype(bf16)
         size = own.shape[0] // tp_size
         return [own[m * size : (m + 1) * size] for m in range(tp_size)]
 
-    out_pieces = reduce_core(out_grad_own, out_grad_other)
-    grad_heads = after(grad_heads, *out_pieces)
+    out_grad_own, out_grad_other = halves_of(attended, grad_att)
+    out_grad_other = out_grad_other.astype(bf16)
+    out_pieces = reduce_core(out_grad_own, swap_core(out_grad_other))
+    grad_heads = onto_rows(after(grad_att, *out_pieces), w_out, jnp.zeros((H * HD,), f32))
+    grad_heads = grad_heads.reshape(batches, rows, H * HD)
     out_pieces = deliver(out_pieces)
     grad_query, grad_key, grad_val = attend_backward(
         queries, grad_heads, keys, keys_t, vals, bias, log_sums, bounds
@@ -697,23 +877,19 @@
     result = residual + total_of(received) + bias_down
     outputs = result.astype(bf16).reshape(batches, rows, D)
     grad_query = grad_query.reshape(batches * rows, H * HD)
-    grad_bias_query = jnp.sum(grad_query.astype(f32), 0)
-
-    query_grad_other = ffn_weight([grad_query[:, cols_half:]], [hidden_one])
-    query_pieces = reduce_core(
-        cols_by_cols(grad_query[:, :cols_half], hidden_one), query_grad_other
-    )
-    out_pieces, shard_up, shard_down = lax.optimization_barrier((out_pieces, shard_up, shard_down))
-    part_out = part_out_sum = total_of(out_pieces).astype(bf16)
+
+    query_grad_other = ffn_weight([after(grad_query, *out_pieces)], [hidden_one], first=cols_half)
+    query_pieces = weight_pieces(grad_query, hidden_one, swap_core(query_grad_other), tp_size)
+    part_out = part_out_sum = total_of(after(out_pieces, *query_pieces)).astype(bf16)
 
     def scatter_chips(part):
         return lax.psum_scatter(
             part, "dp", scatter_dimension=1, axis_index_groups=parity, tiled=True
         )
 
-    part_out = scatter_chips(part_out)
     query_got = deliver(query_pieces)
     grad_query = after(grad_query, *query_pieces)
+    grad_bias_query = jnp.sum(grad_query.astype(f32), 0)
 
     kv_grads = jnp.concatenate([grad_key, grad_val], 2)
     kv_grads = kv_grads.reshape(batches, 2, 2, stretch, 2 * HD)
@@ -722,16 +898,35 @@
     kv_kept = kv_kept + swap_core(kv_sent).astype(f32)
     kv_kept = after(kv_kept, *out_pieces, query_grad_other)
     kv_kept = kv_kept.reshape(batches, 2, tp_size, rows, 2 * HD)
-    kv_total = total_of(
-        deliver([lax.dynamic_slice_in_dim(kv_kept, at, 1, 2) for at in block_of])
-    )
+    kv_got = deliver([lax.dynamic_slice_in_dim(kv_kept, at, 1, 2) for at in block_of])
+    kv_total = total_of(after(kv_got, *query_pieces))
+    part_out, shard_up, shard_down, kv_total, _ = lax.optimization_barrier(
+        (part_out, shard_up, shard_down, kv_total, query_pieces)
+    )
+    part_out = scatter_chips(part_out)
     grad_kv = kv_total[:, 1] + lax.ppermute(
         kv_total[:, 0].astype(bf16), "dp", to_last
     ).astype(f32)
     grad_kv = grad_kv.astype(bf16).reshape(batches * rows, 2 * HD)
     grad_bias_value = jnp.sum(grad_kv[:, HD:].astype(f32), 0)
 
-    grad_hidden_one = plain_dot(grad_query, w_query) + plain_dot(grad_kv, w_keyval)
+    steps_float = step_count[0].astype(f32)
+    scalars = jnp.stack(
+        [
+            learning_rate[0],
+            1.0 - jnp.power(beta_one, steps_float),
+            1.0 - jnp.power(beta_two, steps_float),
+        ]
+    )
+
+    def update_rows(grads, start, filled):
+        block = grads.shape[0] // 2
+        return adam_rows(scalars, master, grads, moment_one, moment_two, start, block, filled)
+
+    state = update_rows(shard_down, row_starts[4], ())
+    state = update_rows(shard_up, row_starts[3], state)
+    grad_kv = after(grad_kv, *state)
+    grad_hidden_one = onto_columns([grad_query, grad_kv], w_query + [w_keyval])
     grad_rows = grad_resid + layer_norm_back(grad_hidden_one, normed_one, inverse_one, gain_one)
     grad_gain_one = jnp.sum(grad_hidden_one * normed_one, 0)
     grad_shift_one = jnp.sum(grad_hidden_one, 0)
@@ -740,7 +935,8 @@
     grad_w_keyval = cols_by_cols(after(grad_kv, part_out_sum), hidden_one)
     kv_rows = [lax.dynamic_slice_in_dim(grad_w_keyval, start, kv_half) for start in kv_starts]
     kv_parts = reduce_core(
-        jnp.concatenate(kv_rows[:tp_size], 0), jnp.concatenate(kv_rows[tp_size:], 0)
+        jnp.concatenate(kv_rows[:tp_size], 0),
+        swap_core(jnp.concatenate(kv_rows[tp_size:], 0).astype(bf16)),
     )
     query_got, kv_parts = lax.optimization_barrier((query_got, kv_parts))
     part_keyval = total_of(deliver(kv_parts))
@@ -785,25 +981,8 @@
     new_vectors, new_vec_one, new_vec_two = adam_step(
         vectors, vec_total, vec_one, vec_two, step_count, learning_rate
     )
-    steps_float = step_count[0].astype(f32)
-    scalars = jnp.stack(
-        [
-            learning_rate[0],
-            1.0 - jnp.power(beta_one, steps_float),
-            1.0 - jnp.power(beta_two, steps_float),
-        ]
-    )
-    state = ()
-    for start, grads in (
-        (row_starts[4], shard_down),
-        (row_starts[3], shard_up),
-        (0, shard_attention),
-    ):
-        block = grads.shape[0] // 2
-        if start == 0:
-            grads = after(grads, *state)
-        state = adam_rows(scalars, master, grads, moment_one, moment_two, start, block, state)
-    new_master, new_moment_one, new_moment_two = state
+    new_state = update_rows(shard_attention, 0, state)
+    new_master, new_moment_one, new_moment_two = new_state
     return (
         outputs,
         input_grads,

time: 764 us -> 681 us (0.89); the launches traced: 765 us -> 669 us
  starting transfers between devices: 126 us -> 55.5 us
  Pallas kernels: 184 us -> 238 us
  matrix products: 48.1 us -> 7.73 us
  local copies, waits for them, and re-layouts: 91.5 us -> 53.3 us
    ppermute x53 -> x60, starting transfers between devices: 123 us -> 53.9 us  [swap(): lax.ppermute(value, axis, [(source, source ^ step) for source in range(co...]
    pallas_call x0 -> x7, Pallas kernels: none -> 61 us  [the longest x2 20.3 us: onto_rows(): pl.pallas_call(onto_rows_kernel, name='onto_rows', grid=(len(pieces),), i...]
    dot_general x3 -> x1, matrix products: 16.9 us -> 0.62 us  [rows_by_rows(): lax.dot_general(left, right, (((1,), (1,)), ((), ())), preferred_element_...]
    dot_general x3 -> x0, matrix products: 14.8 us -> none  [plain_dot(): return jnp.dot(left, right, preferred_element_type=f32)]
    concatenate x7 -> x0, local copies, waits for them, and re-layouts: 13.2 us -> none  [the longest x2 6.94 us: widen_rows(): return jnp.concatenate(received + [other, crossed], 0)]
    unnamed x152 -> x151, local copies, waits for them, and re-layouts: 37.9 us -> 28.1 us
    dot_general x4 -> x3, matrix products: 16.4 us -> 7.11 us  [cols_by_cols(): lax.dot_general(left, right, (((0,), (0,)), ((), ())), preferred_element_...]
    pallas_call x2 -> x1, Pallas kernels: 28.3 us -> 22.2 us  [ffn_up(): pl.pallas_call(ffn_up_kernel, name='ffn_up', grid=(units // tile,), in_sp...]
  transfers between devices with their start and end apart: 63 -> 70, of which waited for: 27 -> 31; matrix products, arithmetic and copies ran while one was open for 22% -> 12% of each run, Pallas kernels for 24% -> 35%
where the time goes in v3:
time: 681 us; the launch traced here: 669 us
  waiting for transfers between devices  240 us (35%)
  Pallas kernels  238 us (35%)
  starting transfers between devices  55.5 us (8%)
  local copies, waits for them, and re-layouts  53.3 us (8%)
  other arithmetic  41 us (6%)
  between operations  17.2 us (3%)
  blocking collectives  16.6 us (2%)
  matrix products  7.73 us (1%)
    ppermute x60, waiting for transfers between devices, swap(): lax.ppermute(value, axis, [(source, source ^ step) for source in range(co...  234 us
    ppermute x60, starting transfers between devices, swap(): lax.ppermute(value, axis, [(source, source ^ step) for source in range(co...  53.9 us
    pallas_call x3, Pallas kernels, ffn_weight(): pl.pallas_call(functools.partial(ffn_weight_kernel, lefts=len(lefts)), na...  52.5 us
    pallas_call x2, Pallas kernels, ffn_product(): pl.pallas_call(functools.partial(ffn_product_kernel, lefts=len(lefts)), n...  37 us
    unnamed x151, local copies, waits for them, and re-layouts  28.1 us
    pallas_call x1, Pallas kernels, ffn_back(): pl.pallas_call(functools.partial(ffn_back_kernel, count=len(pieces)), nam...  24.9 us
    pallas_call x1, Pallas kernels, ffn_up(): pl.pallas_call(ffn_up_kernel, name='ffn_up', grid=(units // tile,), in_sp...  22.2 us
    pallas_call x2, Pallas kernels, onto_rows(): pl.pallas_call(onto_rows_kernel, name='onto_rows', grid=(len(pieces),), i...  20.3 us
  transfers between devices with their start and end apart: 70, of which 31 were waited for; matrix products, arithmetic and copies ran while one was open for 12% of the time, Pallas kernels for 35%

profile of v3, /device:TPU:0, one launch (start us, length us, event | category | flops | bytes accessed | tf_op | source)
XLA Modules:
  0.0 669.4 jit_solution(8974565515921173348)
XLA Ops:
  7.2 2.8 convert.28
  13.2 3.1 fusion.31
  16.9 16.6 %all_gather.16 = bf16[64,2048]{1,0:T(8,128)(2,1)S(1)} all-gather(bf16[64,256]{1,0:T(8,128)(2,1)S(1)} %slice-done), channel_id=1, replica_groups=mesh['dp'=8,'tp'=4] {'dp'}, dimensions={1}, use_global_device_ids=true | all-gather | bytes 294912 | tf_op jit(solution)/shard_map/all_gather | solution.py:762
  48.4 3.3 constant_dynamic-slice_fusion.8
  59.5 18.2 %collective-permute-done.refs_3_ = bf16[256,2048]{1,0:T(8,128)(2,1)S(1)} collective-permute-done((bf16[256,2048]{1,0:T(8,128)(2,1)S(1)}, bf16[256,2048]{1,0:T(8,128)(2,1)S(1)}, u32[]{:S(2)}, u32[]{:S(2)}) %collective-permute-start) | collective-permute-done | bytes 1048608 | tf_op jit(solution)/shard_map/ppermute | solution.py:84
  77.8 23.1 %collective-permute-done.1.refs_4_ = bf16[256,2048]{1,0:T(8,128)(2,1)S(1)} collective-permute-done((bf16[256,2048]{1,0:T(8,128)(2,1)S(1)}, bf16[256,2048]{1,0:T(8,128)(2,1)S(1)}, u32[]{:S(2)}, u32[]{:S(2)}) %collective-permute-start.1) | collective-permute-done | bytes 1048608 | tf_op jit(solution)/shard_map/ppermute | solution.py:84
  109.0 5.0 collective-permute-done.10.refs_1_
  114.0 4.8 collective-permute-done.11.refs_2_
  118.8 2.0 collective-permute-done.12.refs_3_
  122.8 2.8 constant_dynamic-slice_fusion.6
  131.1 7.0 %place_keys.1 = (bf16[3,2048,128]{2,1,0:T(8,128)(2,1)}, bf16[3,128,2048]{2,1,0:T(8,128)(2,1)}, bf16[3,2048,128]{2,1,0:T(8,128)(2,1)}, bf16[3,128,2048]{2,1,0:T(8,128)(2,1)}) custom-call(s32[8]{0:T(128)} %stack.45.starts, bf16[2,3,128,256]{3,2,1,0:T(8,128)(2,1)} %copy-done.44, bf16[2,3,128,256]{3,2,1,0:T(8,128)(2,1)} %copy-done.51, ...), custom_call_target="tpu_custom_call" | custom-call | flops 1048576 | bytes 1048576 | tf_op jit(solution)/shard_map/place_keys/pallas_call | solution.py:576
  138.2 10.1 %onto_rows.2 = bf16[384,2048]{1,0:T(8,128)(2,1)} custom-call(bf16[384,2048]{1,0:T(8,128)(2,1)} %copy-done.17, f32[1,2048]{1,0:T(1,128)} %bitcast.3.refs_1_, bf16[256,2048]{1,0:T(8,128)(2,1)} %copy-done.26, bf16[256,2048]{1,0:T(8,128)(2,1)} %copy-done.28, bf16[256,2048]{1,0:T(8,128)(2,1)} %copy-done.29, bf16[256,2048]{1,0:T(8,128)(2,1)} %collective-permute-done.2.refs_5_, ...), custom_call_target="tpu_custom_call" | custom-call | flops 1048576 | bytes 1048576 | tf_op jit(solution)/shard_map/onto_rows/pallas_call | solution.py:515
  149.8 9.1 %attend_forward.1 = (bf16[3,128,2048]{2,1,0:T(8,128)(2,1)S(1)}, f32[3,4,1,512]{3,2,1,0:T(1,128)S(1)}) custom-call(s32[3,2]{1,0:T(4,128)S(1)} %stack.36.bounds, bf16[3,128,2048]{2,1,0:T(8,128)(2,1)S(1)} %bitcast.107, bf16[3,2048,128]{2,1,0:T(8,128)(2,1)S(1)} %copy-done.6, bf16[3,128,2048]{2,1,0:T(8,128)(2,1)S(1)} %copy-done.10, ...), custom_call_target="tpu_custom_call" | custom-call | flops 1048576 | bytes 1048576 | tf_op jit(solution)/shard_map/attend_forward/pallas_call | solution.py:263
  160.1 14.6 %collective-permute-done.18.refs_3_.refs_4_ = bf16[256,2048]{1,0:T(8,128)(2,1)} collective-permute-done((bf16[256,2048]{1,0:T(8,128)(2,1)S(1)}, bf16[256,2048]{1,0:T(8,128)(2,1)}, u32[]{:S(2)}, u32[]{:S(2)}) %collective-permute-start.18) | collective-permute-done | bytes 1048608 | tf_op jit(solution)/shard_map/ppermute | solution.py:84
  175.2 3.6 collective-permute-done.20.refs_6_.refs_7_
  182.8 8.4 %onto_columns.2 = f32[384,2048]{1,0:T(8,128)} custom-call(bf16[384,2048]{1,0:T(8,128)(2,1)} %bitcast.110, bf16[256,2048]{1,0:T(8,128)(2,1)} %copy-done.27, bf16[256,2048]{1,0:T(8,128)(2,1)} %collective-permute-done.17.refs_2_.refs_3_, bf16[256,2048]{1,0:T(8,128)(2,1)} %collective-permute-done.18.refs_3_.refs_4_, ...), custom_call_target="tpu_custom_call" | custom-call | flops 1048576 | bytes 1048576 | tf_op jit(solution)/shard_map/onto_columns/pallas_call | solution.py:545
  191.2 2.6 fusion.27
  194.9 2.6 add_convert_fusion.2
  200.7 33.3 %collective-permute-done.23.refs_1_.refs_2_ = bf16[384,2048]{1,0:T(8,128)(2,1)S(1)} collective-permute-done((bf16[384,2048]{1,0:T(8,128)(2,1)S(1)}, bf16[384,2048]{1,0:T(8,128)(2,1)S(1)}, u32[]{:S(2)}, u32[]{:S(2)}) %collective-permute-start.23) | collective-permute-done | bytes 1572896 | tf_op jit(solution)/shard_map/ppermute | solution.py:84
  234.0 1.9 collective-permute-start.25
  237.6 15.7 %collective-permute-done.25.refs_3_.refs_4_ = bf16[192,2048]{1,0:T(8,128)(2,1)S(1)} collective-permute-done((bf16[192,2048]{1,0:T(8,128)(2,1)S(1)}, bf16[192,2048]{1,0:T(8,128)(2,1)S(1)}, u32[]{:S(2)}, u32[]{:S(2)}) %collective-permute-start.25) | collective-permute-done | bytes 786464 | tf_op jit(solution)/shard_map/ppermute | solution.py:84
  256.7 1.8 collective-permute-start.29
  259.1 22.2 %ffn_up.1 = (f32[1536,2048]{1,0:T(8,128)}, bf16[1536,2048]{1,0:T(8,128)(2,1)}) custom-call(bf16[384,2048]{1,0:T(8,128)(2,1)} %copy-done.22, bf16[384,2048]{1,0:T(8,128)(2,1)} %copy-done.24, bf16[384,2048]{1,0:T(8,128)(2,1)} %copy-done.25, bf16[192,2048]{1,0:T(8,128)(2,1)} %copy-done.38, bf16[192,2048]{1,0:T(8,128)(2,1)} %copy-done.39, ...), custom_call_target="tpu_custom_call" | custom-call | flops 1048576 | bytes 1048576 | tf_op jit(solution)/shard_map/ffn_up/pallas_call | solution.py:405
  281.3 18.4 %ffn_product.2 = (bf16[384,2048]{1,0:T(8,128)(2,1)}, bf16[384,2048]{1,0:T(8,128)(2,1)}, bf16[384,2048]{1,0:T(8,128)(2,1)}, bf16[384,2048]{1,0:T(8,128)(2,1)}) custom-call(bf16[1536,2048]{1,0:T(8,128)(2,1)} %get-tuple-element.109.refs_0_, bf16[2048,2048]{1,0:T(8,128)(2,1)} %all-gather.11.cloned.1.call-done.refs_1_.refs_4_), custom_call_target="tpu_custom_call" | custom-call | flops 1048576 | bytes 1048576 | tf_op jit(solution)/shard_map/ffn_product/pallas_call | solution.py:448
  303.2 20.7 %collective-permute-done.28.refs_3_.refs_2_ = bf16[384,2048]{1,0:T(8,128)(2,1)} collective-permute-done((bf16[384,2048]{1,0:T(8,128)(2,1)S(1)}, bf16[384,2048]{1,0:T(8,128)(2,1)}, u32[]{:S(2)}, u32[]{:S(2)}) %collective-permute-start.28) | collective-permute-done | bytes 1572896 | tf_op jit(solution)/shard_map/ppermute | solution.py:84
  323.9 2.6 collective-permute-done.29.refs_4_.refs_3_
  326.5 23.2 %ffn_weight.3 = bf16[2048,2048]{1,0:T(8,128)(2,1)} custom-call(bf16[1536,2048]{1,0:T(8,128)(2,1)} %get-tuple-element.109.refs_0_, bf16[384,2048]{1,0:T(8,128)(2,1)} %bitcast.113, bf16[384,2048]{1,0:T(8,128)(2,1)} %collective-permute-done.27.refs_2_.refs_1_, bf16[384,2048]{1,0:T(8,128)(2,1)} %collective-permute-done.28.refs_3_.refs_2_, ...), custom_call_target="tpu_custom_call" | custom-call | flops 1048576 | bytes 1048576 | tf_op jit(solution)/shard_map/ffn_weight/pallas_call | solution.py:464
  349.7 24.9 %ffn_back.1 = (bf16[1536,2048]{1,0:T(8,128)(2,1)}, f32[1,2048]{1,0:T(1,128)}) custom-call(bf16[384,2048]{1,0:T(8,128)(2,1)} %bitcast.114, bf16[384,2048]{1,0:T(8,128)(2,1)} %collective-permute-done.27.refs_2_.refs_1_, bf16[384,2048]{1,0:T(8,128)(2,1)} %collective-permute-done.28.refs_3_.refs_2_, bf16[384,2048]{1,0:T(8,128)(2,1)} %collective-permute-done.29.refs_4_.refs_3_, ...), custom_call_target="tpu_custom_call" | custom-call | flops 1048576 | bytes 1048576 | tf_op jit(solution)/shard_map/ffn_back/pallas_call | solution.py:429
  374.6 18.5 %ffn_product.3 = (bf16[384,2048]{1,0:T(8,128)(2,1)}, bf16[192,2048]{1,0:T(8,128)(2,1)}, bf16[192,2048]{1,0:T(8,128)(2,1)}, bf16[192,2048]{1,0:T(8,128)(2,1)}, bf...) custom-call(bf16[1536,2048]{1,0:T(8,128)(2,1)} %get-tuple-element.131.refs_0_, ...), custom_call_target="tpu_custom_call" | custom-call | flops 1048576 | bytes 1048576 | tf_op jit(solution)/shard_map/ffn_product/pallas_call | solution.py:448
  398.4 16.6 %collective-permute-done.33 = bf16[192,2048]{1,0:T(8,128)(2,1)S(1)} collective-permute-done((bf16[192,2048]{1,0:T(8,128)(2,1)}, bf16[192,2048]{1,0:T(8,128)(2,1)S(1)}, u32[]{:S(2)}, u32[]{:S(2)}) %collective-permute-start.33) | collective-permute-done | bytes 786464 | tf_op jit(solution)/shard_map/ppermute | solution.py:84
  416.4 1.8 collective-permute-start.32
  418.2 23.0 %ffn_weight.4 = bf16[2048,2048]{1,0:T(8,128)(2,1)} custom-call(bf16[1536,2048]{1,0:T(8,128)(2,1)} %get-tuple-element.131.refs_0_, bf16[384,2048]{1,0:T(8,128)(2,1)} %copy-done.22, bf16[384,2048]{1,0:T(8,128)(2,1)} %copy-done.24, bf16[384,2048]{1,0:T(8,128)(2,1)} %copy-done.25, bf16[192,2048]{1,0:T(8,128)(2,1)} %copy-done.38, bf16[192,2048]{1,0:T(8,128)(2,1)} %copy-done.39), custom_call_target="tpu_custom_call" | custom-call | flops 1048576 | bytes 1048576 | tf_op jit(solution)/shard_map/ffn_weight/pallas_call | solution.py:464
  441.2 4.7 collective-permute-done.34.refs_7_
  447.6 8.3 %norm_back.1 = (f32[384,2048]{1,0:T(8,128)}, bf16[384,2048]{1,0:T(8,128)(2,1)}, f32[8,2048]{1,0:T(8,128)}) custom-call(bf16[384,2048]{1,0:T(8,128)(2,1)} %get-tuple-element.132.refs_0_, bf16[384,2048]{1,0:T(8,128)(2,1)} %bitcast.115, f32[384,2048]{1,0:T(8,128)} %get-tuple-element.198.refs_2_, f32[384,1]{1,0:T(8,128)} %rsqrt.20.refs_3_, f32[1,2048]{1,0:T(1,128)} %bitcast.131, ...), custom_call_target="tpu_custom_call" | custom-call | flops 1048576 | bytes 1048576 | tf_op jit(solution)/shard_map/norm_back/pallas_call | solution.py:623
  455.9 3.9 convolution_convert_fusion
  459.9 7.1 %collective-permute-done.36 = bf16[1024,2048]{1,0:T(8,128)(2,1)S(1)} collective-permute-done((bf16[1024,2048]{1,0:T(8,128)(2,1)S(1)}, bf16[1024,2048]{1,0:T(8,128)(2,1)S(1)}, u32[]{:S(2)}, u32[]{:S(2)}) %collective-permute-start.36) | collective-permute-done | bytes 4194336 | tf_op jit(solution)/shard_map/ppermute | solution.py:84
  467.0 2.5 add_convert_fusion
  469.5 2.1 fusion.30
  472.0 1.9 collective-permute-start.41
  475.7 10.2 %onto_rows.3 = bf16[384,2048]{1,0:T(8,128)(2,1)} custom-call(bf16[384,2048]{1,0:T(8,128)(2,1)} %get-tuple-element.134.refs_0_, f32[1,2048]{1,0:T(1,128)} %reshape.214.refs_1_, bf16[256,2048]{1,0:T(8,128)(2,1)} %copy-done.27, bf16[256,2048]{1,0:T(8,128)(2,1)} %collective-permute-done.17.refs_2_.refs_3_, ...), custom_call_target="tpu_custom_call" | custom-call | flops 1048576 | bytes 1048576 | tf_op jit(solution)/shard_map/onto_rows/pallas_call | solution.py:515
  488.7 14.6 %attend_backward.1 = (bf16[3,128,2048]{2,1,0:T(8,128)(2,1)S(1)}, f32[3,2048,128]{2,1,0:T(8,128)S(1)}, f32[3,2048,128]{2,1,0:T(8,128)}) custom-call(s32[3,2]{1,0:T(4,128)S(1)} %stack.36.bounds, bf16[3,128,2048]{2,1,0:T(8,128)(2,1)S(1)} %bitcast.108, bf16[3,128,2048]{2,1,0:T(8,128)(2,1)S(1)} %bitcast.109, bf16[3,2048,128]{2,1,0:T(8,128)(2,1)S(1)} %copy-done.7, ...), custom_call_target="tpu_custom_call" | custom-call | flops 1048576 | bytes 1048576 | tf_op jit(solution)/shard_map/attend_backward/pallas_call | solution.py:298
  504.4 14.7 %collective-permute-done.41 = bf16[256,2048]{1,0:T(8,128)(2,1)} collective-permute-done((bf16[256,2048]{1,0:T(8,128)(2,1)}, bf16[256,2048]{1,0:T(8,128)(2,1)}, u32[]{:S(2)}, u32[]{:S(2)}) %collective-permute-start.41) | collective-permute-done | bytes 1048608 | tf_op jit(solution)/shard_map/ppermute | solution.py:84
  520.0 6.3 ffn_weight.5
  526.4 2.6 pad_maximum_fusion
  529.0 2.7 copy-done.21
  536.5 2.7 bitcast_add_fusion
  540.7 4.6 collective-permute-start.46
  547.0 8.0 %weight_pieces.1 = (bf16[256,2048]{1,0:T(8,128)(2,1)}, bf16[256,2048]{1,0:T(8,128)(2,1)}, bf16[256,2048]{1,0:T(8,128)(2,1)}, bf16[256,2048]{1,0:T(8,128)(2,1)}) custom-call(bf16[384,2048]{1,0:T(8,128)(2,1)} %bitcast.104, bf16[384,2048]{1,0:T(8,128)(2,1)} %copy-done.17, bf16[1024,2048]{1,0:T(8,128)(2,1)} %collective-permute-done.43.add_ref), custom_call_target="tpu_custom_call" | custom-call | flops 1048576 | bytes 1048576 | tf_op jit(solution)/shard_map/weight_pieces/pallas_call | solution.py:489
  556.4 2.0 collective-permute-start.50
  558.4 4.7 collective-permute-done.46
  564.8 3.5 add_convert_fusion.4
  568.3 4.5 reduce-scatter.5.cloned.1.call-done.grads
  573.7 6.4 adam_rows.3
  580.1 6.2 adam_rows.4
  587.0 9.0 %onto_columns.3 = f32[384,2048]{1,0:T(8,128)} custom-call(bf16[384,2048]{1,0:T(8,128)(2,1)} %bitcast.105, bf16[384,256]{1,0:T(8,128)(2,1)} %bitcast.123, bf16[256,2048]{1,0:T(8,128)(2,1)} %copy-done.26, bf16[256,2048]{1,0:T(8,128)(2,1)} %copy-done.28, bf16[256,2048]{1,0:T(8,128)(2,1)} %copy-done.29, bf16[256,2048]{1,0:T(8,128)(2,1)} %collective-permute-done.2.refs_5_, ...), custom_call_target="tpu_custom_call" | custom-call | flops 1048576 | bytes 1048576 | tf_op jit(solution)/shard_map/onto_columns/pallas_call | solution.py:545
  596.1 4.0 fusion.14
  603.1 4.4 collective-permute-done.50
  611.8 2.2 add_convert_fusion.3
  614.1 3.2 collective-permute-done.54
  621.3 8.6 %collective-permute-done.58 = f32[177,128]{1,0:T(8,128)S(1)} collective-permute-done((f32[177,128]{1,0:T(8,128)}, f32[177,128]{1,0:T(8,128)S(1)}, u32[]{:S(2)}, u32[]{:S(2)}) %collective-permute-start.58) | collective-permute-done | bytes 90656 | tf_op jit(solution)/shard_map/ppermute | solution.py:84
  630.7 12.1 %collective-permute-done.59 = f32[177,128]{1,0:T(8,128)S(1)} collective-permute-done((f32[177,128]{1,0:T(8,128)S(1)}, f32[177,128]{1,0:T(8,128)S(1)}, u32[]{:S(2)}, u32[]{:S(2)}) %collective-permute-start.59) | collective-permute-done | bytes 90656 | tf_op jit(solution)/shard_map/ppermute | solution.py:84
  642.9 7.4 %fusion.13 = (bf16[384,2048]{1,0:T(8,128)(2,1)}, bf16[384,2048]{1,0:T(8,128)(2,1)}) fusion(f32[384,2048]{1,0:T(8,128)} %get-tuple-element.143, bf16[3,128,2048]{2,1,0:T(8,128)(2,1)S(1)} %copy-done.15, f32[384,2048]{1,0:T(8,128)} %onto_columns.3, f32[384]{0:T(512)S(1)} %get-tuple-element.242, f32[384]{0:T(512)S(1)} %get-tuple-element.243, ...), kind=kLoop, calls=%fused_computation.22 | loop fusion | flops 17301504 | bytes 20477952 | tf_op jit(solution)/shard_map/convert_element_type | solution.py:933
  652.3 2.8 collective-permute-done.61
  657.8 4.3 adam_rows.5
  (352 shorter events, 105.5 us)
Async XLA Ops:
  7.2 41.2 %all-gather.5.cloned.1.call-start = ((), (), s32[]{:S(2)}) async-start(), calls=%async_computation.4 | async-start | bytes 2359296 | tf_op jit(solution)/shard_map/all_gather | solution.py:762
  12.3 110.5 %all-gather.7.cloned.1.call-start = ((), (), s32[]{:S(2)}) async-start(), calls=%async_computation.5 | async-start | bytes 2359296 | tf_op jit(solution)/shard_map/all_gather | solution.py:762
  13.1 245.9 %all-gather.9.cloned.1.call-start = ((), (), s32[]{:S(2)}) async-start(), calls=%async_computation.6 | async-start | bytes 9437184 | tf_op jit(solution)/shard_map/all_gather | solution.py:762
  16.3 265.0 %all-gather.11.cloned.1.call-start = ((), (), s32[]{:S(2)}) async-start(), calls=%async_computation.7 | async-start | bytes 9437184 | tf_op jit(solution)/shard_map/all_gather | solution.py:762
  16.9 551.4 %reduce-scatter.7.cloned.1.call-start = ((), (), s32[]{:S(2)}) async-start(), calls=%async_computation.9 | async-start | bytes 9437184 | tf_op jit(solution)/shard_map/reduce_scatter | solution.py:830
  33.6 19.6 %collective-permute-start.6 = (bf16[64,2048]{1,0:T(8,128)(2,1)S(1)}, bf16[64,2048]{1,0:T(8,128)(2,1)}, u32[]{:S(2)}, u32[]{:S(2)}) collective-permute-start(bf16[64,2048]{1,0:T(8,128)(2,1)S(1)} %all_gather.16), channel_id=1, source_target_pairs={{0,1},{1,0},{2,3},{3,2},{4,5},{5,4},{6,7},{7,6},{8,9},{9,8},{10,11... | collective-permute-start | bytes 786440 | tf_op jit(solution)/shard_map/ppermute | solution.py:84
  35.1 21.1 %collective-permute-start.7 = (bf16[64,2048]{1,0:T(8,128)(2,1)S(1)}, bf16[64,2048]{1,0:T(8,128)(2,1)}, u32[]{:S(2)}, u32[]{:S(2)}) collective-permute-start(bf16[64,2048]{1,0:T(8,128)(2,1)S(1)} %all_gather.16), channel_id=1, source_target_pairs={{0,2},{1,3},{2,0},{3,1},{4,6},{5,7},{6,4},{7,5},{8,10},{9,11},{10,... | collective-permute-start | bytes 786440 | tf_op jit(solution)/shard_map/ppermute | solution.py:84
  36.6 20.6 %collective-permute-start.8 = (bf16[64,2048]{1,0:T(8,128)(2,1)S(1)}, bf16[64,2048]{1,0:T(8,128)(2,1)}, u32[]{:S(2)}, u32[]{:S(2)}) collective-permute-start(bf16[64,2048]{1,0:T(8,128)(2,1)S(1)} %all_gather.16), channel_id=1, source_target_pairs={{0,3},{1,2},{2,1},{3,0},{4,7},{5,6},{6,5},{7,4},{8,11},{9,10},{10,... | collective-permute-start | bytes 786440 | tf_op jit(solution)/shard_map/ppermute | solution.py:84
  51.7 26.1 %collective-permute-start = (bf16[256,2048]{1,0:T(8,128)(2,1)S(1)}, bf16[256,2048]{1,0:T(8,128)(2,1)S(1)}, u32[]{:S(2)}, u32[]{:S(2)}) collective-permute-start(bf16[256,2048]{1,0:T(8,128)(2,1)S(1)} %get-tuple-element.221.refs_2_), channel_id=1, source_target_pairs={{0,1},{1,0},{2,3},{3,2},{4,5},{5,4},{6,7},{7,6},{8,9},{9,8},{10,11... | collective-permute-start | bytes 3145736 | tf_op jit(solution)/shard_map/ppermute | solution.py:84
  54.1 46.8 %collective-permute-start.1 = (bf16[256,2048]{1,0:T(8,128)(2,1)S(1)}, bf16[256,2048]{1,0:T(8,128)(2,1)S(1)}, u32[]{:S(2)}, u32[]{:S(2)}) collective-permute-start(bf16[256,2048]{1,0:T(8,128)(2,1)S(1)} %get-tuple-element.221.refs_2_), channel_id=1, source_target_pairs={{0,2},{1,3},{2,0},{3,1},{4,6},{5,7},{6,4},{7,5},{8,10},{9,11},{10,... | collective-permute-start | bytes 3145736 | tf_op jit(solution)/shard_map/ppermute | solution.py:84
  55.7 45.2 %collective-permute-start.2 = (bf16[256,2048]{1,0:T(8,128)(2,1)S(1)}, bf16[256,2048]{1,0:T(8,128)(2,1)}, u32[]{:S(2)}, u32[]{:S(2)}) collective-permute-start(bf16[256,2048]{1,0:T(8,128)(2,1)S(1)} %get-tuple-element.221.refs_2_), channel_id=1, source_target_pairs={{0,3},{1,2},{2,1},{3,0},{4,7},{5,6},{6,5},{7,4},{8,11},{9,10},{10,... | collective-permute-start | bytes 3145736 | tf_op jit(solution)/shard_map/ppermute | solution.py:84
  58.8 18.9 %collective-permute-start.9 = (bf16[1,3,128,256]{3,2,1,0:T(8,128)(2,1)S(1)}, bf16[1,3,128,256]{3,2,1,0:T(8,128)(2,1)S(1)}, u32[]{:S(2)}, u32[]{:S(2)}) collective-permute-start(bf16[1,3,128,256]{3,2,1,0:T(8,128)(2,1)S(1)} %bitcast.129), channel_id=1, source_target_pairs={{8,16},{12,20},{9,17},{13,21},{10,18},{14,22},{11,19},{15,23}} | collective-permute-start | bytes 589832 | tf_op jit(solution)/shard_map/ppermute | solution.py:790
  77.8 51.2 %collective-permute-start.3 = (bf16[256,2048]{1,0:T(8,128)(2,1)S(1)}, bf16[256,2048]{1,0:T(8,128)(2,1)}, u32[]{:S(2)}, u32[]{:S(2)}) collective-permute-start(bf16[256,2048]{1,0:T(8,128)(2,1)S(1)} %collective-permute-done.refs_3_), channel_id=1, source_target_pairs={{0,4},{4,0},{8,12},{12,8},{16,20},{20,16},{24,28},{28,24},{1,5},{5... | collective-permute-start | bytes 3145736 | tf_op jit(solution)/shard_map/ppermute | solution.py:84
  101.9 12.1 %collective-permute-start.10 = (bf16[2,3,128,256]{3,2,1,0:T(8,128)(2,1)S(1)}, bf16[2,3,128,256]{3,2,1,0:T(8,128)(2,1)S(1)}, u32[]{:S(2)}, u32[]{:S(2)}) collective-permute-start(bf16[2,3,128,256]{3,2,1,0:T(8,128)(2,1)S(1)} %pad_maximum_fusion.3.refs_0_), channel_id=1, source_target_pairs={{0,1},{1,0},{2,3},{3,2},{4,5},{5,4},{6,7},{7,6},{8,9},{9,8},{10,11... | collective-permute-start | bytes 1179656 | tf_op jit(solution)/shard_map/ppermute | solution.py:84
  102.6 16.2 %collective-permute-start.11 = (bf16[2,3,128,256]{3,2,1,0:T(8,128)(2,1)S(1)}, bf16[2,3,128,256]{3,2,1,0:T(8,128)(2,1)S(1)}, u32[]{:S(2)}, u32[]{:S(2)}) collective-permute-start(bf16[2,3,128,256]{3,2,1,0:T(8,128)(2,1)S(1)} %pad_maximum_fusion.3.refs_0_), channel_id=1, source_target_pairs={{0,2},{1,3},{2,0},{3,1},{4,6},{5,7},{6,4},{7,5},{8,10},{9,11},{10,... | collective-permute-start | bytes 1179656 | tf_op jit(solution)/shard_map/ppermute | solution.py:84
  104.1 16.7 %collective-permute-start.12 = (bf16[2,3,128,256]{3,2,1,0:T(8,128)(2,1)S(1)}, bf16[2,3,128,256]{3,2,1,0:T(8,128)(2,1)}, u32[]{:S(2)}, u32[]{:S(2)}) collective-permute-start(bf16[2,3,128,256]{3,2,1,0:T(8,128)(2,1)S(1)} %pad_maximum_fusion.3.refs_0_), channel_id=1, source_target_pairs={{0,3},{1,2},{2,1},{3,0},{4,7},{5,6},{6,5},{7,4},{8,11},{9,10},{10,... | collective-permute-start | bytes 1179656 | tf_op jit(solution)/shard_map/ppermute | solution.py:84
  108.9 16.8 %collective-permute-start.13 = (bf16[2,3,128,256]{3,2,1,0:T(8,128)(2,1)S(1)}, bf16[2,3,128,256]{3,2,1,0:T(8,128)(2,1)}, u32[]{:S(2)}, u32[]{:S(2)}) collective-permute-start(bf16[2,3,128,256]{3,2,1,0:T(8,128)(2,1)S(1)} %pad_maximum_fusion.3.refs_0_), channel_id=1, source_target_pairs={{0,4},{4,0},{8,12},{12,8},{16,20},{20,16},{24,28},{28,24},{1,5},{5... | collective-permute-start | bytes 1179656 | tf_op jit(solution)/shard_map/ppermute | solution.py:84
  114.0 12.2 %collective-permute-start.14 = (bf16[2,3,128,256]{3,2,1,0:T(8,128)(2,1)S(1)}, bf16[2,3,128,256]{3,2,1,0:T(8,128)(2,1)}, u32[]{:S(2)}, u32[]{:S(2)}) collective-permute-start(bf16[2,3,128,256]{3,2,1,0:T(8,128)(2,1)S(1)} %collective-permute-done.10.refs_1_), channel_id=1, source_target_pairs={{0,4},{4,0},{8,12},{12,8},{16,20},{20,16},{24,28},{28,24},{1,5},{5... | collective-permute-start | bytes 1179656 | tf_op jit(solution)/shard_map/ppermute | solution.py:84
  118.8 7.5 %collective-permute-start.15 = (bf16[2,3,128,256]{3,2,1,0:T(8,128)(2,1)S(1)}, bf16[2,3,128,256]{3,2,1,0:T(8,128)(2,1)}, u32[]{:S(2)}, u32[]{:S(2)}) collective-permute-start(bf16[2,3,128,256]{3,2,1,0:T(8,128)(2,1)S(1)} %collective-permute-done.11.refs_2_), channel_id=1, source_target_pairs={{0,4},{4,0},{8,12},{12,8},{16,20},{20,16},{24,28},{28,24},{1,5},{5... | collective-permute-start | bytes 1179656 | tf_op jit(solution)/shard_map/ppermute | solution.py:84
  120.8 6.4 collective-permute-start.16
  125.7 12.5 %collective-permute-start.4 = (bf16[256,2048]{1,0:T(8,128)(2,1)S(1)}, bf16[256,2048]{1,0:T(8,128)(2,1)}, u32[]{:S(2)}, u32[]{:S(2)}) collective-permute-start(bf16[256,2048]{1,0:T(8,128)(2,1)S(1)} %copy-done.30), channel_id=1, source_target_pairs={{0,4},{4,0},{8,12},{12,8},{16,20},{20,16},{24,28},{28,24},{1,5},{5... | collective-permute-start | bytes 3145736 | tf_op jit(solution)/shard_map/ppermute | solution.py:84
  126.2 12.0 %collective-permute-start.5 = (bf16[256,2048]{1,0:T(8,128)(2,1)}, bf16[256,2048]{1,0:T(8,128)(2,1)}, u32[]{:S(2)}, u32[]{:S(2)}) collective-permute-start(bf16[256,2048]{1,0:T(8,128)(2,1)} %collective-permute-done.2.refs_5_), channel_id=1, source_target_pairs={{0,4},{4,0},{8,12},{12,8},{16,20},{20,16},{24,28},{28,24},{1,5},{5... | collective-permute-start | bytes 3145736 | tf_op jit(solution)/shard_map/ppermute | solution.py:84
  126.3 33.7 %collective-permute-start.17 = (bf16[256,2048]{1,0:T(8,128)(2,1)S(1)}, bf16[256,2048]{1,0:T(8,128)(2,1)}, u32[]{:S(2)}, u32[]{:S(2)}) collective-permute-start(bf16[256,2048]{1,0:T(8,128)(2,1)S(1)} %get-tuple-element.104.refs_1_.refs_2_), channel_id=1, source_target_pairs={{0,1},{1,0},{2,3},{3,2},{4,5},{5,4},{6,7},{7,6},{8,9},{9,8},{10,11... | collective-permute-start | bytes 3145736 | tf_op jit(solution)/shard_map/ppermute | solution.py:84
  127.2 47.5 %collective-permute-start.18 = (bf16[256,2048]{1,0:T(8,128)(2,1)S(1)}, bf16[256,2048]{1,0:T(8,128)(2,1)}, u32[]{:S(2)}, u32[]{:S(2)}) collective-permute-start(bf16[256,2048]{1,0:T(8,128)(2,1)S(1)} %get-tuple-element.104.refs_1_.refs_2_), channel_id=1, source_target_pairs={{0,2},{1,3},{2,0},{3,1},{4,6},{5,7},{6,4},{7,5},{8,10},{9,11},{10,... | collective-permute-start | bytes 3145736 | tf_op jit(solution)/shard_map/ppermute | solution.py:84
  129.0 45.7 %collective-permute-start.19 = (bf16[256,2048]{1,0:T(8,128)(2,1)S(1)}, bf16[256,2048]{1,0:T(8,128)(2,1)}, u32[]{:S(2)}, u32[]{:S(2)}) collective-permute-start(bf16[256,2048]{1,0:T(8,128)(2,1)S(1)} %get-tuple-element.104.refs_1_.refs_2_), channel_id=1, source_target_pairs={{0,3},{1,2},{2,1},{3,0},{4,7},{5,6},{6,5},{7,4},{8,11},{9,10},{10,... | collective-permute-start | bytes 3145736 | tf_op jit(solution)/shard_map/ppermute | solution.py:84
  174.7 5.7 collective-permute-start.21
  175.2 6.6 collective-permute-start.22
  197.5 36.5 %collective-permute-start.23 = (bf16[384,2048]{1,0:T(8,128)(2,1)S(1)}, bf16[384,2048]{1,0:T(8,128)(2,1)S(1)}, u32[]{:S(2)}, u32[]{:S(2)}) collective-permute-start(bf16[384,2048]{1,0:T(8,128)(2,1)S(1)} %get-tuple-element.197.refs_0_.refs_1_), channel_id=1, source_target_pairs={{0,1},{1,0},{2,3},{3,2},{4,5},{5,4},{6,7},{7,6},{8,9},{9,8},{10,11... | collective-permute-start | bytes 4718600 | tf_op jit(solution)/shard_map/ppermute | solution.py:84
  199.2 36.8 %collective-permute-start.24 = (bf16[384,2048]{1,0:T(8,128)(2,1)S(1)}, bf16[384,2048]{1,0:T(8,128)(2,1)S(1)}, u32[]{:S(2)}, u32[]{:S(2)}) collective-permute-start(bf16[384,2048]{1,0:T(8,128)(2,1)S(1)} %get-tuple-element.197.refs_0_.refs_1_), channel_id=1, source_target_pairs={{0,2},{1,3},{2,0},{3,1},{4,6},{5,7},{6,4},{7,5},{8,10},{9,11},{10,... | collective-permute-start | bytes 4718600 | tf_op jit(solution)/shard_map/ppermute | solution.py:84
  234.0 19.2 %collective-permute-start.25 = (bf16[192,2048]{1,0:T(8,128)(2,1)S(1)}, bf16[192,2048]{1,0:T(8,128)(2,1)S(1)}, u32[]{:S(2)}, u32[]{:S(2)}) collective-permute-start(bf16[192,2048]{1,0:T(8,128)(2,1)S(1)} %slice.197), channel_id=1, source_target_pairs={{0,2},{1,3},{2,0},{3,1},{4,6},{5,7},{6,4},{7,5},{8,10},{9,11},{10,... | collective-permute-start | bytes 2359304 | tf_op jit(solution)/shard_map/ppermute | solution.py:84
  236.0 18.8 %collective-permute-start.26 = (bf16[192,2048]{1,0:T(8,128)(2,1)S(1)}, bf16[192,2048]{1,0:T(8,128)(2,1)S(1)}, u32[]{:S(2)}, u32[]{:S(2)}) collective-permute-start(bf16[192,2048]{1,0:T(8,128)(2,1)S(1)} %slice.198), channel_id=1, source_target_pairs={{0,1},{1,0},{2,3},{3,2},{4,5},{5,4},{6,7},{7,6},{8,9},{9,8},{10,11... | collective-permute-start | bytes 2359304 | tf_op jit(solution)/shard_map/ppermute | solution.py:84
  254.9 46.6 %collective-permute-start.27 = (bf16[384,2048]{1,0:T(8,128)(2,1)S(1)}, bf16[384,2048]{1,0:T(8,128)(2,1)}, u32[]{:S(2)}, u32[]{:S(2)}) collective-permute-start(bf16[384,2048]{1,0:T(8,128)(2,1)S(1)} %bitcast.116), channel_id=1, source_target_pairs={{0,1},{1,0},{2,3},{3,2},{4,5},{5,4},{6,7},{7,6},{8,9},{9,8},{10,11... | collective-permute-start | bytes 4718600 | tf_op jit(solution)/shard_map/ppermute | solution.py:84
  256.4 67.6 %collective-permute-start.28 = (bf16[384,2048]{1,0:T(8,128)(2,1)S(1)}, bf16[384,2048]{1,0:T(8,128)(2,1)}, u32[]{:S(2)}, u32[]{:S(2)}) collective-permute-start(bf16[384,2048]{1,0:T(8,128)(2,1)S(1)} %bitcast.117), channel_id=1, source_target_pairs={{0,2},{1,3},{2,0},{3,1},{4,6},{5,7},{6,4},{7,5},{8,10},{9,11},{10,... | collective-permute-start | bytes 4718600 | tf_op jit(solution)/shard_map/ppermute | solution.py:84
  256.7 69.8 %collective-permute-start.29 = (bf16[384,2048]{1,0:T(8,128)(2,1)S(1)}, bf16[384,2048]{1,0:T(8,128)(2,1)}, u32[]{:S(2)}, u32[]{:S(2)}) collective-permute-start(bf16[384,2048]{1,0:T(8,128)(2,1)S(1)} %bitcast.118), channel_id=1, source_target_pairs={{0,3},{1,2},{2,1},{3,0},{4,7},{5,6},{6,5},{7,4},{8,11},{9,10},{10,... | collective-permute-start | bytes 4718600 | tf_op jit(solution)/shard_map/ppermute | solution.py:84
  299.7 93.4 %collective-permute-start.37 = (bf16[384,2048]{1,0:T(8,128)(2,1)}, bf16[384,2048]{1,0:T(8,128)(2,1)S(1)}, u32[]{:S(2)}, u32[]{:S(2)}) collective-permute-start(bf16[384,2048]{1,0:T(8,128)(2,1)} %get-tuple-element.111), channel_id=1, source_target_pairs={{0,1},{1,0},{2,3},{3,2},{4,5},{5,4},{6,7},{7,6},{8,9},{9,8},{10,11... | collective-permute-start | bytes 4718600 | tf_op jit(solution)/shard_map/ppermute | solution.py:84
  301.2 92.0 %collective-permute-start.38 = (bf16[384,2048]{1,0:T(8,128)(2,1)}, bf16[384,2048]{1,0:T(8,128)(2,1)}, u32[]{:S(2)}, u32[]{:S(2)}) collective-permute-start(bf16[384,2048]{1,0:T(8,128)(2,1)} %get-tuple-element.112), channel_id=1, source_target_pairs={{0,2},{1,3},{2,0},{3,1},{4,6},{5,7},{6,4},{7,5},{8,10},{9,11},{10,... | collective-permute-start | bytes 4718600 | tf_op jit(solution)/shard_map/ppermute | solution.py:84
  301.5 91.7 %collective-permute-start.39 = (bf16[384,2048]{1,0:T(8,128)(2,1)}, bf16[384,2048]{1,0:T(8,128)(2,1)}, u32[]{:S(2)}, u32[]{:S(2)}) collective-permute-start(bf16[384,2048]{1,0:T(8,128)(2,1)} %get-tuple-element.113), channel_id=1, source_target_pairs={{0,3},{1,2},{2,1},{3,0},{4,7},{5,6},{6,5},{7,4},{8,11},{9,10},{10,... | collective-permute-start | bytes 4718600 | tf_op jit(solution)/shard_map/ppermute | solution.py:84
  394.3 178.5 %reduce-scatter.5.cloned.1.call-start = ((), (), s32[]{:S(2)}) async-start(), calls=%async_computation.8 | async-start | bytes 9437184 | tf_op jit(solution)/shard_map/reduce_scatter | solution.py:830
  394.3 20.7 %collective-permute-start.33 = (bf16[192,2048]{1,0:T(8,128)(2,1)}, bf16[192,2048]{1,0:T(8,128)(2,1)S(1)}, u32[]{:S(2)}, u32[]{:S(2)}) collective-permute-start(bf16[192,2048]{1,0:T(8,128)(2,1)} %get-tuple-element.130), channel_id=1, source_target_pairs={{0,2},{1,3},{2,0},{3,1},{4,6},{5,7},{6,4},{7,5},{8,10},{9,11},{10,... | collective-permute-start | bytes 2359304 | tf_op jit(solution)/shard_map/ppermute | solution.py:84
  395.4 20.8 %collective-permute-start.31 = (bf16[192,2048]{1,0:T(8,128)(2,1)}, bf16[192,2048]{1,0:T(8,128)(2,1)S(1)}, u32[]{:S(2)}, u32[]{:S(2)}) collective-permute-start(bf16[192,2048]{1,0:T(8,128)(2,1)} %get-tuple-element.129), channel_id=1, source_target_pairs={{0,1},{1,0},{2,3},{3,2},{4,5},{5,4},{6,7},{7,6},{8,9},{9,8},{10,11... | collective-permute-start | bytes 2359304 | tf_op jit(solution)/shard_map/ppermute | solution.py:84
  396.8 44.4 %collective-permute-start.30 = (bf16[192,2048]{1,0:T(8,128)(2,1)}, bf16[192,2048]{1,0:T(8,128)(2,1)S(1)}, u32[]{:S(2)}, u32[]{:S(2)}) collective-permute-start(bf16[192,2048]{1,0:T(8,128)(2,1)} %get-tuple-element.125), channel_id=1, source_target_pairs={{0,1},{1,0},{2,3},{3,2},{4,5},{5,4},{6,7},{7,6},{8,9},{9,8},{10,11... | collective-permute-start | bytes 2359304 | tf_op jit(solution)/shard_map/ppermute | solution.py:84
  397.4 43.8 %collective-permute-start.35 = (bf16[192,2048]{1,0:T(8,128)(2,1)}, bf16[192,2048]{1,0:T(8,128)(2,1)}, u32[]{:S(2)}, u32[]{:S(2)}) collective-permute-start(bf16[192,2048]{1,0:T(8,128)(2,1)} %get-tuple-element.128), channel_id=1, source_target_pairs={{0,2},{1,3},{2,0},{3,1},{4,6},{5,7},{6,4},{7,5},{8,10},{9,11},{10,... | collective-permute-start | bytes 2359304 | tf_op jit(solution)/shard_map/ppermute | solution.py:84
  415.3 30.6 %collective-permute-start.34 = (bf16[192,2048]{1,0:T(8,128)(2,1)S(1)}, bf16[192,2048]{1,0:T(8,128)(2,1)}, u32[]{:S(2)}, u32[]{:S(2)}) collective-permute-start(bf16[192,2048]{1,0:T(8,128)(2,1)S(1)} %add_convert_fusion.5), channel_id=1, source_target_pairs={{0,1},{1,0},{2,3},{3,2},{4,5},{5,4},{6,7},{7,6},{8,9},{9,8},{10,11... | collective-permute-start | bytes 2359304 | tf_op jit(solution)/shard_map/ppermute | solution.py:84
  416.4 29.5 %collective-permute-start.32 = (bf16[192,2048]{1,0:T(8,128)(2,1)S(1)}, bf16[192,2048]{1,0:T(8,128)(2,1)S(1)}, u32[]{:S(2)}, u32[]{:S(2)}) collective-permute-start(bf16[192,2048]{1,0:T(8,128)(2,1)S(1)} %add_convert_fusion.6), channel_id=1, source_target_pairs={{0,2},{1,3},{2,0},{3,1},{4,6},{5,7},{6,4},{7,5},{8,10},{9,11},{10,... | collective-permute-start | bytes 2359304 | tf_op jit(solution)/shard_map/ppermute | solution.py:84
  446.8 171.7 %reduce-scatter.9.cloned.1.call-start = ((), (), s32[]{:S(2)}) async-start(), calls=%async_computation.10 | async-start | bytes 1310720 | tf_op jit(solution)/shard_map/reduce_scatter | solution.py:886
  459.8 7.2 %collective-permute-start.36 = (bf16[1024,2048]{1,0:T(8,128)(2,1)S(1)}, bf16[1024,2048]{1,0:T(8,128)(2,1)S(1)}, u32[]{:S(2)}, u32[]{:S(2)}) collective-permute-start(bf16[1024,2048]{1,0:T(8,128)(2,1)S(1)} %convolution_convert_fusion), channel_id=1, source_target_pairs={{0,4},{4,0},{8,12},{12,8},{16,20},{20,16},{24,28},{28,24},{1,5},{5... | collective-permute-start | bytes 12582920 | tf_op jit(solution)/shard_map/ppermute | solution.py:84
  471.6 32.9 %collective-permute-start.40 = (bf16[256,2048]{1,0:T(8,128)(2,1)}, bf16[256,2048]{1,0:T(8,128)(2,1)}, u32[]{:S(2)}, u32[]{:S(2)}) collective-permute-start(bf16[256,2048]{1,0:T(8,128)(2,1)} %get-tuple-element.201), channel_id=1, source_target_pairs={{0,1},{1,0},{2,3},{3,2},{4,5},{5,4},{6,7},{7,6},{8,9},{9,8},{10,11... | collective-permute-start | bytes 3145736 | tf_op jit(solution)/shard_map/ppermute | solution.py:84
  472.0 47.1 %collective-permute-start.41 = (bf16[256,2048]{1,0:T(8,128)(2,1)}, bf16[256,2048]{1,0:T(8,128)(2,1)}, u32[]{:S(2)}, u32[]{:S(2)}) collective-permute-start(bf16[256,2048]{1,0:T(8,128)(2,1)} %get-tuple-element.200), channel_id=1, source_target_pairs={{0,2},{1,3},{2,0},{3,1},{4,6},{5,7},{6,4},{7,5},{8,10},{9,11},{10,... | collective-permute-start | bytes 3145736 | tf_op jit(solution)/shard_map/ppermute | solution.py:84
  473.9 46.1 %collective-permute-start.42 = (bf16[256,2048]{1,0:T(8,128)(2,1)}, bf16[256,2048]{1,0:T(8,128)(2,1)}, u32[]{:S(2)}, u32[]{:S(2)}) collective-permute-start(bf16[256,2048]{1,0:T(8,128)(2,1)} %get-tuple-element.199), channel_id=1, source_target_pairs={{0,3},{1,2},{2,1},{3,0},{4,7},{5,6},{6,5},{7,4},{8,11},{9,10},{10,... | collective-permute-start | bytes 3145736 | tf_op jit(solution)/shard_map/ppermute | solution.py:84
  526.3 20.7 %collective-permute-start.43 = (bf16[1024,2048]{1,0:T(8,128)(2,1)}, bf16[1024,2048]{1,0:T(8,128)(2,1)}, u32[]{:S(2)}, u32[]{:S(2)}) collective-permute-start(bf16[1024,2048]{1,0:T(8,128)(2,1)} %ffn_weight.5), channel_id=1, source_target_pairs={{0,4},{4,0},{8,12},{12,8},{16,20},{20,16},{24,28},{28,24},{1,5},{5... | collective-permute-start | bytes 12582920 | tf_op jit(solution)/shard_map/ppermute | solution.py:84
  539.3 19.0 %collective-permute-start.45 = (bf16[3,2,1,128,256]{4,3,2,1,0:T(8,128)(2,1)S(1)}, bf16[3,2,1,128,256]{4,3,2,1,0:T(8,128)(2,1)S(1)}, u32[]{:S(2)}, u32[]{:S(2)}) collective-permute-start(bf16[3,2,1,128,256]{4,3,2,1,0:T(8,128)(2,1)S(1)} %get-tuple-element.205), channel_id=1, source_target_pairs={{0,1},{1,0},{2,3},{3,2},{4,5},{5,4},{6,7},{7,6},{8,9},{9,8},{10,11... | collective-permute-start | bytes 1179656 | tf_op jit(solution)/shard_map/ppermute | solution.py:84
  540.7 22.5 %collective-permute-start.46 = (bf16[3,2,1,128,256]{4,3,2,1,0:T(8,128)(2,1)S(1)}, bf16[3,2,1,128,256]{4,3,2,1,0:T(8,128)(2,1)S(1)}, u32[]{:S(2)}, u32[]{:S(2)}) collective-permute-start(bf16[3,2,1,128,256]{4,3,2,1,0:T(8,128)(2,1)S(1)} %get-tuple-element.204), channel_id=1, source_target_pairs={{0,2},{1,3},{2,0},{3,1},{4,6},{5,7},{6,4},{7,5},{8,10},{9,11},{10,... | collective-permute-start | bytes 1179656 | tf_op jit(solution)/shard_map/ppermute | solution.py:84
  545.3 18.4 %collective-permute-start.47 = (bf16[3,2,1,128,256]{4,3,2,1,0:T(8,128)(2,1)S(1)}, bf16[3,2,1,128,256]{4,3,2,1,0:T(8,128)(2,1)S(1)}, u32[]{:S(2)}, u32[]{:S(2)}) collective-permute-start(bf16[3,2,1,128,256]{4,3,2,1,0:T(8,128)(2,1)S(1)} %get-tuple-element.203), channel_id=1, source_target_pairs={{0,3},{1,2},{2,1},{3,0},{4,7},{5,6},{6,5},{7,4},{8,11},{9,10},{10,... | collective-permute-start | bytes 1179656 | tf_op jit(solution)/shard_map/ppermute | solution.py:84
  555.0 48.1 %collective-permute-start.49 = (bf16[256,2048]{1,0:T(8,128)(2,1)}, bf16[256,2048]{1,0:T(8,128)(2,1)S(1)}, u32[]{:S(2)}, u32[]{:S(2)}) collective-permute-start(bf16[256,2048]{1,0:T(8,128)(2,1)} %get-tuple-element.147), channel_id=1, source_target_pairs={{0,1},{1,0},{2,3},{3,2},{4,5},{5,4},{6,7},{7,6},{8,9},{9,8},{10,11... | collective-permute-start | bytes 3145736 | tf_op jit(solution)/shard_map/ppermute | solution.py:84
  556.4 51.1 %collective-permute-start.50 = (bf16[256,2048]{1,0:T(8,128)(2,1)}, bf16[256,2048]{1,0:T(8,128)(2,1)}, u32[]{:S(2)}, u32[]{:S(2)}) collective-permute-start(bf16[256,2048]{1,0:T(8,128)(2,1)} %get-tuple-element.148), channel_id=1, source_target_pairs={{0,2},{1,3},{2,0},{3,1},{4,6},{5,7},{6,4},{7,5},{8,10},{9,11},{10,... | collective-permute-start | bytes 3145736 | tf_op jit(solution)/shard_map/ppermute | solution.py:84
  558.4 49.9 %collective-permute-start.51 = (bf16[256,2048]{1,0:T(8,128)(2,1)}, bf16[256,2048]{1,0:T(8,128)(2,1)}, u32[]{:S(2)}, u32[]{:S(2)}) collective-permute-start(bf16[256,2048]{1,0:T(8,128)(2,1)} %get-tuple-element.149), channel_id=1, source_target_pairs={{0,3},{1,2},{2,1},{3,0},{4,7},{5,6},{6,5},{7,4},{8,11},{9,10},{10,... | collective-permute-start | bytes 3145736 | tf_op jit(solution)/shard_map/ppermute | solution.py:84
  572.9 13.4 %collective-permute-start.48 = (bf16[3,1,128,256]{3,2,0,1:T(8,128)(2,1)S(1)}, bf16[3,1,128,256]{3,2,0,1:T(8,128)(2,1)S(1)}, u32[]{:S(2)}, u32[]{:S(2)}) collective-permute-start(bf16[3,1,128,256]{3,2,0,1:T(8,128)(2,1)S(1)} %fusion.22), channel_id=1, source_target_pairs={{16,8},{20,12},{17,9},{21,13},{18,10},{22,14},{19,11},{23,15}} | collective-permute-start | bytes 589832 | tf_op jit(solution)/shard_map/ppermute | solution.py:907
  573.7 77.4 %reduce-scatter.11.cloned.1.call-start = ((), (), s32[]{:S(2)}) async-start(), calls=%async_computation.11 | async-start | bytes 1474560 | tf_op jit(solution)/shard_map/reduce_scatter | solution.py:886
  608.3 5.8 collective-permute-start.53
  609.7 7.6 %collective-permute-start.54 = (bf16[32,2048]{1,0:T(8,128)(2,1)S(1)}, bf16[32,2048]{1,0:T(8,128)(2,1)S(1)}, u32[]{:S(2)}, u32[]{:S(2)}) collective-permute-start(bf16[32,2048]{1,0:T(8,128)(2,1)S(1)} %get-tuple-element.181), channel_id=1, source_target_pairs={{0,2},{1,3},{2,0},{3,1},{4,6},{5,7},{6,4},{7,5},{8,10},{9,11},{10,... | collective-permute-start | bytes 393224 | tf_op jit(solution)/shard_map/ppermute | solution.py:84
  610.6 6.8 %collective-permute-start.55 = (bf16[32,2048]{1,0:T(8,128)(2,1)S(1)}, bf16[32,2048]{1,0:T(8,128)(2,1)S(1)}, u32[]{:S(2)}, u32[]{:S(2)}) collective-permute-start(bf16[32,2048]{1,0:T(8,128)(2,1)S(1)} %get-tuple-element.182), channel_id=1, source_target_pairs={{0,3},{1,2},{2,1},{3,0},{4,7},{5,6},{6,5},{7,4},{8,11},{9,10},{10,... | collective-permute-start | bytes 393224 | tf_op jit(solution)/shard_map/ppermute | solution.py:84
  621.3 8.6 %collective-permute-start.58 = (f32[177,128]{1,0:T(8,128)}, f32[177,128]{1,0:T(8,128)S(1)}, u32[]{:S(2)}, u32[]{:S(2)}) collective-permute-start(f32[177,128]{1,0:T(8,128)} %bitcast_add_fusion.2), channel_id=1, source_target_pairs={{0,8},{4,12},{8,0},{12,4},{16,24},{20,28},{24,16},{28,20},{1,9},{5... | collective-permute-start | bytes 271880 | tf_op jit(solution)/shard_map/ppermute | solution.py:84
  629.9 12.9 %collective-permute-start.59 = (f32[177,128]{1,0:T(8,128)S(1)}, f32[177,128]{1,0:T(8,128)S(1)}, u32[]{:S(2)}, u32[]{:S(2)}) collective-permute-start(f32[177,128]{1,0:T(8,128)S(1)} %fusion.43), channel_id=1, source_target_pairs={{0,16},{4,20},{8,24},{12,28},{16,0},{20,4},{24,8},{28,12},{1,17},{... | collective-permute-start | bytes 271880 | tf_op jit(solution)/shard_map/ppermute | solution.py:84
  642.8 7.5 %collective-permute-start.60 = (f32[177,128]{1,0:T(8,128)S(1)}, f32[177,128]{1,0:T(8,128)S(1)}, u32[]{:S(2)}, u32[]{:S(2)}) collective-permute-start(f32[177,128]{1,0:T(8,128)S(1)} %add.495), channel_id=1, source_target_pairs={{0,1},{1,0},{2,3},{3,2},{4,5},{5,4},{6,7},{7,6},{8,9},{9,8},{10,11... | collective-permute-start | bytes 271880 | tf_op jit(solution)/shard_map/ppermute | solution.py:84
  (73 other events, 892.0 us)
Sparse Core Ops, SparseCore 0:
  12.5 34.6 all-gather.4
  49.3 32.3 all-gather.6
  83.2 83.4 all-gather.8
  168.1 80.6 all-gather.10
  393.4 89.2 reduce-scatter.6
  484.9 87.9 reduce-scatter.4
  575.1 25.5 reduce-scatter.8
  618.6 29.5 reduce-scatter.10

commit v4 on v3

--- a/solution.py
+++ b/solution.py
@@ -206,8 +206,7 @@
     bias_ref,
     log_ref,
     dq_ref,
-    dk_ref,
-    dv_ref,
+    dkv_ref,
     prob_ref,
     dprob_ref,
 ):
@@ -221,8 +220,7 @@
 
     @pl.when(pl.program_id(1) == 0)
     def _():
-        dk_ref[...] = jnp.zeros_like(dk_ref)
-        dv_ref[...] = jnp.zeros_like(dv_ref)
+        dkv_ref[...] = jnp.zeros_like(dkv_ref)
 
     queries = jnp.concatenate(
         [q_ref[0, :, h * HD : (h + 1) * HD] for h in range(HEAD_GROUP)], 0
@@ -246,8 +244,9 @@
         start = pl.multiple_of(block * KEY_BLOCK, KEY_BLOCK)
         probs = prob_ref[pl.ds(start, KEY_BLOCK), :]
         grad_scores = (probs * (dprob_ref[pl.ds(start, KEY_BLOCK), :] - delta)).astype(bf16)
-        dk_ref[0, pl.ds(start, KEY_BLOCK), :] += plain_dot(grad_scores, queries) * score_scale
-        dv_ref[0, pl.ds(start, KEY_BLOCK), :] += plain_dot(probs.astype(bf16), grads)
+        at = pl.ds(start, KEY_BLOCK)
+        dkv_ref[0, at, :HD] += plain_dot(grad_scores, queries) * score_scale
+        dkv_ref[0, at, HD:] += plain_dot(probs.astype(bf16), grads)
         return acc + plain_dot(kt_ref[0, :, pl.ds(start, KEY_BLOCK)], grad_scores)
 
     acc = lax.fori_loop(first, last, grad_block, jnp.zeros((HD, width), f32)) * score_scale
@@ -310,7 +309,10 @@
                 pl.BlockSpec((1, KEY_ROWS, bias.shape[2]), lambda b, g, *_: (b, 0, 0)),
                 pl.BlockSpec((1, 1, 1, width), lambda b, g, *_: (b, g, 0, 0)),
             ],
-            out_specs=[row_spec, key_spec, key_spec],
+            out_specs=[
+                row_spec,
+                pl.BlockSpec((1, KEY_ROWS, 2 * HD), lambda b, g, *_: (b, 0, 0)),
+            ],
             scratch_shapes=[
                 pltpu.VMEM((KEY_ROWS, width), f32),
                 pltpu.VMEM((KEY_ROWS, width), f32),
@@ -318,8 +320,7 @@
         ),
         out_shape=[
             jax.ShapeDtypeStruct(queries.shape, bf16),
-            jax.ShapeDtypeStruct(keys.shape, f32),
-            jax.ShapeDtypeStruct(keys.shape, f32),
+            jax.ShapeDtypeStruct((batches, KEY_ROWS, 2 * HD), f32),
         ],
         compiler_params=pltpu.CompilerParams(
             dimension_semantics=("arbitrary", "arbitrary"), vmem_limit_bytes=40 << 20
@@ -500,22 +501,26 @@
     )(left, right, addend)
 
 
-def onto_rows_kernel(*refs):
+def onto_rows_kernel(*refs, group):
     left_ref, bias_ref, piece_refs, out_ref = refs[0], refs[1], refs[2:-1], refs[-1]
-    for m, piece_ref in enumerate(piece_refs):
-
-        @pl.when(pl.program_id(0) == m)
+    tile = piece_refs[0].shape[0]
+    for first in range(0, len(piece_refs), group):
+
+        @pl.when(pl.program_id(0) == first // group)
         def _():
-            out_ref[...] = (rows_by_rows(left_ref[...], piece_ref[...]) + bias_ref[...]).astype(bf16)
-
-
-def onto_rows(left, pieces, bias):
-    tile = pieces[0].shape[0]
-    width = tile * len(pieces)
-    return pl.pallas_call(
-        onto_rows_kernel,
+            for m, piece_ref in enumerate(piece_refs[first : first + group]):
+                at = slice(m * tile, (m + 1) * tile)
+                product = rows_by_rows(left_ref[...], piece_ref[...])
+                out_ref[:, at] = (product + bias_ref[:, at]).astype(bf16)
+
+
+def onto_rows(left, pieces, bias, group=4):
+    tile = pieces[0].shape[0] * group
+    width = pieces[0].shape[0] * len(pieces)
+    return pl.pallas_call(
+        functools.partial(onto_rows_kernel, group=group),
         name="onto_rows",
-        grid=(len(pieces),),
+        grid=(len(pieces) // group,),
         in_specs=whole_specs([left])
         + [pl.BlockSpec((1, tile), lambda i: (0, i))]
         + whole_specs(pieces),
@@ -866,16 +871,15 @@
 
     out_grad_own, out_grad_other = halves_of(attended, grad_att)
     out_grad_other = out_grad_other.astype(bf16)
-    out_pieces = reduce_core(out_grad_own, swap_core(out_grad_other))
+    result = residual + total_of(after(received, out_grad_other)) + bias_down
+    outputs = result.astype(bf16).reshape(batches, rows, D)
+    out_pieces = reduce_core(out_grad_own, after(swap_core(out_grad_other), outputs))
     grad_heads = onto_rows(after(grad_att, *out_pieces), w_out, jnp.zeros((H * HD,), f32))
     grad_heads = grad_heads.reshape(batches, rows, H * HD)
     out_pieces = deliver(out_pieces)
-    grad_query, grad_key, grad_val = attend_backward(
+    grad_query, kv_grads = attend_backward(
         queries, grad_heads, keys, keys_t, vals, bias, log_sums, bounds
     )
-    grad_query, received = lax.optimization_barrier((grad_query, received))
-    result = residual + total_of(received) + bias_down
-    outputs = result.astype(bf16).reshape(batches, rows, D)
     grad_query = grad_query.reshape(batches * rows, H * HD)
 
     query_grad_other = ffn_weight([after(grad_query, *out_pieces)], [hidden_one], first=cols_half)
@@ -891,7 +895,6 @@
     grad_query = after(grad_query, *query_pieces)
     grad_bias_query = jnp.sum(grad_query.astype(f32), 0)
 
-    kv_grads = jnp.concatenate([grad_key, grad_val], 2)
     kv_grads = kv_grads.reshape(batches, 2, 2, stretch, 2 * HD)
     kv_kept = lax.dynamic_slice_in_dim(kv_grads, core, 1, 2)
     kv_sent = lax.dynamic_slice_in_dim(kv_grads, 1 - core, 1, 2).astype(bf16)
@@ -900,16 +903,6 @@
     kv_kept = kv_kept.reshape(batches, 2, tp_size, rows, 2 * HD)
     kv_got = deliver([lax.dynamic_slice_in_dim(kv_kept, at, 1, 2) for at in block_of])
     kv_total = total_of(after(kv_got, *query_pieces))
-    part_out, shard_up, shard_down, kv_total, _ = lax.optimization_barrier(
-        (part_out, shard_up, shard_down, kv_total, query_pieces)
-    )
-    part_out = scatter_chips(part_out)
-    grad_kv = kv_total[:, 1] + lax.ppermute(
-        kv_total[:, 0].astype(bf16), "dp", to_last
-    ).astype(f32)
-    grad_kv = grad_kv.astype(bf16).reshape(batches * rows, 2 * HD)
-    grad_bias_value = jnp.sum(grad_kv[:, HD:].astype(f32), 0)
-
     steps_float = step_count[0].astype(f32)
     scalars = jnp.stack(
         [
@@ -923,26 +916,37 @@
         block = grads.shape[0] // 2
         return adam_rows(scalars, master, grads, moment_one, moment_two, start, block, filled)
 
-    state = update_rows(shard_down, row_starts[4], ())
-    state = update_rows(shard_up, row_starts[3], state)
-    grad_kv = after(grad_kv, *state)
+    state = update_rows(after(shard_down, *query_pieces), row_starts[4], ())
+    part_out, shard_up, kv_total, _, _ = lax.optimization_barrier(
+        (part_out, shard_up, kv_total, query_pieces, state)
+    )
+    part_out = scatter_chips(part_out)
+    grad_kv = kv_total[:, 1] + lax.ppermute(
+        kv_total[:, 0].astype(bf16), "dp", to_last
+    ).astype(f32)
+    grad_kv = grad_kv.astype(bf16).reshape(batches * rows, 2 * HD)
+    grad_bias_value = jnp.sum(grad_kv[:, HD:].astype(f32), 0)
+
+    grad_w_keyval = cols_by_cols(after(grad_kv, part_out_sum), hidden_one)
+    kv_rows = [lax.dynamic_slice_in_dim(grad_w_keyval, start, kv_half) for start in kv_starts]
+    kv_parts = reduce_core(
+        jnp.concatenate(kv_rows[:tp_size], 0),
+        swap_core(jnp.concatenate(kv_rows[tp_size:], 0).astype(bf16)),
+    )
+    grad_kv = after(grad_kv, *kv_parts)
+    kv_parts = deliver(kv_parts)
     grad_hidden_one = onto_columns([grad_query, grad_kv], w_query + [w_keyval])
     grad_rows = grad_resid + layer_norm_back(grad_hidden_one, normed_one, inverse_one, gain_one)
     grad_gain_one = jnp.sum(grad_hidden_one * normed_one, 0)
     grad_shift_one = jnp.sum(grad_hidden_one, 0)
     input_grads = grad_rows.astype(bf16).reshape(batches, rows, D)
 
-    grad_w_keyval = cols_by_cols(after(grad_kv, part_out_sum), hidden_one)
-    kv_rows = [lax.dynamic_slice_in_dim(grad_w_keyval, start, kv_half) for start in kv_starts]
-    kv_parts = reduce_core(
-        jnp.concatenate(kv_rows[:tp_size], 0),
-        swap_core(jnp.concatenate(kv_rows[tp_size:], 0).astype(bf16)),
-    )
-    query_got, kv_parts = lax.optimization_barrier((query_got, kv_parts))
-    part_keyval = total_of(deliver(kv_parts))
+    query_got = after(query_got, grad_hidden_one)
+    part_keyval = total_of(after(kv_parts, *query_got))
     part_query = total_of(query_got)
     part_all = jnp.concatenate([part_query, part_keyval], 0).astype(bf16)
-    part_all = scatter_chips(after(part_all, part_out))
+    state = update_rows(after(shard_up, part_all), row_starts[3], state)
+    part_all = after(scatter_chips(after(part_all, part_out)), *state)
     part_all = jnp.concatenate([part_all, part_out], 0)
     width = part_all.shape[1] // 2
     mine = lax.dynamic_slice_in_dim(part_all, core * width, width, 1)

time: 681 us -> 681 us (level); the launches traced: 669 us -> 686 us
  waiting for transfers between devices: 240 us -> 252 us
    reduce_scatter x2, waiting for transfers between devices: 0.01 us -> 18.4 us  [scatter_chips(): lax.psum_scatter(part, 'dp', scatter_dimension=1, axis_index_groups=parit...]
    ppermute x60, waiting for transfers between devices: 234 us -> 220 us  [swap(): lax.ppermute(value, axis, [(source, source ^ step) for source in range(co...]
    reduce_scatter x2, waiting for transfers between devices: 4.52 us -> 12.5 us  [scatter_columns(): return lax.psum_scatter(full, 'dp', scatter_dimension=1, tiled=True)]
    unnamed x151 -> x147, local copies, waits for them, and re-layouts: 28.1 us -> 25.9 us
  transfers between devices with their start and end apart: 70 -> 70, of which waited for: 31 -> 30; matrix products, arithmetic and copies ran while one was open for 12% -> 12% of each run, Pallas kernels for 35% -> 33%
where the time goes in v4:
time: 681 us; the launch traced here: 686 us
  waiting for transfers between devices  252 us (37%)
  Pallas kernels  234 us (34%)
  starting transfers between devices  62.3 us (9%)
  local copies, waits for them, and re-layouts  54.1 us (8%)
  other arithmetic  41.7 us (6%)
  between operations  17.2 us (3%)
  blocking collectives  16.6 us (2%)
  matrix products  7.81 us (1%)
    ppermute x60, waiting for transfers between devices, swap(): lax.ppermute(value, axis, [(source, source ^ step) for source in range(co...  220 us
    ppermute x60, starting transfers between devices, swap(): lax.ppermute(value, axis, [(source, source ^ step) for source in range(co...  60.6 us
    pallas_call x3, Pallas kernels, ffn_weight(): pl.pallas_call(functools.partial(ffn_weight_kernel, lefts=len(lefts)), na...  52.6 us
    pallas_call x2, Pallas kernels, ffn_product(): pl.pallas_call(functools.partial(ffn_product_kernel, lefts=len(lefts)), n...  37 us
    unnamed x147, local copies, waits for them, and re-layouts  25.9 us
    pallas_call x1, Pallas kernels, ffn_back(): pl.pallas_call(functools.partial(ffn_back_kernel, count=len(pieces)), nam...  24.9 us
    pallas_call x1, Pallas kernels, ffn_up(): pl.pallas_call(ffn_up_kernel, name='ffn_up', grid=(units // tile,), in_sp...  22.1 us
    reduce_scatter x2, waiting for transfers between devices, scatter_chips(): lax.psum_scatter(part, 'dp', scatter_dimension=1, axis_index_groups=parit...  18.4 us
  transfers between devices with their start and end apart: 70, of which 30 were waited for; matrix products, arithmetic and copies ran while one was open for 12% of the time, Pallas kernels for 33%

profile of v4, /device:TPU:0, one launch (start us, length us, event | category | flops | bytes accessed | tf_op | source)
XLA Modules:
  0.0 686.3 jit_solution(13472903988781373428)
XLA Ops:
  7.2 2.8 convert.28
  13.2 3.2 fusion.31
  17.0 16.6 %all_gather.16 = bf16[64,2048]{1,0:T(8,128)(2,1)S(1)} all-gather(bf16[64,256]{1,0:T(8,128)(2,1)S(1)} %slice-done), channel_id=1, replica_groups=mesh['dp'=8,'tp'=4] {'dp'}, dimensions={1}, use_global_device_ids=true | all-gather | bytes 294912 | tf_op jit(solution)/shard_map/all_gather | solution.py:767
  48.0 3.3 constant_dynamic-slice_fusion.8
  59.1 18.2 %collective-permute-done.refs_3_ = bf16[256,2048]{1,0:T(8,128)(2,1)S(1)} collective-permute-done((bf16[256,2048]{1,0:T(8,128)(2,1)S(1)}, bf16[256,2048]{1,0:T(8,128)(2,1)S(1)}, u32[]{:S(2)}, u32[]{:S(2)}) %collective-permute-start) | collective-permute-done | bytes 1048608 | tf_op jit(solution)/shard_map/ppermute | solution.py:84
  77.4 23.2 %collective-permute-done.1.refs_4_ = bf16[256,2048]{1,0:T(8,128)(2,1)} collective-permute-done((bf16[256,2048]{1,0:T(8,128)(2,1)S(1)}, bf16[256,2048]{1,0:T(8,128)(2,1)}, u32[]{:S(2)}, u32[]{:S(2)}) %collective-permute-start.1) | collective-permute-done | bytes 1048608 | tf_op jit(solution)/shard_map/ppermute | solution.py:84
  108.2 4.5 collective-permute-done.10.refs_1_
  112.7 4.8 collective-permute-done.11.refs_2_
  117.5 1.9 collective-permute-done.12.refs_3_
  121.5 3.1 constant_dynamic-slice_fusion.6
  126.1 1.8 collective-permute-start.18
  130.1 7.0 %place_keys.1 = (bf16[3,2048,128]{2,1,0:T(8,128)(2,1)}, bf16[3,128,2048]{2,1,0:T(8,128)(2,1)}, bf16[3,2048,128]{2,1,0:T(8,128)(2,1)}, bf16[3,128,2048]{2,1,0:T(8,128)(2,1)}) custom-call(s32[8]{0:T(128)} %stack.45.starts, bf16[2,3,128,256]{3,2,1,0:T(8,128)(2,1)} %copy-done.41, bf16[2,3,128,256]{3,2,1,0:T(8,128)(2,1)} %copy-done.44, ...), custom_call_target="tpu_custom_call" | custom-call | flops 1048576 | bytes 1048576 | tf_op jit(solution)/shard_map/place_keys/pallas_call | solution.py:581
  138.6 8.6 %onto_rows.2 = bf16[384,2048]{1,0:T(8,128)(2,1)} custom-call(bf16[384,2048]{1,0:T(8,128)(2,1)} %copy-done.18, f32[1,2048]{1,0:T(1,128)} %bitcast.3.refs_1_, bf16[256,2048]{1,0:T(8,128)(2,1)} %copy-done.25, bf16[256,2048]{1,0:T(8,128)(2,1)} %copy-done.27, bf16[256,2048]{1,0:T(8,128)(2,1)} %collective-permute-done.1.refs_4_, ...), custom_call_target="tpu_custom_call" | custom-call | flops 1048576 | bytes 1048576 | tf_op jit(solution)/shard_map/onto_rows/pallas_call | solution.py:520
  148.7 9.2 %attend_forward.1 = (bf16[3,128,2048]{2,1,0:T(8,128)(2,1)S(1)}, f32[3,4,1,512]{3,2,1,0:T(1,128)S(1)}) custom-call(s32[3,2]{1,0:T(4,128)S(1)} %stack.36.bounds, bf16[3,128,2048]{2,1,0:T(8,128)(2,1)S(1)} %bitcast.107, bf16[3,2048,128]{2,1,0:T(8,128)(2,1)S(1)} %copy-done.5, bf16[3,128,2048]{2,1,0:T(8,128)(2,1)S(1)} %copy-done.9, ...), custom_call_target="tpu_custom_call" | custom-call | flops 1048576 | bytes 1048576 | tf_op jit(solution)/shard_map/attend_forward/pallas_call | solution.py:262
  159.0 14.8 %collective-permute-done.18.refs_3_.refs_4_ = bf16[256,2048]{1,0:T(8,128)(2,1)} collective-permute-done((bf16[256,2048]{1,0:T(8,128)(2,1)}, bf16[256,2048]{1,0:T(8,128)(2,1)}, u32[]{:S(2)}, u32[]{:S(2)}) %collective-permute-start.18) | collective-permute-done | bytes 1048608 | tf_op jit(solution)/shard_map/ppermute | solution.py:84
  174.3 3.0 collective-permute-done.20.refs_6_.refs_7_
  177.3 2.3 collective-permute-done.21.refs_7_.refs_8_
  182.1 8.3 %onto_columns.2 = f32[384,2048]{1,0:T(8,128)} custom-call(bf16[384,2048]{1,0:T(8,128)(2,1)} %bitcast.110, bf16[256,2048]{1,0:T(8,128)(2,1)} %get-tuple-element.105.refs_1_.refs_2_, bf16[256,2048]{1,0:T(8,128)(2,1)} %collective-permute-done.17.refs_2_.refs_3_, bf16[256,2048]{1,0:T(8,128)(2,1)} %collective-permute-done.18.refs_3_.refs_4_, ...), custom_call_target="tpu_custom_call" | custom-call | flops 1048576 | bytes 1048576 | tf_op jit(solution)/shard_map/onto_columns/pallas_call | solution.py:550
  190.5 2.6 fusion.27
  194.1 2.6 add_convert_fusion.2
  199.6 33.6 %collective-permute-done.23.refs_1_.refs_2_ = bf16[384,2048]{1,0:T(8,128)(2,1)S(1)} collective-permute-done((bf16[384,2048]{1,0:T(8,128)(2,1)S(1)}, bf16[384,2048]{1,0:T(8,128)(2,1)S(1)}, u32[]{:S(2)}, u32[]{:S(2)}) %collective-permute-start.23) | collective-permute-done | bytes 1572896 | tf_op jit(solution)/shard_map/ppermute | solution.py:84
  233.2 1.8 collective-permute-start.25
  236.9 15.4 %collective-permute-done.25.refs_3_.refs_4_ = bf16[192,2048]{1,0:T(8,128)(2,1)} collective-permute-done((bf16[192,2048]{1,0:T(8,128)(2,1)S(1)}, bf16[192,2048]{1,0:T(8,128)(2,1)}, u32[]{:S(2)}, u32[]{:S(2)}) %collective-permute-start.25) | collective-permute-done | bytes 786464 | tf_op jit(solution)/shard_map/ppermute | solution.py:84
  252.2 2.6 collective-permute-done.26.refs_4_.refs_5_
  256.6 1.7 collective-permute-start.32
  258.9 22.1 %ffn_up.1 = (f32[1536,2048]{1,0:T(8,128)}, bf16[1536,2048]{1,0:T(8,128)(2,1)}) custom-call(bf16[384,2048]{1,0:T(8,128)(2,1)} %copy-done.21, bf16[384,2048]{1,0:T(8,128)(2,1)} %copy-done.23, bf16[384,2048]{1,0:T(8,128)(2,1)} %copy-done.24, bf16[192,2048]{1,0:T(8,128)(2,1)} %collective-permute-done.25.refs_3_.refs_4_, ...), custom_call_target="tpu_custom_call" | custom-call | flops 1048576 | bytes 1048576 | tf_op jit(solution)/shard_map/ffn_up/pallas_call | solution.py:406
  281.0 18.4 %ffn_product.2 = (bf16[384,2048]{1,0:T(8,128)(2,1)}, bf16[384,2048]{1,0:T(8,128)(2,1)}, bf16[384,2048]{1,0:T(8,128)(2,1)}, bf16[384,2048]{1,0:T(8,128)(2,1)}) custom-call(bf16[1536,2048]{1,0:T(8,128)(2,1)} %get-tuple-element.109.refs_0_, bf16[2048,2048]{1,0:T(8,128)(2,1)} %all-gather.11.cloned.1.call-done.refs_1_.refs_4_), custom_call_target="tpu_custom_call" | custom-call | flops 1048576 | bytes 1048576 | tf_op jit(solution)/shard_map/ffn_product/pallas_call | solution.py:449
  302.9 24.0 %collective-permute-done.32.refs_4_.refs_3_ = bf16[384,2048]{1,0:T(8,128)(2,1)} collective-permute-done((bf16[384,2048]{1,0:T(8,128)(2,1)}, bf16[384,2048]{1,0:T(8,128)(2,1)}, u32[]{:S(2)}, u32[]{:S(2)}) %collective-permute-start.32) | collective-permute-done | bytes 1572896 | tf_op jit(solution)/shard_map/ppermute | solution.py:84
  326.9 23.2 %ffn_weight.3 = bf16[2048,2048]{1,0:T(8,128)(2,1)} custom-call(bf16[1536,2048]{1,0:T(8,128)(2,1)} %get-tuple-element.109.refs_0_, bf16[384,2048]{1,0:T(8,128)(2,1)} %bitcast.16.refs_1_.refs_0_, bf16[384,2048]{1,0:T(8,128)(2,1)} %collective-permute-done.30.refs_2_.refs_1_, bf16[384,2048]{1,0:T(8,128)(2,1)} %collective-permute-done.31.refs_3_.refs_2_, ...), custom_call_target="tpu_custom_call" | custom-call | flops 1048576 | bytes 1048576 | tf_op jit(solution)/shard_map/ffn_weight/pallas_call | solution.py:465
  350.1 24.9 %ffn_back.1 = (bf16[1536,2048]{1,0:T(8,128)(2,1)}, f32[1,2048]{1,0:T(1,128)}) custom-call(bf16[384,2048]{1,0:T(8,128)(2,1)} %bitcast.16.refs_1_.refs_0_, bf16[384,2048]{1,0:T(8,128)(2,1)} %collective-permute-done.30.refs_2_.refs_1_, bf16[384,2048]{1,0:T(8,128)(2,1)} %collective-permute-done.31.refs_3_.refs_2_, ...), custom_call_target="tpu_custom_call" | custom-call | flops 1048576 | bytes 1048576 | tf_op jit(solution)/shard_map/ffn_back/pallas_call | solution.py:430
  375.1 18.6 %ffn_product.3 = (bf16[384,2048]{1,0:T(8,128)(2,1)}, bf16[192,2048]{1,0:T(8,128)(2,1)}, bf16[192,2048]{1,0:T(8,128)(2,1)}, bf16[192,2048]{1,0:T(8,128)(2,1)}, bf...) custom-call(bf16[1536,2048]{1,0:T(8,128)(2,1)} %get-tuple-element.132.refs_0_, ...), custom_call_target="tpu_custom_call" | custom-call | flops 1048576 | bytes 1048576 | tf_op jit(solution)/shard_map/ffn_product/pallas_call | solution.py:449
  397.9 16.6 %collective-permute-done.36 = bf16[192,2048]{1,0:T(8,128)(2,1)S(1)} collective-permute-done((bf16[192,2048]{1,0:T(8,128)(2,1)}, bf16[192,2048]{1,0:T(8,128)(2,1)S(1)}, u32[]{:S(2)}, u32[]{:S(2)}) %collective-permute-start.36) | collective-permute-done | bytes 786464 | tf_op jit(solution)/shard_map/ppermute | solution.py:84
  414.5 2.3 add_convert_fusion.5
  417.3 2.3 add_convert_fusion.6
  420.9 23.0 %ffn_weight.4 = bf16[2048,2048]{1,0:T(8,128)(2,1)} custom-call(bf16[1536,2048]{1,0:T(8,128)(2,1)} %get-tuple-element.132.refs_0_, bf16[384,2048]{1,0:T(8,128)(2,1)} %copy-done.21, bf16[384,2048]{1,0:T(8,128)(2,1)} %copy-done.23, bf16[384,2048]{1,0:T(8,128)(2,1)} %copy-done.24, bf16[192,2048]{1,0:T(8,128)(2,1)} %collective-permute-done.25.refs_3_.refs_4_, ...), custom_call_target="tpu_custom_call" | custom-call | flops 1048576 | bytes 1048576 | tf_op jit(solution)/shard_map/ffn_weight/pallas_call | solution.py:465
  446.2 8.3 %norm_back.1 = (f32[384,2048]{1,0:T(8,128)}, bf16[384,2048]{1,0:T(8,128)(2,1)}, f32[8,2048]{1,0:T(8,128)}) custom-call(bf16[384,2048]{1,0:T(8,128)(2,1)} %get-tuple-element.133.refs_0_, bf16[384,2048]{1,0:T(8,128)(2,1)} %bitcast.16.refs_1_.refs_0_, f32[384,2048]{1,0:T(8,128)} %get-tuple-element.200.refs_2_, f32[384,1]{1,0:T(8,128)} %rsqrt.20.refs_3_, ...), custom_call_target="tpu_custom_call" | custom-call | flops 1048576 | bytes 1048576 | tf_op jit(solution)/shard_map/norm_back/pallas_call | solution.py:628
  454.6 4.0 convolution_convert_fusion
  458.7 5.5 add_convert_fusion.1
  465.8 2.5 add_convert_fusion
  468.3 2.1 fusion.30
  474.5 8.7 %onto_rows.3 = bf16[384,2048]{1,0:T(8,128)(2,1)} custom-call(bf16[384,2048]{1,0:T(8,128)(2,1)} %get-tuple-element.141.refs_0_, f32[1,2048]{1,0:T(1,128)} %reshape.215.refs_1_, bf16[256,2048]{1,0:T(8,128)(2,1)} %get-tuple-element.105.refs_1_.refs_2_, bf16[256,2048]{1,0:T(8,128)(2,1)} %collective-permute-done.17.refs_2_.refs_3_, ...), custom_call_target="tpu_custom_call" | custom-call | flops 1048576 | bytes 1048576 | tf_op jit(solution)/shard_map/onto_rows/pallas_call | solution.py:520
  486.0 13.4 %attend_backward.1 = (bf16[3,128,2048]{2,1,0:T(8,128)(2,1)S(1)}, f32[3,2048,256]{2,1,0:T(8,128)}) custom-call(s32[3,2]{1,0:T(4,128)S(1)} %stack.36.bounds, bf16[3,128,2048]{2,1,0:T(8,128)(2,1)S(1)} %bitcast.108, bf16[3,128,2048]{2,1,0:T(8,128)(2,1)S(1)} %bitcast.109, bf16[3,2048,128]{2,1,0:T(8,128)(2,1)S(1)} %copy-done.6, ...), custom_call_target="tpu_custom_call" | custom-call | flops 1048576 | bytes 1048576 | tf_op jit(solution)/shard_map/attend_backward/pallas_call | solution.py:297
  500.7 19.1 %collective-permute-done.41 = bf16[256,2048]{1,0:T(8,128)(2,1)} collective-permute-done((bf16[256,2048]{1,0:T(8,128)(2,1)}, bf16[256,2048]{1,0:T(8,128)(2,1)}, u32[]{:S(2)}, u32[]{:S(2)}) %collective-permute-start.41) | collective-permute-done | bytes 1048608 | tf_op jit(solution)/shard_map/ppermute | solution.py:84
  519.8 6.3 ffn_weight.5
  526.1 2.1 bitcast_convert_fusion
  532.9 3.0 collective-permute-done.44
  535.9 2.3 bitcast_add_fusion
  543.0 7.9 %weight_pieces.1 = (bf16[256,2048]{1,0:T(8,128)(2,1)}, bf16[256,2048]{1,0:T(8,128)(2,1)}, bf16[256,2048]{1,0:T(8,128)(2,1)}, bf16[256,2048]{1,0:T(8,128)(2,1)}) custom-call(bf16[384,2048]{1,0:T(8,128)(2,1)} %bitcast.104, bf16[384,2048]{1,0:T(8,128)(2,1)} %copy-done.18, bf16[1024,2048]{1,0:T(8,128)(2,1)} %collective-permute-done.43.add_ref), custom_call_target="tpu_custom_call" | custom-call | flops 1048576 | bytes 1048576 | tf_op jit(solution)/shard_map/weight_pieces/pallas_call | solution.py:490
  554.4 3.3 collective-permute-done.46
  559.8 3.6 add_convert_fusion.4
  563.3 6.3 adam_rows.3
  569.7 12.5 %reduce-scatter.5.cloned.1.call-done.grads = bf16[2048,256]{1,0:T(8,128)(2,1)} async-done(((bf16[2048,2048]{1,0:T(8,128)(2,1)}), bf16[2048,256]{1,0:T(8,128)(2,1)}) %reduce-scatter.5.cloned.1.call-update) | async-done | bytes 1048592 | tf_op jit(solution)/shard_map/reduce_scatter | solution.py:835
  590.4 9.2 %onto_columns.3 = f32[384,2048]{1,0:T(8,128)} custom-call(bf16[384,2048]{1,0:T(8,128)(2,1)} %bitcast.105, bf16[384,256]{1,0:T(8,128)(2,1)} %bitcast.119, bf16[256,2048]{1,0:T(8,128)(2,1)} %copy-done.25, bf16[256,2048]{1,0:T(8,128)(2,1)} %copy-done.27, bf16[256,2048]{1,0:T(8,128)(2,1)} %collective-permute-done.1.refs_4_, ...), custom_call_target="tpu_custom_call" | custom-call | flops 1048576 | bytes 1048576 | tf_op jit(solution)/shard_map/onto_columns/pallas_call | solution.py:550
  600.2 2.5 collective-permute-done.51
  603.9 2.6 add_convert_fusion.3
  610.0 18.3 %reduce-scatter.9.cloned.1.call-done = bf16[256,512]{1,0:T(8,128)(2,1)} async-done(((bf16[256,2048]{1,0:T(8,128)(2,1)}), bf16[256,512]{1,0:T(8,128)(2,1)}) %reduce-scatter.9.cloned.1.call-update) | async-done | bytes 262160 | tf_op jit(solution)/shard_map/reduce_scatter | solution.py:890
  629.9 4.7 collective-permute-done.58
  634.7 9.9 %collective-permute-start.59 = (f32[177,128]{1,0:T(8,128)S(1)}, f32[177,128]{1,0:T(8,128)S(1)}, u32[]{:S(2)}, u32[]{:S(2)}) collective-permute-start(f32[177,128]{1,0:T(8,128)S(1)} %fusion.43), channel_id=1, source_target_pairs={{0,16},{4,20},{8,24},{12,28},{16,0},{20,4},{24,8},{28,12},{1,17},{... | collective-permute-start | bytes 271880 | tf_op jit(solution)/shard_map/ppermute | solution.py:84
  644.6 10.0 %collective-permute-done.59 = f32[177,128]{1,0:T(8,128)S(1)} collective-permute-done((f32[177,128]{1,0:T(8,128)S(1)}, f32[177,128]{1,0:T(8,128)S(1)}, u32[]{:S(2)}, u32[]{:S(2)}) %collective-permute-start.59) | collective-permute-done | bytes 90656 | tf_op jit(solution)/shard_map/ppermute | solution.py:84
  654.6 2.1 collective-permute-start.60
  656.7 5.1 fusion.13
  661.9 6.3 adam_rows.4
  669.4 3.4 collective-permute-done.61
  674.6 4.3 adam_rows.5
  (348 shorter events, 107.5 us)
Async XLA Ops:
  7.2 40.8 %all-gather.5.cloned.1.call-start = ((), (), s32[]{:S(2)}) async-start(), calls=%async_computation.4 | async-start | bytes 2359296 | tf_op jit(solution)/shard_map/all_gather | solution.py:767
  12.3 109.1 %all-gather.7.cloned.1.call-start = ((), (), s32[]{:S(2)}) async-start(), calls=%async_computation.5 | async-start | bytes 2359296 | tf_op jit(solution)/shard_map/all_gather | solution.py:767
  13.1 245.8 %all-gather.9.cloned.1.call-start = ((), (), s32[]{:S(2)}) async-start(), calls=%async_computation.6 | async-start | bytes 9437184 | tf_op jit(solution)/shard_map/all_gather | solution.py:767
  16.4 264.7 %all-gather.11.cloned.1.call-start = ((), (), s32[]{:S(2)}) async-start(), calls=%async_computation.7 | async-start | bytes 9437184 | tf_op jit(solution)/shard_map/all_gather | solution.py:767
  16.9 546.4 %reduce-scatter.7.cloned.1.call-start = ((), (), s32[]{:S(2)}) async-start(), calls=%async_computation.9 | async-start | bytes 9437184 | tf_op jit(solution)/shard_map/reduce_scatter | solution.py:835
  33.6 19.2 %collective-permute-start.6 = (bf16[64,2048]{1,0:T(8,128)(2,1)S(1)}, bf16[64,2048]{1,0:T(8,128)(2,1)}, u32[]{:S(2)}, u32[]{:S(2)}) collective-permute-start(bf16[64,2048]{1,0:T(8,128)(2,1)S(1)} %all_gather.16), channel_id=1, source_target_pairs={{0,1},{1,0},{2,3},{3,2},{4,5},{5,4},{6,7},{7,6},{8,9},{9,8},{10,11... | collective-permute-start | bytes 786440 | tf_op jit(solution)/shard_map/ppermute | solution.py:84
  35.1 20.7 %collective-permute-start.7 = (bf16[64,2048]{1,0:T(8,128)(2,1)S(1)}, bf16[64,2048]{1,0:T(8,128)(2,1)}, u32[]{:S(2)}, u32[]{:S(2)}) collective-permute-start(bf16[64,2048]{1,0:T(8,128)(2,1)S(1)} %all_gather.16), channel_id=1, source_target_pairs={{0,2},{1,3},{2,0},{3,1},{4,6},{5,7},{6,4},{7,5},{8,10},{9,11},{10,... | collective-permute-start | bytes 786440 | tf_op jit(solution)/shard_map/ppermute | solution.py:84
  36.6 20.2 %collective-permute-start.8 = (bf16[64,2048]{1,0:T(8,128)(2,1)S(1)}, bf16[64,2048]{1,0:T(8,128)(2,1)}, u32[]{:S(2)}, u32[]{:S(2)}) collective-permute-start(bf16[64,2048]{1,0:T(8,128)(2,1)S(1)} %all_gather.16), channel_id=1, source_target_pairs={{0,3},{1,2},{2,1},{3,0},{4,7},{5,6},{6,5},{7,4},{8,11},{9,10},{10,... | collective-permute-start | bytes 786440 | tf_op jit(solution)/shard_map/ppermute | solution.py:84
  51.3 26.1 %collective-permute-start = (bf16[256,2048]{1,0:T(8,128)(2,1)S(1)}, bf16[256,2048]{1,0:T(8,128)(2,1)S(1)}, u32[]{:S(2)}, u32[]{:S(2)}) collective-permute-start(bf16[256,2048]{1,0:T(8,128)(2,1)S(1)} %get-tuple-element.223.refs_2_), channel_id=1, source_target_pairs={{0,1},{1,0},{2,3},{3,2},{4,5},{5,4},{6,7},{7,6},{8,9},{9,8},{10,11... | collective-permute-start | bytes 3145736 | tf_op jit(solution)/shard_map/ppermute | solution.py:84
  53.7 46.9 %collective-permute-start.1 = (bf16[256,2048]{1,0:T(8,128)(2,1)S(1)}, bf16[256,2048]{1,0:T(8,128)(2,1)}, u32[]{:S(2)}, u32[]{:S(2)}) collective-permute-start(bf16[256,2048]{1,0:T(8,128)(2,1)S(1)} %get-tuple-element.223.refs_2_), channel_id=1, source_target_pairs={{0,2},{1,3},{2,0},{3,1},{4,6},{5,7},{6,4},{7,5},{8,10},{9,11},{10,... | collective-permute-start | bytes 3145736 | tf_op jit(solution)/shard_map/ppermute | solution.py:84
  55.3 45.3 %collective-permute-start.2 = (bf16[256,2048]{1,0:T(8,128)(2,1)S(1)}, bf16[256,2048]{1,0:T(8,128)(2,1)}, u32[]{:S(2)}, u32[]{:S(2)}) collective-permute-start(bf16[256,2048]{1,0:T(8,128)(2,1)S(1)} %get-tuple-element.223.refs_2_), channel_id=1, source_target_pairs={{0,3},{1,2},{2,1},{3,0},{4,7},{5,6},{6,5},{7,4},{8,11},{9,10},{10,... | collective-permute-start | bytes 3145736 | tf_op jit(solution)/shard_map/ppermute | solution.py:84
  58.4 19.0 %collective-permute-start.9 = (bf16[1,3,128,256]{3,2,1,0:T(8,128)(2,1)S(1)}, bf16[1,3,128,256]{3,2,1,0:T(8,128)(2,1)S(1)}, u32[]{:S(2)}, u32[]{:S(2)}) collective-permute-start(bf16[1,3,128,256]{3,2,1,0:T(8,128)(2,1)S(1)} %bitcast.123), channel_id=1, source_target_pairs={{8,16},{12,20},{9,17},{13,21},{10,18},{14,22},{11,19},{15,23}} | collective-permute-start | bytes 589832 | tf_op jit(solution)/shard_map/ppermute | solution.py:795
  77.4 50.5 %collective-permute-start.3 = (bf16[256,2048]{1,0:T(8,128)(2,1)S(1)}, bf16[256,2048]{1,0:T(8,128)(2,1)S(1)}, u32[]{:S(2)}, u32[]{:S(2)}) collective-permute-start(bf16[256,2048]{1,0:T(8,128)(2,1)S(1)} %collective-permute-done.refs_3_), channel_id=1, source_target_pairs={{0,4},{4,0},{8,12},{12,8},{16,20},{20,16},{24,28},{28,24},{1,5},{5... | collective-permute-start | bytes 3145736 | tf_op jit(solution)/shard_map/ppermute | solution.py:84
  100.7 12.1 %collective-permute-start.10 = (bf16[2,3,128,256]{3,2,1,0:T(8,128)(2,1)S(1)}, bf16[2,3,128,256]{3,2,1,0:T(8,128)(2,1)S(1)}, u32[]{:S(2)}, u32[]{:S(2)}) collective-permute-start(bf16[2,3,128,256]{3,2,1,0:T(8,128)(2,1)S(1)} %pad_maximum_fusion.2.refs_0_), channel_id=1, source_target_pairs={{0,1},{1,0},{2,3},{3,2},{4,5},{5,4},{6,7},{7,6},{8,9},{9,8},{10,11... | collective-permute-start | bytes 1179656 | tf_op jit(solution)/shard_map/ppermute | solution.py:84
  101.3 16.2 %collective-permute-start.11 = (bf16[2,3,128,256]{3,2,1,0:T(8,128)(2,1)S(1)}, bf16[2,3,128,256]{3,2,1,0:T(8,128)(2,1)S(1)}, u32[]{:S(2)}, u32[]{:S(2)}) collective-permute-start(bf16[2,3,128,256]{3,2,1,0:T(8,128)(2,1)S(1)} %pad_maximum_fusion.2.refs_0_), channel_id=1, source_target_pairs={{0,2},{1,3},{2,0},{3,1},{4,6},{5,7},{6,4},{7,5},{8,10},{9,11},{10,... | collective-permute-start | bytes 1179656 | tf_op jit(solution)/shard_map/ppermute | solution.py:84
  102.8 16.6 %collective-permute-start.12 = (bf16[2,3,128,256]{3,2,1,0:T(8,128)(2,1)S(1)}, bf16[2,3,128,256]{3,2,1,0:T(8,128)(2,1)}, u32[]{:S(2)}, u32[]{:S(2)}) collective-permute-start(bf16[2,3,128,256]{3,2,1,0:T(8,128)(2,1)S(1)} %pad_maximum_fusion.2.refs_0_), channel_id=1, source_target_pairs={{0,3},{1,2},{2,1},{3,0},{4,7},{5,6},{6,5},{7,4},{8,11},{9,10},{10,... | collective-permute-start | bytes 1179656 | tf_op jit(solution)/shard_map/ppermute | solution.py:84
  108.2 16.4 %collective-permute-start.13 = (bf16[2,3,128,256]{3,2,1,0:T(8,128)(2,1)S(1)}, bf16[2,3,128,256]{3,2,1,0:T(8,128)(2,1)}, u32[]{:S(2)}, u32[]{:S(2)}) collective-permute-start(bf16[2,3,128,256]{3,2,1,0:T(8,128)(2,1)S(1)} %pad_maximum_fusion.2.refs_0_), channel_id=1, source_target_pairs={{0,4},{4,0},{8,12},{12,8},{16,20},{20,16},{24,28},{28,24},{1,5},{5... | collective-permute-start | bytes 1179656 | tf_op jit(solution)/shard_map/ppermute | solution.py:84
  112.7 12.4 %collective-permute-start.14 = (bf16[2,3,128,256]{3,2,1,0:T(8,128)(2,1)S(1)}, bf16[2,3,128,256]{3,2,1,0:T(8,128)(2,1)}, u32[]{:S(2)}, u32[]{:S(2)}) collective-permute-start(bf16[2,3,128,256]{3,2,1,0:T(8,128)(2,1)S(1)} %collective-permute-done.10.refs_1_), channel_id=1, source_target_pairs={{0,4},{4,0},{8,12},{12,8},{16,20},{20,16},{24,28},{28,24},{1,5},{5... | collective-permute-start | bytes 1179656 | tf_op jit(solution)/shard_map/ppermute | solution.py:84
  117.5 7.7 %collective-permute-start.15 = (bf16[2,3,128,256]{3,2,1,0:T(8,128)(2,1)S(1)}, bf16[2,3,128,256]{3,2,1,0:T(8,128)(2,1)}, u32[]{:S(2)}, u32[]{:S(2)}) collective-permute-start(bf16[2,3,128,256]{3,2,1,0:T(8,128)(2,1)S(1)} %collective-permute-done.11.refs_2_), channel_id=1, source_target_pairs={{0,4},{4,0},{8,12},{12,8},{16,20},{20,16},{24,28},{28,24},{1,5},{5... | collective-permute-start | bytes 1179656 | tf_op jit(solution)/shard_map/ppermute | solution.py:84
  119.5 6.6 collective-permute-start.16
  124.6 12.5 %collective-permute-start.4 = (bf16[256,2048]{1,0:T(8,128)(2,1)}, bf16[256,2048]{1,0:T(8,128)(2,1)S(1)}, u32[]{:S(2)}, u32[]{:S(2)}) collective-permute-start(bf16[256,2048]{1,0:T(8,128)(2,1)} %collective-permute-done.1.refs_4_), channel_id=1, source_target_pairs={{0,4},{4,0},{8,12},{12,8},{16,20},{20,16},{24,28},{28,24},{1,5},{5... | collective-permute-start | bytes 3145736 | tf_op jit(solution)/shard_map/ppermute | solution.py:84
  125.1 12.0 %collective-permute-start.5 = (bf16[256,2048]{1,0:T(8,128)(2,1)}, bf16[256,2048]{1,0:T(8,128)(2,1)S(1)}, u32[]{:S(2)}, u32[]{:S(2)}) collective-permute-start(bf16[256,2048]{1,0:T(8,128)(2,1)} %collective-permute-done.2.refs_5_), channel_id=1, source_target_pairs={{0,4},{4,0},{8,12},{12,8},{16,20},{20,16},{24,28},{28,24},{1,5},{5... | collective-permute-start | bytes 3145736 | tf_op jit(solution)/shard_map/ppermute | solution.py:84
  125.2 33.8 %collective-permute-start.17 = (bf16[256,2048]{1,0:T(8,128)(2,1)}, bf16[256,2048]{1,0:T(8,128)(2,1)}, u32[]{:S(2)}, u32[]{:S(2)}) collective-permute-start(bf16[256,2048]{1,0:T(8,128)(2,1)} %get-tuple-element.105.refs_1_.refs_2_), channel_id=1, source_target_pairs={{0,1},{1,0},{2,3},{3,2},{4,5},{5,4},{6,7},{7,6},{8,9},{9,8},{10,11... | collective-permute-start | bytes 3145736 | tf_op jit(solution)/shard_map/ppermute | solution.py:84
  126.1 47.7 %collective-permute-start.18 = (bf16[256,2048]{1,0:T(8,128)(2,1)}, bf16[256,2048]{1,0:T(8,128)(2,1)}, u32[]{:S(2)}, u32[]{:S(2)}) collective-permute-start(bf16[256,2048]{1,0:T(8,128)(2,1)} %get-tuple-element.105.refs_1_.refs_2_), channel_id=1, source_target_pairs={{0,2},{1,3},{2,0},{3,1},{4,6},{5,7},{6,4},{7,5},{8,10},{9,11},{10,... | collective-permute-start | bytes 3145736 | tf_op jit(solution)/shard_map/ppermute | solution.py:84
  127.9 45.9 %collective-permute-start.19 = (bf16[256,2048]{1,0:T(8,128)(2,1)}, bf16[256,2048]{1,0:T(8,128)(2,1)}, u32[]{:S(2)}, u32[]{:S(2)}) collective-permute-start(bf16[256,2048]{1,0:T(8,128)(2,1)} %get-tuple-element.105.refs_1_.refs_2_), channel_id=1, source_target_pairs={{0,3},{1,2},{2,1},{3,0},{4,7},{5,6},{6,5},{7,4},{8,11},{9,10},{10,... | collective-permute-start | bytes 3145736 | tf_op jit(solution)/shard_map/ppermute | solution.py:84
  173.8 5.9 collective-permute-start.21
  174.3 6.9 collective-permute-start.22
  196.7 36.4 %collective-permute-start.23 = (bf16[384,2048]{1,0:T(8,128)(2,1)S(1)}, bf16[384,2048]{1,0:T(8,128)(2,1)S(1)}, u32[]{:S(2)}, u32[]{:S(2)}) collective-permute-start(bf16[384,2048]{1,0:T(8,128)(2,1)S(1)} %get-tuple-element.199.refs_0_.refs_1_), channel_id=1, source_target_pairs={{0,1},{1,0},{2,3},{3,2},{4,5},{5,4},{6,7},{7,6},{8,9},{9,8},{10,11... | collective-permute-start | bytes 4718600 | tf_op jit(solution)/shard_map/ppermute | solution.py:84
  198.1 36.9 %collective-permute-start.24 = (bf16[384,2048]{1,0:T(8,128)(2,1)S(1)}, bf16[384,2048]{1,0:T(8,128)(2,1)S(1)}, u32[]{:S(2)}, u32[]{:S(2)}) collective-permute-start(bf16[384,2048]{1,0:T(8,128)(2,1)S(1)} %get-tuple-element.199.refs_0_.refs_1_), channel_id=1, source_target_pairs={{0,2},{1,3},{2,0},{3,1},{4,6},{5,7},{6,4},{7,5},{8,10},{9,11},{10,... | collective-permute-start | bytes 4718600 | tf_op jit(solution)/shard_map/ppermute | solution.py:84
  233.2 19.0 %collective-permute-start.25 = (bf16[192,2048]{1,0:T(8,128)(2,1)S(1)}, bf16[192,2048]{1,0:T(8,128)(2,1)}, u32[]{:S(2)}, u32[]{:S(2)}) collective-permute-start(bf16[192,2048]{1,0:T(8,128)(2,1)S(1)} %slice.197), channel_id=1, source_target_pairs={{0,2},{1,3},{2,0},{3,1},{4,6},{5,7},{6,4},{7,5},{8,10},{9,11},{10,... | collective-permute-start | bytes 2359304 | tf_op jit(solution)/shard_map/ppermute | solution.py:84
  236.1 18.7 %collective-permute-start.26 = (bf16[192,2048]{1,0:T(8,128)(2,1)S(1)}, bf16[192,2048]{1,0:T(8,128)(2,1)}, u32[]{:S(2)}, u32[]{:S(2)}) collective-permute-start(bf16[192,2048]{1,0:T(8,128)(2,1)S(1)} %slice.198), channel_id=1, source_target_pairs={{0,1},{1,0},{2,3},{3,2},{4,5},{5,4},{6,7},{7,6},{8,9},{9,8},{10,11... | collective-permute-start | bytes 2359304 | tf_op jit(solution)/shard_map/ppermute | solution.py:84
  254.8 46.4 %collective-permute-start.30 = (bf16[384,2048]{1,0:T(8,128)(2,1)}, bf16[384,2048]{1,0:T(8,128)(2,1)}, u32[]{:S(2)}, u32[]{:S(2)}) collective-permute-start(bf16[384,2048]{1,0:T(8,128)(2,1)} %bitcast.16.refs_1_.refs_0_), channel_id=1, source_target_pairs={{0,1},{1,0},{2,3},{3,2},{4,5},{5,4},{6,7},{7,6},{8,9},{9,8},{10,11... | collective-permute-start | bytes 4718600 | tf_op jit(solution)/shard_map/ppermute | solution.py:84
  255.8 47.1 %collective-permute-start.31 = (bf16[384,2048]{1,0:T(8,128)(2,1)}, bf16[384,2048]{1,0:T(8,128)(2,1)}, u32[]{:S(2)}, u32[]{:S(2)}) collective-permute-start(bf16[384,2048]{1,0:T(8,128)(2,1)} %bitcast.16.refs_1_.refs_0_), channel_id=1, source_target_pairs={{0,2},{1,3},{2,0},{3,1},{4,6},{5,7},{6,4},{7,5},{8,10},{9,11},{10,... | collective-permute-start | bytes 4718600 | tf_op jit(solution)/shard_map/ppermute | solution.py:84
  256.6 70.4 %collective-permute-start.32 = (bf16[384,2048]{1,0:T(8,128)(2,1)}, bf16[384,2048]{1,0:T(8,128)(2,1)}, u32[]{:S(2)}, u32[]{:S(2)}) collective-permute-start(bf16[384,2048]{1,0:T(8,128)(2,1)} %bitcast.16.refs_1_.refs_0_), channel_id=1, source_target_pairs={{0,3},{1,2},{2,1},{3,0},{4,7},{5,6},{6,5},{7,4},{8,11},{9,10},{10,... | collective-permute-start | bytes 4718600 | tf_op jit(solution)/shard_map/ppermute | solution.py:84
  299.4 94.3 %collective-permute-start.27 = (bf16[384,2048]{1,0:T(8,128)(2,1)}, bf16[384,2048]{1,0:T(8,128)(2,1)}, u32[]{:S(2)}, u32[]{:S(2)}) collective-permute-start(bf16[384,2048]{1,0:T(8,128)(2,1)} %get-tuple-element.111), channel_id=1, source_target_pairs={{0,1},{1,0},{2,3},{3,2},{4,5},{5,4},{6,7},{7,6},{8,9},{9,8},{10,11... | collective-permute-start | bytes 4718600 | tf_op jit(solution)/shard_map/ppermute | solution.py:84
  300.4 93.2 %collective-permute-start.28 = (bf16[384,2048]{1,0:T(8,128)(2,1)}, bf16[384,2048]{1,0:T(8,128)(2,1)}, u32[]{:S(2)}, u32[]{:S(2)}) collective-permute-start(bf16[384,2048]{1,0:T(8,128)(2,1)} %get-tuple-element.112), channel_id=1, source_target_pairs={{0,2},{1,3},{2,0},{3,1},{4,6},{5,7},{6,4},{7,5},{8,10},{9,11},{10,... | collective-permute-start | bytes 4718600 | tf_op jit(solution)/shard_map/ppermute | solution.py:84
  301.2 92.5 %collective-permute-start.29 = (bf16[384,2048]{1,0:T(8,128)(2,1)}, bf16[384,2048]{1,0:T(8,128)(2,1)}, u32[]{:S(2)}, u32[]{:S(2)}) collective-permute-start(bf16[384,2048]{1,0:T(8,128)(2,1)} %get-tuple-element.113), channel_id=1, source_target_pairs={{0,3},{1,2},{2,1},{3,0},{4,7},{5,6},{6,5},{7,4},{8,11},{9,10},{10,... | collective-permute-start | bytes 4718600 | tf_op jit(solution)/shard_map/ppermute | solution.py:84
  393.7 188.4 %reduce-scatter.5.cloned.1.call-start = ((), (), s32[]{:S(2)}) async-start(), calls=%async_computation.8 | async-start | bytes 9437184 | tf_op jit(solution)/shard_map/reduce_scatter | solution.py:835
  393.8 20.8 %collective-permute-start.36 = (bf16[192,2048]{1,0:T(8,128)(2,1)}, bf16[192,2048]{1,0:T(8,128)(2,1)S(1)}, u32[]{:S(2)}, u32[]{:S(2)}) collective-permute-start(bf16[192,2048]{1,0:T(8,128)(2,1)} %get-tuple-element.131), channel_id=1, source_target_pairs={{0,2},{1,3},{2,0},{3,1},{4,6},{5,7},{6,4},{7,5},{8,10},{9,11},{10,... | collective-permute-start | bytes 2359304 | tf_op jit(solution)/shard_map/ppermute | solution.py:84
  394.6 22.7 %collective-permute-start.34 = (bf16[192,2048]{1,0:T(8,128)(2,1)}, bf16[192,2048]{1,0:T(8,128)(2,1)S(1)}, u32[]{:S(2)}, u32[]{:S(2)}) collective-permute-start(bf16[192,2048]{1,0:T(8,128)(2,1)} %get-tuple-element.130), channel_id=1, source_target_pairs={{0,1},{1,0},{2,3},{3,2},{4,5},{5,4},{6,7},{7,6},{8,9},{9,8},{10,11... | collective-permute-start | bytes 2359304 | tf_op jit(solution)/shard_map/ppermute | solution.py:84
  395.6 48.3 %collective-permute-start.33 = (bf16[192,2048]{1,0:T(8,128)(2,1)}, bf16[192,2048]{1,0:T(8,128)(2,1)}, u32[]{:S(2)}, u32[]{:S(2)}) collective-permute-start(bf16[192,2048]{1,0:T(8,128)(2,1)} %get-tuple-element.126), channel_id=1, source_target_pairs={{0,1},{1,0},{2,3},{3,2},{4,5},{5,4},{6,7},{7,6},{8,9},{9,8},{10,11... | collective-permute-start | bytes 2359304 | tf_op jit(solution)/shard_map/ppermute | solution.py:84
  396.6 47.4 %collective-permute-start.38 = (bf16[192,2048]{1,0:T(8,128)(2,1)}, bf16[192,2048]{1,0:T(8,128)(2,1)}, u32[]{:S(2)}, u32[]{:S(2)}) collective-permute-start(bf16[192,2048]{1,0:T(8,128)(2,1)} %get-tuple-element.129), channel_id=1, source_target_pairs={{0,2},{1,3},{2,0},{3,1},{4,6},{5,7},{6,4},{7,5},{8,10},{9,11},{10,... | collective-permute-start | bytes 2359304 | tf_op jit(solution)/shard_map/ppermute | solution.py:84
  416.8 28.6 %collective-permute-start.37 = (bf16[192,2048]{1,0:T(8,128)(2,1)}, bf16[192,2048]{1,0:T(8,128)(2,1)}, u32[]{:S(2)}, u32[]{:S(2)}) collective-permute-start(bf16[192,2048]{1,0:T(8,128)(2,1)} %add_convert_fusion.5), channel_id=1, source_target_pairs={{0,1},{1,0},{2,3},{3,2},{4,5},{5,4},{6,7},{7,6},{8,9},{9,8},{10,11... | collective-permute-start | bytes 2359304 | tf_op jit(solution)/shard_map/ppermute | solution.py:84
  419.6 25.8 %collective-permute-start.35 = (bf16[192,2048]{1,0:T(8,128)(2,1)}, bf16[192,2048]{1,0:T(8,128)(2,1)}, u32[]{:S(2)}, u32[]{:S(2)}) collective-permute-start(bf16[192,2048]{1,0:T(8,128)(2,1)} %add_convert_fusion.6), channel_id=1, source_target_pairs={{0,2},{1,3},{2,0},{3,1},{4,6},{5,7},{6,4},{7,5},{8,10},{9,11},{10,... | collective-permute-start | bytes 2359304 | tf_op jit(solution)/shard_map/ppermute | solution.py:84
  445.4 182.9 %reduce-scatter.9.cloned.1.call-start = ((), (), s32[]{:S(2)}) async-start(), calls=%async_computation.10 | async-start | bytes 1310720 | tf_op jit(solution)/shard_map/reduce_scatter | solution.py:890
  458.6 7.2 %collective-permute-start.39 = (bf16[1024,2048]{1,0:T(8,128)(2,1)S(1)}, bf16[1024,2048]{1,0:T(8,128)(2,1)S(1)}, u32[]{:S(2)}, u32[]{:S(2)}) collective-permute-start(bf16[1024,2048]{1,0:T(8,128)(2,1)S(1)} %convolution_convert_fusion), channel_id=1, source_target_pairs={{0,4},{4,0},{8,12},{12,8},{16,20},{20,16},{24,28},{28,24},{1,5},{5... | collective-permute-start | bytes 12582920 | tf_op jit(solution)/shard_map/ppermute | solution.py:84
  470.4 30.4 %collective-permute-start.40 = (bf16[256,2048]{1,0:T(8,128)(2,1)}, bf16[256,2048]{1,0:T(8,128)(2,1)}, u32[]{:S(2)}, u32[]{:S(2)}) collective-permute-start(bf16[256,2048]{1,0:T(8,128)(2,1)} %get-tuple-element.203), channel_id=1, source_target_pairs={{0,1},{1,0},{2,3},{3,2},{4,5},{5,4},{6,7},{7,6},{8,9},{9,8},{10,11... | collective-permute-start | bytes 3145736 | tf_op jit(solution)/shard_map/ppermute | solution.py:84
  472.1 47.7 %collective-permute-start.41 = (bf16[256,2048]{1,0:T(8,128)(2,1)}, bf16[256,2048]{1,0:T(8,128)(2,1)}, u32[]{:S(2)}, u32[]{:S(2)}) collective-permute-start(bf16[256,2048]{1,0:T(8,128)(2,1)} %get-tuple-element.202), channel_id=1, source_target_pairs={{0,2},{1,3},{2,0},{3,1},{4,6},{5,7},{6,4},{7,5},{8,10},{9,11},{10,... | collective-permute-start | bytes 3145736 | tf_op jit(solution)/shard_map/ppermute | solution.py:84
  472.6 47.2 %collective-permute-start.42 = (bf16[256,2048]{1,0:T(8,128)(2,1)}, bf16[256,2048]{1,0:T(8,128)(2,1)}, u32[]{:S(2)}, u32[]{:S(2)}) collective-permute-start(bf16[256,2048]{1,0:T(8,128)(2,1)} %get-tuple-element.201), channel_id=1, source_target_pairs={{0,3},{1,2},{2,1},{3,0},{4,7},{5,6},{6,5},{7,4},{8,11},{9,10},{10,... | collective-permute-start | bytes 3145736 | tf_op jit(solution)/shard_map/ppermute | solution.py:84
  526.1 16.8 %collective-permute-start.43 = (bf16[1024,2048]{1,0:T(8,128)(2,1)}, bf16[1024,2048]{1,0:T(8,128)(2,1)}, u32[]{:S(2)}, u32[]{:S(2)}) collective-permute-start(bf16[1024,2048]{1,0:T(8,128)(2,1)} %ffn_weight.5), channel_id=1, source_target_pairs={{0,4},{4,0},{8,12},{12,8},{16,20},{20,16},{24,28},{28,24},{1,5},{5... | collective-permute-start | bytes 12582920 | tf_op jit(solution)/shard_map/ppermute | solution.py:84
  528.2 7.7 %collective-permute-start.44 = (bf16[3,2,1,512,256]{4,3,1,0,2:T(8,128)(2,1)S(1)}, bf16[3,2,1,512,256]{4,3,1,0,2:T(8,128)(2,1)S(1)}, u32[]{:S(2)}, u32[]{:S(2)}) collective-permute-start(bf16[3,2,1,512,256]{4,3,1,0,2:T(8,128)(2,1)S(1)} %bitcast_convert_fusion), channel_id=1, source_target_pairs={{0,4},{4,0},{8,12},{12,8},{16,20},{20,16},{24,28},{28,24},{1,5},{5... | collective-permute-start | bytes 4718600 | tf_op jit(solution)/shard_map/ppermute | solution.py:84
  538.4 14.5 %collective-permute-start.45 = (bf16[3,2,1,128,256]{4,3,2,1,0:T(8,128)(2,1)S(1)}, bf16[3,2,1,128,256]{4,3,2,1,0:T(8,128)(2,1)S(1)}, u32[]{:S(2)}, u32[]{:S(2)}) collective-permute-start(bf16[3,2,1,128,256]{4,3,2,1,0:T(8,128)(2,1)S(1)} %get-tuple-element.207), channel_id=1, source_target_pairs={{0,1},{1,0},{2,3},{3,2},{4,5},{5,4},{6,7},{7,6},{8,9},{9,8},{10,11... | collective-permute-start | bytes 1179656 | tf_op jit(solution)/shard_map/ppermute | solution.py:84
  538.8 18.9 %collective-permute-start.46 = (bf16[3,2,1,128,256]{4,3,2,1,0:T(8,128)(2,1)S(1)}, bf16[3,2,1,128,256]{4,3,2,1,0:T(8,128)(2,1)S(1)}, u32[]{:S(2)}, u32[]{:S(2)}) collective-permute-start(bf16[3,2,1,128,256]{4,3,2,1,0:T(8,128)(2,1)S(1)} %get-tuple-element.206), channel_id=1, source_target_pairs={{0,2},{1,3},{2,0},{3,1},{4,6},{5,7},{6,4},{7,5},{8,10},{9,11},{10,... | collective-permute-start | bytes 1179656 | tf_op jit(solution)/shard_map/ppermute | solution.py:84
  540.2 18.5 %collective-permute-start.47 = (bf16[3,2,1,128,256]{4,3,2,1,0:T(8,128)(2,1)S(1)}, bf16[3,2,1,128,256]{4,3,2,1,0:T(8,128)(2,1)S(1)}, u32[]{:S(2)}, u32[]{:S(2)}) collective-permute-start(bf16[3,2,1,128,256]{4,3,2,1,0:T(8,128)(2,1)S(1)} %get-tuple-element.205), channel_id=1, source_target_pairs={{0,3},{1,2},{2,1},{3,0},{4,7},{5,6},{6,5},{7,4},{8,11},{9,10},{10,... | collective-permute-start | bytes 1179656 | tf_op jit(solution)/shard_map/ppermute | solution.py:84
  550.9 48.7 %collective-permute-start.50 = (bf16[256,2048]{1,0:T(8,128)(2,1)}, bf16[256,2048]{1,0:T(8,128)(2,1)}, u32[]{:S(2)}, u32[]{:S(2)}) collective-permute-start(bf16[256,2048]{1,0:T(8,128)(2,1)} %get-tuple-element.148), channel_id=1, source_target_pairs={{0,1},{1,0},{2,3},{3,2},{4,5},{5,4},{6,7},{7,6},{8,9},{9,8},{10,11... | collective-permute-start | bytes 3145736 | tf_op jit(solution)/shard_map/ppermute | solution.py:84
  551.4 51.3 %collective-permute-start.51 = (bf16[256,2048]{1,0:T(8,128)(2,1)}, bf16[256,2048]{1,0:T(8,128)(2,1)}, u32[]{:S(2)}, u32[]{:S(2)}) collective-permute-start(bf16[256,2048]{1,0:T(8,128)(2,1)} %get-tuple-element.149), channel_id=1, source_target_pairs={{0,2},{1,3},{2,0},{3,1},{4,6},{5,7},{6,4},{7,5},{8,10},{9,11},{10,... | collective-permute-start | bytes 3145736 | tf_op jit(solution)/shard_map/ppermute | solution.py:84
  552.8 51.0 %collective-permute-start.52 = (bf16[256,2048]{1,0:T(8,128)(2,1)}, bf16[256,2048]{1,0:T(8,128)(2,1)}, u32[]{:S(2)}, u32[]{:S(2)}) collective-permute-start(bf16[256,2048]{1,0:T(8,128)(2,1)} %get-tuple-element.150), channel_id=1, source_target_pairs={{0,3},{1,2},{2,1},{3,0},{4,7},{5,6},{6,5},{7,4},{8,11},{9,10},{10,... | collective-permute-start | bytes 3145736 | tf_op jit(solution)/shard_map/ppermute | solution.py:84
  585.4 82.8 %reduce-scatter.11.cloned.1.call-start = ((), (), s32[]{:S(2)}) async-start(), calls=%async_computation.11 | async-start | bytes 1474560 | tf_op jit(solution)/shard_map/reduce_scatter | solution.py:890
  587.4 20.6 %collective-permute-start.53 = (bf16[32,2048]{1,0:T(8,128)(2,1)S(1)}, bf16[32,2048]{1,0:T(8,128)(2,1)S(1)}, u32[]{:S(2)}, u32[]{:S(2)}) collective-permute-start(bf16[32,2048]{1,0:T(8,128)(2,1)S(1)} %get-tuple-element.228), channel_id=1, source_target_pairs={{0,1},{1,0},{2,3},{3,2},{4,5},{5,4},{6,7},{7,6},{8,9},{9,8},{10,11... | collective-permute-start | bytes 393224 | tf_op jit(solution)/shard_map/ppermute | solution.py:84
  588.9 19.8 %collective-permute-start.54 = (bf16[32,2048]{1,0:T(8,128)(2,1)S(1)}, bf16[32,2048]{1,0:T(8,128)(2,1)S(1)}, u32[]{:S(2)}, u32[]{:S(2)}) collective-permute-start(bf16[32,2048]{1,0:T(8,128)(2,1)S(1)} %get-tuple-element.227), channel_id=1, source_target_pairs={{0,2},{1,3},{2,0},{3,1},{4,6},{5,7},{6,4},{7,5},{8,10},{9,11},{10,... | collective-permute-start | bytes 393224 | tf_op jit(solution)/shard_map/ppermute | solution.py:84
  599.6 9.2 %collective-permute-start.55 = (bf16[32,2048]{1,0:T(8,128)(2,1)S(1)}, bf16[32,2048]{1,0:T(8,128)(2,1)S(1)}, u32[]{:S(2)}, u32[]{:S(2)}) collective-permute-start(bf16[32,2048]{1,0:T(8,128)(2,1)S(1)} %get-tuple-element.226), channel_id=1, source_target_pairs={{0,3},{1,2},{2,1},{3,0},{4,7},{5,6},{6,5},{7,4},{8,11},{9,10},{10,... | collective-permute-start | bytes 393224 | tf_op jit(solution)/shard_map/ppermute | solution.py:84
  629.8 4.8 collective-permute-start.58
  634.7 19.9 %collective-permute-start.59 = (f32[177,128]{1,0:T(8,128)S(1)}, f32[177,128]{1,0:T(8,128)S(1)}, u32[]{:S(2)}, u32[]{:S(2)}) collective-permute-start(f32[177,128]{1,0:T(8,128)S(1)} %fusion.43), channel_id=1, source_target_pairs={{0,16},{4,20},{8,24},{12,28},{16,0},{20,4},{24,8},{28,12},{1,17},{... | collective-permute-start | bytes 271880 | tf_op jit(solution)/shard_map/ppermute | solution.py:84
  654.6 13.6 %collective-permute-start.60 = (f32[177,128]{1,0:T(8,128)S(1)}, f32[177,128]{1,0:T(8,128)S(1)}, u32[]{:S(2)}, u32[]{:S(2)}) collective-permute-start(f32[177,128]{1,0:T(8,128)S(1)} %add.495), channel_id=1, source_target_pairs={{0,1},{1,0},{2,3},{3,2},{4,5},{5,4},{6,7},{7,6},{8,9},{9,8},{10,11... | collective-permute-start | bytes 271880 | tf_op jit(solution)/shard_map/ppermute | solution.py:84
  (71 other events, 652.5 us)
Sparse Core Ops, SparseCore 0:
  12.5 34.6 all-gather.4
  48.7 32.1 all-gather.6
  82.5 83.4 all-gather.8
  167.5 80.7 all-gather.10
  393.8 98.1 reduce-scatter.6
  494.2 87.9 reduce-scatter.4
  585.6 42.6 reduce-scatter.8
  630.7 36.4 reduce-scatter.10

commit v5 on v4

--- a/solution.py
+++ b/solution.py
@@ -14,7 +14,7 @@
 FF = 8192
 CHIP_ROWS = 1024
 KEY_ROWS = 2 * CHIP_ROWS
-KEY_BLOCK = 256
+KEY_BLOCK = 512
 HEAD_GROUP = 4
 
 

time: 681 us -> 671 us (0.985); the launches traced: 686 us -> 662 us
  waiting for transfers between devices: 252 us -> 227 us
    reduce_scatter x2, waiting for transfers between devices: 18.4 us -> 0.02 us  [scatter_chips(): lax.psum_scatter(part, 'dp', scatter_dimension=1, axis_index_groups=parit...]
    reduce_scatter x2, waiting for transfers between devices: 12.5 us -> 4.14 us  [scatter_columns(): return lax.psum_scatter(full, 'dp', scatter_dimension=1, tiled=True)]
  transfers between devices with their start and end apart: 70 -> 70, of which waited for: 30 -> 27; matrix products, arithmetic and copies ran while one was open for 12% -> 13% of each run, Pallas kernels for 33% -> 36%
where the time goes in v5:
time: 671 us; the launch traced here: 662 us
  Pallas kernels  240 us (36%)
  waiting for transfers between devices  227 us (34%)
  starting transfers between devices  57.9 us (9%)
  local copies, waits for them, and re-layouts  54.1 us (8%)
  other arithmetic  41.7 us (6%)
  between operations  17.2 us (3%)
  blocking collectives  16.6 us (2%)
  matrix products  7.8 us (1%)
    ppermute x60, waiting for transfers between devices, swap(): lax.ppermute(value, axis, [(source, source ^ step) for source in range(co...  221 us
    ppermute x60, starting transfers between devices, swap(): lax.ppermute(value, axis, [(source, source ^ step) for source in range(co...  56.2 us
    pallas_call x3, Pallas kernels, ffn_weight(): pl.pallas_call(functools.partial(ffn_weight_kernel, lefts=len(lefts)), na...  52.6 us
    pallas_call x2, Pallas kernels, ffn_product(): pl.pallas_call(functools.partial(ffn_product_kernel, lefts=len(lefts)), n...  37 us
    unnamed x147, local copies, waits for them, and re-layouts  26 us
    pallas_call x1, Pallas kernels, ffn_back(): pl.pallas_call(functools.partial(ffn_back_kernel, count=len(pieces)), nam...  24.9 us
    pallas_call x1, Pallas kernels, ffn_up(): pl.pallas_call(ffn_up_kernel, name='ffn_up', grid=(units // tile,), in_sp...  22.1 us
    pallas_call x2, Pallas kernels, onto_columns(): pl.pallas_call(functools.partial(onto_columns_kernel, lefts=len(lefts)),...  17.7 us
  transfers between devices with their start and end apart: 70, of which 27 were waited for; matrix products, arithmetic and copies ran while one was open for 13% of the time, Pallas kernels for 36%

profile of v5, /device:TPU:0, one launch (start us, length us, event | category | flops | bytes accessed | tf_op | source)
XLA Modules:
  0.0 661.9 jit_solution(12350747156011514337)
XLA Ops:
  7.2 2.8 convert.28
  13.2 3.2 fusion.31
  17.0 16.6 %all_gather.16 = bf16[64,2048]{1,0:T(8,128)(2,1)S(1)} all-gather(bf16[64,256]{1,0:T(8,128)(2,1)S(1)} %slice-done), channel_id=1, replica_groups=mesh['dp'=8,'tp'=4] {'dp'}, dimensions={1}, use_global_device_ids=true | all-gather | bytes 294912 | tf_op jit(solution)/shard_map/all_gather | solution.py:767
  48.0 3.3 constant_dynamic-slice_fusion.8
  59.1 18.2 %collective-permute-done.refs_3_ = bf16[256,2048]{1,0:T(8,128)(2,1)S(1)} collective-permute-done((bf16[256,2048]{1,0:T(8,128)(2,1)S(1)}, bf16[256,2048]{1,0:T(8,128)(2,1)S(1)}, u32[]{:S(2)}, u32[]{:S(2)}) %collective-permute-start) | collective-permute-done | bytes 1048608 | tf_op jit(solution)/shard_map/ppermute | solution.py:84
  77.4 23.2 %collective-permute-done.1.refs_4_ = bf16[256,2048]{1,0:T(8,128)(2,1)} collective-permute-done((bf16[256,2048]{1,0:T(8,128)(2,1)S(1)}, bf16[256,2048]{1,0:T(8,128)(2,1)}, u32[]{:S(2)}, u32[]{:S(2)}) %collective-permute-start.1) | collective-permute-done | bytes 1048608 | tf_op jit(solution)/shard_map/ppermute | solution.py:84
  108.2 4.5 collective-permute-done.10.refs_1_
  112.7 4.8 collective-permute-done.11.refs_2_
  117.5 1.9 collective-permute-done.12.refs_3_
  121.5 3.1 constant_dynamic-slice_fusion.6
  130.1 7.0 %place_keys.1 = (bf16[3,2048,128]{2,1,0:T(8,128)(2,1)}, bf16[3,128,2048]{2,1,0:T(8,128)(2,1)}, bf16[3,2048,128]{2,1,0:T(8,128)(2,1)}, bf16[3,128,2048]{2,1,0:T(8,128)(2,1)}) custom-call(s32[8]{0:T(128)} %stack.45.starts, bf16[2,3,128,256]{3,2,1,0:T(8,128)(2,1)} %copy-done.41, bf16[2,3,128,256]{3,2,1,0:T(8,128)(2,1)} %copy-done.44, ...), custom_call_target="tpu_custom_call" | custom-call | flops 1048576 | bytes 1048576 | tf_op jit(solution)/shard_map/place_keys/pallas_call | solution.py:581
  138.6 8.6 %onto_rows.2 = bf16[384,2048]{1,0:T(8,128)(2,1)} custom-call(bf16[384,2048]{1,0:T(8,128)(2,1)} %copy-done.18, f32[1,2048]{1,0:T(1,128)} %bitcast.3.refs_1_, bf16[256,2048]{1,0:T(8,128)(2,1)} %copy-done.25, bf16[256,2048]{1,0:T(8,128)(2,1)} %copy-done.27, bf16[256,2048]{1,0:T(8,128)(2,1)} %collective-permute-done.1.refs_4_, ...), custom_call_target="tpu_custom_call" | custom-call | flops 1048576 | bytes 1048576 | tf_op jit(solution)/shard_map/onto_rows/pallas_call | solution.py:520
  148.7 11.3 %attend_forward.1 = (bf16[3,128,2048]{2,1,0:T(8,128)(2,1)S(1)}, f32[3,4,1,512]{3,2,1,0:T(1,128)S(1)}) custom-call(s32[3,2]{1,0:T(4,128)S(1)} %stack.36.bounds, bf16[3,128,2048]{2,1,0:T(8,128)(2,1)S(1)} %bitcast.107, bf16[3,2048,128]{2,1,0:T(8,128)(2,1)S(1)} %copy-done.5, bf16[3,128,2048]{2,1,0:T(8,128)(2,1)S(1)} %copy-done.9, ...), custom_call_target="tpu_custom_call" | custom-call | flops 1048576 | bytes 1048576 | tf_op jit(solution)/shard_map/attend_forward/pallas_call | solution.py:262
  161.1 12.7 %collective-permute-done.18.refs_3_.refs_4_ = bf16[256,2048]{1,0:T(8,128)(2,1)} collective-permute-done((bf16[256,2048]{1,0:T(8,128)(2,1)}, bf16[256,2048]{1,0:T(8,128)(2,1)}, u32[]{:S(2)}, u32[]{:S(2)}) %collective-permute-start.18) | collective-permute-done | bytes 1048608 | tf_op jit(solution)/shard_map/ppermute | solution.py:84
  174.3 3.5 collective-permute-done.20.refs_6_.refs_7_
  177.8 1.9 collective-permute-done.21.refs_7_.refs_8_
  182.1 8.3 %onto_columns.2 = f32[384,2048]{1,0:T(8,128)} custom-call(bf16[384,2048]{1,0:T(8,128)(2,1)} %bitcast.110, bf16[256,2048]{1,0:T(8,128)(2,1)} %get-tuple-element.105.refs_1_.refs_2_, bf16[256,2048]{1,0:T(8,128)(2,1)} %collective-permute-done.17.refs_2_.refs_3_, bf16[256,2048]{1,0:T(8,128)(2,1)} %collective-permute-done.18.refs_3_.refs_4_, ...), custom_call_target="tpu_custom_call" | custom-call | flops 1048576 | bytes 1048576 | tf_op jit(solution)/shard_map/onto_columns/pallas_call | solution.py:550
  190.5 2.6 fusion.27
  194.1 2.6 add_convert_fusion.2
  199.6 33.6 %collective-permute-done.23.refs_1_.refs_2_ = bf16[384,2048]{1,0:T(8,128)(2,1)S(1)} collective-permute-done((bf16[384,2048]{1,0:T(8,128)(2,1)S(1)}, bf16[384,2048]{1,0:T(8,128)(2,1)S(1)}, u32[]{:S(2)}, u32[]{:S(2)}) %collective-permute-start.23) | collective-permute-done | bytes 1572896 | tf_op jit(solution)/shard_map/ppermute | solution.py:84
  233.2 1.8 collective-permute-start.25
  236.9 15.4 %collective-permute-done.25.refs_3_.refs_4_ = bf16[192,2048]{1,0:T(8,128)(2,1)} collective-permute-done((bf16[192,2048]{1,0:T(8,128)(2,1)S(1)}, bf16[192,2048]{1,0:T(8,128)(2,1)}, u32[]{:S(2)}, u32[]{:S(2)}) %collective-permute-start.25) | collective-permute-done | bytes 786464 | tf_op jit(solution)/shard_map/ppermute | solution.py:84
  252.2 2.6 collective-permute-done.26.refs_4_.refs_5_
  258.9 22.1 %ffn_up.1 = (f32[1536,2048]{1,0:T(8,128)}, bf16[1536,2048]{1,0:T(8,128)(2,1)}) custom-call(bf16[384,2048]{1,0:T(8,128)(2,1)} %copy-done.21, bf16[384,2048]{1,0:T(8,128)(2,1)} %copy-done.23, bf16[384,2048]{1,0:T(8,128)(2,1)} %copy-done.24, bf16[192,2048]{1,0:T(8,128)(2,1)} %collective-permute-done.25.refs_3_.refs_4_, ...), custom_call_target="tpu_custom_call" | custom-call | flops 1048576 | bytes 1048576 | tf_op jit(solution)/shard_map/ffn_up/pallas_call | solution.py:406
  281.0 18.4 %ffn_product.2 = (bf16[384,2048]{1,0:T(8,128)(2,1)}, bf16[384,2048]{1,0:T(8,128)(2,1)}, bf16[384,2048]{1,0:T(8,128)(2,1)}, bf16[384,2048]{1,0:T(8,128)(2,1)}) custom-call(bf16[1536,2048]{1,0:T(8,128)(2,1)} %get-tuple-element.109.refs_0_, bf16[2048,2048]{1,0:T(8,128)(2,1)} %all-gather.11.cloned.1.call-done.refs_1_.refs_4_), custom_call_target="tpu_custom_call" | custom-call | flops 1048576 | bytes 1048576 | tf_op jit(solution)/shard_map/ffn_product/pallas_call | solution.py:449
  302.9 24.0 %collective-permute-done.32.refs_4_.refs_3_ = bf16[384,2048]{1,0:T(8,128)(2,1)} collective-permute-done((bf16[384,2048]{1,0:T(8,128)(2,1)}, bf16[384,2048]{1,0:T(8,128)(2,1)}, u32[]{:S(2)}, u32[]{:S(2)}) %collective-permute-start.32) | collective-permute-done | bytes 1572896 | tf_op jit(solution)/shard_map/ppermute | solution.py:84
  326.9 23.2 %ffn_weight.3 = bf16[2048,2048]{1,0:T(8,128)(2,1)} custom-call(bf16[1536,2048]{1,0:T(8,128)(2,1)} %get-tuple-element.109.refs_0_, bf16[384,2048]{1,0:T(8,128)(2,1)} %bitcast.16.refs_1_.refs_0_, bf16[384,2048]{1,0:T(8,128)(2,1)} %collective-permute-done.30.refs_2_.refs_1_, bf16[384,2048]{1,0:T(8,128)(2,1)} %collective-permute-done.31.refs_3_.refs_2_, ...), custom_call_target="tpu_custom_call" | custom-call | flops 1048576 | bytes 1048576 | tf_op jit(solution)/shard_map/ffn_weight/pallas_call | solution.py:465
  350.1 24.9 %ffn_back.1 = (bf16[1536,2048]{1,0:T(8,128)(2,1)}, f32[1,2048]{1,0:T(1,128)}) custom-call(bf16[384,2048]{1,0:T(8,128)(2,1)} %bitcast.16.refs_1_.refs_0_, bf16[384,2048]{1,0:T(8,128)(2,1)} %collective-permute-done.30.refs_2_.refs_1_, bf16[384,2048]{1,0:T(8,128)(2,1)} %collective-permute-done.31.refs_3_.refs_2_, ...), custom_call_target="tpu_custom_call" | custom-call | flops 1048576 | bytes 1048576 | tf_op jit(solution)/shard_map/ffn_back/pallas_call | solution.py:430
  375.1 18.6 %ffn_product.3 = (bf16[384,2048]{1,0:T(8,128)(2,1)}, bf16[192,2048]{1,0:T(8,128)(2,1)}, bf16[192,2048]{1,0:T(8,128)(2,1)}, bf16[192,2048]{1,0:T(8,128)(2,1)}, bf...) custom-call(bf16[1536,2048]{1,0:T(8,128)(2,1)} %get-tuple-element.132.refs_0_, ...), custom_call_target="tpu_custom_call" | custom-call | flops 1048576 | bytes 1048576 | tf_op jit(solution)/shard_map/ffn_product/pallas_call | solution.py:449
  397.9 16.6 %collective-permute-done.36 = bf16[192,2048]{1,0:T(8,128)(2,1)S(1)} collective-permute-done((bf16[192,2048]{1,0:T(8,128)(2,1)}, bf16[192,2048]{1,0:T(8,128)(2,1)S(1)}, u32[]{:S(2)}, u32[]{:S(2)}) %collective-permute-start.36) | collective-permute-done | bytes 786464 | tf_op jit(solution)/shard_map/ppermute | solution.py:84
  414.5 2.3 add_convert_fusion.5
  417.3 2.3 add_convert_fusion.6
  420.9 23.0 %ffn_weight.4 = bf16[2048,2048]{1,0:T(8,128)(2,1)} custom-call(bf16[1536,2048]{1,0:T(8,128)(2,1)} %get-tuple-element.132.refs_0_, bf16[384,2048]{1,0:T(8,128)(2,1)} %copy-done.21, bf16[384,2048]{1,0:T(8,128)(2,1)} %copy-done.23, bf16[384,2048]{1,0:T(8,128)(2,1)} %copy-done.24, bf16[192,2048]{1,0:T(8,128)(2,1)} %collective-permute-done.25.refs_3_.refs_4_, ...), custom_call_target="tpu_custom_call" | custom-call | flops 1048576 | bytes 1048576 | tf_op jit(solution)/shard_map/ffn_weight/pallas_call | solution.py:465
  446.2 8.3 %norm_back.1 = (f32[384,2048]{1,0:T(8,128)}, bf16[384,2048]{1,0:T(8,128)(2,1)}, f32[8,2048]{1,0:T(8,128)}) custom-call(bf16[384,2048]{1,0:T(8,128)(2,1)} %get-tuple-element.133.refs_0_, bf16[384,2048]{1,0:T(8,128)(2,1)} %bitcast.16.refs_1_.refs_0_, f32[384,2048]{1,0:T(8,128)} %get-tuple-element.200.refs_2_, f32[384,1]{1,0:T(8,128)} %rsqrt.20.refs_3_, ...), custom_call_target="tpu_custom_call" | custom-call | flops 1048576 | bytes 1048576 | tf_op jit(solution)/shard_map/norm_back/pallas_call | solution.py:628
  454.6 4.0 convolution_convert_fusion
  458.7 5.5 add_convert_fusion.1
  465.8 2.5 add_convert_fusion
  468.3 2.1 fusion.30
  474.5 8.7 %onto_rows.3 = bf16[384,2048]{1,0:T(8,128)(2,1)} custom-call(bf16[384,2048]{1,0:T(8,128)(2,1)} %get-tuple-element.141.refs_0_, f32[1,2048]{1,0:T(1,128)} %reshape.215.refs_1_, bf16[256,2048]{1,0:T(8,128)(2,1)} %get-tuple-element.105.refs_1_.refs_2_, bf16[256,2048]{1,0:T(8,128)(2,1)} %collective-permute-done.17.refs_2_.refs_3_, ...), custom_call_target="tpu_custom_call" | custom-call | flops 1048576 | bytes 1048576 | tf_op jit(solution)/shard_map/onto_rows/pallas_call | solution.py:520
  486.1 16.7 %attend_backward.1 = (bf16[3,128,2048]{2,1,0:T(8,128)(2,1)S(1)}, f32[3,2048,256]{2,1,0:T(8,128)}) custom-call(s32[3,2]{1,0:T(4,128)S(1)} %stack.36.bounds, bf16[3,128,2048]{2,1,0:T(8,128)(2,1)S(1)} %bitcast.108, bf16[3,128,2048]{2,1,0:T(8,128)(2,1)S(1)} %bitcast.109, bf16[3,2048,128]{2,1,0:T(8,128)(2,1)S(1)} %copy-done.6, ...), custom_call_target="tpu_custom_call" | custom-call | flops 1048576 | bytes 1048576 | tf_op jit(solution)/shard_map/attend_backward/pallas_call | solution.py:297
  504.1 15.7 %collective-permute-done.41 = bf16[256,2048]{1,0:T(8,128)(2,1)} collective-permute-done((bf16[256,2048]{1,0:T(8,128)(2,1)}, bf16[256,2048]{1,0:T(8,128)(2,1)}, u32[]{:S(2)}, u32[]{:S(2)}) %collective-permute-start.41) | collective-permute-done | bytes 1048608 | tf_op jit(solution)/shard_map/ppermute | solution.py:84
  519.8 6.4 ffn_weight.5
  526.2 2.1 bitcast_convert_fusion
  533.0 3.0 collective-permute-done.44
  536.0 2.2 bitcast_add_fusion
  539.4 2.6 collective-permute-start.47
  543.0 7.9 %weight_pieces.1 = (bf16[256,2048]{1,0:T(8,128)(2,1)}, bf16[256,2048]{1,0:T(8,128)(2,1)}, bf16[256,2048]{1,0:T(8,128)(2,1)}, bf16[256,2048]{1,0:T(8,128)(2,1)}) custom-call(bf16[384,2048]{1,0:T(8,128)(2,1)} %bitcast.104, bf16[384,2048]{1,0:T(8,128)(2,1)} %copy-done.18, bf16[1024,2048]{1,0:T(8,128)(2,1)} %collective-permute-done.43.add_ref), custom_call_target="tpu_custom_call" | custom-call | flops 1048576 | bytes 1048576 | tf_op jit(solution)/shard_map/weight_pieces/pallas_call | solution.py:490
  551.9 2.6 collective-permute-start.52
  554.4 4.5 collective-permute-done.47
  559.9 3.6 add_convert_fusion.4
  563.5 6.3 adam_rows.3
  569.8 4.1 reduce-scatter.5.cloned.1.call-done.grads
  582.2 9.3 %onto_columns.3 = f32[384,2048]{1,0:T(8,128)} custom-call(bf16[384,2048]{1,0:T(8,128)(2,1)} %bitcast.105, bf16[384,256]{1,0:T(8,128)(2,1)} %bitcast.119, bf16[256,2048]{1,0:T(8,128)(2,1)} %copy-done.25, bf16[256,2048]{1,0:T(8,128)(2,1)} %copy-done.27, bf16[256,2048]{1,0:T(8,128)(2,1)} %collective-permute-done.1.refs_4_, ...), custom_call_target="tpu_custom_call" | custom-call | flops 1048576 | bytes 1048576 | tf_op jit(solution)/shard_map/onto_columns/pallas_call | solution.py:550
  592.0 12.0 %collective-permute-done.52 = bf16[256,2048]{1,0:T(8,128)(2,1)} collective-permute-done((bf16[256,2048]{1,0:T(8,128)(2,1)}, bf16[256,2048]{1,0:T(8,128)(2,1)}, u32[]{:S(2)}, u32[]{:S(2)}) %collective-permute-start.52) | collective-permute-done | bytes 1048608 | tf_op jit(solution)/shard_map/ppermute | solution.py:84
  604.0 2.6 add_convert_fusion.3
  611.5 2.1 collective-permute-start.58
  613.6 3.0 collective-permute-done.58
  616.6 3.1 collective-permute-start.59
  619.8 9.9 %collective-permute-done.59 = f32[177,128]{1,0:T(8,128)S(1)} collective-permute-done((f32[177,128]{1,0:T(8,128)S(1)}, f32[177,128]{1,0:T(8,128)S(1)}, u32[]{:S(2)}, u32[]{:S(2)}) %collective-permute-start.59) | collective-permute-done | bytes 90656 | tf_op jit(solution)/shard_map/ppermute | solution.py:84
  629.6 2.7 collective-permute-start.60
  632.3 5.1 fusion.13
  637.5 6.3 adam_rows.4
  645.0 3.4 collective-permute-done.61
  650.2 4.3 adam_rows.5
  (348 shorter events, 103.3 us)
Async XLA Ops:
  7.2 40.8 %all-gather.5.cloned.1.call-start = ((), (), s32[]{:S(2)}) async-start(), calls=%async_computation.4 | async-start | bytes 2359296 | tf_op jit(solution)/shard_map/all_gather | solution.py:767
  12.3 109.1 %all-gather.7.cloned.1.call-start = ((), (), s32[]{:S(2)}) async-start(), calls=%async_computation.5 | async-start | bytes 2359296 | tf_op jit(solution)/shard_map/all_gather | solution.py:767
  13.1 245.8 %all-gather.9.cloned.1.call-start = ((), (), s32[]{:S(2)}) async-start(), calls=%async_computation.6 | async-start | bytes 9437184 | tf_op jit(solution)/shard_map/all_gather | solution.py:767
  16.4 264.7 %all-gather.11.cloned.1.call-start = ((), (), s32[]{:S(2)}) async-start(), calls=%async_computation.7 | async-start | bytes 9437184 | tf_op jit(solution)/shard_map/all_gather | solution.py:767
  16.9 546.6 %reduce-scatter.7.cloned.1.call-start = ((), (), s32[]{:S(2)}) async-start(), calls=%async_computation.9 | async-start | bytes 9437184 | tf_op jit(solution)/shard_map/reduce_scatter | solution.py:835
  33.6 19.2 %collective-permute-start.6 = (bf16[64,2048]{1,0:T(8,128)(2,1)S(1)}, bf16[64,2048]{1,0:T(8,128)(2,1)}, u32[]{:S(2)}, u32[]{:S(2)}) collective-permute-start(bf16[64,2048]{1,0:T(8,128)(2,1)S(1)} %all_gather.16), channel_id=1, source_target_pairs={{0,1},{1,0},{2,3},{3,2},{4,5},{5,4},{6,7},{7,6},{8,9},{9,8},{10,11... | collective-permute-start | bytes 786440 | tf_op jit(solution)/shard_map/ppermute | solution.py:84
  35.1 20.7 %collective-permute-start.7 = (bf16[64,2048]{1,0:T(8,128)(2,1)S(1)}, bf16[64,2048]{1,0:T(8,128)(2,1)}, u32[]{:S(2)}, u32[]{:S(2)}) collective-permute-start(bf16[64,2048]{1,0:T(8,128)(2,1)S(1)} %all_gather.16), channel_id=1, source_target_pairs={{0,2},{1,3},{2,0},{3,1},{4,6},{5,7},{6,4},{7,5},{8,10},{9,11},{10,... | collective-permute-start | bytes 786440 | tf_op jit(solution)/shard_map/ppermute | solution.py:84
  36.6 20.2 %collective-permute-start.8 = (bf16[64,2048]{1,0:T(8,128)(2,1)S(1)}, bf16[64,2048]{1,0:T(8,128)(2,1)}, u32[]{:S(2)}, u32[]{:S(2)}) collective-permute-start(bf16[64,2048]{1,0:T(8,128)(2,1)S(1)} %all_gather.16), channel_id=1, source_target_pairs={{0,3},{1,2},{2,1},{3,0},{4,7},{5,6},{6,5},{7,4},{8,11},{9,10},{10,... | collective-permute-start | bytes 786440 | tf_op jit(solution)/shard_map/ppermute | solution.py:84
  51.3 26.1 %collective-permute-start = (bf16[256,2048]{1,0:T(8,128)(2,1)S(1)}, bf16[256,2048]{1,0:T(8,128)(2,1)S(1)}, u32[]{:S(2)}, u32[]{:S(2)}) collective-permute-start(bf16[256,2048]{1,0:T(8,128)(2,1)S(1)} %get-tuple-element.223.refs_2_), channel_id=1, source_target_pairs={{0,1},{1,0},{2,3},{3,2},{4,5},{5,4},{6,7},{7,6},{8,9},{9,8},{10,11... | collective-permute-start | bytes 3145736 | tf_op jit(solution)/shard_map/ppermute | solution.py:84
  53.7 46.9 %collective-permute-start.1 = (bf16[256,2048]{1,0:T(8,128)(2,1)S(1)}, bf16[256,2048]{1,0:T(8,128)(2,1)}, u32[]{:S(2)}, u32[]{:S(2)}) collective-permute-start(bf16[256,2048]{1,0:T(8,128)(2,1)S(1)} %get-tuple-element.223.refs_2_), channel_id=1, source_target_pairs={{0,2},{1,3},{2,0},{3,1},{4,6},{5,7},{6,4},{7,5},{8,10},{9,11},{10,... | collective-permute-start | bytes 3145736 | tf_op jit(solution)/shard_map/ppermute | solution.py:84
  55.3 45.3 %collective-permute-start.2 = (bf16[256,2048]{1,0:T(8,128)(2,1)S(1)}, bf16[256,2048]{1,0:T(8,128)(2,1)}, u32[]{:S(2)}, u32[]{:S(2)}) collective-permute-start(bf16[256,2048]{1,0:T(8,128)(2,1)S(1)} %get-tuple-element.223.refs_2_), channel_id=1, source_target_pairs={{0,3},{1,2},{2,1},{3,0},{4,7},{5,6},{6,5},{7,4},{8,11},{9,10},{10,... | collective-permute-start | bytes 3145736 | tf_op jit(solution)/shard_map/ppermute | solution.py:84
  58.4 19.0 %collective-permute-start.9 = (bf16[1,3,128,256]{3,2,1,0:T(8,128)(2,1)S(1)}, bf16[1,3,128,256]{3,2,1,0:T(8,128)(2,1)S(1)}, u32[]{:S(2)}, u32[]{:S(2)}) collective-permute-start(bf16[1,3,128,256]{3,2,1,0:T(8,128)(2,1)S(1)} %bitcast.123), channel_id=1, source_target_pairs={{8,16},{12,20},{9,17},{13,21},{10,18},{14,22},{11,19},{15,23}} | collective-permute-start | bytes 589832 | tf_op jit(solution)/shard_map/ppermute | solution.py:795
  77.4 50.5 %collective-permute-start.3 = (bf16[256,2048]{1,0:T(8,128)(2,1)S(1)}, bf16[256,2048]{1,0:T(8,128)(2,1)S(1)}, u32[]{:S(2)}, u32[]{:S(2)}) collective-permute-start(bf16[256,2048]{1,0:T(8,128)(2,1)S(1)} %collective-permute-done.refs_3_), channel_id=1, source_target_pairs={{0,4},{4,0},{8,12},{12,8},{16,20},{20,16},{24,28},{28,24},{1,5},{5... | collective-permute-start | bytes 3145736 | tf_op jit(solution)/shard_map/ppermute | solution.py:84
  100.7 12.1 %collective-permute-start.10 = (bf16[2,3,128,256]{3,2,1,0:T(8,128)(2,1)S(1)}, bf16[2,3,128,256]{3,2,1,0:T(8,128)(2,1)S(1)}, u32[]{:S(2)}, u32[]{:S(2)}) collective-permute-start(bf16[2,3,128,256]{3,2,1,0:T(8,128)(2,1)S(1)} %pad_maximum_fusion.2.refs_0_), channel_id=1, source_target_pairs={{0,1},{1,0},{2,3},{3,2},{4,5},{5,4},{6,7},{7,6},{8,9},{9,8},{10,11... | collective-permute-start | bytes 1179656 | tf_op jit(solution)/shard_map/ppermute | solution.py:84
  101.3 16.2 %collective-permute-start.11 = (bf16[2,3,128,256]{3,2,1,0:T(8,128)(2,1)S(1)}, bf16[2,3,128,256]{3,2,1,0:T(8,128)(2,1)S(1)}, u32[]{:S(2)}, u32[]{:S(2)}) collective-permute-start(bf16[2,3,128,256]{3,2,1,0:T(8,128)(2,1)S(1)} %pad_maximum_fusion.2.refs_0_), channel_id=1, source_target_pairs={{0,2},{1,3},{2,0},{3,1},{4,6},{5,7},{6,4},{7,5},{8,10},{9,11},{10,... | collective-permute-start | bytes 1179656 | tf_op jit(solution)/shard_map/ppermute | solution.py:84
  102.8 16.6 %collective-permute-start.12 = (bf16[2,3,128,256]{3,2,1,0:T(8,128)(2,1)S(1)}, bf16[2,3,128,256]{3,2,1,0:T(8,128)(2,1)}, u32[]{:S(2)}, u32[]{:S(2)}) collective-permute-start(bf16[2,3,128,256]{3,2,1,0:T(8,128)(2,1)S(1)} %pad_maximum_fusion.2.refs_0_), channel_id=1, source_target_pairs={{0,3},{1,2},{2,1},{3,0},{4,7},{5,6},{6,5},{7,4},{8,11},{9,10},{10,... | collective-permute-start | bytes 1179656 | tf_op jit(solution)/shard_map/ppermute | solution.py:84
  108.2 16.4 %collective-permute-start.13 = (bf16[2,3,128,256]{3,2,1,0:T(8,128)(2,1)S(1)}, bf16[2,3,128,256]{3,2,1,0:T(8,128)(2,1)}, u32[]{:S(2)}, u32[]{:S(2)}) collective-permute-start(bf16[2,3,128,256]{3,2,1,0:T(8,128)(2,1)S(1)} %pad_maximum_fusion.2.refs_0_), channel_id=1, source_target_pairs={{0,4},{4,0},{8,12},{12,8},{16,20},{20,16},{24,28},{28,24},{1,5},{5... | collective-permute-start | bytes 1179656 | tf_op jit(solution)/shard_map/ppermute | solution.py:84
  112.7 12.4 %collective-permute-start.14 = (bf16[2,3,128,256]{3,2,1,0:T(8,128)(2,1)S(1)}, bf16[2,3,128,256]{3,2,1,0:T(8,128)(2,1)}, u32[]{:S(2)}, u32[]{:S(2)}) collective-permute-start(bf16[2,3,128,256]{3,2,1,0:T(8,128)(2,1)S(1)} %collective-permute-done.10.refs_1_), channel_id=1, source_target_pairs={{0,4},{4,0},{8,12},{12,8},{16,20},{20,16},{24,28},{28,24},{1,5},{5... | collective-permute-start | bytes 1179656 | tf_op jit(solution)/shard_map/ppermute | solution.py:84
  117.5 7.7 %collective-permute-start.15 = (bf16[2,3,128,256]{3,2,1,0:T(8,128)(2,1)S(1)}, bf16[2,3,128,256]{3,2,1,0:T(8,128)(2,1)}, u32[]{:S(2)}, u32[]{:S(2)}) collective-permute-start(bf16[2,3,128,256]{3,2,1,0:T(8,128)(2,1)S(1)} %collective-permute-done.11.refs_2_), channel_id=1, source_target_pairs={{0,4},{4,0},{8,12},{12,8},{16,20},{20,16},{24,28},{28,24},{1,5},{5... | collective-permute-start | bytes 1179656 | tf_op jit(solution)/shard_map/ppermute | solution.py:84
  119.5 6.6 %collective-permute-start.16 = (bf16[2,3,128,256]{3,2,1,0:T(8,128)(2,1)}, bf16[2,3,128,256]{3,2,1,0:T(8,128)(2,1)}, u32[]{:S(2)}, u32[]{:S(2)}) collective-permute-start(bf16[2,3,128,256]{3,2,1,0:T(8,128)(2,1)} %collective-permute-done.12.refs_3_), channel_id=1, source_target_pairs={{0,4},{4,0},{8,12},{12,8},{16,20},{20,16},{24,28},{28,24},{1,5},{5... | collective-permute-start | bytes 1179656 | tf_op jit(solution)/shard_map/ppermute | solution.py:84
  124.6 12.5 %collective-permute-start.4 = (bf16[256,2048]{1,0:T(8,128)(2,1)}, bf16[256,2048]{1,0:T(8,128)(2,1)S(1)}, u32[]{:S(2)}, u32[]{:S(2)}) collective-permute-start(bf16[256,2048]{1,0:T(8,128)(2,1)} %collective-permute-done.1.refs_4_), channel_id=1, source_target_pairs={{0,4},{4,0},{8,12},{12,8},{16,20},{20,16},{24,28},{28,24},{1,5},{5... | collective-permute-start | bytes 3145736 | tf_op jit(solution)/shard_map/ppermute | solution.py:84
  125.1 12.0 %collective-permute-start.5 = (bf16[256,2048]{1,0:T(8,128)(2,1)}, bf16[256,2048]{1,0:T(8,128)(2,1)S(1)}, u32[]{:S(2)}, u32[]{:S(2)}) collective-permute-start(bf16[256,2048]{1,0:T(8,128)(2,1)} %collective-permute-done.2.refs_5_), channel_id=1, source_target_pairs={{0,4},{4,0},{8,12},{12,8},{16,20},{20,16},{24,28},{28,24},{1,5},{5... | collective-permute-start | bytes 3145736 | tf_op jit(solution)/shard_map/ppermute | solution.py:84
  125.2 35.9 %collective-permute-start.17 = (bf16[256,2048]{1,0:T(8,128)(2,1)}, bf16[256,2048]{1,0:T(8,128)(2,1)}, u32[]{:S(2)}, u32[]{:S(2)}) collective-permute-start(bf16[256,2048]{1,0:T(8,128)(2,1)} %get-tuple-element.105.refs_1_.refs_2_), channel_id=1, source_target_pairs={{0,1},{1,0},{2,3},{3,2},{4,5},{5,4},{6,7},{7,6},{8,9},{9,8},{10,11... | collective-permute-start | bytes 3145736 | tf_op jit(solution)/shard_map/ppermute | solution.py:84
  126.1 47.7 %collective-permute-start.18 = (bf16[256,2048]{1,0:T(8,128)(2,1)}, bf16[256,2048]{1,0:T(8,128)(2,1)}, u32[]{:S(2)}, u32[]{:S(2)}) collective-permute-start(bf16[256,2048]{1,0:T(8,128)(2,1)} %get-tuple-element.105.refs_1_.refs_2_), channel_id=1, source_target_pairs={{0,2},{1,3},{2,0},{3,1},{4,6},{5,7},{6,4},{7,5},{8,10},{9,11},{10,... | collective-permute-start | bytes 3145736 | tf_op jit(solution)/shard_map/ppermute | solution.py:84
  127.9 45.9 %collective-permute-start.19 = (bf16[256,2048]{1,0:T(8,128)(2,1)}, bf16[256,2048]{1,0:T(8,128)(2,1)}, u32[]{:S(2)}, u32[]{:S(2)}) collective-permute-start(bf16[256,2048]{1,0:T(8,128)(2,1)} %get-tuple-element.105.refs_1_.refs_2_), channel_id=1, source_target_pairs={{0,3},{1,2},{2,1},{3,0},{4,7},{5,6},{6,5},{7,4},{8,11},{9,10},{10,... | collective-permute-start | bytes 3145736 | tf_op jit(solution)/shard_map/ppermute | solution.py:84
  173.8 5.9 collective-permute-start.21
  174.3 6.9 %collective-permute-start.22 = (bf16[256,2048]{1,0:T(8,128)(2,1)}, bf16[256,2048]{1,0:T(8,128)(2,1)S(1)}, u32[]{:S(2)}, u32[]{:S(2)}) collective-permute-start(bf16[256,2048]{1,0:T(8,128)(2,1)} %collective-permute-done.19.refs_4_.refs_5_), channel_id=1, source_target_pairs={{0,4},{4,0},{8,12},{12,8},{16,20},{20,16},{24,28},{28,24},{1,5},{5... | collective-permute-start | bytes 3145736 | tf_op jit(solution)/shard_map/ppermute | solution.py:84
  196.7 36.4 %collective-permute-start.23 = (bf16[384,2048]{1,0:T(8,128)(2,1)S(1)}, bf16[384,2048]{1,0:T(8,128)(2,1)S(1)}, u32[]{:S(2)}, u32[]{:S(2)}) collective-permute-start(bf16[384,2048]{1,0:T(8,128)(2,1)S(1)} %get-tuple-element.199.refs_0_.refs_1_), channel_id=1, source_target_pairs={{0,1},{1,0},{2,3},{3,2},{4,5},{5,4},{6,7},{7,6},{8,9},{9,8},{10,11... | collective-permute-start | bytes 4718600 | tf_op jit(solution)/shard_map/ppermute | solution.py:84
  198.1 36.9 %collective-permute-start.24 = (bf16[384,2048]{1,0:T(8,128)(2,1)S(1)}, bf16[384,2048]{1,0:T(8,128)(2,1)S(1)}, u32[]{:S(2)}, u32[]{:S(2)}) collective-permute-start(bf16[384,2048]{1,0:T(8,128)(2,1)S(1)} %get-tuple-element.199.refs_0_.refs_1_), channel_id=1, source_target_pairs={{0,2},{1,3},{2,0},{3,1},{4,6},{5,7},{6,4},{7,5},{8,10},{9,11},{10,... | collective-permute-start | bytes 4718600 | tf_op jit(solution)/shard_map/ppermute | solution.py:84
  233.2 19.0 %collective-permute-start.25 = (bf16[192,2048]{1,0:T(8,128)(2,1)S(1)}, bf16[192,2048]{1,0:T(8,128)(2,1)}, u32[]{:S(2)}, u32[]{:S(2)}) collective-permute-start(bf16[192,2048]{1,0:T(8,128)(2,1)S(1)} %slice.197), channel_id=1, source_target_pairs={{0,2},{1,3},{2,0},{3,1},{4,6},{5,7},{6,4},{7,5},{8,10},{9,11},{10,... | collective-permute-start | bytes 2359304 | tf_op jit(solution)/shard_map/ppermute | solution.py:84
  236.1 18.7 %collective-permute-start.26 = (bf16[192,2048]{1,0:T(8,128)(2,1)S(1)}, bf16[192,2048]{1,0:T(8,128)(2,1)}, u32[]{:S(2)}, u32[]{:S(2)}) collective-permute-start(bf16[192,2048]{1,0:T(8,128)(2,1)S(1)} %slice.198), channel_id=1, source_target_pairs={{0,1},{1,0},{2,3},{3,2},{4,5},{5,4},{6,7},{7,6},{8,9},{9,8},{10,11... | collective-permute-start | bytes 2359304 | tf_op jit(solution)/shard_map/ppermute | solution.py:84
  254.8 46.4 %collective-permute-start.30 = (bf16[384,2048]{1,0:T(8,128)(2,1)}, bf16[384,2048]{1,0:T(8,128)(2,1)}, u32[]{:S(2)}, u32[]{:S(2)}) collective-permute-start(bf16[384,2048]{1,0:T(8,128)(2,1)} %bitcast.16.refs_1_.refs_0_), channel_id=1, source_target_pairs={{0,1},{1,0},{2,3},{3,2},{4,5},{5,4},{6,7},{7,6},{8,9},{9,8},{10,11... | collective-permute-start | bytes 4718600 | tf_op jit(solution)/shard_map/ppermute | solution.py:84
  255.8 47.1 %collective-permute-start.31 = (bf16[384,2048]{1,0:T(8,128)(2,1)}, bf16[384,2048]{1,0:T(8,128)(2,1)}, u32[]{:S(2)}, u32[]{:S(2)}) collective-permute-start(bf16[384,2048]{1,0:T(8,128)(2,1)} %bitcast.16.refs_1_.refs_0_), channel_id=1, source_target_pairs={{0,2},{1,3},{2,0},{3,1},{4,6},{5,7},{6,4},{7,5},{8,10},{9,11},{10,... | collective-permute-start | bytes 4718600 | tf_op jit(solution)/shard_map/ppermute | solution.py:84
  256.6 70.4 %collective-permute-start.32 = (bf16[384,2048]{1,0:T(8,128)(2,1)}, bf16[384,2048]{1,0:T(8,128)(2,1)}, u32[]{:S(2)}, u32[]{:S(2)}) collective-permute-start(bf16[384,2048]{1,0:T(8,128)(2,1)} %bitcast.16.refs_1_.refs_0_), channel_id=1, source_target_pairs={{0,3},{1,2},{2,1},{3,0},{4,7},{5,6},{6,5},{7,4},{8,11},{9,10},{10,... | collective-permute-start | bytes 4718600 | tf_op jit(solution)/shard_map/ppermute | solution.py:84
  299.4 94.3 %collective-permute-start.27 = (bf16[384,2048]{1,0:T(8,128)(2,1)}, bf16[384,2048]{1,0:T(8,128)(2,1)}, u32[]{:S(2)}, u32[]{:S(2)}) collective-permute-start(bf16[384,2048]{1,0:T(8,128)(2,1)} %get-tuple-element.111), channel_id=1, source_target_pairs={{0,1},{1,0},{2,3},{3,2},{4,5},{5,4},{6,7},{7,6},{8,9},{9,8},{10,11... | collective-permute-start | bytes 4718600 | tf_op jit(solution)/shard_map/ppermute | solution.py:84
  300.4 93.2 %collective-permute-start.28 = (bf16[384,2048]{1,0:T(8,128)(2,1)}, bf16[384,2048]{1,0:T(8,128)(2,1)}, u32[]{:S(2)}, u32[]{:S(2)}) collective-permute-start(bf16[384,2048]{1,0:T(8,128)(2,1)} %get-tuple-element.112), channel_id=1, source_target_pairs={{0,2},{1,3},{2,0},{3,1},{4,6},{5,7},{6,4},{7,5},{8,10},{9,11},{10,... | collective-permute-start | bytes 4718600 | tf_op jit(solution)/shard_map/ppermute | solution.py:84
  301.2 92.5 %collective-permute-start.29 = (bf16[384,2048]{1,0:T(8,128)(2,1)}, bf16[384,2048]{1,0:T(8,128)(2,1)}, u32[]{:S(2)}, u32[]{:S(2)}) collective-permute-start(bf16[384,2048]{1,0:T(8,128)(2,1)} %get-tuple-element.113), channel_id=1, source_target_pairs={{0,3},{1,2},{2,1},{3,0},{4,7},{5,6},{6,5},{7,4},{8,11},{9,10},{10,... | collective-permute-start | bytes 4718600 | tf_op jit(solution)/shard_map/ppermute | solution.py:84
  393.7 180.2 %reduce-scatter.5.cloned.1.call-start = ((), (), s32[]{:S(2)}) async-start(), calls=%async_computation.8 | async-start | bytes 9437184 | tf_op jit(solution)/shard_map/reduce_scatter | solution.py:835
  393.8 20.8 %collective-permute-start.36 = (bf16[192,2048]{1,0:T(8,128)(2,1)}, bf16[192,2048]{1,0:T(8,128)(2,1)S(1)}, u32[]{:S(2)}, u32[]{:S(2)}) collective-permute-start(bf16[192,2048]{1,0:T(8,128)(2,1)} %get-tuple-element.131), channel_id=1, source_target_pairs={{0,2},{1,3},{2,0},{3,1},{4,6},{5,7},{6,4},{7,5},{8,10},{9,11},{10,... | collective-permute-start | bytes 2359304 | tf_op jit(solution)/shard_map/ppermute | solution.py:84
  394.6 22.7 %collective-permute-start.34 = (bf16[192,2048]{1,0:T(8,128)(2,1)}, bf16[192,2048]{1,0:T(8,128)(2,1)S(1)}, u32[]{:S(2)}, u32[]{:S(2)}) collective-permute-start(bf16[192,2048]{1,0:T(8,128)(2,1)} %get-tuple-element.130), channel_id=1, source_target_pairs={{0,1},{1,0},{2,3},{3,2},{4,5},{5,4},{6,7},{7,6},{8,9},{9,8},{10,11... | collective-permute-start | bytes 2359304 | tf_op jit(solution)/shard_map/ppermute | solution.py:84
  395.6 48.4 %collective-permute-start.33 = (bf16[192,2048]{1,0:T(8,128)(2,1)}, bf16[192,2048]{1,0:T(8,128)(2,1)}, u32[]{:S(2)}, u32[]{:S(2)}) collective-permute-start(bf16[192,2048]{1,0:T(8,128)(2,1)} %get-tuple-element.126), channel_id=1, source_target_pairs={{0,1},{1,0},{2,3},{3,2},{4,5},{5,4},{6,7},{7,6},{8,9},{9,8},{10,11... | collective-permute-start | bytes 2359304 | tf_op jit(solution)/shard_map/ppermute | solution.py:84
  396.6 47.4 %collective-permute-start.38 = (bf16[192,2048]{1,0:T(8,128)(2,1)}, bf16[192,2048]{1,0:T(8,128)(2,1)}, u32[]{:S(2)}, u32[]{:S(2)}) collective-permute-start(bf16[192,2048]{1,0:T(8,128)(2,1)} %get-tuple-element.129), channel_id=1, source_target_pairs={{0,2},{1,3},{2,0},{3,1},{4,6},{5,7},{6,4},{7,5},{8,10},{9,11},{10,... | collective-permute-start | bytes 2359304 | tf_op jit(solution)/shard_map/ppermute | solution.py:84
  416.8 28.6 %collective-permute-start.37 = (bf16[192,2048]{1,0:T(8,128)(2,1)}, bf16[192,2048]{1,0:T(8,128)(2,1)}, u32[]{:S(2)}, u32[]{:S(2)}) collective-permute-start(bf16[192,2048]{1,0:T(8,128)(2,1)} %add_convert_fusion.5), channel_id=1, source_target_pairs={{0,1},{1,0},{2,3},{3,2},{4,5},{5,4},{6,7},{7,6},{8,9},{9,8},{10,11... | collective-permute-start | bytes 2359304 | tf_op jit(solution)/shard_map/ppermute | solution.py:84
  419.6 25.8 %collective-permute-start.35 = (bf16[192,2048]{1,0:T(8,128)(2,1)}, bf16[192,2048]{1,0:T(8,128)(2,1)}, u32[]{:S(2)}, u32[]{:S(2)}) collective-permute-start(bf16[192,2048]{1,0:T(8,128)(2,1)} %add_convert_fusion.6), channel_id=1, source_target_pairs={{0,2},{1,3},{2,0},{3,1},{4,6},{5,7},{6,4},{7,5},{8,10},{9,11},{10,... | collective-permute-start | bytes 2359304 | tf_op jit(solution)/shard_map/ppermute | solution.py:84
  445.4 164.6 %reduce-scatter.9.cloned.1.call-start = ((), (), s32[]{:S(2)}) async-start(), calls=%async_computation.10 | async-start | bytes 1310720 | tf_op jit(solution)/shard_map/reduce_scatter | solution.py:890
  458.6 7.2 %collective-permute-start.39 = (bf16[1024,2048]{1,0:T(8,128)(2,1)S(1)}, bf16[1024,2048]{1,0:T(8,128)(2,1)S(1)}, u32[]{:S(2)}, u32[]{:S(2)}) collective-permute-start(bf16[1024,2048]{1,0:T(8,128)(2,1)S(1)} %convolution_convert_fusion), channel_id=1, source_target_pairs={{0,4},{4,0},{8,12},{12,8},{16,20},{20,16},{24,28},{28,24},{1,5},{5... | collective-permute-start | bytes 12582920 | tf_op jit(solution)/shard_map/ppermute | solution.py:84
  470.4 33.7 %collective-permute-start.40 = (bf16[256,2048]{1,0:T(8,128)(2,1)}, bf16[256,2048]{1,0:T(8,128)(2,1)}, u32[]{:S(2)}, u32[]{:S(2)}) collective-permute-start(bf16[256,2048]{1,0:T(8,128)(2,1)} %get-tuple-element.203), channel_id=1, source_target_pairs={{0,1},{1,0},{2,3},{3,2},{4,5},{5,4},{6,7},{7,6},{8,9},{9,8},{10,11... | collective-permute-start | bytes 3145736 | tf_op jit(solution)/shard_map/ppermute | solution.py:84
  472.1 47.7 %collective-permute-start.41 = (bf16[256,2048]{1,0:T(8,128)(2,1)}, bf16[256,2048]{1,0:T(8,128)(2,1)}, u32[]{:S(2)}, u32[]{:S(2)}) collective-permute-start(bf16[256,2048]{1,0:T(8,128)(2,1)} %get-tuple-element.202), channel_id=1, source_target_pairs={{0,2},{1,3},{2,0},{3,1},{4,6},{5,7},{6,4},{7,5},{8,10},{9,11},{10,... | collective-permute-start | bytes 3145736 | tf_op jit(solution)/shard_map/ppermute | solution.py:84
  472.6 47.2 %collective-permute-start.42 = (bf16[256,2048]{1,0:T(8,128)(2,1)}, bf16[256,2048]{1,0:T(8,128)(2,1)}, u32[]{:S(2)}, u32[]{:S(2)}) collective-permute-start(bf16[256,2048]{1,0:T(8,128)(2,1)} %get-tuple-element.201), channel_id=1, source_target_pairs={{0,3},{1,2},{2,1},{3,0},{4,7},{5,6},{6,5},{7,4},{8,11},{9,10},{10,... | collective-permute-start | bytes 3145736 | tf_op jit(solution)/shard_map/ppermute | solution.py:84
  526.2 16.8 %collective-permute-start.43 = (bf16[1024,2048]{1,0:T(8,128)(2,1)}, bf16[1024,2048]{1,0:T(8,128)(2,1)}, u32[]{:S(2)}, u32[]{:S(2)}) collective-permute-start(bf16[1024,2048]{1,0:T(8,128)(2,1)} %ffn_weight.5), channel_id=1, source_target_pairs={{0,4},{4,0},{8,12},{12,8},{16,20},{20,16},{24,28},{28,24},{1,5},{5... | collective-permute-start | bytes 12582920 | tf_op jit(solution)/shard_map/ppermute | solution.py:84
  528.2 7.7 %collective-permute-start.44 = (bf16[3,2,1,512,256]{4,3,1,0,2:T(8,128)(2,1)S(1)}, bf16[3,2,1,512,256]{4,3,1,0,2:T(8,128)(2,1)S(1)}, u32[]{:S(2)}, u32[]{:S(2)}) collective-permute-start(bf16[3,2,1,512,256]{4,3,1,0,2:T(8,128)(2,1)S(1)} %bitcast_convert_fusion), channel_id=1, source_target_pairs={{0,4},{4,0},{8,12},{12,8},{16,20},{20,16},{24,28},{28,24},{1,5},{5... | collective-permute-start | bytes 4718600 | tf_op jit(solution)/shard_map/ppermute | solution.py:84
  538.4 13.5 %collective-permute-start.45 = (bf16[3,2,1,128,256]{4,3,2,1,0:T(8,128)(2,1)S(1)}, bf16[3,2,1,128,256]{4,3,2,1,0:T(8,128)(2,1)S(1)}, u32[]{:S(2)}, u32[]{:S(2)}) collective-permute-start(bf16[3,2,1,128,256]{4,3,2,1,0:T(8,128)(2,1)S(1)} %get-tuple-element.207), channel_id=1, source_target_pairs={{0,1},{1,0},{2,3},{3,2},{4,5},{5,4},{6,7},{7,6},{8,9},{9,8},{10,11... | collective-permute-start | bytes 1179656 | tf_op jit(solution)/shard_map/ppermute | solution.py:84
  538.5 16.0 %collective-permute-start.46 = (bf16[3,2,1,128,256]{4,3,2,1,0:T(8,128)(2,1)S(1)}, bf16[3,2,1,128,256]{4,3,2,1,0:T(8,128)(2,1)S(1)}, u32[]{:S(2)}, u32[]{:S(2)}) collective-permute-start(bf16[3,2,1,128,256]{4,3,2,1,0:T(8,128)(2,1)S(1)} %get-tuple-element.206), channel_id=1, source_target_pairs={{0,2},{1,3},{2,0},{3,1},{4,6},{5,7},{6,4},{7,5},{8,10},{9,11},{10,... | collective-permute-start | bytes 1179656 | tf_op jit(solution)/shard_map/ppermute | solution.py:84
  539.4 19.5 %collective-permute-start.47 = (bf16[3,2,1,128,256]{4,3,2,1,0:T(8,128)(2,1)S(1)}, bf16[3,2,1,128,256]{4,3,2,1,0:T(8,128)(2,1)S(1)}, u32[]{:S(2)}, u32[]{:S(2)}) collective-permute-start(bf16[3,2,1,128,256]{4,3,2,1,0:T(8,128)(2,1)S(1)} %get-tuple-element.205), channel_id=1, source_target_pairs={{0,3},{1,2},{2,1},{3,0},{4,7},{5,6},{6,5},{7,4},{8,11},{9,10},{10,... | collective-permute-start | bytes 1179656 | tf_op jit(solution)/shard_map/ppermute | solution.py:84
  550.9 40.7 %collective-permute-start.50 = (bf16[256,2048]{1,0:T(8,128)(2,1)}, bf16[256,2048]{1,0:T(8,128)(2,1)}, u32[]{:S(2)}, u32[]{:S(2)}) collective-permute-start(bf16[256,2048]{1,0:T(8,128)(2,1)} %get-tuple-element.148), channel_id=1, source_target_pairs={{0,1},{1,0},{2,3},{3,2},{4,5},{5,4},{6,7},{7,6},{8,9},{9,8},{10,11... | collective-permute-start | bytes 3145736 | tf_op jit(solution)/shard_map/ppermute | solution.py:84
  551.1 40.9 %collective-permute-start.51 = (bf16[256,2048]{1,0:T(8,128)(2,1)}, bf16[256,2048]{1,0:T(8,128)(2,1)}, u32[]{:S(2)}, u32[]{:S(2)}) collective-permute-start(bf16[256,2048]{1,0:T(8,128)(2,1)} %get-tuple-element.149), channel_id=1, source_target_pairs={{0,2},{1,3},{2,0},{3,1},{4,6},{5,7},{6,4},{7,5},{8,10},{9,11},{10,... | collective-permute-start | bytes 3145736 | tf_op jit(solution)/shard_map/ppermute | solution.py:84
  551.9 52.1 %collective-permute-start.52 = (bf16[256,2048]{1,0:T(8,128)(2,1)}, bf16[256,2048]{1,0:T(8,128)(2,1)}, u32[]{:S(2)}, u32[]{:S(2)}) collective-permute-start(bf16[256,2048]{1,0:T(8,128)(2,1)} %get-tuple-element.150), channel_id=1, source_target_pairs={{0,3},{1,2},{2,1},{3,0},{4,7},{5,6},{6,5},{7,4},{8,11},{9,10},{10,... | collective-permute-start | bytes 3145736 | tf_op jit(solution)/shard_map/ppermute | solution.py:84
  577.2 66.6 %reduce-scatter.11.cloned.1.call-start = ((), (), s32[]{:S(2)}) async-start(), calls=%async_computation.11 | async-start | bytes 1474560 | tf_op jit(solution)/shard_map/reduce_scatter | solution.py:890
  579.2 28.9 %collective-permute-start.53 = (bf16[32,2048]{1,0:T(8,128)(2,1)S(1)}, bf16[32,2048]{1,0:T(8,128)(2,1)S(1)}, u32[]{:S(2)}, u32[]{:S(2)}) collective-permute-start(bf16[32,2048]{1,0:T(8,128)(2,1)S(1)} %get-tuple-element.228), channel_id=1, source_target_pairs={{0,1},{1,0},{2,3},{3,2},{4,5},{5,4},{6,7},{7,6},{8,9},{9,8},{10,11... | collective-permute-start | bytes 393224 | tf_op jit(solution)/shard_map/ppermute | solution.py:84
  580.7 27.4 %collective-permute-start.54 = (bf16[32,2048]{1,0:T(8,128)(2,1)S(1)}, bf16[32,2048]{1,0:T(8,128)(2,1)S(1)}, u32[]{:S(2)}, u32[]{:S(2)}) collective-permute-start(bf16[32,2048]{1,0:T(8,128)(2,1)S(1)} %get-tuple-element.227), channel_id=1, source_target_pairs={{0,2},{1,3},{2,0},{3,1},{4,6},{5,7},{6,4},{7,5},{8,10},{9,11},{10,... | collective-permute-start | bytes 393224 | tf_op jit(solution)/shard_map/ppermute | solution.py:84
  591.6 17.2 %collective-permute-start.55 = (bf16[32,2048]{1,0:T(8,128)(2,1)S(1)}, bf16[32,2048]{1,0:T(8,128)(2,1)S(1)}, u32[]{:S(2)}, u32[]{:S(2)}) collective-permute-start(bf16[32,2048]{1,0:T(8,128)(2,1)S(1)} %get-tuple-element.226), channel_id=1, source_target_pairs={{0,3},{1,2},{2,1},{3,0},{4,7},{5,6},{6,5},{7,4},{8,11},{9,10},{10,... | collective-permute-start | bytes 393224 | tf_op jit(solution)/shard_map/ppermute | solution.py:84
  611.5 5.1 collective-permute-start.58
  616.6 13.0 %collective-permute-start.59 = (f32[177,128]{1,0:T(8,128)S(1)}, f32[177,128]{1,0:T(8,128)S(1)}, u32[]{:S(2)}, u32[]{:S(2)}) collective-permute-start(f32[177,128]{1,0:T(8,128)S(1)} %fusion.43), channel_id=1, source_target_pairs={{0,16},{4,20},{8,24},{12,28},{16,0},{20,4},{24,8},{28,12},{1,17},{... | collective-permute-start | bytes 271880 | tf_op jit(solution)/shard_map/ppermute | solution.py:84
  629.6 14.1 %collective-permute-start.60 = (f32[177,128]{1,0:T(8,128)S(1)}, f32[177,128]{1,0:T(8,128)S(1)}, u32[]{:S(2)}, u32[]{:S(2)}) collective-permute-start(f32[177,128]{1,0:T(8,128)S(1)} %add.495), channel_id=1, source_target_pairs={{0,1},{1,0},{2,3},{3,2},{4,5},{5,4},{6,7},{7,6},{8,9},{9,8},{10,11... | collective-permute-start | bytes 271880 | tf_op jit(solution)/shard_map/ppermute | solution.py:84
  (71 other events, 685.3 us)
Sparse Core Ops, SparseCore 0:
  12.5 34.6 all-gather.4
  48.7 32.1 all-gather.6
  82.5 83.4 all-gather.8
  167.5 80.6 all-gather.10
  393.8 89.9 reduce-scatter.6
  485.9 87.9 reduce-scatter.4
  577.4 32.4 reduce-scatter.8
  612.3 30.5 reduce-scatter.10
